TPU v7x, 128 devices: a whole 4x4x4 slice. The times are simulated.
128 devices in a mesh: row: 16 (over x, y), col: 8 (over z, core).
Axes of the slice: x: 4, y: 4, z: 4, core: 2. Of those that a mesh axis runs over, the one named last changes fastest.
Arguments:
- panels: bfloat16 [8192, 8192], P('row', 'col'), may hold values from -0.125 to 0.125
- scaling: float32 [8192], P('col'), may hold values from 0.1 to 10
- tile_mask: int32 [32, 32], P('row'), may hold values 0 or 1
- owner_rows: int32 [32, 32], P('row', 'col'), may hold values from 0 to 15, as said below
Outputs:
- assembled: bfloat16 [256, 8, 256, 256], P('row', 'col')
Inputs may be any that keep to these rules, and one draw needn't show every extreme that they name: `owner_rows`: within each block of 2 x 4 tiles (block rows r * 2 to (r+1) * 2 - 1, block columns c * 4 to (c+1) * 4 - 1), the 8 tiles name 8 distinct owner rows (no owner row is named by more than 1 tile).
All inputs are finite; a program needn't handle non-finite values. No bound on the sum of `tile_mask` on one device may be relied on, other than what follows from the above.
Results may differ from a plain program's by a relative error of at most 0.0053.
Values may be sent and summed in bfloat16 or wider, within the bound.
No kernel may reach another device: no remote copies, remote signals or barrier semaphores. Data moves between devices by JAX's collectives and lax.ppermute only.
A program may use at most 128 MiB of HBM per device.

v0:
```python
import jax
import jax.numpy as jnp
from jax import lax
from jax.experimental import pallas as pl
from jax.experimental.pallas import tpu as pltpu
from jax.sharding import PartitionSpec as P


TILE = 256
HALF = 128


def along_y(step):
    return [(4 * x + y, 4 * x + (y + step) % 4) for x in range(4) for y in range(4)]


def along_x(step):
    return [(4 * x + y, 4 * ((x + step) % 4) + y) for x in range(4) for y in range(4)]


def along_z(step):
    return [(2 * z + k, 2 * ((z + step) % 4) + k) for z in range(4) for k in range(2)]


SWAP = [(c, c ^ 1) for c in range(8)]


def block_round(m):
    pairs = []
    for x in range(4):
        for y in range(4):
            for z in range(4):
                for k in range(2):
                    u = 2 * (y % 2) + k
                    source = (4 * x + y) * 8 + 2 * z + k
                    target = (4 * x + (u + m) % 4) * 8 + 2 * z + y // 2
                    pairs.append((source, target))
    return pairs


def position():
    row, col = lax.axis_index("row"), lax.axis_index("col")
    return row >> 2, row & 3, col >> 1, col & 1


def scale_body(mask_hbm, panels_hbm, scaling_hbm, mine_ref, swap_ref, top_ref, low_ref, *scratch):
    mask_ref, panels_ref, scaling_ref, sems = scratch
    _, _, z, k = position()
    copies = [
        pltpu.make_async_copy(panels_hbm.at[pl.ds(0, TILE)], panels_ref.at[pl.ds(0, TILE)], sems.at[0]),
        pltpu.make_async_copy(panels_hbm.at[pl.ds(TILE, TILE)], panels_ref.at[pl.ds(TILE, TILE)], sems.at[1]),
        pltpu.make_async_copy(scaling_hbm, scaling_ref, sems.at[2]),
        pltpu.make_async_copy(mask_hbm, mask_ref, sems.at[3]),
    ]
    for copy in copies:
        copy.start()
    copies[3].wait()
    copies[2].wait()
    root = jnp.sqrt(scaling_ref[...])
    for i in range(2):
        copies[i].wait()
        for b in range(4):
            rows, cols = pl.ds(i * TILE, TILE), pl.ds(b * TILE, TILE)
            mask = mask_ref[i, 4 * (2 * z + k) + b].astype(jnp.float32)
            tile = (
                panels_ref[rows, cols].astype(jnp.float32) * mask * root[:, b * TILE : (b + 1) * TILE]
            ).astype(jnp.bfloat16)
            top_ref[pl.ds(i * HALF, HALF), cols] = tile[:HALF]
            low_ref[pl.ds(i * HALF, HALF), cols] = tile[HALF:]

            @pl.when(k == i)
            def _():
                mine_ref[:, cols] = tile

            @pl.when(k != i)
            def _():
                swap_ref[:, cols] = tile


def scale(tile_mask, panels, scaling):
    part = jax.ShapeDtypeStruct((TILE, panels.shape[1]), jnp.bfloat16)
    return pl.pallas_call(
        scale_body,
        out_shape=(part, part, part, part),
        in_specs=[pl.BlockSpec(memory_space=pltpu.HBM)] * 3,
        out_specs=tuple(pl.BlockSpec(memory_space=pltpu.VMEM) for _ in range(4)),
        scratch_shapes=[
            pltpu.SMEM(tile_mask.shape, jnp.int32),
            pltpu.VMEM(panels.shape, jnp.bfloat16),
            pltpu.VMEM((1, panels.shape[1]), jnp.float32),
            pltpu.SemaphoreType.DMA((4,)),
        ],
        compiler_params=pltpu.CompilerParams(vmem_limit_bytes=12 * 1024 * 1024),
        name="scale",
    )(tile_mask, panels, scaling.reshape(1, -1))


def product_body(*refs):
    rows, cols, outs = refs[:8], refs[8:16], refs[16:24]
    rows_ref, cols_ref, row_sems, col_sems = refs[24:]
    x, y, z, k = position()
    u = 2 * (y % 2) + k
    copies = []
    for d in range(4):
        for h in range(2):
            across = pl.ds(1024 * h, 1024)
            copies.append(
                pltpu.make_async_copy(
                    cols[2 * d + h], cols_ref.at[(x + d) % 4, :, across], col_sems.at[2 * d + h]
                )
            )
            copies.append(
                pltpu.make_async_copy(
                    rows[2 * d + h], rows_ref.at[(y + d - u + 4) % 4, :, across], row_sems.at[2 * d + h]
                )
            )
    for copy in copies:
        copy.start()
    for copy in copies:
        copy.wait()
    for at, d in enumerate((2, 1, 3, 0)):
        right = cols_ref[(z + d) % 4]
        for m in range(4):
            out = outs[2 * at + m // 2]
            out[m % 2] = lax.dot_general(
                rows_ref[m], right, (((1,), (1,)), ((), ())), preferred_element_type=jnp.float32
            ).astype(out.dtype)


def product(rows, cols):
    sent = jax.ShapeDtypeStruct((2, TILE, TILE), jnp.bfloat16)
    kept = jax.ShapeDtypeStruct((2, TILE, TILE), jnp.float32)
    return pl.pallas_call(
        product_body,
        out_shape=(sent,) * 6 + (kept,) * 2,
        in_specs=[pl.BlockSpec(memory_space=pl.ANY)] * 16,
        out_specs=tuple(pl.BlockSpec(memory_space=pltpu.VMEM) for _ in range(8)),
        scratch_shapes=[
            pltpu.VMEM((4, TILE, 2048), jnp.bfloat16),
            pltpu.VMEM((4, TILE, 2048), jnp.bfloat16),
            pltpu.SemaphoreType.DMA((8,)),
            pltpu.SemaphoreType.DMA((8,)),
        ],
        compiler_params=pltpu.CompilerParams(vmem_limit_bytes=32 * 1024 * 1024),
        name="product",
    )(*rows, *cols)


def pack_body(owners_ref, *refs):
    arrived, out_ref, sems = refs[:4], refs[4], refs[5]
    _, y, _, _ = position()
    out_ref[...] = jnp.zeros_like(out_ref)
    copies = []
    for m in range(4):
        column = (y - m + 4) % 4
        for i in range(2):
            copies.append(
                pltpu.make_async_copy(
                    arrived[m].at[pl.ds(i * HALF, HALF)],
                    out_ref.at[owners_ref[i, column], 0],
                    sems.at[2 * m + i],
                )
            )
    for copy in copies:
        copy.start()
    for copy in copies:
        copy.wait()


def pack(owners, arrived):
    return pl.pallas_call(
        pack_body,
        out_shape=jax.ShapeDtypeStruct((16, 1, HALF, TILE), jnp.bfloat16),
        in_specs=[pl.BlockSpec(memory_space=pltpu.SMEM)] + [pl.BlockSpec(memory_space=pl.ANY)] * 4,
        out_specs=pl.BlockSpec(memory_space=pltpu.VMEM),
        scratch_shapes=[pltpu.SemaphoreType.DMA((8,))],
        compiler_params=pltpu.CompilerParams(vmem_limit_bytes=4 * 1024 * 1024),
        name="pack",
    )(owners, *arrived)


def ypass(value, step):
    return lax.ppermute(value, "row", along_y(step))


def xpass(value, step):
    return lax.ppermute(value, "row", along_x(step))


def zpass(value, step):
    return lax.ppermute(value, "col", along_z(step))


def swap(value):
    return lax.ppermute(value, "col", SWAP)


def add(*parts):
    return sum(part.astype(jnp.float32) for part in parts).astype(jnp.bfloat16)


def reduce_along_z(partials):
    opp_a, opp_b, next_a, next_b, prev_a, prev_b, own_a, own_b = partials
    opp_up, opp_down = zpass(opp_a, 1), zpass(opp_b, -1)
    far_b, far_a = zpass(next_b, 1), zpass(prev_a, -1)
    sum_a = zpass(add(next_a, opp_up), 1)
    sum_b = zpass(add(prev_b, opp_down), -1)
    return tuple(
        add(own[m], far[m], total[m])
        for own, far, total in ((own_a, far_a, sum_a), (own_b, far_b, sum_b))
        for m in range(2)
    )


def to_blocks(rounds):
    return [lax.ppermute(rounds[m], ("row", "col"), block_round(m)) for m in range(4)]


def to_owners(owners, arrived):
    outgoing = pack(owners, arrived)
    return lax.all_to_all(outgoing, "row", split_axis=0, concat_axis=0, tiled=True)


def shards(panels, scaling, tile_mask, owner_rows):
    c0, other, top, low = scale(tile_mask, panels, scaling)
    c1 = swap(other)
    cm0, cp0 = xpass(c0, 1), xpass(c0, -1)
    top_m, low_p = ypass(top, 1), ypass(low, -1)
    cp1, cm1 = xpass(c1, -1), xpass(c1, 1)
    low_m, top_p = ypass(low, 1), ypass(top, -1)
    co0, co1 = xpass(cm0, 1), xpass(cp1, -1)
    top_o, low_o = ypass(top_m, 1), ypass(low_p, -1)
    cols = (c0, c1, cp0, cp1, co0, co1, cm0, cm1)
    halves = []
    for pieces in ((top, top_p, top_o, top_m), (low, low_p, low_o, low_m)):
        rows = [piece for value in pieces for piece in (value, swap(value))]
        halves.append(product(rows, cols))
    rounds = reduce_along_z(halves[0])
    *rounds, later = lax.optimization_barrier((*rounds, halves[1]))
    arrived = to_blocks(rounds)
    first = to_owners(owner_rows, arrived)
    arrived = to_blocks(reduce_along_z(later))
    second = to_owners(owner_rows, arrived)
    return jnp.concatenate((first, second), axis=2)


def solution(mesh):
    placed = (P("row", "col"), P("col"), P("row", None), P("row", "col"))
    return jax.shard_map(
        shards, mesh=mesh, in_specs=placed, out_specs=P("row", "col", None, None), check_vma=False
    )
```

profile of v0, /device:TPU:0, one launch (start us, length us, event | category | flops | bytes accessed | tf_op | source)
XLA Modules:
  0.0 159.3 jit_solution(13579746519568327213)
XLA Ops:
  3.7 1.8 %collective-permute-start.3 = (bf16[256,1024]{1,0:T(8,128)(2,1)S(1)}, bf16[256,1024]{1,0:T(8,128)(2,1)S(1)}, u32[]{:S(2)}, u32[]{:S(2)}) collective-permute-start(bf16[256,1024]{1,0:T(8,128)(2,1)S(1)} %get-tuple-element.37.refs_0_), channel_id=1, source_target_pairs={{0,8},{8,16},{16,24},{24,0},{32,40},{40,48},{48,56},{56,32},{64,72... | collective-permute-start | bytes 1572872 | tf_op jit(solution)/shard_map/ppermute | solution.py:183
  8.7 1.7 %collective-permute-start.8 = (bf16[256,1024]{1,0:T(8,128)(2,1)S(1)}, bf16[256,1024]{1,0:T(8,128)(2,1)S(1)}, u32[]{:S(2)}, u32[]{:S(2)}) collective-permute-start(bf16[256,1024]{1,0:T(8,128)(2,1)S(1)} %get-tuple-element.38.refs_8_), channel_id=1, source_target_pairs={{0,96},{8,104},{16,112},{24,120},{32,0},{40,8},{48,16},{56,24},{64... | collective-permute-start | bytes 1572872 | tf_op jit(solution)/shard_map/ppermute | solution.py:187
  10.3 9.1 %collective-permute-done.3.refs_6_ = bf16[256,1024]{1,0:T(8,128)(2,1)S(1)} collective-permute-done((bf16[256,1024]{1,0:T(8,128)(2,1)S(1)}, bf16[256,1024]{1,0:T(8,128)(2,1)S(1)}, u32[]{:S(2)}, u32[]{:S(2)}) %collective-permute-start.3) | collective-permute-done | bytes 524320 | tf_op jit(solution)/shard_map/ppermute | solution.py:183
  19.5 1.7 %collective-permute-start.21 = (bf16[256,1024]{1,0:T(8,128)(2,1)S(1)}, bf16[256,1024]{1,0:T(8,128)(2,1)S(1)}, u32[]{:S(2)}, u32[]{:S(2)}) collective-permute-start(bf16[256,1024]{1,0:T(8,128)(2,1)S(1)} %get-tuple-element.48.refs_0_), channel_id=1, source_target_pairs={{0,24},{8,0},{16,8},{24,16},{32,56},{40,32},{48,40},{56,48},{64,88... | collective-permute-start | bytes 1572872 | tf_op jit(solution)/shard_map/ppermute | solution.py:183
  22.7 1.7 %collective-permute-start.9 = (bf16[256,1024]{1,0:T(8,128)(2,1)S(1)}, bf16[256,1024]{1,0:T(8,128)(2,1)S(1)}, u32[]{:S(2)}, u32[]{:S(2)}) collective-permute-start(bf16[256,1024]{1,0:T(8,128)(2,1)S(1)} %collective-permute-done.7.refs_9_), channel_id=1, source_target_pairs={{0,96},{8,104},{16,112},{24,120},{32,0},{40,8},{48,16},{56,24},{64... | collective-permute-start | bytes 1572872 | tf_op jit(solution)/shard_map/ppermute | solution.py:187
  24.7 8.3 %collective-permute-done.21.refs_2_ = bf16[256,1024]{1,0:T(8,128)(2,1)S(1)} collective-permute-done((bf16[256,1024]{1,0:T(8,128)(2,1)S(1)}, bf16[256,1024]{1,0:T(8,128)(2,1)S(1)}, u32[]{:S(2)}, u32[]{:S(2)}) %collective-permute-start.21) | collective-permute-done | bytes 524320 | tf_op jit(solution)/shard_map/ppermute | solution.py:183
  33.0 2.5 %collective-permute-done.13.refs_15_ = bf16[256,1024]{1,0:T(8,128)(2,1)S(1)} collective-permute-done((bf16[256,1024]{1,0:T(8,128)(2,1)S(1)}, bf16[256,1024]{1,0:T(8,128)(2,1)S(1)}, u32[]{:S(2)}, u32[]{:S(2)}) %collective-permute-start.13) | collective-permute-done | bytes 524320 | tf_op jit(solution)/shard_map/ppermute | solution.py:187
  35.8 3.0 %collective-permute-start.12 = (bf16[256,1024]{1,0:T(8,128)(2,1)S(1)}, bf16[256,1024]{1,0:T(8,128)(2,1)S(1)}, u32[]{:S(2)}, u32[]{:S(2)}) collective-permute-start(bf16[256,1024]{1,0:T(8,128)(2,1)S(1)} %collective-permute-done.9.refs_11_), channel_id=1, source_target_pairs={{0,96},{8,104},{16,112},{24,120},{32,0},{40,8},{48,16},{56,24},{64... | collective-permute-start | bytes 1572872 | tf_op jit(solution)/shard_map/ppermute | solution.py:187
  39.3 2.8 %collective-permute-start.23 = (bf16[256,1024]{1,0:T(8,128)(2,1)S(1)}, bf16[256,1024]{1,0:T(8,128)(2,1)S(1)}, u32[]{:S(2)}, u32[]{:S(2)}) collective-permute-start(bf16[256,1024]{1,0:T(8,128)(2,1)S(1)} %collective-permute-done.21.refs_2_), channel_id=1, source_target_pairs={{0,24},{8,0},{16,8},{24,16},{32,56},{40,32},{48,40},{56,48},{64,88... | collective-permute-start | bytes 1572872 | tf_op jit(solution)/shard_map/ppermute | solution.py:183
  42.1 6.9 %collective-permute-done.11.refs_12_ = bf16[256,1024]{1,0:T(8,128)(2,1)S(1)} collective-permute-done((bf16[256,1024]{1,0:T(8,128)(2,1)S(1)}, bf16[256,1024]{1,0:T(8,128)(2,1)S(1)}, u32[]{:S(2)}, u32[]{:S(2)}) %collective-permute-start.11) | collective-permute-done | bytes 524320 | tf_op jit(solution)/shard_map/ppermute | solution.py:187
  49.0 5.5 %product.2 = (bf16[2,256,256]{2,1,0:T(8,128)(2,1)S(1)}, bf16[2,256,256]{2,1,0:T(8,128)(2,1)S(1)}, bf16[2,256,256]{2,1,0:T(8,128)(2,1)S(1)}, bf16[2,256,256]{2,1,...) custom-call(bf16[256,1024]{1,0:T(8,128)(2,1)S(1)} %get-tuple-element, ...), custom_call_target="tpu_custom_call" | custom-call | tf_op jit(solution)/shard_map/product/pallas_call | solution.py:133
  54.5 2.0 %collective-permute-start.15 = (bf16[2,256,256]{2,1,0:T(8,128)(2,1)S(1)}, bf16[2,256,256]{2,1,0:T(8,128)(2,1)S(1)}, u32[]{:S(2)}, u32[]{:S(2)}) collective-permute-start(bf16[2,256,256]{2,1,0:T(8,128)(2,1)S(1)} %get-tuple-element.43), channel_id=1, source_target_pairs={{0,2},{1,3},{2,4},{3,5},{4,6},{5,7},{6,0},{7,1},{8,10},{9,11},{10,... | collective-permute-start | bytes 786440 | tf_op jit(solution)/shard_map/ppermute | solution.py:191
  57.0 2.3 %collective-permute-start.18 = (bf16[2,256,256]{2,1,0:T(8,128)(2,1)S(1)}, bf16[2,256,256]{2,1,0:T(8,128)(2,1)S(1)}, u32[]{:S(2)}, u32[]{:S(2)}) collective-permute-start(bf16[2,256,256]{2,1,0:T(8,128)(2,1)S(1)} %get-tuple-element.47), channel_id=1, source_target_pairs={{0,6},{1,7},{2,0},{3,1},{4,2},{5,3},{6,4},{7,5},{8,14},{9,15},{10,... | collective-permute-start | bytes 786440 | tf_op jit(solution)/shard_map/ppermute | solution.py:191
  59.3 6.3 %collective-permute-done.15 = bf16[2,256,256]{2,1,0:T(8,128)(2,1)S(1)} collective-permute-done((bf16[2,256,256]{2,1,0:T(8,128)(2,1)S(1)}, bf16[2,256,256]{2,1,0:T(8,128)(2,1)S(1)}, u32[]{:S(2)}, u32[]{:S(2)}) %collective-permute-start.15) | collective-permute-done | bytes 262176 | tf_op jit(solution)/shard_map/ppermute | solution.py:191
  65.6 2.0 %collective-permute-start.14 = (bf16[2,256,256]{2,1,0:T(8,128)(2,1)S(1)}, bf16[2,256,256]{2,1,0:T(8,128)(2,1)S(1)}, u32[]{:S(2)}, u32[]{:S(2)}) collective-permute-start(bf16[2,256,256]{2,1,0:T(8,128)(2,1)S(1)} %get-tuple-element.41), channel_id=1, source_target_pairs={{0,6},{1,7},{2,0},{3,1},{4,2},{5,3},{6,4},{7,5},{8,14},{9,15},{10,... | collective-permute-start | bytes 786440 | tf_op jit(solution)/shard_map/ppermute | solution.py:191
  69.1 2.2 %collective-permute-start.19 = (bf16[2,256,256]{2,1,0:T(8,128)(2,1)S(1)}, bf16[2,256,256]{2,1,0:T(8,128)(2,1)S(1)}, u32[]{:S(2)}, u32[]{:S(2)}) collective-permute-start(bf16[2,256,256]{2,1,0:T(8,128)(2,1)S(1)} %add_convert_fusion.2), channel_id=1, source_target_pairs={{0,6},{1,7},{2,0},{3,1},{4,2},{5,3},{6,4},{7,5},{8,14},{9,15},{10,... | collective-permute-start | bytes 786440 | tf_op jit(solution)/shard_map/ppermute | solution.py:191
  71.3 5.4 %product.3 = (bf16[2,256,256]{2,1,0:T(8,128)(2,1)S(1)}, bf16[2,256,256]{2,1,0:T(8,128)(2,1)S(1)}, bf16[2,256,256]{2,1,0:T(8,128)(2,1)S(1)}, bf16[2,256,256]{2,1,...) custom-call(bf16[256,1024]{1,0:T(8,128)(2,1)S(1)} %get-tuple-element, ...), custom_call_target="tpu_custom_call" | custom-call | tf_op jit(solution)/shard_map/product/pallas_call | solution.py:133
  78.1 4.8 %collective-permute-done.17 = bf16[2,256,256]{2,1,0:T(8,128)(2,1)S(1)} collective-permute-done((bf16[2,256,256]{2,1,0:T(8,128)(2,1)S(1)}, bf16[2,256,256]{2,1,0:T(8,128)(2,1)S(1)}, u32[]{:S(2)}, u32[]{:S(2)}) %collective-permute-start.17) | collective-permute-done | bytes 262176 | tf_op jit(solution)/shard_map/ppermute | solution.py:191
  83.7 4.4 %collective-permute-start.28 = (bf16[256,256]{1,0:T(8,128)(2,1)S(1)}, bf16[256,256]{1,0:T(8,128)(2,1)S(1)}, u32[]{:S(2)}, u32[]{:S(2)}) collective-permute-start(bf16[256,256]{1,0:T(8,128)(2,1)S(1)} %get-tuple-element.58), channel_id=1, source_target_pairs={{0,8},{1,16},{2,10},{3,18},{4,12},{5,20},{6,14},{7,22},{8,24},{9,0... | collective-permute-start | bytes 393224 | tf_op jit(solution)/shard_map/ppermute | solution.py:216
  88.2 3.8 %collective-permute-start.29 = (bf16[256,256]{1,0:T(8,128)(2,1)S(1)}, bf16[256,256]{1,0:T(8,128)(2,1)S(1)}, u32[]{:S(2)}, u32[]{:S(2)}) collective-permute-start(bf16[256,256]{1,0:T(8,128)(2,1)S(1)} %get-tuple-element.59), channel_id=1, source_target_pairs={{0,16},{1,24},{2,18},{3,26},{4,20},{5,28},{6,22},{7,30},{8,0},{9,8... | collective-permute-start | bytes 393224 | tf_op jit(solution)/shard_map/ppermute | solution.py:216
  91.9 2.4 %collective-permute-start.30 = (bf16[256,256]{1,0:T(8,128)(2,1)S(1)}, bf16[256,256]{1,0:T(8,128)(2,1)S(1)}, u32[]{:S(2)}, u32[]{:S(2)}) collective-permute-start(bf16[256,256]{1,0:T(8,128)(2,1)S(1)} %get-tuple-element.60), channel_id=1, source_target_pairs={{0,24},{1,0},{2,26},{3,2},{4,28},{5,4},{6,30},{7,6},{8,8},{9,16},{... | collective-permute-start | bytes 393224 | tf_op jit(solution)/shard_map/ppermute | solution.py:216
  94.3 3.0 %collective-permute-start.37 = (bf16[2,256,256]{2,1,0:T(8,128)(2,1)S(1)}, bf16[2,256,256]{2,1,0:T(8,128)(2,1)S(1)}, u32[]{:S(2)}, u32[]{:S(2)}) collective-permute-start(bf16[2,256,256]{2,1,0:T(8,128)(2,1)S(1)} %get-tuple-element.68), channel_id=1, source_target_pairs={{0,6},{1,7},{2,0},{3,1},{4,2},{5,3},{6,4},{7,5},{8,14},{9,15},{10,... | collective-permute-start | bytes 786440 | tf_op jit(solution)/shard_map/ppermute | solution.py:191
  97.4 2.3 %pack.2 = bf16[16,1,128,256]{3,2,1,0:T(8,128)(2,1)} custom-call(s32[2,4]{1,0:T(2,128)S(1)} %copy-done.2, bf16[256,256]{1,0:T(8,128)(2,1)S(1)} %collective-permute-done.27.refs_0_, bf16[256,256]{1,0:T(8,128)(2,1)S(1)} %collective-permute-done.28.refs_1_, bf16[256,256]{1,0:T(8,128)(2,1)S(1)} %collective-permute-done.29.refs_2_, ...), custom_call_target="tpu_custom_call" | custom-call | tf_op jit(solution)/shard_map/pack/pallas_call | solution.py:171
  99.8 5.3 %all-to-all-start = ((bf16[16,1,128,256]{3,2,1,0:T(8,128)(2,1)}), bf16[16,1,128,256]{3,2,1,0:T(8,128)(2,1)}, u32[]{:S(2)}, u32[]{:S(2)}) async-start(bf16[16,1,128,256]{3,2,1,0:T(8,128)(2,1)} %pack.2), calls=%async_computation | async-start | bytes 2097152 | tf_op jit(solution)/shard_map/all_to_all | solution.py:221
  107.0 2.6 %collective-permute-start.38 = (bf16[2,256,256]{2,1,0:T(8,128)(2,1)S(1)}, bf16[2,256,256]{2,1,0:T(8,128)(2,1)S(1)}, u32[]{:S(2)}, u32[]{:S(2)}) collective-permute-start(bf16[2,256,256]{2,1,0:T(8,128)(2,1)S(1)} %add_convert_fusion), channel_id=1, source_target_pairs={{0,6},{1,7},{2,0},{3,1},{4,2},{5,3},{6,4},{7,5},{8,14},{9,15},{10,... | collective-permute-start | bytes 786440 | tf_op jit(solution)/shard_map/ppermute | solution.py:191
  109.6 6.0 %collective-permute-done.33 = bf16[2,256,256]{2,1,0:T(8,128)(2,1)S(1)} collective-permute-done((bf16[2,256,256]{2,1,0:T(8,128)(2,1)S(1)}, bf16[2,256,256]{2,1,0:T(8,128)(2,1)S(1)}, u32[]{:S(2)}, u32[]{:S(2)}) %collective-permute-start.33) | collective-permute-done | bytes 262176 | tf_op jit(solution)/shard_map/ppermute | solution.py:191
  115.7 3.8 %collective-permute-start.35 = (bf16[256,256]{1,0:T(8,128)(2,1)S(1)}, bf16[256,256]{1,0:T(8,128)(2,1)S(1)}, u32[]{:S(2)}, u32[]{:S(2)}) collective-permute-start(bf16[256,256]{1,0:T(8,128)(2,1)S(1)} %get-tuple-element.71), channel_id=1, source_target_pairs={{0,8},{1,16},{2,10},{3,18},{4,12},{5,20},{6,14},{7,22},{8,24},{9,0... | collective-permute-start | bytes 393224 | tf_op jit(solution)/shard_map/ppermute | solution.py:216
  120.3 4.4 %collective-permute-start.40 = (bf16[256,256]{1,0:T(8,128)(2,1)S(1)}, bf16[256,256]{1,0:T(8,128)(2,1)S(1)}, u32[]{:S(2)}, u32[]{:S(2)}) collective-permute-start(bf16[256,256]{1,0:T(8,128)(2,1)S(1)} %get-tuple-element.69), channel_id=1, source_target_pairs={{0,24},{1,0},{2,26},{3,2},{4,28},{5,4},{6,30},{7,6},{8,8},{9,16},{... | collective-permute-start | bytes 393224 | tf_op jit(solution)/shard_map/ppermute | solution.py:216
  124.7 3.6 %collective-permute-start.39 = (bf16[256,256]{1,0:T(8,128)(2,1)S(1)}, bf16[256,256]{1,0:T(8,128)(2,1)S(1)}, u32[]{:S(2)}, u32[]{:S(2)}) collective-permute-start(bf16[256,256]{1,0:T(8,128)(2,1)S(1)} %get-tuple-element.70), channel_id=1, source_target_pairs={{0,16},{1,24},{2,18},{3,26},{4,20},{5,28},{6,22},{7,30},{8,0},{9,8... | collective-permute-start | bytes 393224 | tf_op jit(solution)/shard_map/ppermute | solution.py:216
  128.3 2.5 %collective-permute-done.39.refs_2_ = bf16[256,256]{1,0:T(8,128)(2,1)S(1)} collective-permute-done((bf16[256,256]{1,0:T(8,128)(2,1)S(1)}, bf16[256,256]{1,0:T(8,128)(2,1)S(1)}, u32[]{:S(2)}, u32[]{:S(2)}) %collective-permute-start.39) | collective-permute-done | bytes 131104 | tf_op jit(solution)/shard_map/ppermute | solution.py:216
  132.2 24.4 %all_to_all.10 = bf16[16,1,128,256]{3,2,1,0:T(8,128)(2,1)S(1)} all-to-all(bf16[16,1,128,256]{3,2,1,0:T(8,128)(2,1)S(1)} %pack.3), channel_id=1, replica_groups=mesh['row'=16,'col'=8] {'row'}, dimensions={0} | all-to-all | bytes 2097152 | tf_op jit(solution)/shard_map/all_to_all | solution.py:221
  156.6 2.7 %pad_maximum_fusion = bf16[16,1,256,256]{3,2,1,0:T(8,128)(2,1)} fusion(bf16[16,1,128,256]{3,2,1,0:T(8,128)(2,1)S(1)} %all_to_all.10, bf16[16,1,128,256]{3,2,1,0:T(8,128)(2,1)} %all-to-all-done), kind=kLoop, calls=%fused_computation | loop fusion | flops 4194304 | bytes 4194304 | tf_op jit(solution)/shard_map/concatenate | solution.py:244
  (75 shorter events, 18.0 us)
Async XLA Ops:
  3.7 15.7 %collective-permute-start.3 = (bf16[256,1024]{1,0:T(8,128)(2,1)S(1)}, bf16[256,1024]{1,0:T(8,128)(2,1)S(1)}, u32[]{:S(2)}, u32[]{:S(2)}) collective-permute-start(bf16[256,1024]{1,0:T(8,128)(2,1)S(1)} %get-tuple-element.37.refs_0_), channel_id=1, source_target_pairs={{0,8},{8,16},{16,24},{24,0},{32,40},{40,48},{48,56},{56,32},{64,72... | collective-permute-start | bytes 1572872 | tf_op jit(solution)/shard_map/ppermute | solution.py:183
  5.5 15.7 %collective-permute-start.1 = (bf16[256,1024]{1,0:T(8,128)(2,1)S(1)}, bf16[256,1024]{1,0:T(8,128)(2,1)S(1)}, u32[]{:S(2)}, u32[]{:S(2)}) collective-permute-start(bf16[256,1024]{1,0:T(8,128)(2,1)S(1)} %get-tuple-element.37.refs_0_), channel_id=1, source_target_pairs={{0,24},{8,0},{16,8},{24,16},{32,56},{40,32},{48,40},{56,48},{64,88... | collective-permute-start | bytes 1572872 | tf_op jit(solution)/shard_map/ppermute | solution.py:183
  7.1 15.6 %collective-permute-start = (bf16[256,1024]{1,0:T(8,128)(2,1)S(1)}, bf16[256,1024]{1,0:T(8,128)(2,1)S(1)}, u32[]{:S(2)}, u32[]{:S(2)}) collective-permute-start(bf16[256,1024]{1,0:T(8,128)(2,1)S(1)} %get-tuple-element.37.refs_0_), channel_id=1, source_target_pairs={{0,1},{1,0},{2,3},{3,2},{4,5},{5,4},{6,7},{7,6},{8,9},{9,8},{10,11... | collective-permute-start | bytes 1572872 | tf_op jit(solution)/shard_map/ppermute | solution.py:195
  7.1 17.4 %collective-permute-start.10 = (bf16[256,1024]{1,0:T(8,128)(2,1)S(1)}, bf16[256,1024]{1,0:T(8,128)(2,1)S(1)}, u32[]{:S(2)}, u32[]{:S(2)}) collective-permute-start(bf16[256,1024]{1,0:T(8,128)(2,1)S(1)} %get-tuple-element.38.refs_8_), channel_id=1, source_target_pairs={{0,32},{8,40},{16,48},{24,56},{32,64},{40,72},{48,80},{56,88},{64,... | collective-permute-start | bytes 1572872 | tf_op jit(solution)/shard_map/ppermute | solution.py:187
  8.7 16.1 %collective-permute-start.8 = (bf16[256,1024]{1,0:T(8,128)(2,1)S(1)}, bf16[256,1024]{1,0:T(8,128)(2,1)S(1)}, u32[]{:S(2)}, u32[]{:S(2)}) collective-permute-start(bf16[256,1024]{1,0:T(8,128)(2,1)S(1)} %get-tuple-element.38.refs_8_), channel_id=1, source_target_pairs={{0,96},{8,104},{16,112},{24,120},{32,0},{40,8},{48,16},{56,24},{64... | collective-permute-start | bytes 1572872 | tf_op jit(solution)/shard_map/ppermute | solution.py:187
  19.5 13.6 %collective-permute-start.21 = (bf16[256,1024]{1,0:T(8,128)(2,1)S(1)}, bf16[256,1024]{1,0:T(8,128)(2,1)S(1)}, u32[]{:S(2)}, u32[]{:S(2)}) collective-permute-start(bf16[256,1024]{1,0:T(8,128)(2,1)S(1)} %get-tuple-element.48.refs_0_), channel_id=1, source_target_pairs={{0,24},{8,0},{16,8},{24,16},{32,56},{40,32},{48,40},{56,48},{64,88... | collective-permute-start | bytes 1572872 | tf_op jit(solution)/shard_map/ppermute | solution.py:183
  21.2 14.3 %collective-permute-start.13 = (bf16[256,1024]{1,0:T(8,128)(2,1)S(1)}, bf16[256,1024]{1,0:T(8,128)(2,1)S(1)}, u32[]{:S(2)}, u32[]{:S(2)}) collective-permute-start(bf16[256,1024]{1,0:T(8,128)(2,1)S(1)} %collective-permute-done.7.refs_9_), channel_id=1, source_target_pairs={{0,32},{8,40},{16,48},{24,56},{32,64},{40,72},{48,80},{56,88},{64,... | collective-permute-start | bytes 1572872 | tf_op jit(solution)/shard_map/ppermute | solution.py:187
  22.7 13.1 %collective-permute-start.9 = (bf16[256,1024]{1,0:T(8,128)(2,1)S(1)}, bf16[256,1024]{1,0:T(8,128)(2,1)S(1)}, u32[]{:S(2)}, u32[]{:S(2)}) collective-permute-start(bf16[256,1024]{1,0:T(8,128)(2,1)S(1)} %collective-permute-done.7.refs_9_), channel_id=1, source_target_pairs={{0,96},{8,104},{16,112},{24,120},{32,0},{40,8},{48,16},{56,24},{64... | collective-permute-start | bytes 1572872 | tf_op jit(solution)/shard_map/ppermute | solution.py:187
  24.4 14.3 %collective-permute-start.4 = (bf16[256,1024]{1,0:T(8,128)(2,1)S(1)}, bf16[256,1024]{1,0:T(8,128)(2,1)S(1)}, u32[]{:S(2)}, u32[]{:S(2)}) collective-permute-start(bf16[256,1024]{1,0:T(8,128)(2,1)S(1)} %collective-permute-done.3.refs_6_), channel_id=1, source_target_pairs={{0,8},{8,16},{16,24},{24,0},{32,40},{40,48},{48,56},{56,32},{64,72... | collective-permute-start | bytes 1572872 | tf_op jit(solution)/shard_map/ppermute | solution.py:183
  24.7 14.1 %collective-permute-start.6 = (bf16[256,1024]{1,0:T(8,128)(2,1)S(1)}, bf16[256,1024]{1,0:T(8,128)(2,1)S(1)}, u32[]{:S(2)}, u32[]{:S(2)}) collective-permute-start(bf16[256,1024]{1,0:T(8,128)(2,1)S(1)} %collective-permute-done.3.refs_6_), channel_id=1, source_target_pairs={{0,1},{1,0},{2,3},{3,2},{4,5},{5,4},{6,7},{7,6},{8,9},{9,8},{10,11... | collective-permute-start | bytes 1572872 | tf_op jit(solution)/shard_map/ppermute | solution.py:195
  35.5 13.5 %collective-permute-start.11 = (bf16[256,1024]{1,0:T(8,128)(2,1)S(1)}, bf16[256,1024]{1,0:T(8,128)(2,1)S(1)}, u32[]{:S(2)}, u32[]{:S(2)}) collective-permute-start(bf16[256,1024]{1,0:T(8,128)(2,1)S(1)} %collective-permute-done.10.refs_14_), channel_id=1, source_target_pairs={{0,32},{8,40},{16,48},{24,56},{32,64},{40,72},{48,80},{56,88},{64,... | collective-permute-start | bytes 1572872 | tf_op jit(solution)/shard_map/ppermute | solution.py:187
  35.8 13.2 %collective-permute-start.12 = (bf16[256,1024]{1,0:T(8,128)(2,1)S(1)}, bf16[256,1024]{1,0:T(8,128)(2,1)S(1)}, u32[]{:S(2)}, u32[]{:S(2)}) collective-permute-start(bf16[256,1024]{1,0:T(8,128)(2,1)S(1)} %collective-permute-done.9.refs_11_), channel_id=1, source_target_pairs={{0,96},{8,104},{16,112},{24,120},{32,0},{40,8},{48,16},{56,24},{64... | collective-permute-start | bytes 1572872 | tf_op jit(solution)/shard_map/ppermute | solution.py:187
  38.8 17.7 %collective-permute-start.25 = (bf16[256,1024]{1,0:T(8,128)(2,1)S(1)}, bf16[256,1024]{1,0:T(8,128)(2,1)S(1)}, u32[]{:S(2)}, u32[]{:S(2)}) collective-permute-start(bf16[256,1024]{1,0:T(8,128)(2,1)S(1)} %get-tuple-element.48.refs_0_), channel_id=1, source_target_pairs={{0,8},{8,16},{16,24},{24,0},{32,40},{40,48},{48,56},{56,32},{64,72... | collective-permute-start | bytes 1572872 | tf_op jit(solution)/shard_map/ppermute | solution.py:183
  39.3 17.7 %collective-permute-start.23 = (bf16[256,1024]{1,0:T(8,128)(2,1)S(1)}, bf16[256,1024]{1,0:T(8,128)(2,1)S(1)}, u32[]{:S(2)}, u32[]{:S(2)}) collective-permute-start(bf16[256,1024]{1,0:T(8,128)(2,1)S(1)} %collective-permute-done.21.refs_2_), channel_id=1, source_target_pairs={{0,24},{8,0},{16,8},{24,16},{32,56},{40,32},{48,40},{56,48},{64,88... | collective-permute-start | bytes 1572872 | tf_op jit(solution)/shard_map/ppermute | solution.py:183
  49.0 16.6 %collective-permute-start.20 = (bf16[256,1024]{1,0:T(8,128)(2,1)S(1)}, bf16[256,1024]{1,0:T(8,128)(2,1)S(1)}, u32[]{:S(2)}, u32[]{:S(2)}) collective-permute-start(bf16[256,1024]{1,0:T(8,128)(2,1)S(1)} %get-tuple-element.48.refs_0_), channel_id=1, source_target_pairs={{0,1},{1,0},{2,3},{3,2},{4,5},{5,4},{6,7},{7,6},{8,9},{9,8},{10,11... | collective-permute-start | bytes 1572872 | tf_op jit(solution)/shard_map/ppermute | solution.py:195
  54.5 11.0 %collective-permute-start.15 = (bf16[2,256,256]{2,1,0:T(8,128)(2,1)S(1)}, bf16[2,256,256]{2,1,0:T(8,128)(2,1)S(1)}, u32[]{:S(2)}, u32[]{:S(2)}) collective-permute-start(bf16[2,256,256]{2,1,0:T(8,128)(2,1)S(1)} %get-tuple-element.43), channel_id=1, source_target_pairs={{0,2},{1,3},{2,4},{3,5},{4,6},{5,7},{6,0},{7,1},{8,10},{9,11},{10,... | collective-permute-start | bytes 786440 | tf_op jit(solution)/shard_map/ppermute | solution.py:191
  56.5 11.5 %collective-permute-start.26 = (bf16[256,1024]{1,0:T(8,128)(2,1)S(1)}, bf16[256,1024]{1,0:T(8,128)(2,1)S(1)}, u32[]{:S(2)}, u32[]{:S(2)}) collective-permute-start(bf16[256,1024]{1,0:T(8,128)(2,1)S(1)} %collective-permute-done.25.refs_6_), channel_id=1, source_target_pairs={{0,1},{1,0},{2,3},{3,2},{4,5},{5,4},{6,7},{7,6},{8,9},{9,8},{10,11... | collective-permute-start | bytes 1572872 | tf_op jit(solution)/shard_map/ppermute | solution.py:195
  56.7 12.4 %collective-permute-start.22 = (bf16[256,1024]{1,0:T(8,128)(2,1)S(1)}, bf16[256,1024]{1,0:T(8,128)(2,1)S(1)}, u32[]{:S(2)}, u32[]{:S(2)}) collective-permute-start(bf16[256,1024]{1,0:T(8,128)(2,1)S(1)} %collective-permute-done.21.refs_2_), channel_id=1, source_target_pairs={{0,1},{1,0},{2,3},{3,2},{4,5},{5,4},{6,7},{7,6},{8,9},{9,8},{10,11... | collective-permute-start | bytes 1572872 | tf_op jit(solution)/shard_map/ppermute | solution.py:195
  57.0 10.6 %collective-permute-start.18 = (bf16[2,256,256]{2,1,0:T(8,128)(2,1)S(1)}, bf16[2,256,256]{2,1,0:T(8,128)(2,1)S(1)}, u32[]{:S(2)}, u32[]{:S(2)}) collective-permute-start(bf16[2,256,256]{2,1,0:T(8,128)(2,1)S(1)} %get-tuple-element.47), channel_id=1, source_target_pairs={{0,6},{1,7},{2,0},{3,1},{4,2},{5,3},{6,4},{7,5},{8,14},{9,15},{10,... | collective-permute-start | bytes 786440 | tf_op jit(solution)/shard_map/ppermute | solution.py:191
  65.6 11.1 %collective-permute-start.14 = (bf16[2,256,256]{2,1,0:T(8,128)(2,1)S(1)}, bf16[2,256,256]{2,1,0:T(8,128)(2,1)S(1)}, u32[]{:S(2)}, u32[]{:S(2)}) collective-permute-start(bf16[2,256,256]{2,1,0:T(8,128)(2,1)S(1)} %get-tuple-element.41), channel_id=1, source_target_pairs={{0,6},{1,7},{2,0},{3,1},{4,2},{5,3},{6,4},{7,5},{8,14},{9,15},{10,... | collective-permute-start | bytes 786440 | tf_op jit(solution)/shard_map/ppermute | solution.py:191
  68.0 14.9 %collective-permute-start.17 = (bf16[2,256,256]{2,1,0:T(8,128)(2,1)S(1)}, bf16[2,256,256]{2,1,0:T(8,128)(2,1)S(1)}, u32[]{:S(2)}, u32[]{:S(2)}) collective-permute-start(bf16[2,256,256]{2,1,0:T(8,128)(2,1)S(1)} %get-tuple-element.45), channel_id=1, source_target_pairs={{0,2},{1,3},{2,4},{3,5},{4,6},{5,7},{6,0},{7,1},{8,10},{9,11},{10,... | collective-permute-start | bytes 786440 | tf_op jit(solution)/shard_map/ppermute | solution.py:191
  69.1 13.8 %collective-permute-start.19 = (bf16[2,256,256]{2,1,0:T(8,128)(2,1)S(1)}, bf16[2,256,256]{2,1,0:T(8,128)(2,1)S(1)}, u32[]{:S(2)}, u32[]{:S(2)}) collective-permute-start(bf16[2,256,256]{2,1,0:T(8,128)(2,1)S(1)} %add_convert_fusion.2), channel_id=1, source_target_pairs={{0,6},{1,7},{2,0},{3,1},{4,2},{5,3},{6,4},{7,5},{8,14},{9,15},{10,... | collective-permute-start | bytes 786440 | tf_op jit(solution)/shard_map/ppermute | solution.py:191
  83.0 22.1 %collective-permute-start.32 = (bf16[2,256,256]{2,1,0:T(8,128)(2,1)S(1)}, bf16[2,256,256]{2,1,0:T(8,128)(2,1)S(1)}, u32[]{:S(2)}, u32[]{:S(2)}) collective-permute-start(bf16[2,256,256]{2,1,0:T(8,128)(2,1)S(1)} %get-tuple-element.64), channel_id=1, source_target_pairs={{0,2},{1,3},{2,4},{3,5},{4,6},{5,7},{6,0},{7,1},{8,10},{9,11},{10,... | collective-permute-start | bytes 786440 | tf_op jit(solution)/shard_map/ppermute | solution.py:191
  83.0 11.3 %collective-permute-start.27 = (bf16[256,256]{1,0:T(8,128)(2,1)S(1)}, bf16[256,256]{1,0:T(8,128)(2,1)S(1)}, u32[]{:S(2)}, u32[]{:S(2)}) collective-permute-start(bf16[256,256]{1,0:T(8,128)(2,1)S(1)} %get-tuple-element.57), channel_id=1, source_target_pairs={{0,0},{1,8},{2,2},{3,10},{4,4},{5,12},{6,6},{7,14},{8,16},{9,24},{... | collective-permute-start | bytes 393224 | tf_op jit(solution)/shard_map/ppermute | solution.py:216
  83.7 13.6 %collective-permute-start.28 = (bf16[256,256]{1,0:T(8,128)(2,1)S(1)}, bf16[256,256]{1,0:T(8,128)(2,1)S(1)}, u32[]{:S(2)}, u32[]{:S(2)}) collective-permute-start(bf16[256,256]{1,0:T(8,128)(2,1)S(1)} %get-tuple-element.58), channel_id=1, source_target_pairs={{0,8},{1,16},{2,10},{3,18},{4,12},{5,20},{6,14},{7,22},{8,24},{9,0... | collective-permute-start | bytes 393224 | tf_op jit(solution)/shard_map/ppermute | solution.py:216
  94.3 12.6 %collective-permute-start.37 = (bf16[2,256,256]{2,1,0:T(8,128)(2,1)S(1)}, bf16[2,256,256]{2,1,0:T(8,128)(2,1)S(1)}, u32[]{:S(2)}, u32[]{:S(2)}) collective-permute-start(bf16[2,256,256]{2,1,0:T(8,128)(2,1)S(1)} %get-tuple-element.68), channel_id=1, source_target_pairs={{0,6},{1,7},{2,0},{3,1},{4,2},{5,3},{6,4},{7,5},{8,14},{9,15},{10,... | collective-permute-start | bytes 786440 | tf_op jit(solution)/shard_map/ppermute | solution.py:191
  97.3 12.3 %collective-permute-start.31 = (bf16[2,256,256]{2,1,0:T(8,128)(2,1)S(1)}, bf16[2,256,256]{2,1,0:T(8,128)(2,1)S(1)}, u32[]{:S(2)}, u32[]{:S(2)}) collective-permute-start(bf16[2,256,256]{2,1,0:T(8,128)(2,1)S(1)} %get-tuple-element.62), channel_id=1, source_target_pairs={{0,6},{1,7},{2,0},{3,1},{4,2},{5,3},{6,4},{7,5},{8,14},{9,15},{10,... | collective-permute-start | bytes 786440 | tf_op jit(solution)/shard_map/ppermute | solution.py:191
  99.8 32.4 %all-to-all-start = ((bf16[16,1,128,256]{3,2,1,0:T(8,128)(2,1)}), bf16[16,1,128,256]{3,2,1,0:T(8,128)(2,1)}, u32[]{:S(2)}, u32[]{:S(2)}) async-start(bf16[16,1,128,256]{3,2,1,0:T(8,128)(2,1)} %pack.2), calls=%async_computation | async-start | bytes 2097152 | tf_op jit(solution)/shard_map/all_to_all | solution.py:221
  105.2 10.5 %collective-permute-start.33 = (bf16[2,256,256]{2,1,0:T(8,128)(2,1)S(1)}, bf16[2,256,256]{2,1,0:T(8,128)(2,1)S(1)}, u32[]{:S(2)}, u32[]{:S(2)}) collective-permute-start(bf16[2,256,256]{2,1,0:T(8,128)(2,1)S(1)} %add_convert_fusion.1), channel_id=1, source_target_pairs={{0,2},{1,3},{2,4},{3,5},{4,6},{5,7},{6,0},{7,1},{8,10},{9,11},{10,... | collective-permute-start | bytes 786440 | tf_op jit(solution)/shard_map/ppermute | solution.py:191
  106.2 13.9 %collective-permute-start.36 = (bf16[2,256,256]{2,1,0:T(8,128)(2,1)S(1)}, bf16[2,256,256]{2,1,0:T(8,128)(2,1)S(1)}, u32[]{:S(2)}, u32[]{:S(2)}) collective-permute-start(bf16[2,256,256]{2,1,0:T(8,128)(2,1)S(1)} %get-tuple-element.66), channel_id=1, source_target_pairs={{0,2},{1,3},{2,4},{3,5},{4,6},{5,7},{6,0},{7,1},{8,10},{9,11},{10,... | collective-permute-start | bytes 786440 | tf_op jit(solution)/shard_map/ppermute | solution.py:191
  107.0 13.2 %collective-permute-start.38 = (bf16[2,256,256]{2,1,0:T(8,128)(2,1)S(1)}, bf16[2,256,256]{2,1,0:T(8,128)(2,1)S(1)}, u32[]{:S(2)}, u32[]{:S(2)}) collective-permute-start(bf16[2,256,256]{2,1,0:T(8,128)(2,1)S(1)} %add_convert_fusion), channel_id=1, source_target_pairs={{0,6},{1,7},{2,0},{3,1},{4,2},{5,3},{6,4},{7,5},{8,14},{9,15},{10,... | collective-permute-start | bytes 786440 | tf_op jit(solution)/shard_map/ppermute | solution.py:191
  115.7 12.6 %collective-permute-start.35 = (bf16[256,256]{1,0:T(8,128)(2,1)S(1)}, bf16[256,256]{1,0:T(8,128)(2,1)S(1)}, u32[]{:S(2)}, u32[]{:S(2)}) collective-permute-start(bf16[256,256]{1,0:T(8,128)(2,1)S(1)} %get-tuple-element.71), channel_id=1, source_target_pairs={{0,8},{1,16},{2,10},{3,18},{4,12},{5,20},{6,14},{7,22},{8,24},{9,0... | collective-permute-start | bytes 393224 | tf_op jit(solution)/shard_map/ppermute | solution.py:216
  (14 other events, 98.6 us)
where the time goes:
time: 160 us; the launch traced here: 159 us
  starting transfers between devices  65.3 us (41%)
  waiting for transfers between devices  47.8 us (30%)
  blocking collectives  24.4 us (15%)
  Pallas kernels  15.6 us (10%)
  other arithmetic  3.34 us (2%)
  local copies, waits for them, and re-layouts  2.6 us (2%)
    all_to_all x1, blocking collectives, to_owners(): lax.all_to_all(outgoing, 'row', split_axis=0, concat_axis=0, tiled=True)  24.4 us
    ppermute x8, starting transfers between devices, to_blocks(): lax.ppermute(rounds[m], ('row', 'col'), block_round(m))  23.7 us
    ppermute x12, waiting for transfers between devices, zpass(): return lax.ppermute(value, 'col', along_z(step))  18.3 us
    ppermute x6, waiting for transfers between devices, ypass(): return lax.ppermute(value, 'row', along_y(step))  17.4 us
    ppermute x12, starting transfers between devices, zpass(): return lax.ppermute(value, 'col', along_z(step))  17.4 us
    pallas_call x2, Pallas kernels, product(): pl.pallas_call(product_body, out_shape=(sent,) * 6 + (kept,) * 2, in_spec...  10.9 us
    ppermute x6, starting transfers between devices, xpass(): return lax.ppermute(value, 'row', along_x(step))  9.71 us
    ppermute x6, waiting for transfers between devices, xpass(): return lax.ppermute(value, 'row', along_x(step))  9.43 us
  transfers between devices with their start and end apart: 42, of which 9 were waited for; matrix products, arithmetic and copies ran while one was open for 0% of the time, Pallas kernels for 9%

commit v1 on v0

--- a/solution.py
+++ b/solution.py
@@ -100,27 +100,28 @@
     rows_ref, cols_ref, row_sems, col_sems = refs[24:]
     x, y, z, k = position()
     u = 2 * (y % 2) + k
-    copies = []
+    across = (pl.ds(0, 1024), pl.ds(1024, 1024))
+    col_copies, row_copies = [], []
     for d in range(4):
         for h in range(2):
-            across = pl.ds(1024 * h, 1024)
-            copies.append(
-                pltpu.make_async_copy(
-                    cols[2 * d + h], cols_ref.at[(x + d) % 4, :, across], col_sems.at[2 * d + h]
-                )
-            )
-            copies.append(
-                pltpu.make_async_copy(
-                    rows[2 * d + h], rows_ref.at[(y + d - u + 4) % 4, :, across], row_sems.at[2 * d + h]
-                )
-            )
-    for copy in copies:
-        copy.start()
-    for copy in copies:
+            target = cols_ref.at[(x + d) % 4, :, across[h]]
+            col_copies.append(pltpu.make_async_copy(cols[2 * d + h], target, col_sems.at[2 * d + h]))
+    for d in range(4):
+        slot = (y + d - u + 4) % 4
+        for h in range(2):
+            target = rows_ref.at[slot, :, across[h]]
+            row_copies.append(pltpu.make_async_copy(rows[2 * d + h], target, row_sems.at[2 * slot + h]))
+    for copy in col_copies + row_copies:
+        copy.start()
+    for copy in col_copies:
         copy.wait()
     for at, d in enumerate((2, 1, 3, 0)):
         right = cols_ref[(z + d) % 4]
         for m in range(4):
+            if at == 0:
+                for h in range(2):
+                    target = rows_ref.at[m, :, across[h]]
+                    pltpu.make_async_copy(rows[h], target, row_sems.at[2 * m + h]).wait()
             out = outs[2 * at + m // 2]
             out[m % 2] = lax.dot_general(
                 rows_ref[m], right, (((1,), (1,)), ((), ())), preferred_element_type=jnp.float32
@@ -179,6 +180,24 @@
     )(owners, *arrived)
 
 
+def place_half(half, value, *whole):
+    def body(value_ref, *refs):
+        out_ref, sem = refs[-2:]
+        copy = pltpu.make_async_copy(value_ref, out_ref.at[:, :, pl.ds(half * HALF, HALF)], sem)
+        copy.start()
+        copy.wait()
+
+    return pl.pallas_call(
+        body,
+        out_shape=jax.ShapeDtypeStruct((16, 1, TILE, TILE), jnp.bfloat16),
+        in_specs=[pl.BlockSpec(memory_space=pl.ANY)] * (1 + len(whole)),
+        out_specs=pl.BlockSpec(memory_space=pl.ANY),
+        scratch_shapes=[pltpu.SemaphoreType.DMA],
+        input_output_aliases={1: 0} if whole else {},
+        compiler_params=pltpu.CompilerParams(vmem_limit_bytes=1024 * 1024),
+    )(value, *whole)
+
+
 def ypass(value, step):
     return lax.ppermute(value, "row", along_y(step))
 
@@ -235,13 +254,11 @@
     for pieces in ((top, top_p, top_o, top_m), (low, low_p, low_o, low_m)):
         rows = [piece for value in pieces for piece in (value, swap(value))]
         halves.append(product(rows, cols))
-    rounds = reduce_along_z(halves[0])
-    *rounds, later = lax.optimization_barrier((*rounds, halves[1]))
-    arrived = to_blocks(rounds)
+    arrived = to_blocks(reduce_along_z(halves[0]))
     first = to_owners(owner_rows, arrived)
-    arrived = to_blocks(reduce_along_z(later))
+    arrived = to_blocks(reduce_along_z(halves[1]))
     second = to_owners(owner_rows, arrived)
-    return jnp.concatenate((first, second), axis=2)
+    return place_half(1, second, place_half(0, first))
 
 
 def solution(mesh):

time: 160 us -> 168 us (1.050)
  blocking collectives: 24.4 us -> 0 us
  waiting for transfers between devices: 47.8 us -> 67.4 us
  starting transfers between devices: 65.3 us -> 72 us
  Pallas kernels: 15.6 us -> 21.9 us
    all_to_all x1 -> x0, blocking collectives: 24.4 us -> none  [to_owners(): lax.all_to_all(outgoing, 'row', split_axis=0, concat_axis=0, tiled=True)]
    all_to_all x1 -> x2, waiting for transfers between devices: 0.01 us -> 16.3 us  [to_owners(): lax.all_to_all(outgoing, 'row', split_axis=0, concat_axis=0, tiled=True)]
    ppermute x6, waiting for transfers between devices: 9.43 us -> 19.4 us  [xpass(): return lax.ppermute(value, 'row', along_x(step))]
    all_to_all x1 -> x2, starting transfers between devices: 5.28 us -> 13.3 us  [to_owners(): lax.all_to_all(outgoing, 'row', split_axis=0, concat_axis=0, tiled=True)]
    ppermute x6, waiting for transfers between devices: 17.4 us -> 10.4 us  [ypass(): return lax.ppermute(value, 'row', along_y(step))]
    pallas_call x2, Pallas kernels: 10.9 us -> 14.2 us  [product(): pl.pallas_call(product_body, out_shape=(sent,) * 6 + (kept,) * 2, in_spec...]
    convert_element_type x8, other arithmetic: 0.61 us -> 3.47 us  [add(): sum((part.astype(jnp.float32) for part in parts)).astype(jnp.bfloat16)]
    concatenate x1 -> x0, other arithmetic: 2.73 us -> none  [shards(): return jnp.concatenate((first, second), axis=2)]
  transfers between devices with their start and end apart: 42 -> 43, of which waited for: 9 -> 11; matrix products, arithmetic and copies ran while one was open for 0% -> 2% of each run, Pallas kernels for 9% -> 12%
where the time goes in v1:
time: 168 us
  starting transfers between devices  72 us (43%)
  waiting for transfers between devices  67.4 us (40%)
  Pallas kernels  21.9 us (13%)
  other arithmetic  3.47 us (2%)
  local copies, waits for them, and re-layouts  2.6 us (2%)
    ppermute x8, starting transfers between devices, to_blocks(): lax.ppermute(rounds[m], ('row', 'col'), block_round(m))  22.2 us
    ppermute x6, waiting for transfers between devices, xpass(): return lax.ppermute(value, 'row', along_x(step))  19.4 us
    ppermute x12, waiting for transfers between devices, zpass(): return lax.ppermute(value, 'col', along_z(step))  18.7 us
    ppermute x12, starting transfers between devices, zpass(): return lax.ppermute(value, 'col', along_z(step))  17 us
    all_to_all x2, waiting for transfers between devices, to_owners(): lax.all_to_all(outgoing, 'row', split_axis=0, concat_axis=0, tiled=True)  16.3 us
    pallas_call x2, Pallas kernels, product(): pl.pallas_call(product_body, out_shape=(sent,) * 6 + (kept,) * 2, in_spec...  14.2 us
    all_to_all x2, starting transfers between devices, to_owners(): lax.all_to_all(outgoing, 'row', split_axis=0, concat_axis=0, tiled=True)  13.3 us
    ppermute x6, waiting for transfers between devices, ypass(): return lax.ppermute(value, 'row', along_y(step))  10.4 us
  transfers between devices with their start and end apart: 43, of which 11 were waited for; matrix products, arithmetic and copies ran while one was open for 2% of the time, Pallas kernels for 12%

profile of v1, /device:TPU:0, one launch (start us, length us, event | category | flops | bytes accessed | tf_op | source)
XLA Modules:
  0.0 167.8 jit_solution(17626551232563066398)
XLA Ops:
  3.7 3.2 %collective-permute-start.1 = (bf16[256,1024]{1,0:T(8,128)(2,1)S(1)}, bf16[256,1024]{1,0:T(8,128)(2,1)S(1)}, u32[]{:S(2)}, u32[]{:S(2)}) collective-permute-start(bf16[256,1024]{1,0:T(8,128)(2,1)S(1)} %get-tuple-element.25.refs_0_), channel_id=1, source_target_pairs={{0,24},{8,0},{16,8},{24,16},{32,56},{40,32},{48,40},{56,48},{64,88... | collective-permute-start | bytes 1572872 | tf_op jit(solution)/shard_map/ppermute | solution.py:202
  8.4 1.7 %collective-permute-start.8 = (bf16[256,1024]{1,0:T(8,128)(2,1)S(1)}, bf16[256,1024]{1,0:T(8,128)(2,1)S(1)}, u32[]{:S(2)}, u32[]{:S(2)}) collective-permute-start(bf16[256,1024]{1,0:T(8,128)(2,1)S(1)} %get-tuple-element.26.refs_8_), channel_id=1, source_target_pairs={{0,96},{8,104},{16,112},{24,120},{32,0},{40,8},{48,16},{56,24},{64... | collective-permute-start | bytes 1572872 | tf_op jit(solution)/shard_map/ppermute | solution.py:206
  10.2 3.2 %collective-permute-start.25 = (bf16[256,1024]{1,0:T(8,128)(2,1)S(1)}, bf16[256,1024]{1,0:T(8,128)(2,1)S(1)}, u32[]{:S(2)}, u32[]{:S(2)}) collective-permute-start(bf16[256,1024]{1,0:T(8,128)(2,1)S(1)} %get-tuple-element.36.refs_0_), channel_id=1, source_target_pairs={{0,24},{8,0},{16,8},{24,16},{32,56},{40,32},{48,40},{56,48},{64,88... | collective-permute-start | bytes 1572872 | tf_op jit(solution)/shard_map/ppermute | solution.py:202
  13.4 5.8 %collective-permute-done.1.refs_2_ = bf16[256,1024]{1,0:T(8,128)(2,1)S(1)} collective-permute-done((bf16[256,1024]{1,0:T(8,128)(2,1)S(1)}, bf16[256,1024]{1,0:T(8,128)(2,1)S(1)}, u32[]{:S(2)}, u32[]{:S(2)}) %collective-permute-start.1) | collective-permute-done | bytes 524320 | tf_op jit(solution)/shard_map/ppermute | solution.py:202
  19.3 2.9 %collective-permute-done.10.refs_14_ = bf16[256,1024]{1,0:T(8,128)(2,1)S(1)} collective-permute-done((bf16[256,1024]{1,0:T(8,128)(2,1)S(1)}, bf16[256,1024]{1,0:T(8,128)(2,1)S(1)}, u32[]{:S(2)}, u32[]{:S(2)}) %collective-permute-start.10) | collective-permute-done | bytes 524320 | tf_op jit(solution)/shard_map/ppermute | solution.py:206
  22.4 3.0 %collective-permute-start.9 = (bf16[256,1024]{1,0:T(8,128)(2,1)S(1)}, bf16[256,1024]{1,0:T(8,128)(2,1)S(1)}, u32[]{:S(2)}, u32[]{:S(2)}) collective-permute-start(bf16[256,1024]{1,0:T(8,128)(2,1)S(1)} %collective-permute-done.7.refs_9_), channel_id=1, source_target_pairs={{0,96},{8,104},{16,112},{24,120},{32,0},{40,8},{48,16},{56,24},{64... | collective-permute-start | bytes 1572872 | tf_op jit(solution)/shard_map/ppermute | solution.py:206
  25.4 4.6 %collective-permute-done.25.refs_2_ = bf16[256,1024]{1,0:T(8,128)(2,1)S(1)} collective-permute-done((bf16[256,1024]{1,0:T(8,128)(2,1)S(1)}, bf16[256,1024]{1,0:T(8,128)(2,1)S(1)}, u32[]{:S(2)}, u32[]{:S(2)}) %collective-permute-start.25) | collective-permute-done | bytes 524320 | tf_op jit(solution)/shard_map/ppermute | solution.py:202
  31.5 6.7 %collective-permute-done.13.refs_15_ = bf16[256,1024]{1,0:T(8,128)(2,1)S(1)} collective-permute-done((bf16[256,1024]{1,0:T(8,128)(2,1)S(1)}, bf16[256,1024]{1,0:T(8,128)(2,1)S(1)}, u32[]{:S(2)}, u32[]{:S(2)}) %collective-permute-start.13) | collective-permute-done | bytes 524320 | tf_op jit(solution)/shard_map/ppermute | solution.py:206
  39.4 8.3 %collective-permute-done.11.refs_12_ = bf16[256,1024]{1,0:T(8,128)(2,1)S(1)} collective-permute-done((bf16[256,1024]{1,0:T(8,128)(2,1)S(1)}, bf16[256,1024]{1,0:T(8,128)(2,1)S(1)}, u32[]{:S(2)}, u32[]{:S(2)}) %collective-permute-start.11) | collective-permute-done | bytes 524320 | tf_op jit(solution)/shard_map/ppermute | solution.py:206
  47.7 3.2 %collective-permute-start.3 = (bf16[256,1024]{1,0:T(8,128)(2,1)S(1)}, bf16[256,1024]{1,0:T(8,128)(2,1)S(1)}, u32[]{:S(2)}, u32[]{:S(2)}) collective-permute-start(bf16[256,1024]{1,0:T(8,128)(2,1)S(1)} %collective-permute-done.1.refs_2_), channel_id=1, source_target_pairs={{0,24},{8,0},{16,8},{24,16},{32,56},{40,32},{48,40},{56,48},{64,88... | collective-permute-start | bytes 1572872 | tf_op jit(solution)/shard_map/ppermute | solution.py:202
  52.5 7.1 %product.3 = (bf16[2,256,256]{2,1,0:T(8,128)(2,1)S(1)}, bf16[2,256,256]{2,1,0:T(8,128)(2,1)S(1)}, bf16[2,256,256]{2,1,0:T(8,128)(2,1)S(1)}, bf16[2,256,256]{2,1,...) custom-call(bf16[256,1024]{1,0:T(8,128)(2,1)S(1)} %get-tuple-element, ...), custom_call_target="tpu_custom_call" | custom-call | tf_op jit(solution)/shard_map/product/pallas_call | solution.py:134
  59.6 2.0 %collective-permute-start.32 = (bf16[2,256,256]{2,1,0:T(8,128)(2,1)S(1)}, bf16[2,256,256]{2,1,0:T(8,128)(2,1)S(1)}, u32[]{:S(2)}, u32[]{:S(2)}) collective-permute-start(bf16[2,256,256]{2,1,0:T(8,128)(2,1)S(1)} %get-tuple-element.40), channel_id=1, source_target_pairs={{0,2},{1,3},{2,4},{3,5},{4,6},{5,7},{6,0},{7,1},{8,10},{9,11},{10,... | collective-permute-start | bytes 786440 | tf_op jit(solution)/shard_map/ppermute | solution.py:210
  62.1 7.7 %collective-permute-done.32 = bf16[2,256,256]{2,1,0:T(8,128)(2,1)S(1)} collective-permute-done((bf16[2,256,256]{2,1,0:T(8,128)(2,1)S(1)}, bf16[2,256,256]{2,1,0:T(8,128)(2,1)S(1)}, u32[]{:S(2)}, u32[]{:S(2)}) %collective-permute-start.32) | collective-permute-done | bytes 262176 | tf_op jit(solution)/shard_map/ppermute | solution.py:210
  72.1 6.9 %collective-permute-done.37 = bf16[2,256,256]{2,1,0:T(8,128)(2,1)S(1)} collective-permute-done((bf16[2,256,256]{2,1,0:T(8,128)(2,1)S(1)}, bf16[2,256,256]{2,1,0:T(8,128)(2,1)S(1)}, u32[]{:S(2)}, u32[]{:S(2)}) %collective-permute-start.37) | collective-permute-done | bytes 262176 | tf_op jit(solution)/shard_map/ppermute | solution.py:210
  80.7 1.8 %collective-permute-start.38 = (bf16[2,256,256]{2,1,0:T(8,128)(2,1)S(1)}, bf16[2,256,256]{2,1,0:T(8,128)(2,1)S(1)}, u32[]{:S(2)}, u32[]{:S(2)}) collective-permute-start(bf16[2,256,256]{2,1,0:T(8,128)(2,1)S(1)} %add_convert_fusion), channel_id=1, source_target_pairs={{0,6},{1,7},{2,0},{3,1},{4,2},{5,3},{6,4},{7,5},{8,14},{9,15},{10,... | collective-permute-start | bytes 786440 | tf_op jit(solution)/shard_map/ppermute | solution.py:210
  82.5 7.1 %product.2 = (bf16[2,256,256]{2,1,0:T(8,128)(2,1)}, bf16[2,256,256]{2,1,0:T(8,128)(2,1)S(1)}, bf16[2,256,256]{2,1,0:T(8,128)(2,1)S(1)}, bf16[2,256,256]{2,1,0:T(...) custom-call(bf16[256,1024]{1,0:T(8,128)(2,1)S(1)} %get-tuple-element, ...), custom_call_target="tpu_custom_call" | custom-call | tf_op jit(solution)/shard_map/product/pallas_call | solution.py:134
  90.8 1.9 %collective-permute-start.35 = (bf16[256,256]{1,0:T(8,128)(2,1)S(1)}, bf16[256,256]{1,0:T(8,128)(2,1)S(1)}, u32[]{:S(2)}, u32[]{:S(2)}) collective-permute-start(bf16[256,256]{1,0:T(8,128)(2,1)S(1)} %get-tuple-element.47), channel_id=1, source_target_pairs={{0,8},{1,16},{2,10},{3,18},{4,12},{5,20},{6,14},{7,22},{8,24},{9,0... | collective-permute-start | bytes 393224 | tf_op jit(solution)/shard_map/ppermute | solution.py:235
  93.6 4.0 %collective-permute-start.40 = (bf16[256,256]{1,0:T(8,128)(2,1)S(1)}, bf16[256,256]{1,0:T(8,128)(2,1)S(1)}, u32[]{:S(2)}, u32[]{:S(2)}) collective-permute-start(bf16[256,256]{1,0:T(8,128)(2,1)S(1)} %get-tuple-element.45), channel_id=1, source_target_pairs={{0,24},{1,0},{2,26},{3,2},{4,28},{5,4},{6,30},{7,6},{8,8},{9,16},{... | collective-permute-start | bytes 393224 | tf_op jit(solution)/shard_map/ppermute | solution.py:235
  97.6 3.1 %collective-permute-start.39 = (bf16[256,256]{1,0:T(8,128)(2,1)S(1)}, bf16[256,256]{1,0:T(8,128)(2,1)S(1)}, u32[]{:S(2)}, u32[]{:S(2)}) collective-permute-start(bf16[256,256]{1,0:T(8,128)(2,1)S(1)} %get-tuple-element.46), channel_id=1, source_target_pairs={{0,16},{1,24},{2,18},{3,26},{4,20},{5,28},{6,22},{7,30},{8,0},{9,8... | collective-permute-start | bytes 393224 | tf_op jit(solution)/shard_map/ppermute | solution.py:235
  100.7 2.1 %collective-permute-start.20 = (bf16[2,256,256]{2,1,0:T(8,128)(2,1)S(1)}, bf16[2,256,256]{2,1,0:T(8,128)(2,1)}, u32[]{:S(2)}, u32[]{:S(2)}) collective-permute-start(bf16[2,256,256]{2,1,0:T(8,128)(2,1)S(1)} %get-tuple-element.35), channel_id=1, source_target_pairs={{0,6},{1,7},{2,0},{3,1},{4,2},{5,3},{6,4},{7,5},{8,14},{9,15},{10,... | collective-permute-start | bytes 786440 | tf_op jit(solution)/shard_map/ppermute | solution.py:210
  103.5 2.3 %pack.3 = bf16[16,1,128,256]{3,2,1,0:T(8,128)(2,1)} custom-call(s32[2,4]{1,0:T(2,128)S(1)} %copy-done.2, bf16[256,256]{1,0:T(8,128)(2,1)S(1)} %collective-permute-done.34.refs_0_, bf16[256,256]{1,0:T(8,128)(2,1)S(1)} %collective-permute-done.35.refs_1_, bf16[256,256]{1,0:T(8,128)(2,1)S(1)} %collective-permute-done.39.refs_2_, ...), custom_call_target="tpu_custom_call" | custom-call | tf_op jit(solution)/shard_map/pack/pallas_call | solution.py:172
  105.9 5.6 %all-to-all-start.1 = ((bf16[16,1,128,256]{3,2,1,0:T(8,128)(2,1)}), bf16[16,1,128,256]{3,2,1,0:T(8,128)(2,1)S(1)}, u32[]{:S(2)}, u32[]{:S(2)}) async-start(bf16[16,1,128,256]{3,2,1,0:T(8,128)(2,1)} %pack.3), calls=%async_computation.1 | async-start | bytes 2097152 | tf_op jit(solution)/shard_map/all_to_all | solution.py:240
  112.5 2.0 %collective-permute-start.16 = (bf16[2,256,256]{2,1,0:T(8,128)(2,1)S(1)}, bf16[2,256,256]{2,1,0:T(8,128)(2,1)S(1)}, u32[]{:S(2)}, u32[]{:S(2)}) collective-permute-start(bf16[2,256,256]{2,1,0:T(8,128)(2,1)S(1)} %add_convert_fusion.3), channel_id=1, source_target_pairs={{0,2},{1,3},{2,4},{3,5},{4,6},{5,7},{6,0},{7,1},{8,10},{9,11},{10,... | collective-permute-start | bytes 786440 | tf_op jit(solution)/shard_map/ppermute | solution.py:210
  115.9 3.0 %collective-permute-start.21 = (bf16[2,256,256]{2,1,0:T(8,128)(2,1)S(1)}, bf16[2,256,256]{2,1,0:T(8,128)(2,1)S(1)}, u32[]{:S(2)}, u32[]{:S(2)}) collective-permute-start(bf16[2,256,256]{2,1,0:T(8,128)(2,1)S(1)} %add_convert_fusion.2), channel_id=1, source_target_pairs={{0,6},{1,7},{2,0},{3,1},{4,2},{5,3},{6,4},{7,5},{8,14},{9,15},{10,... | collective-permute-start | bytes 786440 | tf_op jit(solution)/shard_map/ppermute | solution.py:210
  118.9 4.1 %collective-permute-done.16 = bf16[2,256,256]{2,1,0:T(8,128)(2,1)S(1)} collective-permute-done((bf16[2,256,256]{2,1,0:T(8,128)(2,1)S(1)}, bf16[2,256,256]{2,1,0:T(8,128)(2,1)S(1)}, u32[]{:S(2)}, u32[]{:S(2)}) %collective-permute-start.16) | collective-permute-done | bytes 262176 | tf_op jit(solution)/shard_map/ppermute | solution.py:210
  124.0 3.8 %collective-permute-start.18 = (bf16[256,256]{1,0:T(8,128)(2,1)S(1)}, bf16[256,256]{1,0:T(8,128)(2,1)S(1)}, u32[]{:S(2)}, u32[]{:S(2)}) collective-permute-start(bf16[256,256]{1,0:T(8,128)(2,1)S(1)} %get-tuple-element.51), channel_id=1, source_target_pairs={{0,8},{1,16},{2,10},{3,18},{4,12},{5,20},{6,14},{7,22},{8,24},{9,0... | collective-permute-start | bytes 393224 | tf_op jit(solution)/shard_map/ppermute | solution.py:235
  128.7 4.4 %collective-permute-start.23 = (bf16[256,256]{1,0:T(8,128)(2,1)S(1)}, bf16[256,256]{1,0:T(8,128)(2,1)S(1)}, u32[]{:S(2)}, u32[]{:S(2)}) collective-permute-start(bf16[256,256]{1,0:T(8,128)(2,1)S(1)} %get-tuple-element.49), channel_id=1, source_target_pairs={{0,24},{1,0},{2,26},{3,2},{4,28},{5,4},{6,30},{7,6},{8,8},{9,16},{... | collective-permute-start | bytes 393224 | tf_op jit(solution)/shard_map/ppermute | solution.py:235
  133.0 3.6 %collective-permute-start.22 = (bf16[256,256]{1,0:T(8,128)(2,1)S(1)}, bf16[256,256]{1,0:T(8,128)(2,1)S(1)}, u32[]{:S(2)}, u32[]{:S(2)}) collective-permute-start(bf16[256,256]{1,0:T(8,128)(2,1)S(1)} %get-tuple-element.50), channel_id=1, source_target_pairs={{0,16},{1,24},{2,18},{3,26},{4,20},{5,28},{6,22},{7,30},{8,0},{9,8... | collective-permute-start | bytes 393224 | tf_op jit(solution)/shard_map/ppermute | solution.py:235
  136.7 2.5 %collective-permute-done.22.refs_2_ = bf16[256,256]{1,0:T(8,128)(2,1)S(1)} collective-permute-done((bf16[256,256]{1,0:T(8,128)(2,1)S(1)}, bf16[256,256]{1,0:T(8,128)(2,1)S(1)}, u32[]{:S(2)}, u32[]{:S(2)}) %collective-permute-start.22) | collective-permute-done | bytes 131104 | tf_op jit(solution)/shard_map/ppermute | solution.py:235
  139.2 2.4 %pack.2 = bf16[16,1,128,256]{3,2,1,0:T(8,128)(2,1)} custom-call(s32[2,4]{1,0:T(2,128)S(1)} %copy-done.2, bf16[256,256]{1,0:T(8,128)(2,1)S(1)} %collective-permute-done.17.refs_0_, bf16[256,256]{1,0:T(8,128)(2,1)S(1)} %collective-permute-done.18.refs_1_, bf16[256,256]{1,0:T(8,128)(2,1)S(1)} %collective-permute-done.22.refs_2_, ...), custom_call_target="tpu_custom_call" | custom-call | tf_op jit(solution)/shard_map/pack/pallas_call | solution.py:172
  141.6 7.8 %all-to-all-start = ((bf16[16,1,128,256]{3,2,1,0:T(8,128)(2,1)}), bf16[16,1,128,256]{3,2,1,0:T(8,128)(2,1)S(1)}, u32[]{:S(2)}, u32[]{:S(2)}) async-start(bf16[16,1,128,256]{3,2,1,0:T(8,128)(2,1)} %pack.2), calls=%async_computation | async-start | bytes 2097152 | tf_op jit(solution)/shard_map/all_to_all | solution.py:240
  150.3 16.3 %all-to-all-done.value_ref = bf16[16,1,128,256]{3,2,1,0:T(8,128)(2,1)S(1)} async-done(((bf16[16,1,128,256]{3,2,1,0:T(8,128)(2,1)}), bf16[16,1,128,256]{3,2,1,0:T(8,128)(2,1)S(1)}, u32[]{:S(2)}, u32[]{:S(2)}) %all-to-all-start) | async-done | bytes 1048608 | tf_op jit(solution)/shard_map/all_to_all | solution.py:240
  (77 shorter events, 23.2 us)
Async XLA Ops:
  3.7 15.5 %collective-permute-start.1 = (bf16[256,1024]{1,0:T(8,128)(2,1)S(1)}, bf16[256,1024]{1,0:T(8,128)(2,1)S(1)}, u32[]{:S(2)}, u32[]{:S(2)}) collective-permute-start(bf16[256,1024]{1,0:T(8,128)(2,1)S(1)} %get-tuple-element.25.refs_0_), channel_id=1, source_target_pairs={{0,24},{8,0},{16,8},{24,16},{32,56},{40,32},{48,40},{56,48},{64,88... | collective-permute-start | bytes 1572872 | tf_op jit(solution)/shard_map/ppermute | solution.py:202
  6.9 15.2 %collective-permute-start.10 = (bf16[256,1024]{1,0:T(8,128)(2,1)S(1)}, bf16[256,1024]{1,0:T(8,128)(2,1)S(1)}, u32[]{:S(2)}, u32[]{:S(2)}) collective-permute-start(bf16[256,1024]{1,0:T(8,128)(2,1)S(1)} %get-tuple-element.26.refs_8_), channel_id=1, source_target_pairs={{0,32},{8,40},{16,48},{24,56},{32,64},{40,72},{48,80},{56,88},{64,... | collective-permute-start | bytes 1572872 | tf_op jit(solution)/shard_map/ppermute | solution.py:206
  8.4 14.0 %collective-permute-start.8 = (bf16[256,1024]{1,0:T(8,128)(2,1)S(1)}, bf16[256,1024]{1,0:T(8,128)(2,1)S(1)}, u32[]{:S(2)}, u32[]{:S(2)}) collective-permute-start(bf16[256,1024]{1,0:T(8,128)(2,1)S(1)} %get-tuple-element.26.refs_8_), channel_id=1, source_target_pairs={{0,96},{8,104},{16,112},{24,120},{32,0},{40,8},{48,16},{56,24},{64... | collective-permute-start | bytes 1572872 | tf_op jit(solution)/shard_map/ppermute | solution.py:206
  10.2 15.2 %collective-permute-start.27 = (bf16[256,1024]{1,0:T(8,128)(2,1)S(1)}, bf16[256,1024]{1,0:T(8,128)(2,1)S(1)}, u32[]{:S(2)}, u32[]{:S(2)}) collective-permute-start(bf16[256,1024]{1,0:T(8,128)(2,1)S(1)} %get-tuple-element.36.refs_0_), channel_id=1, source_target_pairs={{0,8},{8,16},{16,24},{24,0},{32,40},{40,48},{48,56},{56,32},{64,72... | collective-permute-start | bytes 1572872 | tf_op jit(solution)/shard_map/ppermute | solution.py:202
  10.2 19.8 %collective-permute-start.25 = (bf16[256,1024]{1,0:T(8,128)(2,1)S(1)}, bf16[256,1024]{1,0:T(8,128)(2,1)S(1)}, u32[]{:S(2)}, u32[]{:S(2)}) collective-permute-start(bf16[256,1024]{1,0:T(8,128)(2,1)S(1)} %get-tuple-element.36.refs_0_), channel_id=1, source_target_pairs={{0,24},{8,0},{16,8},{24,16},{32,56},{40,32},{48,40},{56,48},{64,88... | collective-permute-start | bytes 1572872 | tf_op jit(solution)/shard_map/ppermute | solution.py:202
  19.3 12.2 %collective-permute-start.24 = (bf16[256,1024]{1,0:T(8,128)(2,1)S(1)}, bf16[256,1024]{1,0:T(8,128)(2,1)S(1)}, u32[]{:S(2)}, u32[]{:S(2)}) collective-permute-start(bf16[256,1024]{1,0:T(8,128)(2,1)S(1)} %get-tuple-element.36.refs_0_), channel_id=1, source_target_pairs={{0,1},{1,0},{2,3},{3,2},{4,5},{5,4},{6,7},{7,6},{8,9},{9,8},{10,11... | collective-permute-start | bytes 1572872 | tf_op jit(solution)/shard_map/ppermute | solution.py:214
  22.1 16.0 %collective-permute-start.13 = (bf16[256,1024]{1,0:T(8,128)(2,1)S(1)}, bf16[256,1024]{1,0:T(8,128)(2,1)S(1)}, u32[]{:S(2)}, u32[]{:S(2)}) collective-permute-start(bf16[256,1024]{1,0:T(8,128)(2,1)S(1)} %collective-permute-done.7.refs_9_), channel_id=1, source_target_pairs={{0,32},{8,40},{16,48},{24,56},{32,64},{40,72},{48,80},{56,88},{64,... | collective-permute-start | bytes 1572872 | tf_op jit(solution)/shard_map/ppermute | solution.py:206
  22.4 15.7 %collective-permute-start.9 = (bf16[256,1024]{1,0:T(8,128)(2,1)S(1)}, bf16[256,1024]{1,0:T(8,128)(2,1)S(1)}, u32[]{:S(2)}, u32[]{:S(2)}) collective-permute-start(bf16[256,1024]{1,0:T(8,128)(2,1)S(1)} %collective-permute-done.7.refs_9_), channel_id=1, source_target_pairs={{0,96},{8,104},{16,112},{24,120},{32,0},{40,8},{48,16},{56,24},{64... | collective-permute-start | bytes 1572872 | tf_op jit(solution)/shard_map/ppermute | solution.py:206
  25.4 14.1 %collective-permute-start.28 = (bf16[256,1024]{1,0:T(8,128)(2,1)S(1)}, bf16[256,1024]{1,0:T(8,128)(2,1)S(1)}, u32[]{:S(2)}, u32[]{:S(2)}) collective-permute-start(bf16[256,1024]{1,0:T(8,128)(2,1)S(1)} %collective-permute-done.27.refs_6_), channel_id=1, source_target_pairs={{0,8},{8,16},{16,24},{24,0},{32,40},{40,48},{48,56},{56,32},{64,72... | collective-permute-start | bytes 1572872 | tf_op jit(solution)/shard_map/ppermute | solution.py:202
  30.0 17.7 %collective-permute-start.11 = (bf16[256,1024]{1,0:T(8,128)(2,1)S(1)}, bf16[256,1024]{1,0:T(8,128)(2,1)S(1)}, u32[]{:S(2)}, u32[]{:S(2)}) collective-permute-start(bf16[256,1024]{1,0:T(8,128)(2,1)S(1)} %collective-permute-done.10.refs_14_), channel_id=1, source_target_pairs={{0,32},{8,40},{16,48},{24,56},{32,64},{40,72},{48,80},{56,88},{64,... | collective-permute-start | bytes 1572872 | tf_op jit(solution)/shard_map/ppermute | solution.py:206
  31.4 16.3 %collective-permute-start.30 = (bf16[256,1024]{1,0:T(8,128)(2,1)S(1)}, bf16[256,1024]{1,0:T(8,128)(2,1)S(1)}, u32[]{:S(2)}, u32[]{:S(2)}) collective-permute-start(bf16[256,1024]{1,0:T(8,128)(2,1)S(1)} %collective-permute-done.27.refs_6_), channel_id=1, source_target_pairs={{0,1},{1,0},{2,3},{3,2},{4,5},{5,4},{6,7},{7,6},{8,9},{9,8},{10,11... | collective-permute-start | bytes 1572872 | tf_op jit(solution)/shard_map/ppermute | solution.py:214
  38.1 12.8 %collective-permute-start.26 = (bf16[256,1024]{1,0:T(8,128)(2,1)S(1)}, bf16[256,1024]{1,0:T(8,128)(2,1)S(1)}, u32[]{:S(2)}, u32[]{:S(2)}) collective-permute-start(bf16[256,1024]{1,0:T(8,128)(2,1)S(1)} %collective-permute-done.25.refs_2_), channel_id=1, source_target_pairs={{0,1},{1,0},{2,3},{3,2},{4,5},{5,4},{6,7},{7,6},{8,9},{9,8},{10,11... | collective-permute-start | bytes 1572872 | tf_op jit(solution)/shard_map/ppermute | solution.py:214
  38.1 14.3 %collective-permute-start.12 = (bf16[256,1024]{1,0:T(8,128)(2,1)S(1)}, bf16[256,1024]{1,0:T(8,128)(2,1)S(1)}, u32[]{:S(2)}, u32[]{:S(2)}) collective-permute-start(bf16[256,1024]{1,0:T(8,128)(2,1)S(1)} %collective-permute-done.9.refs_11_), channel_id=1, source_target_pairs={{0,96},{8,104},{16,112},{24,120},{32,0},{40,8},{48,16},{56,24},{64... | collective-permute-start | bytes 1572872 | tf_op jit(solution)/shard_map/ppermute | solution.py:206
  39.4 13.1 %collective-permute-start.29 = (bf16[256,1024]{1,0:T(8,128)(2,1)S(1)}, bf16[256,1024]{1,0:T(8,128)(2,1)S(1)}, u32[]{:S(2)}, u32[]{:S(2)}) collective-permute-start(bf16[256,1024]{1,0:T(8,128)(2,1)S(1)} %collective-permute-done.28.refs_4_), channel_id=1, source_target_pairs={{0,1},{1,0},{2,3},{3,2},{4,5},{5,4},{6,7},{7,6},{8,9},{9,8},{10,11... | collective-permute-start | bytes 1572872 | tf_op jit(solution)/shard_map/ppermute | solution.py:214
  47.7 13.9 %collective-permute-start.5 = (bf16[256,1024]{1,0:T(8,128)(2,1)S(1)}, bf16[256,1024]{1,0:T(8,128)(2,1)S(1)}, u32[]{:S(2)}, u32[]{:S(2)}) collective-permute-start(bf16[256,1024]{1,0:T(8,128)(2,1)S(1)} %get-tuple-element.25.refs_0_), channel_id=1, source_target_pairs={{0,8},{8,16},{16,24},{24,0},{32,40},{40,48},{48,56},{56,32},{64,72... | collective-permute-start | bytes 1572872 | tf_op jit(solution)/shard_map/ppermute | solution.py:202
  47.7 14.4 %collective-permute-start.3 = (bf16[256,1024]{1,0:T(8,128)(2,1)S(1)}, bf16[256,1024]{1,0:T(8,128)(2,1)S(1)}, u32[]{:S(2)}, u32[]{:S(2)}) collective-permute-start(bf16[256,1024]{1,0:T(8,128)(2,1)S(1)} %collective-permute-done.1.refs_2_), channel_id=1, source_target_pairs={{0,24},{8,0},{16,8},{24,16},{32,56},{40,32},{48,40},{56,48},{64,88... | collective-permute-start | bytes 1572872 | tf_op jit(solution)/shard_map/ppermute | solution.py:202
  50.9 20.7 %collective-permute-start = (bf16[256,1024]{1,0:T(8,128)(2,1)S(1)}, bf16[256,1024]{1,0:T(8,128)(2,1)S(1)}, u32[]{:S(2)}, u32[]{:S(2)}) collective-permute-start(bf16[256,1024]{1,0:T(8,128)(2,1)S(1)} %get-tuple-element.25.refs_0_), channel_id=1, source_target_pairs={{0,1},{1,0},{2,3},{3,2},{4,5},{5,4},{6,7},{7,6},{8,9},{9,8},{10,11... | collective-permute-start | bytes 1572872 | tf_op jit(solution)/shard_map/ppermute | solution.py:214
  61.6 17.5 %collective-permute-start.6 = (bf16[256,1024]{1,0:T(8,128)(2,1)S(1)}, bf16[256,1024]{1,0:T(8,128)(2,1)S(1)}, u32[]{:S(2)}, u32[]{:S(2)}) collective-permute-start(bf16[256,1024]{1,0:T(8,128)(2,1)S(1)} %collective-permute-done.5.refs_6_), channel_id=1, source_target_pairs={{0,1},{1,0},{2,3},{3,2},{4,5},{5,4},{6,7},{7,6},{8,9},{9,8},{10,11... | collective-permute-start | bytes 1572872 | tf_op jit(solution)/shard_map/ppermute | solution.py:214
  61.6 19.1 %collective-permute-start.2 = (bf16[256,1024]{1,0:T(8,128)(2,1)S(1)}, bf16[256,1024]{1,0:T(8,128)(2,1)S(1)}, u32[]{:S(2)}, u32[]{:S(2)}) collective-permute-start(bf16[256,1024]{1,0:T(8,128)(2,1)S(1)} %collective-permute-done.1.refs_2_), channel_id=1, source_target_pairs={{0,1},{1,0},{2,3},{3,2},{4,5},{5,4},{6,7},{7,6},{8,9},{9,8},{10,11... | collective-permute-start | bytes 1572872 | tf_op jit(solution)/shard_map/ppermute | solution.py:214
  62.1 20.4 %collective-permute-start.4 = (bf16[256,1024]{1,0:T(8,128)(2,1)S(1)}, bf16[256,1024]{1,0:T(8,128)(2,1)S(1)}, u32[]{:S(2)}, u32[]{:S(2)}) collective-permute-start(bf16[256,1024]{1,0:T(8,128)(2,1)S(1)} %collective-permute-done.3.refs_4_), channel_id=1, source_target_pairs={{0,1},{1,0},{2,3},{3,2},{4,5},{5,4},{6,7},{7,6},{8,9},{9,8},{10,11... | collective-permute-start | bytes 1572872 | tf_op jit(solution)/shard_map/ppermute | solution.py:214
  71.6 19.1 %collective-permute-start.31 = (bf16[2,256,256]{2,1,0:T(8,128)(2,1)S(1)}, bf16[2,256,256]{2,1,0:T(8,128)(2,1)S(1)}, u32[]{:S(2)}, u32[]{:S(2)}) collective-permute-start(bf16[2,256,256]{2,1,0:T(8,128)(2,1)S(1)} %get-tuple-element.38), channel_id=1, source_target_pairs={{0,6},{1,7},{2,0},{3,1},{4,2},{5,3},{6,4},{7,5},{8,14},{9,15},{10,... | collective-permute-start | bytes 786440 | tf_op jit(solution)/shard_map/ppermute | solution.py:210
  79.0 11.8 %collective-permute-start.33 = (bf16[2,256,256]{2,1,0:T(8,128)(2,1)S(1)}, bf16[2,256,256]{2,1,0:T(8,128)(2,1)S(1)}, u32[]{:S(2)}, u32[]{:S(2)}) collective-permute-start(bf16[2,256,256]{2,1,0:T(8,128)(2,1)S(1)} %add_convert_fusion.1), channel_id=1, source_target_pairs={{0,2},{1,3},{2,4},{3,5},{4,6},{5,7},{6,0},{7,1},{8,10},{9,11},{10,... | collective-permute-start | bytes 786440 | tf_op jit(solution)/shard_map/ppermute | solution.py:210
  79.1 14.4 %collective-permute-start.36 = (bf16[2,256,256]{2,1,0:T(8,128)(2,1)S(1)}, bf16[2,256,256]{2,1,0:T(8,128)(2,1)S(1)}, u32[]{:S(2)}, u32[]{:S(2)}) collective-permute-start(bf16[2,256,256]{2,1,0:T(8,128)(2,1)S(1)} %get-tuple-element.42), channel_id=1, source_target_pairs={{0,2},{1,3},{2,4},{3,5},{4,6},{5,7},{6,0},{7,1},{8,10},{9,11},{10,... | collective-permute-start | bytes 786440 | tf_op jit(solution)/shard_map/ppermute | solution.py:210
  80.7 12.8 %collective-permute-start.38 = (bf16[2,256,256]{2,1,0:T(8,128)(2,1)S(1)}, bf16[2,256,256]{2,1,0:T(8,128)(2,1)S(1)}, u32[]{:S(2)}, u32[]{:S(2)}) collective-permute-start(bf16[2,256,256]{2,1,0:T(8,128)(2,1)S(1)} %add_convert_fusion), channel_id=1, source_target_pairs={{0,6},{1,7},{2,0},{3,1},{4,2},{5,3},{6,4},{7,5},{8,14},{9,15},{10,... | collective-permute-start | bytes 786440 | tf_op jit(solution)/shard_map/ppermute | solution.py:210
  89.6 21.9 %collective-permute-start.15 = (bf16[2,256,256]{2,1,0:T(8,128)(2,1)}, bf16[2,256,256]{2,1,0:T(8,128)(2,1)}, u32[]{:S(2)}, u32[]{:S(2)}) collective-permute-start(bf16[2,256,256]{2,1,0:T(8,128)(2,1)} %get-tuple-element.31), channel_id=1, source_target_pairs={{0,2},{1,3},{2,4},{3,5},{4,6},{5,7},{6,0},{7,1},{8,10},{9,11},{10,... | collective-permute-start | bytes 786440 | tf_op jit(solution)/shard_map/ppermute | solution.py:210
  100.7 14.2 %collective-permute-start.20 = (bf16[2,256,256]{2,1,0:T(8,128)(2,1)S(1)}, bf16[2,256,256]{2,1,0:T(8,128)(2,1)}, u32[]{:S(2)}, u32[]{:S(2)}) collective-permute-start(bf16[2,256,256]{2,1,0:T(8,128)(2,1)S(1)} %get-tuple-element.35), channel_id=1, source_target_pairs={{0,6},{1,7},{2,0},{3,1},{4,2},{5,3},{6,4},{7,5},{8,14},{9,15},{10,... | collective-permute-start | bytes 786440 | tf_op jit(solution)/shard_map/ppermute | solution.py:210
  102.8 16.1 %collective-permute-start.14 = (bf16[2,256,256]{2,1,0:T(8,128)(2,1)S(1)}, bf16[2,256,256]{2,1,0:T(8,128)(2,1)}, u32[]{:S(2)}, u32[]{:S(2)}) collective-permute-start(bf16[2,256,256]{2,1,0:T(8,128)(2,1)S(1)} %get-tuple-element.29), channel_id=1, source_target_pairs={{0,6},{1,7},{2,0},{3,1},{4,2},{5,3},{6,4},{7,5},{8,14},{9,15},{10,... | collective-permute-start | bytes 786440 | tf_op jit(solution)/shard_map/ppermute | solution.py:210
  105.9 35.7 %all-to-all-start.1 = ((bf16[16,1,128,256]{3,2,1,0:T(8,128)(2,1)}), bf16[16,1,128,256]{3,2,1,0:T(8,128)(2,1)S(1)}, u32[]{:S(2)}, u32[]{:S(2)}) async-start(bf16[16,1,128,256]{3,2,1,0:T(8,128)(2,1)} %pack.3), calls=%async_computation.1 | async-start | bytes 2097152 | tf_op jit(solution)/shard_map/all_to_all | solution.py:240
  114.5 14.0 %collective-permute-start.19 = (bf16[2,256,256]{2,1,0:T(8,128)(2,1)S(1)}, bf16[2,256,256]{2,1,0:T(8,128)(2,1)S(1)}, u32[]{:S(2)}, u32[]{:S(2)}) collective-permute-start(bf16[2,256,256]{2,1,0:T(8,128)(2,1)S(1)} %get-tuple-element.33), channel_id=1, source_target_pairs={{0,2},{1,3},{2,4},{3,5},{4,6},{5,7},{6,0},{7,1},{8,10},{9,11},{10,... | collective-permute-start | bytes 786440 | tf_op jit(solution)/shard_map/ppermute | solution.py:210
  115.9 12.7 %collective-permute-start.21 = (bf16[2,256,256]{2,1,0:T(8,128)(2,1)S(1)}, bf16[2,256,256]{2,1,0:T(8,128)(2,1)S(1)}, u32[]{:S(2)}, u32[]{:S(2)}) collective-permute-start(bf16[2,256,256]{2,1,0:T(8,128)(2,1)S(1)} %add_convert_fusion.2), channel_id=1, source_target_pairs={{0,6},{1,7},{2,0},{3,1},{4,2},{5,3},{6,4},{7,5},{8,14},{9,15},{10,... | collective-permute-start | bytes 786440 | tf_op jit(solution)/shard_map/ppermute | solution.py:210
  124.0 12.6 %collective-permute-start.18 = (bf16[256,256]{1,0:T(8,128)(2,1)S(1)}, bf16[256,256]{1,0:T(8,128)(2,1)S(1)}, u32[]{:S(2)}, u32[]{:S(2)}) collective-permute-start(bf16[256,256]{1,0:T(8,128)(2,1)S(1)} %get-tuple-element.51), channel_id=1, source_target_pairs={{0,8},{1,16},{2,10},{3,18},{4,12},{5,20},{6,14},{7,22},{8,24},{9,0... | collective-permute-start | bytes 393224 | tf_op jit(solution)/shard_map/ppermute | solution.py:235
  141.6 25.1 %all-to-all-start = ((bf16[16,1,128,256]{3,2,1,0:T(8,128)(2,1)}), bf16[16,1,128,256]{3,2,1,0:T(8,128)(2,1)S(1)}, u32[]{:S(2)}, u32[]{:S(2)}) async-start(bf16[16,1,128,256]{3,2,1,0:T(8,128)(2,1)} %pack.2), calls=%async_computation | async-start | bytes 2097152 | tf_op jit(solution)/shard_map/all_to_all | solution.py:240
  (15 other events, 111.7 us)

commit v2 on v1

--- a/solution.py
+++ b/solution.py
@@ -23,19 +23,6 @@
 
 
 SWAP = [(c, c ^ 1) for c in range(8)]
-
-
-def block_round(m):
-    pairs = []
-    for x in range(4):
-        for y in range(4):
-            for z in range(4):
-                for k in range(2):
-                    u = 2 * (y % 2) + k
-                    source = (4 * x + y) * 8 + 2 * z + k
-                    target = (4 * x + (u + m) % 4) * 8 + 2 * z + y // 2
-                    pairs.append((source, target))
-    return pairs
 
 
 def position():
@@ -96,46 +83,48 @@
 
 
 def product_body(*refs):
-    rows, cols, outs = refs[:8], refs[8:16], refs[16:24]
-    rows_ref, cols_ref, row_sems, col_sems = refs[24:]
-    x, y, z, k = position()
-    u = 2 * (y % 2) + k
-    across = (pl.ds(0, 1024), pl.ds(1024, 1024))
-    col_copies, row_copies = [], []
+    rows, cols = refs[:8], refs[8:16]
+    up, down, next_low, prev_high, own = refs[16:21]
+    rows_ref, cols_ref, row_sems, col_sems = refs[21:]
+    x, _, z, _ = position()
+    copies = []
     for d in range(4):
         for h in range(2):
-            target = cols_ref.at[(x + d) % 4, :, across[h]]
-            col_copies.append(pltpu.make_async_copy(cols[2 * d + h], target, col_sems.at[2 * d + h]))
-    for d in range(4):
-        slot = (y + d - u + 4) % 4
-        for h in range(2):
-            target = rows_ref.at[slot, :, across[h]]
-            row_copies.append(pltpu.make_async_copy(rows[2 * d + h], target, row_sems.at[2 * slot + h]))
-    for copy in col_copies + row_copies:
+            across = pl.ds(1024 * h, 1024)
+            at = 2 * d + h
+            copies.append(
+                pltpu.make_async_copy(cols[at], cols_ref.at[(x + d) % 4, :, across], col_sems.at[at])
+            )
+            copies.append(
+                pltpu.make_async_copy(rows[at], rows_ref.at[d, :, across], row_sems.at[at])
+            )
+    for copy in copies:
         copy.start()
-    for copy in col_copies:
+    for copy in copies:
         copy.wait()
-    for at, d in enumerate((2, 1, 3, 0)):
+    places = (
+        (2, ((up, 0), (up, 1), (down, 0), (down, 1))),
+        (1, ((next_low, 0), (next_low, 1), (up, 2), (up, 3))),
+        (3, ((down, 2), (down, 3), (prev_high, 0), (prev_high, 1))),
+        (0, ((own, 0), (own, 1), (own, 2), (own, 3))),
+    )
+    for d, targets in places:
         right = cols_ref[(z + d) % 4]
-        for m in range(4):
-            if at == 0:
-                for h in range(2):
-                    target = rows_ref.at[m, :, across[h]]
-                    pltpu.make_async_copy(rows[h], target, row_sems.at[2 * m + h]).wait()
-            out = outs[2 * at + m // 2]
-            out[m % 2] = lax.dot_general(
-                rows_ref[m], right, (((1,), (1,)), ((), ())), preferred_element_type=jnp.float32
+        for j, (out, at) in enumerate(targets):
+            out[at] = lax.dot_general(
+                rows_ref[j], right, (((1,), (1,)), ((), ())), preferred_element_type=jnp.float32
             ).astype(out.dtype)
 
 
 def product(rows, cols):
-    sent = jax.ShapeDtypeStruct((2, TILE, TILE), jnp.bfloat16)
-    kept = jax.ShapeDtypeStruct((2, TILE, TILE), jnp.float32)
+    four = jax.ShapeDtypeStruct((4, TILE, TILE), jnp.bfloat16)
+    two = jax.ShapeDtypeStruct((2, TILE, TILE), jnp.bfloat16)
+    kept = jax.ShapeDtypeStruct((4, TILE, TILE), jnp.float32)
     return pl.pallas_call(
         product_body,
-        out_shape=(sent,) * 6 + (kept,) * 2,
+        out_shape=(four, four, two, two, kept),
         in_specs=[pl.BlockSpec(memory_space=pl.ANY)] * 16,
-        out_specs=tuple(pl.BlockSpec(memory_space=pltpu.VMEM) for _ in range(8)),
+        out_specs=tuple(pl.BlockSpec(memory_space=pltpu.VMEM) for _ in range(5)),
         scratch_shapes=[
             pltpu.VMEM((4, TILE, 2048), jnp.bfloat16),
             pltpu.VMEM((4, TILE, 2048), jnp.bfloat16),
@@ -147,34 +136,72 @@
     )(*rows, *cols)
 
 
+def finish_body(own, got_up, got_down, sum_up, sum_down, *outs):
+    for j in range(2):
+        outs[j][...] = (
+            own[j] + got_down[2 + j].astype(jnp.float32) + sum_up[j].astype(jnp.float32)
+        ).astype(jnp.bfloat16)
+        outs[2 + j][...] = (
+            own[2 + j] + got_up[2 + j].astype(jnp.float32) + sum_down[j].astype(jnp.float32)
+        ).astype(jnp.bfloat16)
+
+
+def finish(*parts):
+    piece = jax.ShapeDtypeStruct((TILE, TILE), jnp.bfloat16)
+    return pl.pallas_call(
+        finish_body,
+        out_shape=(piece,) * 4,
+        in_specs=[pl.BlockSpec(memory_space=pltpu.VMEM)] * 5,
+        out_specs=(pl.BlockSpec(memory_space=pltpu.VMEM),) * 4,
+        compiler_params=pltpu.CompilerParams(vmem_limit_bytes=8 * 1024 * 1024),
+        name="finish",
+    )(*parts)
+
+
 def pack_body(owners_ref, *refs):
-    arrived, out_ref, sems = refs[:4], refs[4], refs[5]
-    _, y, _, _ = position()
+    arrived, out_ref, sems = refs[:8], refs[8], refs[9]
+    _, y, _, k = position()
     out_ref[...] = jnp.zeros_like(out_ref)
-    copies = []
-    for m in range(4):
-        column = (y - m + 4) % 4
-        for i in range(2):
-            copies.append(
-                pltpu.make_async_copy(
-                    arrived[m].at[pl.ds(i * HALF, HALF)],
-                    out_ref.at[owners_ref[i, column], 0],
-                    sems.at[2 * m + i],
+
+    def copies(e):
+        line = (y + e) % 4
+        found = []
+        for source, parity in ((arrived[e], k), (arrived[4 + e], 1 - k)):
+            for i in range(2):
+                owner = owners_ref[i, 2 * (line & 1) + parity]
+                found.append(
+                    pltpu.make_async_copy(
+                        source.at[pl.ds(i * HALF, HALF)],
+                        out_ref.at[owner, 0],
+                        sems.at[4 * e + len(found)],
+                    )
                 )
-            )
-    for copy in copies:
-        copy.start()
-    for copy in copies:
-        copy.wait()
+        return line >> 1 == k, found
+
+    for e in range(4):
+        wanted, found = copies(e)
+
+        @pl.when(wanted)
+        def _():
+            for copy in found:
+                copy.start()
+
+    for e in range(4):
+        wanted, found = copies(e)
+
+        @pl.when(wanted)
+        def _():
+            for copy in found:
+                copy.wait()
 
 
 def pack(owners, arrived):
     return pl.pallas_call(
         pack_body,
         out_shape=jax.ShapeDtypeStruct((16, 1, HALF, TILE), jnp.bfloat16),
-        in_specs=[pl.BlockSpec(memory_space=pltpu.SMEM)] + [pl.BlockSpec(memory_space=pl.ANY)] * 4,
+        in_specs=[pl.BlockSpec(memory_space=pltpu.SMEM)] + [pl.BlockSpec(memory_space=pl.ANY)] * 8,
         out_specs=pl.BlockSpec(memory_space=pltpu.VMEM),
-        scratch_shapes=[pltpu.SemaphoreType.DMA((8,))],
+        scratch_shapes=[pltpu.SemaphoreType.DMA((16,))],
         compiler_params=pltpu.CompilerParams(vmem_limit_bytes=4 * 1024 * 1024),
         name="pack",
     )(owners, *arrived)
@@ -219,24 +246,20 @@
 
 
 def reduce_along_z(partials):
-    opp_a, opp_b, next_a, next_b, prev_a, prev_b, own_a, own_b = partials
-    opp_up, opp_down = zpass(opp_a, 1), zpass(opp_b, -1)
-    far_b, far_a = zpass(next_b, 1), zpass(prev_a, -1)
-    sum_a = zpass(add(next_a, opp_up), 1)
-    sum_b = zpass(add(prev_b, opp_down), -1)
-    return tuple(
-        add(own[m], far[m], total[m])
-        for own, far, total in ((own_a, far_a, sum_a), (own_b, far_b, sum_b))
-        for m in range(2)
-    )
-
-
-def to_blocks(rounds):
-    return [lax.ppermute(rounds[m], ("row", "col"), block_round(m)) for m in range(4)]
-
-
-def to_owners(owners, arrived):
-    outgoing = pack(owners, arrived)
+    up, down, next_low, prev_high, own = partials
+    got_down, got_up = zpass(down, -1), zpass(up, 1)
+    sum_down = zpass(add(prev_high, got_down[:2]), -1)
+    sum_up = zpass(add(next_low, got_up[:2]), 1)
+    return finish(own, got_up, got_down, sum_up, sum_down)
+
+
+def to_owners(owners, sums):
+    own, after, opp, before = sums
+    from_opp = ypass(opp, 2)
+    from_before, from_after = ypass(after, 1), ypass(before, -1)
+    mine = (own, from_after, from_opp, from_before)
+    other = [swap(value) for value in mine]
+    outgoing = pack(owners, (*mine, *other))
     return lax.all_to_all(outgoing, "row", split_axis=0, concat_axis=0, tiled=True)
 
 
@@ -254,10 +277,8 @@
     for pieces in ((top, top_p, top_o, top_m), (low, low_p, low_o, low_m)):
         rows = [piece for value in pieces for piece in (value, swap(value))]
         halves.append(product(rows, cols))
-    arrived = to_blocks(reduce_along_z(halves[0]))
-    first = to_owners(owner_rows, arrived)
-    arrived = to_blocks(reduce_along_z(halves[1]))
-    second = to_owners(owner_rows, arrived)
+    first = to_owners(owner_rows, reduce_along_z(halves[0]))
+    second = to_owners(owner_rows, reduce_along_z(halves[1]))
     return place_half(1, second, place_half(0, first))
 
 

time: 168 us -> 156 us (0.929)
  starting transfers between devices: 72 us -> 49 us
  waiting for transfers between devices: 67.4 us -> 83 us
  Pallas kernels: 21.9 us -> 19.2 us
  other arithmetic: 3.47 us -> 1.21 us
    ppermute x8 -> x0, starting transfers between devices: 22.2 us -> none  [to_blocks(): lax.ppermute(rounds[m], ('row', 'col'), block_round(m))]
    ppermute x6 -> x12, waiting for transfers between devices: 10.4 us -> 25.7 us  [ypass(): return lax.ppermute(value, 'row', along_y(step))]
    ppermute x6 -> x12, starting transfers between devices: 9.67 us -> 16.3 us  [ypass(): return lax.ppermute(value, 'row', along_y(step))]
    all_to_all x2, starting transfers between devices: 13.3 us -> 7.96 us  [to_owners(): lax.all_to_all(outgoing, 'row', split_axis=0, concat_axis=0, tiled=True)]
    pallas_call x2 -> x4, Pallas kernels: 14.2 us -> 11.2 us  [the longest x2 10.9 us: product(): pl.pallas_call(product_body, out_shape=(four, four, two, two, kept), in_s...]
    ppermute x12 -> x8, starting transfers between devices: 17 us -> 14.3 us  [zpass(): return lax.ppermute(value, 'col', along_z(step))]
    ppermute x8 -> x0, waiting for transfers between devices: 2.53 us -> none  [to_blocks(): lax.ppermute(rounds[m], ('row', 'col'), block_round(m))]
    ppermute x9 -> x17, waiting for transfers between devices: 0.02 us -> 2.38 us  [swap(): return lax.ppermute(value, 'col', SWAP)]
  transfers between devices with their start and end apart: 43 -> 45, of which waited for: 11 -> 19; matrix products, arithmetic and copies ran while one was open for 2% -> 1% of each run, Pallas kernels for 12% -> 11%
where the time goes in v2:
time: 156 us; the launch traced here: 155 us
  waiting for transfers between devices  83 us (53%)
  starting transfers between devices  49 us (31%)
  Pallas kernels  19.2 us (12%)
  local copies, waits for them, and re-layouts  2.6 us (2%)
    ppermute x12, waiting for transfers between devices, ypass(): return lax.ppermute(value, 'row', along_y(step))  25.7 us
    ppermute x6, waiting for transfers between devices, xpass(): return lax.ppermute(value, 'row', along_x(step))  19.4 us
    ppermute x8, waiting for transfers between devices, zpass(): return lax.ppermute(value, 'col', along_z(step))  18.4 us
    all_to_all x2, waiting for transfers between devices, to_owners(): lax.all_to_all(outgoing, 'row', split_axis=0, concat_axis=0, tiled=True)  17.2 us
    ppermute x12, starting transfers between devices, ypass(): return lax.ppermute(value, 'row', along_y(step))  16.3 us
    ppermute x8, starting transfers between devices, zpass(): return lax.ppermute(value, 'col', along_z(step))  14.3 us
    pallas_call x2, Pallas kernels, product(): pl.pallas_call(product_body, out_shape=(four, four, two, two, kept), in_s...  10.9 us
    ppermute x6, starting transfers between devices, xpass(): return lax.ppermute(value, 'row', along_x(step))  9.25 us
  transfers between devices with their start and end apart: 45, of which 19 were waited for; matrix products, arithmetic and copies ran while one was open for 1% of the time, Pallas kernels for 11%

profile of v2, /device:TPU:0, one launch (start us, length us, event | category | flops | bytes accessed | tf_op | source)
XLA Modules:
  0.0 155.4 jit_solution(3180079433152892280)
XLA Ops:
  3.7 3.2 %collective-permute-start.1 = (bf16[256,1024]{1,0:T(8,128)(2,1)S(1)}, bf16[256,1024]{1,0:T(8,128)(2,1)S(1)}, u32[]{:S(2)}, u32[]{:S(2)}) collective-permute-start(bf16[256,1024]{1,0:T(8,128)(2,1)S(1)} %get-tuple-element.27.refs_0_), channel_id=1, source_target_pairs={{0,24},{8,0},{16,8},{24,16},{32,56},{40,32},{48,40},{56,48},{64,88... | collective-permute-start | bytes 1572872 | tf_op jit(solution)/shard_map/ppermute | solution.py:229
  6.9 1.5 collective-permute-start.10
  8.4 1.7 %collective-permute-start.8 = (bf16[256,1024]{1,0:T(8,128)(2,1)S(1)}, bf16[256,1024]{1,0:T(8,128)(2,1)S(1)}, u32[]{:S(2)}, u32[]{:S(2)}) collective-permute-start(bf16[256,1024]{1,0:T(8,128)(2,1)S(1)} %get-tuple-element.28.refs_8_), channel_id=1, source_target_pairs={{0,96},{8,104},{16,112},{24,120},{32,0},{40,8},{48,16},{56,24},{64... | collective-permute-start | bytes 1572872 | tf_op jit(solution)/shard_map/ppermute | solution.py:233
  10.2 3.2 %collective-permute-start.26 = (bf16[256,1024]{1,0:T(8,128)(2,1)S(1)}, bf16[256,1024]{1,0:T(8,128)(2,1)S(1)}, u32[]{:S(2)}, u32[]{:S(2)}) collective-permute-start(bf16[256,1024]{1,0:T(8,128)(2,1)S(1)} %get-tuple-element.39.refs_0_), channel_id=1, source_target_pairs={{0,24},{8,0},{16,8},{24,16},{32,56},{40,32},{48,40},{56,48},{64,88... | collective-permute-start | bytes 1572872 | tf_op jit(solution)/shard_map/ppermute | solution.py:229
  13.4 5.8 %collective-permute-done.1.refs_2_ = bf16[256,1024]{1,0:T(8,128)(2,1)S(1)} collective-permute-done((bf16[256,1024]{1,0:T(8,128)(2,1)S(1)}, bf16[256,1024]{1,0:T(8,128)(2,1)S(1)}, u32[]{:S(2)}, u32[]{:S(2)}) %collective-permute-start.1) | collective-permute-done | bytes 524320 | tf_op jit(solution)/shard_map/ppermute | solution.py:229
  19.3 2.9 %collective-permute-done.10.refs_14_ = bf16[256,1024]{1,0:T(8,128)(2,1)S(1)} collective-permute-done((bf16[256,1024]{1,0:T(8,128)(2,1)S(1)}, bf16[256,1024]{1,0:T(8,128)(2,1)S(1)}, u32[]{:S(2)}, u32[]{:S(2)}) %collective-permute-start.10) | collective-permute-done | bytes 524320 | tf_op jit(solution)/shard_map/ppermute | solution.py:233
  22.4 3.0 %collective-permute-start.9 = (bf16[256,1024]{1,0:T(8,128)(2,1)S(1)}, bf16[256,1024]{1,0:T(8,128)(2,1)S(1)}, u32[]{:S(2)}, u32[]{:S(2)}) collective-permute-start(bf16[256,1024]{1,0:T(8,128)(2,1)S(1)} %collective-permute-done.7.refs_9_), channel_id=1, source_target_pairs={{0,96},{8,104},{16,112},{24,120},{32,0},{40,8},{48,16},{56,24},{64... | collective-permute-start | bytes 1572872 | tf_op jit(solution)/shard_map/ppermute | solution.py:233
  25.4 4.6 %collective-permute-done.26.refs_2_ = bf16[256,1024]{1,0:T(8,128)(2,1)S(1)} collective-permute-done((bf16[256,1024]{1,0:T(8,128)(2,1)S(1)}, bf16[256,1024]{1,0:T(8,128)(2,1)S(1)}, u32[]{:S(2)}, u32[]{:S(2)}) %collective-permute-start.26) | collective-permute-done | bytes 524320 | tf_op jit(solution)/shard_map/ppermute | solution.py:229
  30.0 1.5 collective-permute-start.11
  31.5 6.7 %collective-permute-done.13.refs_15_ = bf16[256,1024]{1,0:T(8,128)(2,1)S(1)} collective-permute-done((bf16[256,1024]{1,0:T(8,128)(2,1)S(1)}, bf16[256,1024]{1,0:T(8,128)(2,1)S(1)}, u32[]{:S(2)}, u32[]{:S(2)}) %collective-permute-start.13) | collective-permute-done | bytes 524320 | tf_op jit(solution)/shard_map/ppermute | solution.py:233
  39.4 8.3 %collective-permute-done.11.refs_12_ = bf16[256,1024]{1,0:T(8,128)(2,1)S(1)} collective-permute-done((bf16[256,1024]{1,0:T(8,128)(2,1)S(1)}, bf16[256,1024]{1,0:T(8,128)(2,1)S(1)}, u32[]{:S(2)}, u32[]{:S(2)}) %collective-permute-start.11) | collective-permute-done | bytes 524320 | tf_op jit(solution)/shard_map/ppermute | solution.py:233
  47.7 3.2 %collective-permute-start.3 = (bf16[256,1024]{1,0:T(8,128)(2,1)S(1)}, bf16[256,1024]{1,0:T(8,128)(2,1)S(1)}, u32[]{:S(2)}, u32[]{:S(2)}) collective-permute-start(bf16[256,1024]{1,0:T(8,128)(2,1)S(1)} %collective-permute-done.1.refs_2_), channel_id=1, source_target_pairs={{0,24},{8,0},{16,8},{24,16},{32,56},{40,32},{48,40},{56,48},{64,88... | collective-permute-start | bytes 1572872 | tf_op jit(solution)/shard_map/ppermute | solution.py:229
  50.9 1.5 collective-permute-done.12.refs_13_
  52.5 5.4 %product.3 = (bf16[4,256,256]{2,1,0:T(8,128)(2,1)S(1)}, bf16[4,256,256]{2,1,0:T(8,128)(2,1)S(1)}, bf16[2,256,256]{2,1,0:T(8,128)(2,1)S(1)}, bf16[2,256,256]{2,1,0:T(8,128)(2,1)S(1)}, f32[4,256,256]{2,1,0:T(8,128)S(1)}) custom-call(bf16[256,1024]{1,0:T(8,128)(2,1)S(1)} %get-tuple-element.39.refs_0_, bf16[256,1024]{1,0:T(8,128)(2,1)S(1)} %collective-permute-done.25.refs_1_, ...), custom_call_target="tpu_custom_call" | custom-call | tf_op jit(solution)/shard_map/product/pallas_call | solution.py:123
  57.9 2.0 %collective-permute-start.32 = (bf16[4,256,256]{2,1,0:T(8,128)(2,1)S(1)}, bf16[4,256,256]{2,1,0:T(8,128)(2,1)S(1)}, u32[]{:S(2)}, u32[]{:S(2)}) collective-permute-start(bf16[4,256,256]{2,1,0:T(8,128)(2,1)S(1)} %get-tuple-element.41), channel_id=1, source_target_pairs={{0,2},{1,3},{2,4},{3,5},{4,6},{5,7},{6,0},{7,1},{8,10},{9,11},{10,... | collective-permute-start | bytes 1572872 | tf_op jit(solution)/shard_map/ppermute | solution.py:237
  59.9 2.2 %collective-permute-start.33 = (bf16[4,256,256]{2,1,0:T(8,128)(2,1)S(1)}, bf16[4,256,256]{2,1,0:T(8,128)(2,1)S(1)}, u32[]{:S(2)}, u32[]{:S(2)}) collective-permute-start(bf16[4,256,256]{2,1,0:T(8,128)(2,1)S(1)} %get-tuple-element.42), channel_id=1, source_target_pairs={{0,6},{1,7},{2,0},{3,1},{4,2},{5,3},{6,4},{7,5},{8,14},{9,15},{10,... | collective-permute-start | bytes 1572872 | tf_op jit(solution)/shard_map/ppermute | solution.py:237
  62.7 11.1 %collective-permute-done.32.got_up = bf16[4,256,256]{2,1,0:T(8,128)(2,1)S(1)} collective-permute-done((bf16[4,256,256]{2,1,0:T(8,128)(2,1)S(1)}, bf16[4,256,256]{2,1,0:T(8,128)(2,1)S(1)}, u32[]{:S(2)}, u32[]{:S(2)}) %collective-permute-start.32) | collective-permute-done | bytes 524320 | tf_op jit(solution)/shard_map/ppermute | solution.py:237
  75.1 2.4 %collective-permute-start.35 = (bf16[2,256,256]{2,1,0:T(8,128)(2,1)S(1)}, bf16[2,256,256]{2,1,0:T(8,128)(2,1)S(1)}, u32[]{:S(2)}, u32[]{:S(2)}) collective-permute-start(bf16[2,256,256]{2,1,0:T(8,128)(2,1)S(1)} %add_convert_fusion), channel_id=1, source_target_pairs={{0,6},{1,7},{2,0},{3,1},{4,2},{5,3},{6,4},{7,5},{8,14},{9,15},{10,... | collective-permute-start | bytes 786440 | tf_op jit(solution)/shard_map/ppermute | solution.py:237
  77.5 5.4 %product.2 = (bf16[4,256,256]{2,1,0:T(8,128)(2,1)}, bf16[4,256,256]{2,1,0:T(8,128)(2,1)}, bf16[2,256,256]{2,1,0:T(8,128)(2,1)S(1)}, bf16[2,256,256]{2,1,0:T(8,128)(2,1)S(1)}, f32[4,256,256]{2,1,0:T(8,128)S(1)}) custom-call(bf16[256,1024]{1,0:T(8,128)(2,1)S(1)} %get-tuple-element.27.refs_0_, bf16[256,1024]{1,0:T(8,128)(2,1)S(1)} %collective-permute-done.refs_1_, ...), custom_call_target="tpu_custom_call" | custom-call | tf_op jit(solution)/shard_map/product/pallas_call | solution.py:123
  85.1 3.1 %collective-permute-start.15 = (bf16[4,256,256]{2,1,0:T(8,128)(2,1)}, bf16[4,256,256]{2,1,0:T(8,128)(2,1)S(1)}, u32[]{:S(2)}, u32[]{:S(2)}) collective-permute-start(bf16[4,256,256]{2,1,0:T(8,128)(2,1)} %get-tuple-element.32), channel_id=1, source_target_pairs={{0,6},{1,7},{2,0},{3,1},{4,2},{5,3},{6,4},{7,5},{8,14},{9,15},{10,... | collective-permute-start | bytes 1572872 | tf_op jit(solution)/shard_map/ppermute | solution.py:237
  89.6 5.9 %collective-permute-done.37.refs_2_ = bf16[256,256]{1,0:T(8,128)(2,1)S(1)} collective-permute-done((bf16[256,256]{1,0:T(8,128)(2,1)S(1)}, bf16[256,256]{1,0:T(8,128)(2,1)S(1)}, u32[]{:S(2)}, u32[]{:S(2)}) %collective-permute-start.37) | collective-permute-done | bytes 131104 | tf_op jit(solution)/shard_map/ppermute | solution.py:229
  98.2 2.5 %pack.3 = bf16[16,1,128,256]{3,2,1,0:T(8,128)(2,1)} custom-call(s32[2,4]{1,0:T(2,128)S(1)} %copy-done.3, bf16[256,256]{1,0:T(8,128)(2,1)S(1)} %get-tuple-element.45.refs_0_, bf16[256,256]{1,0:T(8,128)(2,1)S(1)} %collective-permute-done.36.refs_1_, bf16[256,256]{1,0:T(8,128)(2,1)S(1)} %collective-permute-done.37.refs_2_, ...), custom_call_target="tpu_custom_call" | custom-call | tf_op jit(solution)/shard_map/pack/pallas_call | solution.py:199
  100.7 3.7 %all-to-all-start.1 = ((bf16[16,1,128,256]{3,2,1,0:T(8,128)(2,1)}), bf16[16,1,128,256]{3,2,1,0:T(8,128)(2,1)S(1)}, u32[]{:S(2)}, u32[]{:S(2)}) async-start(bf16[16,1,128,256]{3,2,1,0:T(8,128)(2,1)} %pack.3), calls=%async_computation.1 | async-start | bytes 2097152 | tf_op jit(solution)/shard_map/all_to_all | solution.py:263
  105.6 3.3 %collective-permute-start.17 = (bf16[2,256,256]{2,1,0:T(8,128)(2,1)S(1)}, bf16[2,256,256]{2,1,0:T(8,128)(2,1)S(1)}, u32[]{:S(2)}, u32[]{:S(2)}) collective-permute-start(bf16[2,256,256]{2,1,0:T(8,128)(2,1)S(1)} %add_convert_fusion.2), channel_id=1, source_target_pairs={{0,6},{1,7},{2,0},{3,1},{4,2},{5,3},{6,4},{7,5},{8,14},{9,15},{10,... | collective-permute-start | bytes 786440 | tf_op jit(solution)/shard_map/ppermute | solution.py:237
  108.9 6.4 %collective-permute-done.16.sum_up = bf16[2,256,256]{2,1,0:T(8,128)(2,1)S(1)} collective-permute-done((bf16[2,256,256]{2,1,0:T(8,128)(2,1)S(1)}, bf16[2,256,256]{2,1,0:T(8,128)(2,1)S(1)}, u32[]{:S(2)}, u32[]{:S(2)}) %collective-permute-start.16) | collective-permute-done | bytes 262176 | tf_op jit(solution)/shard_map/ppermute | solution.py:237
  115.4 2.8 %collective-permute-start.18 = (bf16[256,256]{1,0:T(8,128)(2,1)S(1)}, bf16[256,256]{1,0:T(8,128)(2,1)S(1)}, u32[]{:S(2)}, u32[]{:S(2)}) collective-permute-start(bf16[256,256]{1,0:T(8,128)(2,1)S(1)} %get-tuple-element.36), channel_id=1, source_target_pairs={{0,24},{8,0},{16,8},{24,16},{32,56},{40,32},{48,40},{56,48},{64,88... | collective-permute-start | bytes 393224 | tf_op jit(solution)/shard_map/ppermute | solution.py:229
  119.9 4.7 %collective-permute-done.18.refs_1_ = bf16[256,256]{1,0:T(8,128)(2,1)S(1)} collective-permute-done((bf16[256,256]{1,0:T(8,128)(2,1)S(1)}, bf16[256,256]{1,0:T(8,128)(2,1)S(1)}, u32[]{:S(2)}, u32[]{:S(2)}) %collective-permute-start.18) | collective-permute-done | bytes 131104 | tf_op jit(solution)/shard_map/ppermute | solution.py:229
  124.6 1.5 collective-permute-done.19.refs_2_
  126.1 1.8 %collective-permute-done.20.refs_3_ = bf16[256,256]{1,0:T(8,128)(2,1)S(1)} collective-permute-done((bf16[256,256]{1,0:T(8,128)(2,1)S(1)}, bf16[256,256]{1,0:T(8,128)(2,1)S(1)}, u32[]{:S(2)}, u32[]{:S(2)}) %collective-permute-start.20) | collective-permute-done | bytes 131104 | tf_op jit(solution)/shard_map/ppermute | solution.py:229
  129.3 2.5 %pack.2 = bf16[16,1,128,256]{3,2,1,0:T(8,128)(2,1)} custom-call(s32[2,4]{1,0:T(2,128)S(1)} %copy-done.3, bf16[256,256]{1,0:T(8,128)(2,1)S(1)} %get-tuple-element.35.refs_0_, bf16[256,256]{1,0:T(8,128)(2,1)S(1)} %collective-permute-done.18.refs_1_, bf16[256,256]{1,0:T(8,128)(2,1)S(1)} %collective-permute-done.19.refs_2_, ...), custom_call_target="tpu_custom_call" | custom-call | tf_op jit(solution)/shard_map/pack/pallas_call | solution.py:199
  131.8 4.3 %all-to-all-start = ((bf16[16,1,128,256]{3,2,1,0:T(8,128)(2,1)}), bf16[16,1,128,256]{3,2,1,0:T(8,128)(2,1)S(1)}, u32[]{:S(2)}, u32[]{:S(2)}) async-start(bf16[16,1,128,256]{3,2,1,0:T(8,128)(2,1)} %pack.2), calls=%async_computation | async-start | bytes 2097152 | tf_op jit(solution)/shard_map/all_to_all | solution.py:263
  137.1 17.2 %all-to-all-done.value_ref = bf16[16,1,128,256]{3,2,1,0:T(8,128)(2,1)S(1)} async-done(((bf16[16,1,128,256]{3,2,1,0:T(8,128)(2,1)}), bf16[16,1,128,256]{3,2,1,0:T(8,128)(2,1)S(1)}, u32[]{:S(2)}, u32[]{:S(2)}) %all-to-all-start) | async-done | bytes 1048608 | tf_op jit(solution)/shard_map/all_to_all | solution.py:263
  (81 shorter events, 19.9 us)
Async XLA Ops:
  3.7 15.5 %collective-permute-start.1 = (bf16[256,1024]{1,0:T(8,128)(2,1)S(1)}, bf16[256,1024]{1,0:T(8,128)(2,1)S(1)}, u32[]{:S(2)}, u32[]{:S(2)}) collective-permute-start(bf16[256,1024]{1,0:T(8,128)(2,1)S(1)} %get-tuple-element.27.refs_0_), channel_id=1, source_target_pairs={{0,24},{8,0},{16,8},{24,16},{32,56},{40,32},{48,40},{56,48},{64,88... | collective-permute-start | bytes 1572872 | tf_op jit(solution)/shard_map/ppermute | solution.py:229
  6.9 15.2 %collective-permute-start.10 = (bf16[256,1024]{1,0:T(8,128)(2,1)S(1)}, bf16[256,1024]{1,0:T(8,128)(2,1)S(1)}, u32[]{:S(2)}, u32[]{:S(2)}) collective-permute-start(bf16[256,1024]{1,0:T(8,128)(2,1)S(1)} %get-tuple-element.28.refs_8_), channel_id=1, source_target_pairs={{0,32},{8,40},{16,48},{24,56},{32,64},{40,72},{48,80},{56,88},{64,... | collective-permute-start | bytes 1572872 | tf_op jit(solution)/shard_map/ppermute | solution.py:233
  8.4 14.0 %collective-permute-start.8 = (bf16[256,1024]{1,0:T(8,128)(2,1)S(1)}, bf16[256,1024]{1,0:T(8,128)(2,1)S(1)}, u32[]{:S(2)}, u32[]{:S(2)}) collective-permute-start(bf16[256,1024]{1,0:T(8,128)(2,1)S(1)} %get-tuple-element.28.refs_8_), channel_id=1, source_target_pairs={{0,96},{8,104},{16,112},{24,120},{32,0},{40,8},{48,16},{56,24},{64... | collective-permute-start | bytes 1572872 | tf_op jit(solution)/shard_map/ppermute | solution.py:233
  10.2 15.2 %collective-permute-start.28 = (bf16[256,1024]{1,0:T(8,128)(2,1)S(1)}, bf16[256,1024]{1,0:T(8,128)(2,1)S(1)}, u32[]{:S(2)}, u32[]{:S(2)}) collective-permute-start(bf16[256,1024]{1,0:T(8,128)(2,1)S(1)} %get-tuple-element.39.refs_0_), channel_id=1, source_target_pairs={{0,8},{8,16},{16,24},{24,0},{32,40},{40,48},{48,56},{56,32},{64,72... | collective-permute-start | bytes 1572872 | tf_op jit(solution)/shard_map/ppermute | solution.py:229
  10.2 19.8 %collective-permute-start.26 = (bf16[256,1024]{1,0:T(8,128)(2,1)S(1)}, bf16[256,1024]{1,0:T(8,128)(2,1)S(1)}, u32[]{:S(2)}, u32[]{:S(2)}) collective-permute-start(bf16[256,1024]{1,0:T(8,128)(2,1)S(1)} %get-tuple-element.39.refs_0_), channel_id=1, source_target_pairs={{0,24},{8,0},{16,8},{24,16},{32,56},{40,32},{48,40},{56,48},{64,88... | collective-permute-start | bytes 1572872 | tf_op jit(solution)/shard_map/ppermute | solution.py:229
  19.3 10.7 %collective-permute-start.25 = (bf16[256,1024]{1,0:T(8,128)(2,1)S(1)}, bf16[256,1024]{1,0:T(8,128)(2,1)S(1)}, u32[]{:S(2)}, u32[]{:S(2)}) collective-permute-start(bf16[256,1024]{1,0:T(8,128)(2,1)S(1)} %get-tuple-element.39.refs_0_), channel_id=1, source_target_pairs={{0,1},{1,0},{2,3},{3,2},{4,5},{5,4},{6,7},{7,6},{8,9},{9,8},{10,11... | collective-permute-start | bytes 1572872 | tf_op jit(solution)/shard_map/ppermute | solution.py:241
  22.1 16.0 %collective-permute-start.13 = (bf16[256,1024]{1,0:T(8,128)(2,1)S(1)}, bf16[256,1024]{1,0:T(8,128)(2,1)S(1)}, u32[]{:S(2)}, u32[]{:S(2)}) collective-permute-start(bf16[256,1024]{1,0:T(8,128)(2,1)S(1)} %collective-permute-done.7.refs_9_), channel_id=1, source_target_pairs={{0,32},{8,40},{16,48},{24,56},{32,64},{40,72},{48,80},{56,88},{64,... | collective-permute-start | bytes 1572872 | tf_op jit(solution)/shard_map/ppermute | solution.py:233
  22.4 15.7 %collective-permute-start.9 = (bf16[256,1024]{1,0:T(8,128)(2,1)S(1)}, bf16[256,1024]{1,0:T(8,128)(2,1)S(1)}, u32[]{:S(2)}, u32[]{:S(2)}) collective-permute-start(bf16[256,1024]{1,0:T(8,128)(2,1)S(1)} %collective-permute-done.7.refs_9_), channel_id=1, source_target_pairs={{0,96},{8,104},{16,112},{24,120},{32,0},{40,8},{48,16},{56,24},{64... | collective-permute-start | bytes 1572872 | tf_op jit(solution)/shard_map/ppermute | solution.py:233
  25.4 14.1 %collective-permute-start.29 = (bf16[256,1024]{1,0:T(8,128)(2,1)S(1)}, bf16[256,1024]{1,0:T(8,128)(2,1)S(1)}, u32[]{:S(2)}, u32[]{:S(2)}) collective-permute-start(bf16[256,1024]{1,0:T(8,128)(2,1)S(1)} %collective-permute-done.28.refs_6_), channel_id=1, source_target_pairs={{0,8},{8,16},{16,24},{24,0},{32,40},{40,48},{48,56},{56,32},{64,72... | collective-permute-start | bytes 1572872 | tf_op jit(solution)/shard_map/ppermute | solution.py:229
  30.0 17.8 %collective-permute-start.31 = (bf16[256,1024]{1,0:T(8,128)(2,1)S(1)}, bf16[256,1024]{1,0:T(8,128)(2,1)S(1)}, u32[]{:S(2)}, u32[]{:S(2)}) collective-permute-start(bf16[256,1024]{1,0:T(8,128)(2,1)S(1)} %collective-permute-done.28.refs_6_), channel_id=1, source_target_pairs={{0,1},{1,0},{2,3},{3,2},{4,5},{5,4},{6,7},{7,6},{8,9},{9,8},{10,11... | collective-permute-start | bytes 1572872 | tf_op jit(solution)/shard_map/ppermute | solution.py:241
  30.0 17.7 %collective-permute-start.11 = (bf16[256,1024]{1,0:T(8,128)(2,1)S(1)}, bf16[256,1024]{1,0:T(8,128)(2,1)S(1)}, u32[]{:S(2)}, u32[]{:S(2)}) collective-permute-start(bf16[256,1024]{1,0:T(8,128)(2,1)S(1)} %collective-permute-done.10.refs_14_), channel_id=1, source_target_pairs={{0,32},{8,40},{16,48},{24,56},{32,64},{40,72},{48,80},{56,88},{64,... | collective-permute-start | bytes 1572872 | tf_op jit(solution)/shard_map/ppermute | solution.py:233
  38.1 12.8 %collective-permute-start.27 = (bf16[256,1024]{1,0:T(8,128)(2,1)S(1)}, bf16[256,1024]{1,0:T(8,128)(2,1)S(1)}, u32[]{:S(2)}, u32[]{:S(2)}) collective-permute-start(bf16[256,1024]{1,0:T(8,128)(2,1)S(1)} %collective-permute-done.26.refs_2_), channel_id=1, source_target_pairs={{0,1},{1,0},{2,3},{3,2},{4,5},{5,4},{6,7},{7,6},{8,9},{9,8},{10,11... | collective-permute-start | bytes 1572872 | tf_op jit(solution)/shard_map/ppermute | solution.py:241
  38.1 14.3 %collective-permute-start.12 = (bf16[256,1024]{1,0:T(8,128)(2,1)S(1)}, bf16[256,1024]{1,0:T(8,128)(2,1)S(1)}, u32[]{:S(2)}, u32[]{:S(2)}) collective-permute-start(bf16[256,1024]{1,0:T(8,128)(2,1)S(1)} %collective-permute-done.9.refs_11_), channel_id=1, source_target_pairs={{0,96},{8,104},{16,112},{24,120},{32,0},{40,8},{48,16},{56,24},{64... | collective-permute-start | bytes 1572872 | tf_op jit(solution)/shard_map/ppermute | solution.py:233
  39.4 13.1 %collective-permute-start.30 = (bf16[256,1024]{1,0:T(8,128)(2,1)S(1)}, bf16[256,1024]{1,0:T(8,128)(2,1)S(1)}, u32[]{:S(2)}, u32[]{:S(2)}) collective-permute-start(bf16[256,1024]{1,0:T(8,128)(2,1)S(1)} %collective-permute-done.29.refs_4_), channel_id=1, source_target_pairs={{0,1},{1,0},{2,3},{3,2},{4,5},{5,4},{6,7},{7,6},{8,9},{9,8},{10,11... | collective-permute-start | bytes 1572872 | tf_op jit(solution)/shard_map/ppermute | solution.py:241
  47.7 14.4 %collective-permute-start.5 = (bf16[256,1024]{1,0:T(8,128)(2,1)S(1)}, bf16[256,1024]{1,0:T(8,128)(2,1)S(1)}, u32[]{:S(2)}, u32[]{:S(2)}) collective-permute-start(bf16[256,1024]{1,0:T(8,128)(2,1)S(1)} %get-tuple-element.27.refs_0_), channel_id=1, source_target_pairs={{0,8},{8,16},{16,24},{24,0},{32,40},{40,48},{48,56},{56,32},{64,72... | collective-permute-start | bytes 1572872 | tf_op jit(solution)/shard_map/ppermute | solution.py:229
  47.7 14.9 %collective-permute-start.3 = (bf16[256,1024]{1,0:T(8,128)(2,1)S(1)}, bf16[256,1024]{1,0:T(8,128)(2,1)S(1)}, u32[]{:S(2)}, u32[]{:S(2)}) collective-permute-start(bf16[256,1024]{1,0:T(8,128)(2,1)S(1)} %collective-permute-done.1.refs_2_), channel_id=1, source_target_pairs={{0,24},{8,0},{16,8},{24,16},{32,56},{40,32},{48,40},{56,48},{64,88... | collective-permute-start | bytes 1572872 | tf_op jit(solution)/shard_map/ppermute | solution.py:229
  57.9 15.8 %collective-permute-start.32 = (bf16[4,256,256]{2,1,0:T(8,128)(2,1)S(1)}, bf16[4,256,256]{2,1,0:T(8,128)(2,1)S(1)}, u32[]{:S(2)}, u32[]{:S(2)}) collective-permute-start(bf16[4,256,256]{2,1,0:T(8,128)(2,1)S(1)} %get-tuple-element.41), channel_id=1, source_target_pairs={{0,2},{1,3},{2,4},{3,5},{4,6},{5,7},{6,0},{7,1},{8,10},{9,11},{10,... | collective-permute-start | bytes 1572872 | tf_op jit(solution)/shard_map/ppermute | solution.py:237
  59.9 13.9 %collective-permute-start.33 = (bf16[4,256,256]{2,1,0:T(8,128)(2,1)S(1)}, bf16[4,256,256]{2,1,0:T(8,128)(2,1)S(1)}, u32[]{:S(2)}, u32[]{:S(2)}) collective-permute-start(bf16[4,256,256]{2,1,0:T(8,128)(2,1)S(1)} %get-tuple-element.42), channel_id=1, source_target_pairs={{0,6},{1,7},{2,0},{3,1},{4,2},{5,3},{6,4},{7,5},{8,14},{9,15},{10,... | collective-permute-start | bytes 1572872 | tf_op jit(solution)/shard_map/ppermute | solution.py:237
  62.1 13.0 %collective-permute-start = (bf16[256,1024]{1,0:T(8,128)(2,1)S(1)}, bf16[256,1024]{1,0:T(8,128)(2,1)S(1)}, u32[]{:S(2)}, u32[]{:S(2)}) collective-permute-start(bf16[256,1024]{1,0:T(8,128)(2,1)S(1)} %get-tuple-element.27.refs_0_), channel_id=1, source_target_pairs={{0,1},{1,0},{2,3},{3,2},{4,5},{5,4},{6,7},{7,6},{8,9},{9,8},{10,11... | collective-permute-start | bytes 1572872 | tf_op jit(solution)/shard_map/ppermute | solution.py:241
  62.1 15.4 %collective-permute-start.2 = (bf16[256,1024]{1,0:T(8,128)(2,1)S(1)}, bf16[256,1024]{1,0:T(8,128)(2,1)S(1)}, u32[]{:S(2)}, u32[]{:S(2)}) collective-permute-start(bf16[256,1024]{1,0:T(8,128)(2,1)S(1)} %collective-permute-done.1.refs_2_), channel_id=1, source_target_pairs={{0,1},{1,0},{2,3},{3,2},{4,5},{5,4},{6,7},{7,6},{8,9},{9,8},{10,11... | collective-permute-start | bytes 1572872 | tf_op jit(solution)/shard_map/ppermute | solution.py:241
  62.6 14.9 %collective-permute-start.6 = (bf16[256,1024]{1,0:T(8,128)(2,1)S(1)}, bf16[256,1024]{1,0:T(8,128)(2,1)S(1)}, u32[]{:S(2)}, u32[]{:S(2)}) collective-permute-start(bf16[256,1024]{1,0:T(8,128)(2,1)S(1)} %collective-permute-done.5.refs_6_), channel_id=1, source_target_pairs={{0,1},{1,0},{2,3},{3,2},{4,5},{5,4},{6,7},{7,6},{8,9},{9,8},{10,11... | collective-permute-start | bytes 1572872 | tf_op jit(solution)/shard_map/ppermute | solution.py:241
  73.8 10.2 %collective-permute-start.34 = (bf16[2,256,256]{2,1,0:T(8,128)(2,1)S(1)}, bf16[2,256,256]{2,1,0:T(8,128)(2,1)S(1)}, u32[]{:S(2)}, u32[]{:S(2)}) collective-permute-start(bf16[2,256,256]{2,1,0:T(8,128)(2,1)S(1)} %add_convert_fusion.1), channel_id=1, source_target_pairs={{0,2},{1,3},{2,4},{3,5},{4,6},{5,7},{6,0},{7,1},{8,10},{9,11},{10,... | collective-permute-start | bytes 786440 | tf_op jit(solution)/shard_map/ppermute | solution.py:237
  75.1 8.9 %collective-permute-start.35 = (bf16[2,256,256]{2,1,0:T(8,128)(2,1)S(1)}, bf16[2,256,256]{2,1,0:T(8,128)(2,1)S(1)}, u32[]{:S(2)}, u32[]{:S(2)}) collective-permute-start(bf16[2,256,256]{2,1,0:T(8,128)(2,1)S(1)} %add_convert_fusion), channel_id=1, source_target_pairs={{0,6},{1,7},{2,0},{3,1},{4,2},{5,3},{6,4},{7,5},{8,14},{9,15},{10,... | collective-permute-start | bytes 786440 | tf_op jit(solution)/shard_map/ppermute | solution.py:237
  83.0 21.4 %collective-permute-start.14 = (bf16[4,256,256]{2,1,0:T(8,128)(2,1)}, bf16[4,256,256]{2,1,0:T(8,128)(2,1)S(1)}, u32[]{:S(2)}, u32[]{:S(2)}) collective-permute-start(bf16[4,256,256]{2,1,0:T(8,128)(2,1)} %get-tuple-element.31), channel_id=1, source_target_pairs={{0,2},{1,3},{2,4},{3,5},{4,6},{5,7},{6,0},{7,1},{8,10},{9,11},{10,... | collective-permute-start | bytes 1572872 | tf_op jit(solution)/shard_map/ppermute | solution.py:237
  85.1 20.4 %collective-permute-start.15 = (bf16[4,256,256]{2,1,0:T(8,128)(2,1)}, bf16[4,256,256]{2,1,0:T(8,128)(2,1)S(1)}, u32[]{:S(2)}, u32[]{:S(2)}) collective-permute-start(bf16[4,256,256]{2,1,0:T(8,128)(2,1)} %get-tuple-element.32), channel_id=1, source_target_pairs={{0,6},{1,7},{2,0},{3,1},{4,2},{5,3},{6,4},{7,5},{8,14},{9,15},{10,... | collective-permute-start | bytes 1572872 | tf_op jit(solution)/shard_map/ppermute | solution.py:237
  88.2 8.5 %collective-permute-start.38 = (bf16[256,256]{1,0:T(8,128)(2,1)S(1)}, bf16[256,256]{1,0:T(8,128)(2,1)S(1)}, u32[]{:S(2)}, u32[]{:S(2)}) collective-permute-start(bf16[256,256]{1,0:T(8,128)(2,1)S(1)} %get-tuple-element.48), channel_id=1, source_target_pairs={{0,8},{8,16},{16,24},{24,0},{32,40},{40,48},{48,56},{56,32},{64,72... | collective-permute-start | bytes 393224 | tf_op jit(solution)/shard_map/ppermute | solution.py:229
  100.7 31.1 %all-to-all-start.1 = ((bf16[16,1,128,256]{3,2,1,0:T(8,128)(2,1)}), bf16[16,1,128,256]{3,2,1,0:T(8,128)(2,1)S(1)}, u32[]{:S(2)}, u32[]{:S(2)}) async-start(bf16[16,1,128,256]{3,2,1,0:T(8,128)(2,1)} %pack.3), calls=%async_computation.1 | async-start | bytes 2097152 | tf_op jit(solution)/shard_map/all_to_all | solution.py:263
  105.4 9.8 %collective-permute-start.16 = (bf16[2,256,256]{2,1,0:T(8,128)(2,1)S(1)}, bf16[2,256,256]{2,1,0:T(8,128)(2,1)S(1)}, u32[]{:S(2)}, u32[]{:S(2)}) collective-permute-start(bf16[2,256,256]{2,1,0:T(8,128)(2,1)S(1)} %add_convert_fusion.3), channel_id=1, source_target_pairs={{0,2},{1,3},{2,4},{3,5},{4,6},{5,7},{6,0},{7,1},{8,10},{9,11},{10,... | collective-permute-start | bytes 786440 | tf_op jit(solution)/shard_map/ppermute | solution.py:237
  105.6 9.7 %collective-permute-start.17 = (bf16[2,256,256]{2,1,0:T(8,128)(2,1)S(1)}, bf16[2,256,256]{2,1,0:T(8,128)(2,1)S(1)}, u32[]{:S(2)}, u32[]{:S(2)}) collective-permute-start(bf16[2,256,256]{2,1,0:T(8,128)(2,1)S(1)} %add_convert_fusion.2), channel_id=1, source_target_pairs={{0,6},{1,7},{2,0},{3,1},{4,2},{5,3},{6,4},{7,5},{8,14},{9,15},{10,... | collective-permute-start | bytes 786440 | tf_op jit(solution)/shard_map/ppermute | solution.py:237
  115.4 9.2 %collective-permute-start.18 = (bf16[256,256]{1,0:T(8,128)(2,1)S(1)}, bf16[256,256]{1,0:T(8,128)(2,1)S(1)}, u32[]{:S(2)}, u32[]{:S(2)}) collective-permute-start(bf16[256,256]{1,0:T(8,128)(2,1)S(1)} %get-tuple-element.36), channel_id=1, source_target_pairs={{0,24},{8,0},{16,8},{24,16},{32,56},{40,32},{48,40},{56,48},{64,88... | collective-permute-start | bytes 393224 | tf_op jit(solution)/shard_map/ppermute | solution.py:229
  119.1 8.8 %collective-permute-start.20 = (bf16[256,256]{1,0:T(8,128)(2,1)S(1)}, bf16[256,256]{1,0:T(8,128)(2,1)S(1)}, u32[]{:S(2)}, u32[]{:S(2)}) collective-permute-start(bf16[256,256]{1,0:T(8,128)(2,1)S(1)} %get-tuple-element.38), channel_id=1, source_target_pairs={{0,8},{8,16},{16,24},{24,0},{32,40},{40,48},{48,56},{56,32},{64,72... | collective-permute-start | bytes 393224 | tf_op jit(solution)/shard_map/ppermute | solution.py:229
  131.8 22.5 %all-to-all-start = ((bf16[16,1,128,256]{3,2,1,0:T(8,128)(2,1)}), bf16[16,1,128,256]{3,2,1,0:T(8,128)(2,1)S(1)}, u32[]{:S(2)}, u32[]{:S(2)}) async-start(bf16[16,1,128,256]{3,2,1,0:T(8,128)(2,1)} %pack.2), calls=%async_computation | async-start | bytes 2097152 | tf_op jit(solution)/shard_map/all_to_all | solution.py:263
  (18 other events, 77.0 us)

commit v3 on v2

--- a/solution.py
+++ b/solution.py
@@ -77,9 +77,29 @@
             pltpu.VMEM((1, panels.shape[1]), jnp.float32),
             pltpu.SemaphoreType.DMA((4,)),
         ],
-        compiler_params=pltpu.CompilerParams(vmem_limit_bytes=12 * 1024 * 1024),
+        compiler_params=pltpu.CompilerParams(vmem_limit_bytes=58000 * 1024),
         name="scale",
     )(tile_mask, panels, scaling.reshape(1, -1))
+
+
+def stage_body(*refs):
+    copies = [pltpu.make_async_copy(refs[at], refs[3 + at], refs[6].at[at]) for at in range(3)]
+    for copy in copies:
+        copy.start()
+    for copy in copies:
+        copy.wait()
+
+
+def stage(*values):
+    return pl.pallas_call(
+        stage_body,
+        out_shape=tuple(jax.ShapeDtypeStruct(value.shape, value.dtype) for value in values),
+        in_specs=[pl.BlockSpec(memory_space=pl.ANY)] * 3,
+        out_specs=(pl.BlockSpec(memory_space=pltpu.VMEM),) * 3,
+        scratch_shapes=[pltpu.SemaphoreType.DMA((3,))],
+        compiler_params=pltpu.CompilerParams(vmem_limit_bytes=4 * 1024 * 1024),
+        name="stage",
+    )(*values)
 
 
 def product_body(*refs):
@@ -159,11 +179,10 @@
 
 
 def pack_body(owners_ref, *refs):
-    arrived, out_ref, sems = refs[:8], refs[8], refs[9]
+    arrived, out_ref, zero_ref, sems, zero_sems = refs[:8], refs[8], refs[9], refs[10], refs[11]
     _, y, _, k = position()
-    out_ref[...] = jnp.zeros_like(out_ref)
-
-    def copies(e):
+
+    def tiles(e):
         line = (y + e) % 4
         found = []
         for source, parity in ((arrived[e], k), (arrived[4 + e], 1 - k)):
@@ -178,21 +197,27 @@
                 )
         return line >> 1 == k, found
 
-    for e in range(4):
-        wanted, found = copies(e)
-
-        @pl.when(wanted)
-        def _():
-            for copy in found:
-                copy.start()
-
-    for e in range(4):
-        wanted, found = copies(e)
-
-        @pl.when(wanted)
-        def _():
-            for copy in found:
-                copy.wait()
+    def blank(slot):
+        used = owners_ref[0, 0] == slot
+        for at in range(1, 8):
+            used = used | (owners_ref[at // 4, at % 4] == slot)
+        return jnp.logical_not(used), [
+            pltpu.make_async_copy(zero_ref, out_ref.at[slot, 0], zero_sems.at[slot])
+        ]
+
+    def each(act):
+        for make, count in ((tiles, 4), (blank, 16)):
+            for at in range(count):
+                wanted, found = make(at)
+
+                @pl.when(wanted)
+                def _():
+                    for copy in found:
+                        act(copy)
+
+    zero_ref[...] = jnp.zeros_like(zero_ref)
+    each(lambda copy: copy.start())
+    each(lambda copy: copy.wait())
 
 
 def pack(owners, arrived):
@@ -200,9 +225,13 @@
         pack_body,
         out_shape=jax.ShapeDtypeStruct((16, 1, HALF, TILE), jnp.bfloat16),
         in_specs=[pl.BlockSpec(memory_space=pltpu.SMEM)] + [pl.BlockSpec(memory_space=pl.ANY)] * 8,
-        out_specs=pl.BlockSpec(memory_space=pltpu.VMEM),
-        scratch_shapes=[pltpu.SemaphoreType.DMA((16,))],
-        compiler_params=pltpu.CompilerParams(vmem_limit_bytes=4 * 1024 * 1024),
+        out_specs=pl.BlockSpec(memory_space=pl.ANY),
+        scratch_shapes=[
+            pltpu.VMEM((HALF, TILE), jnp.bfloat16),
+            pltpu.SemaphoreType.DMA((16,)),
+            pltpu.SemaphoreType.DMA((16,)),
+        ],
+        compiler_params=pltpu.CompilerParams(vmem_limit_bytes=2 * 1024 * 1024),
         name="pack",
     )(owners, *arrived)
 
@@ -272,10 +301,15 @@
     low_m, top_p = ypass(low, 1), ypass(top, -1)
     co0, co1 = xpass(cm0, 1), xpass(cp1, -1)
     top_o, low_o = ypass(top_m, 1), ypass(low_p, -1)
+    sent_top, sent_low = top, low
+    c0, top, low = stage(c0, top, low)
     cols = (c0, c1, cp0, cp1, co0, co1, cm0, cm1)
     halves = []
-    for pieces in ((top, top_p, top_o, top_m), (low, low_p, low_o, low_m)):
-        rows = [piece for value in pieces for piece in (value, swap(value))]
+    for own, pieces in (
+        (top, (sent_top, top_p, top_o, top_m)), (low, (sent_low, low_p, low_o, low_m))
+    ):
+        others = [swap(value) for value in pieces]
+        rows = [piece for pair in zip((own, *pieces[1:]), others) for piece in pair]
         halves.append(product(rows, cols))
     first = to_owners(owner_rows, reduce_along_z(halves[0]))
     second = to_owners(owner_rows, reduce_along_z(halves[1]))

time: 156 us -> 153 us (0.981)
  starting transfers between devices: 49 us -> 46.4 us
  Pallas kernels: 19.2 us -> 20.8 us
    ppermute x12, waiting for transfers between devices: 25.7 us -> 32.8 us  [ypass(): return lax.ppermute(value, 'row', along_y(step))]
    ppermute x6, waiting for transfers between devices: 19.4 us -> 13.7 us  [xpass(): return lax.ppermute(value, 'row', along_x(step))]
    ppermute x6, starting transfers between devices: 9.25 us -> 6.31 us  [xpass(): return lax.ppermute(value, 'row', along_x(step))]
    ppermute x8, waiting for transfers between devices: 18.4 us -> 15.9 us  [zpass(): return lax.ppermute(value, 'col', along_z(step))]
    pallas_call x1, Pallas kernels: 1.06 us -> 2.88 us  [scale(): pl.pallas_call(scale_body, out_shape=(part, part, part, part), in_specs=[...]
where the time goes in v3:
time: 153 us
  waiting for transfers between devices  82 us (54%)
  starting transfers between devices  46.4 us (30%)
  Pallas kernels  20.8 us (14%)
  local copies, waits for them, and re-layouts  2.09 us (1%)
    ppermute x12, waiting for transfers between devices, ypass(): return lax.ppermute(value, 'row', along_y(step))  32.8 us
    all_to_all x2, waiting for transfers between devices, to_owners(): lax.all_to_all(outgoing, 'row', split_axis=0, concat_axis=0, tiled=True)  17.1 us
    ppermute x12, starting transfers between devices, ypass(): return lax.ppermute(value, 'row', along_y(step))  16.7 us
    ppermute x8, waiting for transfers between devices, zpass(): return lax.ppermute(value, 'col', along_z(step))  15.9 us
    ppermute x8, starting transfers between devices, zpass(): return lax.ppermute(value, 'col', along_z(step))  14.3 us
    ppermute x6, waiting for transfers between devices, xpass(): return lax.ppermute(value, 'row', along_x(step))  13.7 us
    pallas_call x2, Pallas kernels, product(): pl.pallas_call(product_body, out_shape=(four, four, two, two, kept), in_s...  10.9 us
    all_to_all x2, starting transfers between devices, to_owners(): lax.all_to_all(outgoing, 'row', split_axis=0, concat_axis=0, tiled=True)  8.06 us
  transfers between devices with their start and end apart: 45, of which 19 were waited for; matrix products, arithmetic and copies ran while one was open for 1% of the time, Pallas kernels for 11%

profile of v3, /device:TPU:0, one launch (start us, length us, event | category | flops | bytes accessed | tf_op | source)
XLA Modules:
  0.0 152.9 jit_solution(1447373896985381648)
XLA Ops:
  0.0 2.9 %scale.1 = (bf16[256,1024]{1,0:T(8,128)(2,1)}, bf16[256,1024]{1,0:T(8,128)(2,1)}, bf16[256,1024]{1,0:T(8,128)(2,1)}, bf16[256,1024]{1,0:T(8,128)(2,1)}) custom-call(s32[2,32]{1,0:T(2,128)} %mask_hbm.1, bf16[512,1024]{1,0:T(8,128)(2,1)} %panels_hbm.1, f32[1,1024]{1,0:T(1,128)} %bitcast.1), custom_call_target="tpu_custom_call" | custom-call | tf_op jit(solution)/shard_map/scale/pallas_call | solution.py:69
  2.9 3.2 %collective-permute-start.1 = (bf16[256,1024]{1,0:T(8,128)(2,1)}, bf16[256,1024]{1,0:T(8,128)(2,1)S(1)}, u32[]{:S(2)}, u32[]{:S(2)}) collective-permute-start(bf16[256,1024]{1,0:T(8,128)(2,1)} %get-tuple-element.32.refs_2_), channel_id=1, source_target_pairs={{0,24},{8,0},{16,8},{24,16},{32,56},{40,32},{48,40},{56,48},{64,88... | collective-permute-start | bytes 1572872 | tf_op jit(solution)/shard_map/ppermute | solution.py:258
  6.1 2.8 %collective-permute-start.8 = (bf16[256,1024]{1,0:T(8,128)(2,1)}, bf16[256,1024]{1,0:T(8,128)(2,1)S(1)}, u32[]{:S(2)}, u32[]{:S(2)}) collective-permute-start(bf16[256,1024]{1,0:T(8,128)(2,1)} %get-tuple-element.30.refs_0_), channel_id=1, source_target_pairs={{0,96},{8,104},{16,112},{24,120},{32,0},{40,8},{48,16},{56,24},{64... | collective-permute-start | bytes 1572872 | tf_op jit(solution)/shard_map/ppermute | solution.py:262
  8.8 8.7 %collective-permute-done.1.refs_2_ = bf16[256,1024]{1,0:T(8,128)(2,1)S(1)} collective-permute-done((bf16[256,1024]{1,0:T(8,128)(2,1)}, bf16[256,1024]{1,0:T(8,128)(2,1)S(1)}, u32[]{:S(2)}, u32[]{:S(2)}) %collective-permute-start.1) | collective-permute-done | bytes 524320 | tf_op jit(solution)/shard_map/ppermute | solution.py:258
  17.6 3.6 %collective-permute-start.26 = (bf16[256,1024]{1,0:T(8,128)(2,1)}, bf16[256,1024]{1,0:T(8,128)(2,1)S(1)}, u32[]{:S(2)}, u32[]{:S(2)}) collective-permute-start(bf16[256,1024]{1,0:T(8,128)(2,1)} %get-tuple-element.31.refs_1_), channel_id=1, source_target_pairs={{0,24},{8,0},{16,8},{24,16},{32,56},{40,32},{48,40},{56,48},{64,88... | collective-permute-start | bytes 1572872 | tf_op jit(solution)/shard_map/ppermute | solution.py:258
  21.2 3.4 %collective-permute-start.9 = (bf16[256,1024]{1,0:T(8,128)(2,1)S(1)}, bf16[256,1024]{1,0:T(8,128)(2,1)S(1)}, u32[]{:S(2)}, u32[]{:S(2)}) collective-permute-start(bf16[256,1024]{1,0:T(8,128)(2,1)S(1)} %collective-permute-done.7.refs_9_), channel_id=1, source_target_pairs={{0,96},{8,104},{16,112},{24,120},{32,0},{40,8},{48,16},{56,24},{64... | collective-permute-start | bytes 1572872 | tf_op jit(solution)/shard_map/ppermute | solution.py:262
  24.8 8.5 %collective-permute-done.26.refs_2_ = bf16[256,1024]{1,0:T(8,128)(2,1)S(1)} collective-permute-done((bf16[256,1024]{1,0:T(8,128)(2,1)}, bf16[256,1024]{1,0:T(8,128)(2,1)S(1)}, u32[]{:S(2)}, u32[]{:S(2)}) %collective-permute-start.26) | collective-permute-done | bytes 524320 | tf_op jit(solution)/shard_map/ppermute | solution.py:258
  33.3 2.2 %collective-permute-done.9.refs_11_ = bf16[256,1024]{1,0:T(8,128)(2,1)S(1)} collective-permute-done((bf16[256,1024]{1,0:T(8,128)(2,1)S(1)}, bf16[256,1024]{1,0:T(8,128)(2,1)S(1)}, u32[]{:S(2)}, u32[]{:S(2)}) %collective-permute-start.9) | collective-permute-done | bytes 524320 | tf_op jit(solution)/shard_map/ppermute | solution.py:262
  35.6 5.0 %collective-permute-done.11.refs_12_ = bf16[256,1024]{1,0:T(8,128)(2,1)S(1)} collective-permute-done((bf16[256,1024]{1,0:T(8,128)(2,1)S(1)}, bf16[256,1024]{1,0:T(8,128)(2,1)S(1)}, u32[]{:S(2)}, u32[]{:S(2)}) %collective-permute-start.11) | collective-permute-done | bytes 524320 | tf_op jit(solution)/shard_map/ppermute | solution.py:262
  43.9 6.4 %collective-permute-done.13.refs_15_ = bf16[256,1024]{1,0:T(8,128)(2,1)S(1)} collective-permute-done((bf16[256,1024]{1,0:T(8,128)(2,1)S(1)}, bf16[256,1024]{1,0:T(8,128)(2,1)S(1)}, u32[]{:S(2)}, u32[]{:S(2)}) %collective-permute-start.13) | collective-permute-done | bytes 524320 | tf_op jit(solution)/shard_map/ppermute | solution.py:262
  50.3 3.2 %collective-permute-start.3 = (bf16[256,1024]{1,0:T(8,128)(2,1)S(1)}, bf16[256,1024]{1,0:T(8,128)(2,1)S(1)}, u32[]{:S(2)}, u32[]{:S(2)}) collective-permute-start(bf16[256,1024]{1,0:T(8,128)(2,1)S(1)} %collective-permute-done.1.refs_2_), channel_id=1, source_target_pairs={{0,24},{8,0},{16,8},{24,16},{32,56},{40,32},{48,40},{56,48},{64,88... | collective-permute-start | bytes 1572872 | tf_op jit(solution)/shard_map/ppermute | solution.py:258
  53.5 5.4 %product.3 = (bf16[4,256,256]{2,1,0:T(8,128)(2,1)S(1)}, bf16[4,256,256]{2,1,0:T(8,128)(2,1)S(1)}, bf16[2,256,256]{2,1,0:T(8,128)(2,1)S(1)}, bf16[2,256,256]{2,1,0:T(8,128)(2,1)S(1)}, f32[4,256,256]{2,1,0:T(8,128)S(1)}) custom-call(bf16[256,1024]{1,0:T(8,128)(2,1)S(1)} %get-tuple-element.45.refs_0_, bf16[256,1024]{1,0:T(8,128)(2,1)S(1)} %collective-permute-done.25.refs_1_, ...), custom_call_target="tpu_custom_call" | custom-call | tf_op jit(solution)/shard_map/product/pallas_call | solution.py:143
  58.9 2.0 %collective-permute-start.32 = (bf16[4,256,256]{2,1,0:T(8,128)(2,1)S(1)}, bf16[4,256,256]{2,1,0:T(8,128)(2,1)S(1)}, u32[]{:S(2)}, u32[]{:S(2)}) collective-permute-start(bf16[4,256,256]{2,1,0:T(8,128)(2,1)S(1)} %get-tuple-element.47), channel_id=1, source_target_pairs={{0,2},{1,3},{2,4},{3,5},{4,6},{5,7},{6,0},{7,1},{8,10},{9,11},{10,... | collective-permute-start | bytes 1572872 | tf_op jit(solution)/shard_map/ppermute | solution.py:266
  60.9 2.2 %collective-permute-start.33 = (bf16[4,256,256]{2,1,0:T(8,128)(2,1)S(1)}, bf16[4,256,256]{2,1,0:T(8,128)(2,1)S(1)}, u32[]{:S(2)}, u32[]{:S(2)}) collective-permute-start(bf16[4,256,256]{2,1,0:T(8,128)(2,1)S(1)} %get-tuple-element.48), channel_id=1, source_target_pairs={{0,6},{1,7},{2,0},{3,1},{4,2},{5,3},{6,4},{7,5},{8,14},{9,15},{10,... | collective-permute-start | bytes 1572872 | tf_op jit(solution)/shard_map/ppermute | solution.py:266
  64.5 8.6 %collective-permute-done.32.got_up = bf16[4,256,256]{2,1,0:T(8,128)(2,1)S(1)} collective-permute-done((bf16[4,256,256]{2,1,0:T(8,128)(2,1)S(1)}, bf16[4,256,256]{2,1,0:T(8,128)(2,1)S(1)}, u32[]{:S(2)}, u32[]{:S(2)}) %collective-permute-start.32) | collective-permute-done | bytes 524320 | tf_op jit(solution)/shard_map/ppermute | solution.py:266
  73.2 1.2 collective-permute-start.34
  74.4 2.4 %collective-permute-start.35 = (bf16[2,256,256]{2,1,0:T(8,128)(2,1)S(1)}, bf16[2,256,256]{2,1,0:T(8,128)(2,1)S(1)}, u32[]{:S(2)}, u32[]{:S(2)}) collective-permute-start(bf16[2,256,256]{2,1,0:T(8,128)(2,1)S(1)} %add_convert_fusion), channel_id=1, source_target_pairs={{0,6},{1,7},{2,0},{3,1},{4,2},{5,3},{6,4},{7,5},{8,14},{9,15},{10,... | collective-permute-start | bytes 786440 | tf_op jit(solution)/shard_map/ppermute | solution.py:266
  76.8 5.4 %product.2 = (bf16[4,256,256]{2,1,0:T(8,128)(2,1)}, bf16[4,256,256]{2,1,0:T(8,128)(2,1)}, bf16[2,256,256]{2,1,0:T(8,128)(2,1)S(1)}, bf16[2,256,256]{2,1,0:T(8,128)(2,1)S(1)}, f32[4,256,256]{2,1,0:T(8,128)S(1)}) custom-call(bf16[256,1024]{1,0:T(8,128)(2,1)S(1)} %get-tuple-element.33.refs_0_, bf16[256,1024]{1,0:T(8,128)(2,1)S(1)} %collective-permute-done.refs_1_, ...), custom_call_target="tpu_custom_call" | custom-call | tf_op jit(solution)/shard_map/product/pallas_call | solution.py:143
  83.9 3.1 %collective-permute-start.15 = (bf16[4,256,256]{2,1,0:T(8,128)(2,1)}, bf16[4,256,256]{2,1,0:T(8,128)(2,1)S(1)}, u32[]{:S(2)}, u32[]{:S(2)}) collective-permute-start(bf16[4,256,256]{2,1,0:T(8,128)(2,1)} %get-tuple-element.38), channel_id=1, source_target_pairs={{0,6},{1,7},{2,0},{3,1},{4,2},{5,3},{6,4},{7,5},{8,14},{9,15},{10,... | collective-permute-start | bytes 1572872 | tf_op jit(solution)/shard_map/ppermute | solution.py:266
  88.9 5.9 %collective-permute-done.37.refs_2_ = bf16[256,256]{1,0:T(8,128)(2,1)S(1)} collective-permute-done((bf16[256,256]{1,0:T(8,128)(2,1)S(1)}, bf16[256,256]{1,0:T(8,128)(2,1)S(1)}, u32[]{:S(2)}, u32[]{:S(2)}) %collective-permute-start.37) | collective-permute-done | bytes 131104 | tf_op jit(solution)/shard_map/ppermute | solution.py:258
  97.1 1.8 %pack.3 = bf16[16,1,128,256]{3,2,1,0:T(8,128)(2,1)} custom-call(s32[2,4]{1,0:T(2,128)S(1)} %copy-done.3, bf16[256,256]{1,0:T(8,128)(2,1)S(1)} %get-tuple-element.51.refs_0_, bf16[256,256]{1,0:T(8,128)(2,1)S(1)} %collective-permute-done.36.refs_1_, bf16[256,256]{1,0:T(8,128)(2,1)S(1)} %collective-permute-done.37.refs_2_, ...), custom_call_target="tpu_custom_call" | custom-call | tf_op jit(solution)/shard_map/pack/pallas_call | solution.py:224
  98.9 3.7 %all-to-all-start.1 = ((bf16[16,1,128,256]{3,2,1,0:T(8,128)(2,1)}), bf16[16,1,128,256]{3,2,1,0:T(8,128)(2,1)S(1)}, u32[]{:S(2)}, u32[]{:S(2)}) async-start(bf16[16,1,128,256]{3,2,1,0:T(8,128)(2,1)} %pack.3), calls=%async_computation.1 | async-start | bytes 2097152 | tf_op jit(solution)/shard_map/all_to_all | solution.py:292
  103.8 3.3 %collective-permute-start.17 = (bf16[2,256,256]{2,1,0:T(8,128)(2,1)S(1)}, bf16[2,256,256]{2,1,0:T(8,128)(2,1)S(1)}, u32[]{:S(2)}, u32[]{:S(2)}) collective-permute-start(bf16[2,256,256]{2,1,0:T(8,128)(2,1)S(1)} %add_convert_fusion.2), channel_id=1, source_target_pairs={{0,6},{1,7},{2,0},{3,1},{4,2},{5,3},{6,4},{7,5},{8,14},{9,15},{10,... | collective-permute-start | bytes 786440 | tf_op jit(solution)/shard_map/ppermute | solution.py:266
  107.1 6.4 %collective-permute-done.16.sum_up = bf16[2,256,256]{2,1,0:T(8,128)(2,1)S(1)} collective-permute-done((bf16[2,256,256]{2,1,0:T(8,128)(2,1)S(1)}, bf16[2,256,256]{2,1,0:T(8,128)(2,1)S(1)}, u32[]{:S(2)}, u32[]{:S(2)}) %collective-permute-start.16) | collective-permute-done | bytes 262176 | tf_op jit(solution)/shard_map/ppermute | solution.py:266
  113.7 2.8 %collective-permute-start.18 = (bf16[256,256]{1,0:T(8,128)(2,1)S(1)}, bf16[256,256]{1,0:T(8,128)(2,1)S(1)}, u32[]{:S(2)}, u32[]{:S(2)}) collective-permute-start(bf16[256,256]{1,0:T(8,128)(2,1)S(1)} %get-tuple-element.42), channel_id=1, source_target_pairs={{0,24},{8,0},{16,8},{24,16},{32,56},{40,32},{48,40},{56,48},{64,88... | collective-permute-start | bytes 393224 | tf_op jit(solution)/shard_map/ppermute | solution.py:258
  118.2 4.7 %collective-permute-done.18.refs_1_ = bf16[256,256]{1,0:T(8,128)(2,1)S(1)} collective-permute-done((bf16[256,256]{1,0:T(8,128)(2,1)S(1)}, bf16[256,256]{1,0:T(8,128)(2,1)S(1)}, u32[]{:S(2)}, u32[]{:S(2)}) %collective-permute-start.18) | collective-permute-done | bytes 131104 | tf_op jit(solution)/shard_map/ppermute | solution.py:258
  122.9 1.5 collective-permute-done.19.refs_2_
  124.4 1.7 %collective-permute-done.20.refs_3_ = bf16[256,256]{1,0:T(8,128)(2,1)S(1)} collective-permute-done((bf16[256,256]{1,0:T(8,128)(2,1)S(1)}, bf16[256,256]{1,0:T(8,128)(2,1)S(1)}, u32[]{:S(2)}, u32[]{:S(2)}) %collective-permute-start.20) | collective-permute-done | bytes 131104 | tf_op jit(solution)/shard_map/ppermute | solution.py:258
  126.1 1.3 collective-permute-done.24.refs_7_
  127.4 1.8 %pack.2 = bf16[16,1,128,256]{3,2,1,0:T(8,128)(2,1)} custom-call(s32[2,4]{1,0:T(2,128)S(1)} %copy-done.3, bf16[256,256]{1,0:T(8,128)(2,1)S(1)} %get-tuple-element.41.refs_0_, bf16[256,256]{1,0:T(8,128)(2,1)S(1)} %collective-permute-done.18.refs_1_, bf16[256,256]{1,0:T(8,128)(2,1)S(1)} %collective-permute-done.19.refs_2_, ...), custom_call_target="tpu_custom_call" | custom-call | tf_op jit(solution)/shard_map/pack/pallas_call | solution.py:224
  129.3 4.4 %all-to-all-start = ((bf16[16,1,128,256]{3,2,1,0:T(8,128)(2,1)}), bf16[16,1,128,256]{3,2,1,0:T(8,128)(2,1)S(1)}, u32[]{:S(2)}, u32[]{:S(2)}) async-start(bf16[16,1,128,256]{3,2,1,0:T(8,128)(2,1)} %pack.2), calls=%async_computation | async-start | bytes 2097152 | tf_op jit(solution)/shard_map/all_to_all | solution.py:292
  134.6 17.1 %all-to-all-done.value_ref = bf16[16,1,128,256]{3,2,1,0:T(8,128)(2,1)S(1)} async-done(((bf16[16,1,128,256]{3,2,1,0:T(8,128)(2,1)}), bf16[16,1,128,256]{3,2,1,0:T(8,128)(2,1)S(1)}, u32[]{:S(2)}, u32[]{:S(2)}) %all-to-all-start) | async-done | bytes 1048608 | tf_op jit(solution)/shard_map/all_to_all | solution.py:292
  (80 shorter events, 15.9 us)
Async XLA Ops:
  2.9 14.7 %collective-permute-start.1 = (bf16[256,1024]{1,0:T(8,128)(2,1)}, bf16[256,1024]{1,0:T(8,128)(2,1)S(1)}, u32[]{:S(2)}, u32[]{:S(2)}) collective-permute-start(bf16[256,1024]{1,0:T(8,128)(2,1)} %get-tuple-element.32.refs_2_), channel_id=1, source_target_pairs={{0,24},{8,0},{16,8},{24,16},{32,56},{40,32},{48,40},{56,48},{64,88... | collective-permute-start | bytes 1572872 | tf_op jit(solution)/shard_map/ppermute | solution.py:258
  6.1 11.5 %collective-permute-start.7 = (bf16[256,1024]{1,0:T(8,128)(2,1)}, bf16[256,1024]{1,0:T(8,128)(2,1)S(1)}, u32[]{:S(2)}, u32[]{:S(2)}) collective-permute-start(bf16[256,1024]{1,0:T(8,128)(2,1)} %get-tuple-element.35), channel_id=1, source_target_pairs={{0,1},{1,0},{2,3},{3,2},{4,5},{5,4},{6,7},{7,6},{8,9},{9,8},{10,11... | collective-permute-start | bytes 1572872 | tf_op jit(solution)/shard_map/ppermute | solution.py:270
  6.1 15.1 %collective-permute-start.8 = (bf16[256,1024]{1,0:T(8,128)(2,1)}, bf16[256,1024]{1,0:T(8,128)(2,1)S(1)}, u32[]{:S(2)}, u32[]{:S(2)}) collective-permute-start(bf16[256,1024]{1,0:T(8,128)(2,1)} %get-tuple-element.30.refs_0_), channel_id=1, source_target_pairs={{0,96},{8,104},{16,112},{24,120},{32,0},{40,8},{48,16},{56,24},{64... | collective-permute-start | bytes 1572872 | tf_op jit(solution)/shard_map/ppermute | solution.py:262
  8.8 15.8 %collective-permute-start.10 = (bf16[256,1024]{1,0:T(8,128)(2,1)}, bf16[256,1024]{1,0:T(8,128)(2,1)S(1)}, u32[]{:S(2)}, u32[]{:S(2)}) collective-permute-start(bf16[256,1024]{1,0:T(8,128)(2,1)} %get-tuple-element.30.refs_0_), channel_id=1, source_target_pairs={{0,32},{8,40},{16,48},{24,56},{32,64},{40,72},{48,80},{56,88},{64,... | collective-permute-start | bytes 1572872 | tf_op jit(solution)/shard_map/ppermute | solution.py:262
  8.8 15.8 %collective-permute-start.28 = (bf16[256,1024]{1,0:T(8,128)(2,1)}, bf16[256,1024]{1,0:T(8,128)(2,1)S(1)}, u32[]{:S(2)}, u32[]{:S(2)}) collective-permute-start(bf16[256,1024]{1,0:T(8,128)(2,1)} %get-tuple-element.31.refs_1_), channel_id=1, source_target_pairs={{0,8},{8,16},{16,24},{24,0},{32,40},{40,48},{48,56},{56,32},{64,72... | collective-permute-start | bytes 1572872 | tf_op jit(solution)/shard_map/ppermute | solution.py:258
  17.6 15.8 %collective-permute-start.26 = (bf16[256,1024]{1,0:T(8,128)(2,1)}, bf16[256,1024]{1,0:T(8,128)(2,1)S(1)}, u32[]{:S(2)}, u32[]{:S(2)}) collective-permute-start(bf16[256,1024]{1,0:T(8,128)(2,1)} %get-tuple-element.31.refs_1_), channel_id=1, source_target_pairs={{0,24},{8,0},{16,8},{24,16},{32,56},{40,32},{48,40},{56,48},{64,88... | collective-permute-start | bytes 1572872 | tf_op jit(solution)/shard_map/ppermute | solution.py:258
  21.2 14.4 %collective-permute-start.9 = (bf16[256,1024]{1,0:T(8,128)(2,1)S(1)}, bf16[256,1024]{1,0:T(8,128)(2,1)S(1)}, u32[]{:S(2)}, u32[]{:S(2)}) collective-permute-start(bf16[256,1024]{1,0:T(8,128)(2,1)S(1)} %collective-permute-done.7.refs_9_), channel_id=1, source_target_pairs={{0,96},{8,104},{16,112},{24,120},{32,0},{40,8},{48,16},{56,24},{64... | collective-permute-start | bytes 1572872 | tf_op jit(solution)/shard_map/ppermute | solution.py:262
  24.6 16.0 %collective-permute-start.11 = (bf16[256,1024]{1,0:T(8,128)(2,1)S(1)}, bf16[256,1024]{1,0:T(8,128)(2,1)S(1)}, u32[]{:S(2)}, u32[]{:S(2)}) collective-permute-start(bf16[256,1024]{1,0:T(8,128)(2,1)S(1)} %collective-permute-done.10.refs_14_), channel_id=1, source_target_pairs={{0,32},{8,40},{16,48},{24,56},{32,64},{40,72},{48,80},{56,88},{64,... | collective-permute-start | bytes 1572872 | tf_op jit(solution)/shard_map/ppermute | solution.py:262
  24.6 16.0 %collective-permute-start.29 = (bf16[256,1024]{1,0:T(8,128)(2,1)S(1)}, bf16[256,1024]{1,0:T(8,128)(2,1)S(1)}, u32[]{:S(2)}, u32[]{:S(2)}) collective-permute-start(bf16[256,1024]{1,0:T(8,128)(2,1)S(1)} %collective-permute-done.28.refs_6_), channel_id=1, source_target_pairs={{0,8},{8,16},{16,24},{24,0},{32,40},{40,48},{48,56},{56,32},{64,72... | collective-permute-start | bytes 1572872 | tf_op jit(solution)/shard_map/ppermute | solution.py:258
  24.7 25.5 %collective-permute-start.13 = (bf16[256,1024]{1,0:T(8,128)(2,1)S(1)}, bf16[256,1024]{1,0:T(8,128)(2,1)S(1)}, u32[]{:S(2)}, u32[]{:S(2)}) collective-permute-start(bf16[256,1024]{1,0:T(8,128)(2,1)S(1)} %collective-permute-done.7.refs_9_), channel_id=1, source_target_pairs={{0,32},{8,40},{16,48},{24,56},{32,64},{40,72},{48,80},{56,88},{64,... | collective-permute-start | bytes 1572872 | tf_op jit(solution)/shard_map/ppermute | solution.py:262
  33.3 20.1 %collective-permute-start.31 = (bf16[256,1024]{1,0:T(8,128)(2,1)S(1)}, bf16[256,1024]{1,0:T(8,128)(2,1)S(1)}, u32[]{:S(2)}, u32[]{:S(2)}) collective-permute-start(bf16[256,1024]{1,0:T(8,128)(2,1)S(1)} %collective-permute-done.28.refs_6_), channel_id=1, source_target_pairs={{0,1},{1,0},{2,3},{3,2},{4,5},{5,4},{6,7},{7,6},{8,9},{9,8},{10,11... | collective-permute-start | bytes 1572872 | tf_op jit(solution)/shard_map/ppermute | solution.py:270
  35.6 14.7 %collective-permute-start.27 = (bf16[256,1024]{1,0:T(8,128)(2,1)S(1)}, bf16[256,1024]{1,0:T(8,128)(2,1)S(1)}, u32[]{:S(2)}, u32[]{:S(2)}) collective-permute-start(bf16[256,1024]{1,0:T(8,128)(2,1)S(1)} %collective-permute-done.26.refs_2_), channel_id=1, source_target_pairs={{0,1},{1,0},{2,3},{3,2},{4,5},{5,4},{6,7},{7,6},{8,9},{9,8},{10,11... | collective-permute-start | bytes 1572872 | tf_op jit(solution)/shard_map/ppermute | solution.py:270
  40.6 12.9 %collective-permute-start.12 = (bf16[256,1024]{1,0:T(8,128)(2,1)S(1)}, bf16[256,1024]{1,0:T(8,128)(2,1)S(1)}, u32[]{:S(2)}, u32[]{:S(2)}) collective-permute-start(bf16[256,1024]{1,0:T(8,128)(2,1)S(1)} %collective-permute-done.9.refs_11_), channel_id=1, source_target_pairs={{0,96},{8,104},{16,112},{24,120},{32,0},{40,8},{48,16},{56,24},{64... | collective-permute-start | bytes 1572872 | tf_op jit(solution)/shard_map/ppermute | solution.py:262
  40.6 12.9 %collective-permute-start.30 = (bf16[256,1024]{1,0:T(8,128)(2,1)S(1)}, bf16[256,1024]{1,0:T(8,128)(2,1)S(1)}, u32[]{:S(2)}, u32[]{:S(2)}) collective-permute-start(bf16[256,1024]{1,0:T(8,128)(2,1)S(1)} %collective-permute-done.29.refs_4_), channel_id=1, source_target_pairs={{0,1},{1,0},{2,3},{3,2},{4,5},{5,4},{6,7},{7,6},{8,9},{9,8},{10,11... | collective-permute-start | bytes 1572872 | tf_op jit(solution)/shard_map/ppermute | solution.py:270
  50.2 13.8 %collective-permute-start.5 = (bf16[256,1024]{1,0:T(8,128)(2,1)}, bf16[256,1024]{1,0:T(8,128)(2,1)S(1)}, u32[]{:S(2)}, u32[]{:S(2)}) collective-permute-start(bf16[256,1024]{1,0:T(8,128)(2,1)} %get-tuple-element.32.refs_2_), channel_id=1, source_target_pairs={{0,8},{8,16},{16,24},{24,0},{32,40},{40,48},{48,56},{56,32},{64,72... | collective-permute-start | bytes 1572872 | tf_op jit(solution)/shard_map/ppermute | solution.py:258
  50.3 13.8 %collective-permute-start.3 = (bf16[256,1024]{1,0:T(8,128)(2,1)S(1)}, bf16[256,1024]{1,0:T(8,128)(2,1)S(1)}, u32[]{:S(2)}, u32[]{:S(2)}) collective-permute-start(bf16[256,1024]{1,0:T(8,128)(2,1)S(1)} %collective-permute-done.1.refs_2_), channel_id=1, source_target_pairs={{0,24},{8,0},{16,8},{24,16},{32,56},{40,32},{48,40},{56,48},{64,88... | collective-permute-start | bytes 1572872 | tf_op jit(solution)/shard_map/ppermute | solution.py:258
  58.9 14.1 %collective-permute-start.32 = (bf16[4,256,256]{2,1,0:T(8,128)(2,1)S(1)}, bf16[4,256,256]{2,1,0:T(8,128)(2,1)S(1)}, u32[]{:S(2)}, u32[]{:S(2)}) collective-permute-start(bf16[4,256,256]{2,1,0:T(8,128)(2,1)S(1)} %get-tuple-element.47), channel_id=1, source_target_pairs={{0,2},{1,3},{2,4},{3,5},{4,6},{5,7},{6,0},{7,1},{8,10},{9,11},{10,... | collective-permute-start | bytes 1572872 | tf_op jit(solution)/shard_map/ppermute | solution.py:266
  60.9 12.2 %collective-permute-start.33 = (bf16[4,256,256]{2,1,0:T(8,128)(2,1)S(1)}, bf16[4,256,256]{2,1,0:T(8,128)(2,1)S(1)}, u32[]{:S(2)}, u32[]{:S(2)}) collective-permute-start(bf16[4,256,256]{2,1,0:T(8,128)(2,1)S(1)} %get-tuple-element.48), channel_id=1, source_target_pairs={{0,6},{1,7},{2,0},{3,1},{4,2},{5,3},{6,4},{7,5},{8,14},{9,15},{10,... | collective-permute-start | bytes 1572872 | tf_op jit(solution)/shard_map/ppermute | solution.py:266
  63.1 11.3 %collective-permute-start = (bf16[256,1024]{1,0:T(8,128)(2,1)}, bf16[256,1024]{1,0:T(8,128)(2,1)S(1)}, u32[]{:S(2)}, u32[]{:S(2)}) collective-permute-start(bf16[256,1024]{1,0:T(8,128)(2,1)} %get-tuple-element.32.refs_2_), channel_id=1, source_target_pairs={{0,1},{1,0},{2,3},{3,2},{4,5},{5,4},{6,7},{7,6},{8,9},{9,8},{10,11... | collective-permute-start | bytes 1572872 | tf_op jit(solution)/shard_map/ppermute | solution.py:270
  64.0 12.8 %collective-permute-start.2 = (bf16[256,1024]{1,0:T(8,128)(2,1)S(1)}, bf16[256,1024]{1,0:T(8,128)(2,1)S(1)}, u32[]{:S(2)}, u32[]{:S(2)}) collective-permute-start(bf16[256,1024]{1,0:T(8,128)(2,1)S(1)} %collective-permute-done.1.refs_2_), channel_id=1, source_target_pairs={{0,1},{1,0},{2,3},{3,2},{4,5},{5,4},{6,7},{7,6},{8,9},{9,8},{10,11... | collective-permute-start | bytes 1572872 | tf_op jit(solution)/shard_map/ppermute | solution.py:270
  64.0 12.8 %collective-permute-start.6 = (bf16[256,1024]{1,0:T(8,128)(2,1)S(1)}, bf16[256,1024]{1,0:T(8,128)(2,1)S(1)}, u32[]{:S(2)}, u32[]{:S(2)}) collective-permute-start(bf16[256,1024]{1,0:T(8,128)(2,1)S(1)} %collective-permute-done.5.refs_6_), channel_id=1, source_target_pairs={{0,1},{1,0},{2,3},{3,2},{4,5},{5,4},{6,7},{7,6},{8,9},{9,8},{10,11... | collective-permute-start | bytes 1572872 | tf_op jit(solution)/shard_map/ppermute | solution.py:270
  73.2 10.2 %collective-permute-start.34 = (bf16[2,256,256]{2,1,0:T(8,128)(2,1)S(1)}, bf16[2,256,256]{2,1,0:T(8,128)(2,1)S(1)}, u32[]{:S(2)}, u32[]{:S(2)}) collective-permute-start(bf16[2,256,256]{2,1,0:T(8,128)(2,1)S(1)} %add_convert_fusion.1), channel_id=1, source_target_pairs={{0,2},{1,3},{2,4},{3,5},{4,6},{5,7},{6,0},{7,1},{8,10},{9,11},{10,... | collective-permute-start | bytes 786440 | tf_op jit(solution)/shard_map/ppermute | solution.py:266
  74.4 8.9 %collective-permute-start.35 = (bf16[2,256,256]{2,1,0:T(8,128)(2,1)S(1)}, bf16[2,256,256]{2,1,0:T(8,128)(2,1)S(1)}, u32[]{:S(2)}, u32[]{:S(2)}) collective-permute-start(bf16[2,256,256]{2,1,0:T(8,128)(2,1)S(1)} %add_convert_fusion), channel_id=1, source_target_pairs={{0,6},{1,7},{2,0},{3,1},{4,2},{5,3},{6,4},{7,5},{8,14},{9,15},{10,... | collective-permute-start | bytes 786440 | tf_op jit(solution)/shard_map/ppermute | solution.py:266
  82.3 20.3 %collective-permute-start.14 = (bf16[4,256,256]{2,1,0:T(8,128)(2,1)}, bf16[4,256,256]{2,1,0:T(8,128)(2,1)S(1)}, u32[]{:S(2)}, u32[]{:S(2)}) collective-permute-start(bf16[4,256,256]{2,1,0:T(8,128)(2,1)} %get-tuple-element.37), channel_id=1, source_target_pairs={{0,2},{1,3},{2,4},{3,5},{4,6},{5,7},{6,0},{7,1},{8,10},{9,11},{10,... | collective-permute-start | bytes 1572872 | tf_op jit(solution)/shard_map/ppermute | solution.py:266
  83.9 19.8 %collective-permute-start.15 = (bf16[4,256,256]{2,1,0:T(8,128)(2,1)}, bf16[4,256,256]{2,1,0:T(8,128)(2,1)S(1)}, u32[]{:S(2)}, u32[]{:S(2)}) collective-permute-start(bf16[4,256,256]{2,1,0:T(8,128)(2,1)} %get-tuple-element.38), channel_id=1, source_target_pairs={{0,6},{1,7},{2,0},{3,1},{4,2},{5,3},{6,4},{7,5},{8,14},{9,15},{10,... | collective-permute-start | bytes 1572872 | tf_op jit(solution)/shard_map/ppermute | solution.py:266
  98.9 30.3 %all-to-all-start.1 = ((bf16[16,1,128,256]{3,2,1,0:T(8,128)(2,1)}), bf16[16,1,128,256]{3,2,1,0:T(8,128)(2,1)S(1)}, u32[]{:S(2)}, u32[]{:S(2)}) async-start(bf16[16,1,128,256]{3,2,1,0:T(8,128)(2,1)} %pack.3), calls=%async_computation.1 | async-start | bytes 2097152 | tf_op jit(solution)/shard_map/all_to_all | solution.py:292
  103.6 9.8 %collective-permute-start.16 = (bf16[2,256,256]{2,1,0:T(8,128)(2,1)S(1)}, bf16[2,256,256]{2,1,0:T(8,128)(2,1)S(1)}, u32[]{:S(2)}, u32[]{:S(2)}) collective-permute-start(bf16[2,256,256]{2,1,0:T(8,128)(2,1)S(1)} %add_convert_fusion.3), channel_id=1, source_target_pairs={{0,2},{1,3},{2,4},{3,5},{4,6},{5,7},{6,0},{7,1},{8,10},{9,11},{10,... | collective-permute-start | bytes 786440 | tf_op jit(solution)/shard_map/ppermute | solution.py:266
  103.8 9.7 %collective-permute-start.17 = (bf16[2,256,256]{2,1,0:T(8,128)(2,1)S(1)}, bf16[2,256,256]{2,1,0:T(8,128)(2,1)S(1)}, u32[]{:S(2)}, u32[]{:S(2)}) collective-permute-start(bf16[2,256,256]{2,1,0:T(8,128)(2,1)S(1)} %add_convert_fusion.2), channel_id=1, source_target_pairs={{0,6},{1,7},{2,0},{3,1},{4,2},{5,3},{6,4},{7,5},{8,14},{9,15},{10,... | collective-permute-start | bytes 786440 | tf_op jit(solution)/shard_map/ppermute | solution.py:266
  113.7 9.2 %collective-permute-start.18 = (bf16[256,256]{1,0:T(8,128)(2,1)S(1)}, bf16[256,256]{1,0:T(8,128)(2,1)S(1)}, u32[]{:S(2)}, u32[]{:S(2)}) collective-permute-start(bf16[256,256]{1,0:T(8,128)(2,1)S(1)} %get-tuple-element.42), channel_id=1, source_target_pairs={{0,24},{8,0},{16,8},{24,16},{32,56},{40,32},{48,40},{56,48},{64,88... | collective-permute-start | bytes 393224 | tf_op jit(solution)/shard_map/ppermute | solution.py:258
  116.5 7.9 %collective-permute-start.19 = (bf16[256,256]{1,0:T(8,128)(2,1)S(1)}, bf16[256,256]{1,0:T(8,128)(2,1)S(1)}, u32[]{:S(2)}, u32[]{:S(2)}) collective-permute-start(bf16[256,256]{1,0:T(8,128)(2,1)S(1)} %get-tuple-element.43), channel_id=1, source_target_pairs={{0,16},{8,24},{16,0},{24,8},{32,48},{40,56},{48,32},{56,40},{64,80... | collective-permute-start | bytes 393224 | tf_op jit(solution)/shard_map/ppermute | solution.py:258
  117.3 8.7 %collective-permute-start.20 = (bf16[256,256]{1,0:T(8,128)(2,1)S(1)}, bf16[256,256]{1,0:T(8,128)(2,1)S(1)}, u32[]{:S(2)}, u32[]{:S(2)}) collective-permute-start(bf16[256,256]{1,0:T(8,128)(2,1)S(1)} %get-tuple-element.44), channel_id=1, source_target_pairs={{0,8},{8,16},{16,24},{24,0},{32,40},{40,48},{48,56},{56,32},{64,72... | collective-permute-start | bytes 393224 | tf_op jit(solution)/shard_map/ppermute | solution.py:258
  129.3 22.5 %all-to-all-start = ((bf16[16,1,128,256]{3,2,1,0:T(8,128)(2,1)}), bf16[16,1,128,256]{3,2,1,0:T(8,128)(2,1)S(1)}, u32[]{:S(2)}, u32[]{:S(2)}) async-start(bf16[16,1,128,256]{3,2,1,0:T(8,128)(2,1)} %pack.2), calls=%async_computation | async-start | bytes 2097152 | tf_op jit(solution)/shard_map/all_to_all | solution.py:292
  (17 other events, 75.3 us)

commit v4 on v3

--- a/solution.py
+++ b/solution.py
@@ -102,49 +102,49 @@
     )(*values)
 
 
-def product_body(*refs):
-    rows, cols = refs[:8], refs[8:16]
-    up, down, next_low, prev_high, own = refs[16:21]
-    rows_ref, cols_ref, row_sems, col_sems = refs[21:]
-    x, _, z, _ = position()
+def load(pieces, place, sems):
     copies = []
     for d in range(4):
         for h in range(2):
-            across = pl.ds(1024 * h, 1024)
             at = 2 * d + h
-            copies.append(
-                pltpu.make_async_copy(cols[at], cols_ref.at[(x + d) % 4, :, across], col_sems.at[at])
-            )
-            copies.append(
-                pltpu.make_async_copy(rows[at], rows_ref.at[d, :, across], row_sems.at[at])
-            )
+            copies.append(pltpu.make_async_copy(pieces[at], place(d, pl.ds(1024 * h, 1024)), sems.at[at]))
+    return copies
+
+
+def blocks(rows_ref, right, targets):
+    for j, (out, at) in enumerate(targets):
+        out[at] = lax.dot_general(
+            rows_ref[j], right, (((1,), (1,)), ((), ())), preferred_element_type=jnp.float32
+        ).astype(out.dtype)
+
+
+def product_body(*refs, keep):
+    rows, cols = refs[:8], refs[8:16]
+    up, down, next_low, prev_high = refs[16:20]
+    rows_ref, cols_ref, row_sems, col_sems = refs[-4:]
+    x, _, z, _ = position()
+    copies = load(cols, lambda d, across: cols_ref.at[(x + d) % 4, :, across], col_sems)
+    copies += load(rows, lambda d, across: rows_ref.at[d, :, across], row_sems)
     for copy in copies:
         copy.start()
     for copy in copies:
         copy.wait()
-    places = (
-        (2, ((up, 0), (up, 1), (down, 0), (down, 1))),
-        (1, ((next_low, 0), (next_low, 1), (up, 2), (up, 3))),
-        (3, ((down, 2), (down, 3), (prev_high, 0), (prev_high, 1))),
-        (0, ((own, 0), (own, 1), (own, 2), (own, 3))),
-    )
-    for d, targets in places:
-        right = cols_ref[(z + d) % 4]
-        for j, (out, at) in enumerate(targets):
-            out[at] = lax.dot_general(
-                rows_ref[j], right, (((1,), (1,)), ((), ())), preferred_element_type=jnp.float32
-            ).astype(out.dtype)
-
-
-def product(rows, cols):
+    blocks(rows_ref, cols_ref[(z + 2) % 4], ((up, 0), (up, 1), (down, 0), (down, 1)))
+    blocks(rows_ref, cols_ref[(z + 1) % 4], ((next_low, 0), (next_low, 1), (up, 2), (up, 3)))
+    blocks(rows_ref, cols_ref[(z + 3) % 4], ((down, 2), (down, 3), (prev_high, 0), (prev_high, 1)))
+    if keep:
+        blocks(rows_ref, cols_ref[z], tuple((refs[20], j) for j in range(4)))
+
+
+def product(rows, cols, keep):
     four = jax.ShapeDtypeStruct((4, TILE, TILE), jnp.bfloat16)
     two = jax.ShapeDtypeStruct((2, TILE, TILE), jnp.bfloat16)
-    kept = jax.ShapeDtypeStruct((4, TILE, TILE), jnp.float32)
-    return pl.pallas_call(
-        product_body,
-        out_shape=(four, four, two, two, kept),
+    kept = (jax.ShapeDtypeStruct((4, TILE, TILE), jnp.float32),) * keep
+    return pl.pallas_call(
+        lambda *refs: product_body(*refs, keep=keep),
+        out_shape=(four, four, two, two, *kept),
         in_specs=[pl.BlockSpec(memory_space=pl.ANY)] * 16,
-        out_specs=tuple(pl.BlockSpec(memory_space=pltpu.VMEM) for _ in range(5)),
+        out_specs=(pl.BlockSpec(memory_space=pltpu.VMEM),) * (4 + keep),
         scratch_shapes=[
             pltpu.VMEM((4, TILE, 2048), jnp.bfloat16),
             pltpu.VMEM((4, TILE, 2048), jnp.bfloat16),
@@ -153,6 +153,42 @@
         ],
         compiler_params=pltpu.CompilerParams(vmem_limit_bytes=32 * 1024 * 1024),
         name="product",
+    )(*rows, *cols)
+
+
+def kept_body(*refs):
+    rows, cols, own = refs[:8], refs[8:16], refs[16]
+    rows_ref, right_ref, row_sems, col_sems = refs[17:]
+    x, _, z, _ = position()
+    right = load(cols, lambda d, across: right_ref.at[:, across], col_sems)
+    copies = load(rows, lambda d, across: rows_ref.at[d, :, across], row_sems)
+    for act in (lambda copy: copy.start(), lambda copy: copy.wait()):
+        for d in range(4):
+
+            @pl.when((x + d) % 4 == z)
+            def _():
+                for copy in right[2 * d : 2 * d + 2]:
+                    act(copy)
+
+        for copy in copies:
+            act(copy)
+    blocks(rows_ref, right_ref[...], tuple((own, j) for j in range(4)))
+
+
+def kept_product(rows, cols):
+    return pl.pallas_call(
+        kept_body,
+        out_shape=jax.ShapeDtypeStruct((4, TILE, TILE), jnp.float32),
+        in_specs=[pl.BlockSpec(memory_space=pl.ANY)] * 16,
+        out_specs=pl.BlockSpec(memory_space=pltpu.VMEM),
+        scratch_shapes=[
+            pltpu.VMEM((4, TILE, 2048), jnp.bfloat16),
+            pltpu.VMEM((TILE, 2048), jnp.bfloat16),
+            pltpu.SemaphoreType.DMA((8,)),
+            pltpu.SemaphoreType.DMA((8,)),
+        ],
+        compiler_params=pltpu.CompilerParams(vmem_limit_bytes=32 * 1024 * 1024),
+        name="kept",
     )(*rows, *cols)
 
 
@@ -310,7 +346,11 @@
     ):
         others = [swap(value) for value in pieces]
         rows = [piece for pair in zip((own, *pieces[1:]), others) for piece in pair]
-        halves.append(product(rows, cols))
+        if halves:
+            halves.append(product(rows, cols, 1))
+        else:
+            sent = product(rows, cols, 0)
+            halves.append((*sent, kept_product(rows, cols)))
     first = to_owners(owner_rows, reduce_along_z(halves[0]))
     second = to_owners(owner_rows, reduce_along_z(halves[1]))
     return place_half(1, second, place_half(0, first))

time: 153 us -> 153 us (level)
    ppermute x8, waiting for transfers between devices: 15.9 us -> 14 us  [zpass(): return lax.ppermute(value, 'col', along_z(step))]
    unnamed x8 -> x10, local copies, waits for them, and re-layouts: 2.09 us -> 3.13 us
    pallas_call x2 -> x3, Pallas kernels: 10.9 us -> 11.7 us  [the longest x2 9.79 us: product(): pl.pallas_call(lambda *refs: product_body(*refs, keep=keep), out_shape=(f...]
  transfers between devices with their start and end apart: 45 -> 45, of which waited for: 19 -> 18; matrix products, arithmetic and copies ran while one was open for 1% -> 1% of each run, Pallas kernels for 11% -> 11%
where the time goes in v4:
time: 153 us
  waiting for transfers between devices  81.1 us (53%)
  starting transfers between devices  46.4 us (30%)
  Pallas kernels  20.7 us (14%)
  local copies, waits for them, and re-layouts  3.13 us (2%)
    ppermute x12, waiting for transfers between devices, ypass(): return lax.ppermute(value, 'row', along_y(step))  33.9 us
    all_to_all x2, waiting for transfers between devices, to_owners(): lax.all_to_all(outgoing, 'row', split_axis=0, concat_axis=0, tiled=True)  17.2 us
    ppermute x12, starting transfers between devices, ypass(): return lax.ppermute(value, 'row', along_y(step))  16.7 us
    ppermute x8, starting transfers between devices, zpass(): return lax.ppermute(value, 'col', along_z(step))  14.4 us
    ppermute x8, waiting for transfers between devices, zpass(): return lax.ppermute(value, 'col', along_z(step))  14 us
    ppermute x6, waiting for transfers between devices, xpass(): return lax.ppermute(value, 'row', along_x(step))  13.6 us
    pallas_call x2, Pallas kernels, product(): pl.pallas_call(lambda *refs: product_body(*refs, keep=keep), out_shape=(f...  9.79 us
    all_to_all x2, starting transfers between devices, to_owners(): lax.all_to_all(outgoing, 'row', split_axis=0, concat_axis=0, tiled=True)  8.02 us
  transfers between devices with their start and end apart: 45, of which 18 were waited for; matrix products, arithmetic and copies ran while one was open for 1% of the time, Pallas kernels for 11%

profile of v4, /device:TPU:0, one launch (start us, length us, event | category | flops | bytes accessed | tf_op | source)
XLA Modules:
  0.0 153.0 jit_solution(15567391806028941121)
XLA Ops:
  0.0 2.9 %scale.1 = (bf16[256,1024]{1,0:T(8,128)(2,1)}, bf16[256,1024]{1,0:T(8,128)(2,1)}, bf16[256,1024]{1,0:T(8,128)(2,1)}, bf16[256,1024]{1,0:T(8,128)(2,1)}) custom-call(s32[2,32]{1,0:T(2,128)} %mask_hbm.1, bf16[512,1024]{1,0:T(8,128)(2,1)} %panels_hbm.1, f32[1,1024]{1,0:T(1,128)} %bitcast.1), custom_call_target="tpu_custom_call" | custom-call | tf_op jit(solution)/shard_map/scale/pallas_call | solution.py:69
  2.9 3.2 %collective-permute-start.1 = (bf16[256,1024]{1,0:T(8,128)(2,1)}, bf16[256,1024]{1,0:T(8,128)(2,1)S(1)}, u32[]{:S(2)}, u32[]{:S(2)}) collective-permute-start(bf16[256,1024]{1,0:T(8,128)(2,1)} %get-tuple-element.31.refs_2_), channel_id=1, source_target_pairs={{0,24},{8,0},{16,8},{24,16},{32,56},{40,32},{48,40},{56,48},{64,88... | collective-permute-start | bytes 1572872 | tf_op jit(solution)/shard_map/ppermute | solution.py:294
  6.1 2.8 %collective-permute-start.8 = (bf16[256,1024]{1,0:T(8,128)(2,1)}, bf16[256,1024]{1,0:T(8,128)(2,1)S(1)}, u32[]{:S(2)}, u32[]{:S(2)}) collective-permute-start(bf16[256,1024]{1,0:T(8,128)(2,1)} %get-tuple-element.29.refs_0_), channel_id=1, source_target_pairs={{0,96},{8,104},{16,112},{24,120},{32,0},{40,8},{48,16},{56,24},{64... | collective-permute-start | bytes 1572872 | tf_op jit(solution)/shard_map/ppermute | solution.py:298
  8.8 8.7 %collective-permute-done.1.refs_2_ = bf16[256,1024]{1,0:T(8,128)(2,1)S(1)} collective-permute-done((bf16[256,1024]{1,0:T(8,128)(2,1)}, bf16[256,1024]{1,0:T(8,128)(2,1)S(1)}, u32[]{:S(2)}, u32[]{:S(2)}) %collective-permute-start.1) | collective-permute-done | bytes 524320 | tf_op jit(solution)/shard_map/ppermute | solution.py:294
  17.6 3.6 %collective-permute-start.26 = (bf16[256,1024]{1,0:T(8,128)(2,1)}, bf16[256,1024]{1,0:T(8,128)(2,1)S(1)}, u32[]{:S(2)}, u32[]{:S(2)}) collective-permute-start(bf16[256,1024]{1,0:T(8,128)(2,1)} %get-tuple-element.30.refs_1_), channel_id=1, source_target_pairs={{0,24},{8,0},{16,8},{24,16},{32,56},{40,32},{48,40},{56,48},{64,88... | collective-permute-start | bytes 1572872 | tf_op jit(solution)/shard_map/ppermute | solution.py:294
  21.2 3.4 %collective-permute-start.9 = (bf16[256,1024]{1,0:T(8,128)(2,1)S(1)}, bf16[256,1024]{1,0:T(8,128)(2,1)S(1)}, u32[]{:S(2)}, u32[]{:S(2)}) collective-permute-start(bf16[256,1024]{1,0:T(8,128)(2,1)S(1)} %collective-permute-done.7.refs_9_), channel_id=1, source_target_pairs={{0,96},{8,104},{16,112},{24,120},{32,0},{40,8},{48,16},{56,24},{64... | collective-permute-start | bytes 1572872 | tf_op jit(solution)/shard_map/ppermute | solution.py:298
  24.8 8.5 %collective-permute-done.26.refs_2_ = bf16[256,1024]{1,0:T(8,128)(2,1)S(1)} collective-permute-done((bf16[256,1024]{1,0:T(8,128)(2,1)}, bf16[256,1024]{1,0:T(8,128)(2,1)S(1)}, u32[]{:S(2)}, u32[]{:S(2)}) %collective-permute-start.26) | collective-permute-done | bytes 524320 | tf_op jit(solution)/shard_map/ppermute | solution.py:294
  33.3 2.2 %collective-permute-done.9.refs_11_ = bf16[256,1024]{1,0:T(8,128)(2,1)S(1)} collective-permute-done((bf16[256,1024]{1,0:T(8,128)(2,1)S(1)}, bf16[256,1024]{1,0:T(8,128)(2,1)S(1)}, u32[]{:S(2)}, u32[]{:S(2)}) %collective-permute-start.9) | collective-permute-done | bytes 524320 | tf_op jit(solution)/shard_map/ppermute | solution.py:298
  35.6 5.0 %collective-permute-done.11.refs_12_ = bf16[256,1024]{1,0:T(8,128)(2,1)S(1)} collective-permute-done((bf16[256,1024]{1,0:T(8,128)(2,1)S(1)}, bf16[256,1024]{1,0:T(8,128)(2,1)S(1)}, u32[]{:S(2)}, u32[]{:S(2)}) %collective-permute-start.11) | collective-permute-done | bytes 524320 | tf_op jit(solution)/shard_map/ppermute | solution.py:298
  43.9 6.3 %collective-permute-done.13.refs_15_ = bf16[256,1024]{1,0:T(8,128)(2,1)S(1)} collective-permute-done((bf16[256,1024]{1,0:T(8,128)(2,1)S(1)}, bf16[256,1024]{1,0:T(8,128)(2,1)S(1)}, u32[]{:S(2)}, u32[]{:S(2)}) %collective-permute-start.13) | collective-permute-done | bytes 524320 | tf_op jit(solution)/shard_map/ppermute | solution.py:298
  50.2 3.2 %collective-permute-start.3 = (bf16[256,1024]{1,0:T(8,128)(2,1)S(1)}, bf16[256,1024]{1,0:T(8,128)(2,1)S(1)}, u32[]{:S(2)}, u32[]{:S(2)}) collective-permute-start(bf16[256,1024]{1,0:T(8,128)(2,1)S(1)} %collective-permute-done.1.refs_2_), channel_id=1, source_target_pairs={{0,24},{8,0},{16,8},{24,16},{32,56},{40,32},{48,40},{56,48},{64,88... | collective-permute-start | bytes 1572872 | tf_op jit(solution)/shard_map/ppermute | solution.py:294
  53.5 4.4 %product.3 = (bf16[4,256,256]{2,1,0:T(8,128)(2,1)S(1)}, bf16[4,256,256]{2,1,0:T(8,128)(2,1)S(1)}, bf16[2,256,256]{2,1,0:T(8,128)(2,1)S(1)}, bf16[2,256,256]{2,1,0:T(8,128)(2,1)S(1)}) custom-call(bf16[256,1024]{1,0:T(8,128)(2,1)S(1)} %get-tuple-element.44.refs_0_, bf16[256,1024]{1,0:T(8,128)(2,1)S(1)} %collective-permute-done.25.refs_1_, ...), custom_call_target="tpu_custom_call" | custom-call | tf_op jit(solution)/shard_map/product/pallas_call | solution.py:143
  57.9 2.0 %collective-permute-start.32 = (bf16[4,256,256]{2,1,0:T(8,128)(2,1)S(1)}, bf16[4,256,256]{2,1,0:T(8,128)(2,1)S(1)}, u32[]{:S(2)}, u32[]{:S(2)}) collective-permute-start(bf16[4,256,256]{2,1,0:T(8,128)(2,1)S(1)} %get-tuple-element.45), channel_id=1, source_target_pairs={{0,2},{1,3},{2,4},{3,5},{4,6},{5,7},{6,0},{7,1},{8,10},{9,11},{10,... | collective-permute-start | bytes 1572872 | tf_op jit(solution)/shard_map/ppermute | solution.py:302
  59.8 2.2 %collective-permute-start.33 = (bf16[4,256,256]{2,1,0:T(8,128)(2,1)S(1)}, bf16[4,256,256]{2,1,0:T(8,128)(2,1)S(1)}, u32[]{:S(2)}, u32[]{:S(2)}) collective-permute-start(bf16[4,256,256]{2,1,0:T(8,128)(2,1)S(1)} %get-tuple-element.46), channel_id=1, source_target_pairs={{0,6},{1,7},{2,0},{3,1},{4,2},{5,3},{6,4},{7,5},{8,14},{9,15},{10,... | collective-permute-start | bytes 1572872 | tf_op jit(solution)/shard_map/ppermute | solution.py:302
  62.0 1.7 %collective-permute-done.5.refs_6_ = bf16[256,1024]{1,0:T(8,128)(2,1)S(1)} collective-permute-done((bf16[256,1024]{1,0:T(8,128)(2,1)S(1)}, bf16[256,1024]{1,0:T(8,128)(2,1)S(1)}, u32[]{:S(2)}, u32[]{:S(2)}) %collective-permute-start.5) | collective-permute-done | bytes 524320 | tf_op jit(solution)/shard_map/ppermute | solution.py:294
  64.3 7.7 %collective-permute-done.32.got_up = bf16[4,256,256]{2,1,0:T(8,128)(2,1)S(1)} collective-permute-done((bf16[4,256,256]{2,1,0:T(8,128)(2,1)S(1)}, bf16[4,256,256]{2,1,0:T(8,128)(2,1)S(1)}, u32[]{:S(2)}, u32[]{:S(2)}) %collective-permute-start.32) | collective-permute-done | bytes 524320 | tf_op jit(solution)/shard_map/ppermute | solution.py:302
  73.3 2.4 %collective-permute-start.35 = (bf16[2,256,256]{2,1,0:T(8,128)(2,1)S(1)}, bf16[2,256,256]{2,1,0:T(8,128)(2,1)S(1)}, u32[]{:S(2)}, u32[]{:S(2)}) collective-permute-start(bf16[2,256,256]{2,1,0:T(8,128)(2,1)S(1)} %add_convert_fusion), channel_id=1, source_target_pairs={{0,6},{1,7},{2,0},{3,1},{4,2},{5,3},{6,4},{7,5},{8,14},{9,15},{10,... | collective-permute-start | bytes 786440 | tf_op jit(solution)/shard_map/ppermute | solution.py:302
  75.7 5.4 %product.2 = (bf16[4,256,256]{2,1,0:T(8,128)(2,1)}, bf16[4,256,256]{2,1,0:T(8,128)(2,1)}, bf16[2,256,256]{2,1,0:T(8,128)(2,1)S(1)}, bf16[2,256,256]{2,1,0:T(8,128)(2,1)S(1)}, f32[4,256,256]{2,1,0:T(8,128)S(1)}) custom-call(bf16[256,1024]{1,0:T(8,128)(2,1)S(1)} %get-tuple-element.32.refs_0_, bf16[256,1024]{1,0:T(8,128)(2,1)S(1)} %collective-permute-done.refs_1_, ...), custom_call_target="tpu_custom_call" | custom-call | tf_op jit(solution)/shard_map/product/pallas_call | solution.py:143
  81.3 1.9 %kept.1.own = f32[4,256,256]{2,1,0:T(8,128)S(1)} custom-call(bf16[256,1024]{1,0:T(8,128)(2,1)S(1)} %get-tuple-element.44.refs_0_, bf16[256,1024]{1,0:T(8,128)(2,1)S(1)} %collective-permute-done.25.refs_1_, bf16[256,1024]{1,0:T(8,128)(2,1)S(1)} %collective-permute-done.26.refs_2_, bf16[256,1024]{1,0:T(8,128)(2,1)S(1)} %collective-permute-done.27.refs_3_, ...), custom_call_target="tpu_custom_call" | custom-call | tf_op jit(solution)/shard_map/kept/pallas_call | solution.py:179
  83.8 3.2 %collective-permute-start.15 = (bf16[4,256,256]{2,1,0:T(8,128)(2,1)}, bf16[4,256,256]{2,1,0:T(8,128)(2,1)S(1)}, u32[]{:S(2)}, u32[]{:S(2)}) collective-permute-start(bf16[4,256,256]{2,1,0:T(8,128)(2,1)} %get-tuple-element.37), channel_id=1, source_target_pairs={{0,6},{1,7},{2,0},{3,1},{4,2},{5,3},{6,4},{7,5},{8,14},{9,15},{10,... | collective-permute-start | bytes 1572872 | tf_op jit(solution)/shard_map/ppermute | solution.py:302
  89.0 5.6 %collective-permute-done.37.refs_2_ = bf16[256,256]{1,0:T(8,128)(2,1)S(1)} collective-permute-done((bf16[256,256]{1,0:T(8,128)(2,1)S(1)}, bf16[256,256]{1,0:T(8,128)(2,1)S(1)}, u32[]{:S(2)}, u32[]{:S(2)}) %collective-permute-start.37) | collective-permute-done | bytes 131104 | tf_op jit(solution)/shard_map/ppermute | solution.py:294
  97.4 1.8 %pack.3 = bf16[16,1,128,256]{3,2,1,0:T(8,128)(2,1)} custom-call(s32[2,4]{1,0:T(2,128)S(1)} %copy-done.4, bf16[256,256]{1,0:T(8,128)(2,1)S(1)} %get-tuple-element.49.refs_0_, bf16[256,256]{1,0:T(8,128)(2,1)S(1)} %collective-permute-done.36.refs_1_, bf16[256,256]{1,0:T(8,128)(2,1)S(1)} %collective-permute-done.37.refs_2_, ...), custom_call_target="tpu_custom_call" | custom-call | tf_op jit(solution)/shard_map/pack/pallas_call | solution.py:260
  99.2 3.7 %all-to-all-start.1 = ((bf16[16,1,128,256]{3,2,1,0:T(8,128)(2,1)}), bf16[16,1,128,256]{3,2,1,0:T(8,128)(2,1)S(1)}, u32[]{:S(2)}, u32[]{:S(2)}) async-start(bf16[16,1,128,256]{3,2,1,0:T(8,128)(2,1)} %pack.3), calls=%async_computation.1 | async-start | bytes 2097152 | tf_op jit(solution)/shard_map/all_to_all | solution.py:328
  104.1 3.3 %collective-permute-start.17 = (bf16[2,256,256]{2,1,0:T(8,128)(2,1)S(1)}, bf16[2,256,256]{2,1,0:T(8,128)(2,1)S(1)}, u32[]{:S(2)}, u32[]{:S(2)}) collective-permute-start(bf16[2,256,256]{2,1,0:T(8,128)(2,1)S(1)} %add_convert_fusion.2), channel_id=1, source_target_pairs={{0,6},{1,7},{2,0},{3,1},{4,2},{5,3},{6,4},{7,5},{8,14},{9,15},{10,... | collective-permute-start | bytes 786440 | tf_op jit(solution)/shard_map/ppermute | solution.py:302
  107.4 6.3 %collective-permute-done.16.sum_up = bf16[2,256,256]{2,1,0:T(8,128)(2,1)S(1)} collective-permute-done((bf16[2,256,256]{2,1,0:T(8,128)(2,1)S(1)}, bf16[2,256,256]{2,1,0:T(8,128)(2,1)S(1)}, u32[]{:S(2)}, u32[]{:S(2)}) %collective-permute-start.16) | collective-permute-done | bytes 262176 | tf_op jit(solution)/shard_map/ppermute | solution.py:302
  113.9 2.8 %collective-permute-start.18 = (bf16[256,256]{1,0:T(8,128)(2,1)S(1)}, bf16[256,256]{1,0:T(8,128)(2,1)S(1)}, u32[]{:S(2)}, u32[]{:S(2)}) collective-permute-start(bf16[256,256]{1,0:T(8,128)(2,1)S(1)} %get-tuple-element.41), channel_id=1, source_target_pairs={{0,24},{8,0},{16,8},{24,16},{32,56},{40,32},{48,40},{56,48},{64,88... | collective-permute-start | bytes 393224 | tf_op jit(solution)/shard_map/ppermute | solution.py:294
  118.5 4.7 %collective-permute-done.18.refs_1_ = bf16[256,256]{1,0:T(8,128)(2,1)S(1)} collective-permute-done((bf16[256,256]{1,0:T(8,128)(2,1)S(1)}, bf16[256,256]{1,0:T(8,128)(2,1)S(1)}, u32[]{:S(2)}, u32[]{:S(2)}) %collective-permute-start.18) | collective-permute-done | bytes 131104 | tf_op jit(solution)/shard_map/ppermute | solution.py:294
  123.1 1.5 collective-permute-done.19.refs_2_
  124.6 1.6 %collective-permute-done.20.refs_3_ = bf16[256,256]{1,0:T(8,128)(2,1)S(1)} collective-permute-done((bf16[256,256]{1,0:T(8,128)(2,1)S(1)}, bf16[256,256]{1,0:T(8,128)(2,1)S(1)}, u32[]{:S(2)}, u32[]{:S(2)}) %collective-permute-start.20) | collective-permute-done | bytes 131104 | tf_op jit(solution)/shard_map/ppermute | solution.py:294
  127.6 1.8 %pack.2 = bf16[16,1,128,256]{3,2,1,0:T(8,128)(2,1)} custom-call(s32[2,4]{1,0:T(2,128)S(1)} %copy-done.4, bf16[256,256]{1,0:T(8,128)(2,1)S(1)} %get-tuple-element.40.refs_0_, bf16[256,256]{1,0:T(8,128)(2,1)S(1)} %collective-permute-done.18.refs_1_, bf16[256,256]{1,0:T(8,128)(2,1)S(1)} %collective-permute-done.19.refs_2_, ...), custom_call_target="tpu_custom_call" | custom-call | tf_op jit(solution)/shard_map/pack/pallas_call | solution.py:260
  129.4 4.3 %all-to-all-start = ((bf16[16,1,128,256]{3,2,1,0:T(8,128)(2,1)}), bf16[16,1,128,256]{3,2,1,0:T(8,128)(2,1)S(1)}, u32[]{:S(2)}, u32[]{:S(2)}) async-start(bf16[16,1,128,256]{3,2,1,0:T(8,128)(2,1)} %pack.2), calls=%async_computation | async-start | bytes 2097152 | tf_op jit(solution)/shard_map/all_to_all | solution.py:328
  134.7 17.2 %all-to-all-done.value_ref = bf16[16,1,128,256]{3,2,1,0:T(8,128)(2,1)S(1)} async-done(((bf16[16,1,128,256]{3,2,1,0:T(8,128)(2,1)}), bf16[16,1,128,256]{3,2,1,0:T(8,128)(2,1)S(1)}, u32[]{:S(2)}, u32[]{:S(2)}) %all-to-all-start) | async-done | bytes 1048608 | tf_op jit(solution)/shard_map/all_to_all | solution.py:328
  (83 shorter events, 17.1 us)
Async XLA Ops:
  2.9 14.7 %collective-permute-start.1 = (bf16[256,1024]{1,0:T(8,128)(2,1)}, bf16[256,1024]{1,0:T(8,128)(2,1)S(1)}, u32[]{:S(2)}, u32[]{:S(2)}) collective-permute-start(bf16[256,1024]{1,0:T(8,128)(2,1)} %get-tuple-element.31.refs_2_), channel_id=1, source_target_pairs={{0,24},{8,0},{16,8},{24,16},{32,56},{40,32},{48,40},{56,48},{64,88... | collective-permute-start | bytes 1572872 | tf_op jit(solution)/shard_map/ppermute | solution.py:294
  6.1 11.5 %collective-permute-start.7 = (bf16[256,1024]{1,0:T(8,128)(2,1)}, bf16[256,1024]{1,0:T(8,128)(2,1)S(1)}, u32[]{:S(2)}, u32[]{:S(2)}) collective-permute-start(bf16[256,1024]{1,0:T(8,128)(2,1)} %get-tuple-element.34), channel_id=1, source_target_pairs={{0,1},{1,0},{2,3},{3,2},{4,5},{5,4},{6,7},{7,6},{8,9},{9,8},{10,11... | collective-permute-start | bytes 1572872 | tf_op jit(solution)/shard_map/ppermute | solution.py:306
  6.1 15.1 %collective-permute-start.8 = (bf16[256,1024]{1,0:T(8,128)(2,1)}, bf16[256,1024]{1,0:T(8,128)(2,1)S(1)}, u32[]{:S(2)}, u32[]{:S(2)}) collective-permute-start(bf16[256,1024]{1,0:T(8,128)(2,1)} %get-tuple-element.29.refs_0_), channel_id=1, source_target_pairs={{0,96},{8,104},{16,112},{24,120},{32,0},{40,8},{48,16},{56,24},{64... | collective-permute-start | bytes 1572872 | tf_op jit(solution)/shard_map/ppermute | solution.py:298
  8.8 15.8 %collective-permute-start.10 = (bf16[256,1024]{1,0:T(8,128)(2,1)}, bf16[256,1024]{1,0:T(8,128)(2,1)S(1)}, u32[]{:S(2)}, u32[]{:S(2)}) collective-permute-start(bf16[256,1024]{1,0:T(8,128)(2,1)} %get-tuple-element.29.refs_0_), channel_id=1, source_target_pairs={{0,32},{8,40},{16,48},{24,56},{32,64},{40,72},{48,80},{56,88},{64,... | collective-permute-start | bytes 1572872 | tf_op jit(solution)/shard_map/ppermute | solution.py:298
  8.8 15.8 %collective-permute-start.28 = (bf16[256,1024]{1,0:T(8,128)(2,1)}, bf16[256,1024]{1,0:T(8,128)(2,1)S(1)}, u32[]{:S(2)}, u32[]{:S(2)}) collective-permute-start(bf16[256,1024]{1,0:T(8,128)(2,1)} %get-tuple-element.30.refs_1_), channel_id=1, source_target_pairs={{0,8},{8,16},{16,24},{24,0},{32,40},{40,48},{48,56},{56,32},{64,72... | collective-permute-start | bytes 1572872 | tf_op jit(solution)/shard_map/ppermute | solution.py:294
  17.6 15.8 %collective-permute-start.26 = (bf16[256,1024]{1,0:T(8,128)(2,1)}, bf16[256,1024]{1,0:T(8,128)(2,1)S(1)}, u32[]{:S(2)}, u32[]{:S(2)}) collective-permute-start(bf16[256,1024]{1,0:T(8,128)(2,1)} %get-tuple-element.30.refs_1_), channel_id=1, source_target_pairs={{0,24},{8,0},{16,8},{24,16},{32,56},{40,32},{48,40},{56,48},{64,88... | collective-permute-start | bytes 1572872 | tf_op jit(solution)/shard_map/ppermute | solution.py:294
  21.2 14.4 %collective-permute-start.9 = (bf16[256,1024]{1,0:T(8,128)(2,1)S(1)}, bf16[256,1024]{1,0:T(8,128)(2,1)S(1)}, u32[]{:S(2)}, u32[]{:S(2)}) collective-permute-start(bf16[256,1024]{1,0:T(8,128)(2,1)S(1)} %collective-permute-done.7.refs_9_), channel_id=1, source_target_pairs={{0,96},{8,104},{16,112},{24,120},{32,0},{40,8},{48,16},{56,24},{64... | collective-permute-start | bytes 1572872 | tf_op jit(solution)/shard_map/ppermute | solution.py:298
  24.6 16.0 %collective-permute-start.11 = (bf16[256,1024]{1,0:T(8,128)(2,1)S(1)}, bf16[256,1024]{1,0:T(8,128)(2,1)S(1)}, u32[]{:S(2)}, u32[]{:S(2)}) collective-permute-start(bf16[256,1024]{1,0:T(8,128)(2,1)S(1)} %collective-permute-done.10.refs_14_), channel_id=1, source_target_pairs={{0,32},{8,40},{16,48},{24,56},{32,64},{40,72},{48,80},{56,88},{64,... | collective-permute-start | bytes 1572872 | tf_op jit(solution)/shard_map/ppermute | solution.py:298
  24.6 16.0 %collective-permute-start.29 = (bf16[256,1024]{1,0:T(8,128)(2,1)S(1)}, bf16[256,1024]{1,0:T(8,128)(2,1)S(1)}, u32[]{:S(2)}, u32[]{:S(2)}) collective-permute-start(bf16[256,1024]{1,0:T(8,128)(2,1)S(1)} %collective-permute-done.28.refs_6_), channel_id=1, source_target_pairs={{0,8},{8,16},{16,24},{24,0},{32,40},{40,48},{48,56},{56,32},{64,72... | collective-permute-start | bytes 1572872 | tf_op jit(solution)/shard_map/ppermute | solution.py:294
  24.7 25.5 %collective-permute-start.13 = (bf16[256,1024]{1,0:T(8,128)(2,1)S(1)}, bf16[256,1024]{1,0:T(8,128)(2,1)S(1)}, u32[]{:S(2)}, u32[]{:S(2)}) collective-permute-start(bf16[256,1024]{1,0:T(8,128)(2,1)S(1)} %collective-permute-done.7.refs_9_), channel_id=1, source_target_pairs={{0,32},{8,40},{16,48},{24,56},{32,64},{40,72},{48,80},{56,88},{64,... | collective-permute-start | bytes 1572872 | tf_op jit(solution)/shard_map/ppermute | solution.py:298
  33.3 20.1 %collective-permute-start.31 = (bf16[256,1024]{1,0:T(8,128)(2,1)S(1)}, bf16[256,1024]{1,0:T(8,128)(2,1)S(1)}, u32[]{:S(2)}, u32[]{:S(2)}) collective-permute-start(bf16[256,1024]{1,0:T(8,128)(2,1)S(1)} %collective-permute-done.28.refs_6_), channel_id=1, source_target_pairs={{0,1},{1,0},{2,3},{3,2},{4,5},{5,4},{6,7},{7,6},{8,9},{9,8},{10,11... | collective-permute-start | bytes 1572872 | tf_op jit(solution)/shard_map/ppermute | solution.py:306
  35.6 14.7 %collective-permute-start.27 = (bf16[256,1024]{1,0:T(8,128)(2,1)S(1)}, bf16[256,1024]{1,0:T(8,128)(2,1)S(1)}, u32[]{:S(2)}, u32[]{:S(2)}) collective-permute-start(bf16[256,1024]{1,0:T(8,128)(2,1)S(1)} %collective-permute-done.26.refs_2_), channel_id=1, source_target_pairs={{0,1},{1,0},{2,3},{3,2},{4,5},{5,4},{6,7},{7,6},{8,9},{9,8},{10,11... | collective-permute-start | bytes 1572872 | tf_op jit(solution)/shard_map/ppermute | solution.py:306
  40.6 12.9 %collective-permute-start.12 = (bf16[256,1024]{1,0:T(8,128)(2,1)S(1)}, bf16[256,1024]{1,0:T(8,128)(2,1)S(1)}, u32[]{:S(2)}, u32[]{:S(2)}) collective-permute-start(bf16[256,1024]{1,0:T(8,128)(2,1)S(1)} %collective-permute-done.9.refs_11_), channel_id=1, source_target_pairs={{0,96},{8,104},{16,112},{24,120},{32,0},{40,8},{48,16},{56,24},{64... | collective-permute-start | bytes 1572872 | tf_op jit(solution)/shard_map/ppermute | solution.py:298
  40.6 12.9 %collective-permute-start.30 = (bf16[256,1024]{1,0:T(8,128)(2,1)S(1)}, bf16[256,1024]{1,0:T(8,128)(2,1)S(1)}, u32[]{:S(2)}, u32[]{:S(2)}) collective-permute-start(bf16[256,1024]{1,0:T(8,128)(2,1)S(1)} %collective-permute-done.29.refs_4_), channel_id=1, source_target_pairs={{0,1},{1,0},{2,3},{3,2},{4,5},{5,4},{6,7},{7,6},{8,9},{9,8},{10,11... | collective-permute-start | bytes 1572872 | tf_op jit(solution)/shard_map/ppermute | solution.py:306
  50.2 13.6 %collective-permute-start.5 = (bf16[256,1024]{1,0:T(8,128)(2,1)S(1)}, bf16[256,1024]{1,0:T(8,128)(2,1)S(1)}, u32[]{:S(2)}, u32[]{:S(2)}) collective-permute-start(bf16[256,1024]{1,0:T(8,128)(2,1)S(1)} %copy-done), channel_id=1, source_target_pairs={{0,8},{8,16},{16,24},{24,0},{32,40},{40,48},{48,56},{56,32},{64,72... | collective-permute-start | bytes 1572872 | tf_op jit(solution)/shard_map/ppermute | solution.py:294
  50.2 13.6 %collective-permute-start.3 = (bf16[256,1024]{1,0:T(8,128)(2,1)S(1)}, bf16[256,1024]{1,0:T(8,128)(2,1)S(1)}, u32[]{:S(2)}, u32[]{:S(2)}) collective-permute-start(bf16[256,1024]{1,0:T(8,128)(2,1)S(1)} %collective-permute-done.1.refs_2_), channel_id=1, source_target_pairs={{0,24},{8,0},{16,8},{24,16},{32,56},{40,32},{48,40},{56,48},{64,88... | collective-permute-start | bytes 1572872 | tf_op jit(solution)/shard_map/ppermute | solution.py:294
  57.9 14.2 %collective-permute-start.32 = (bf16[4,256,256]{2,1,0:T(8,128)(2,1)S(1)}, bf16[4,256,256]{2,1,0:T(8,128)(2,1)S(1)}, u32[]{:S(2)}, u32[]{:S(2)}) collective-permute-start(bf16[4,256,256]{2,1,0:T(8,128)(2,1)S(1)} %get-tuple-element.45), channel_id=1, source_target_pairs={{0,2},{1,3},{2,4},{3,5},{4,6},{5,7},{6,0},{7,1},{8,10},{9,11},{10,... | collective-permute-start | bytes 1572872 | tf_op jit(solution)/shard_map/ppermute | solution.py:302
  59.8 12.2 %collective-permute-start.33 = (bf16[4,256,256]{2,1,0:T(8,128)(2,1)S(1)}, bf16[4,256,256]{2,1,0:T(8,128)(2,1)S(1)}, u32[]{:S(2)}, u32[]{:S(2)}) collective-permute-start(bf16[4,256,256]{2,1,0:T(8,128)(2,1)S(1)} %get-tuple-element.46), channel_id=1, source_target_pairs={{0,6},{1,7},{2,0},{3,1},{4,2},{5,3},{6,4},{7,5},{8,14},{9,15},{10,... | collective-permute-start | bytes 1572872 | tf_op jit(solution)/shard_map/ppermute | solution.py:302
  62.0 11.3 %collective-permute-start = (bf16[256,1024]{1,0:T(8,128)(2,1)S(1)}, bf16[256,1024]{1,0:T(8,128)(2,1)S(1)}, u32[]{:S(2)}, u32[]{:S(2)}) collective-permute-start(bf16[256,1024]{1,0:T(8,128)(2,1)S(1)} %copy-done), channel_id=1, source_target_pairs={{0,1},{1,0},{2,3},{3,2},{4,5},{5,4},{6,7},{7,6},{8,9},{9,8},{10,11... | collective-permute-start | bytes 1572872 | tf_op jit(solution)/shard_map/ppermute | solution.py:306
  63.8 11.9 %collective-permute-start.2 = (bf16[256,1024]{1,0:T(8,128)(2,1)S(1)}, bf16[256,1024]{1,0:T(8,128)(2,1)S(1)}, u32[]{:S(2)}, u32[]{:S(2)}) collective-permute-start(bf16[256,1024]{1,0:T(8,128)(2,1)S(1)} %collective-permute-done.1.refs_2_), channel_id=1, source_target_pairs={{0,1},{1,0},{2,3},{3,2},{4,5},{5,4},{6,7},{7,6},{8,9},{9,8},{10,11... | collective-permute-start | bytes 1572872 | tf_op jit(solution)/shard_map/ppermute | solution.py:306
  63.8 11.9 %collective-permute-start.6 = (bf16[256,1024]{1,0:T(8,128)(2,1)S(1)}, bf16[256,1024]{1,0:T(8,128)(2,1)S(1)}, u32[]{:S(2)}, u32[]{:S(2)}) collective-permute-start(bf16[256,1024]{1,0:T(8,128)(2,1)S(1)} %collective-permute-done.5.refs_6_), channel_id=1, source_target_pairs={{0,1},{1,0},{2,3},{3,2},{4,5},{5,4},{6,7},{7,6},{8,9},{9,8},{10,11... | collective-permute-start | bytes 1572872 | tf_op jit(solution)/shard_map/ppermute | solution.py:306
  72.1 11.2 %collective-permute-start.34 = (bf16[2,256,256]{2,1,0:T(8,128)(2,1)S(1)}, bf16[2,256,256]{2,1,0:T(8,128)(2,1)S(1)}, u32[]{:S(2)}, u32[]{:S(2)}) collective-permute-start(bf16[2,256,256]{2,1,0:T(8,128)(2,1)S(1)} %add_convert_fusion.1), channel_id=1, source_target_pairs={{0,2},{1,3},{2,4},{3,5},{4,6},{5,7},{6,0},{7,1},{8,10},{9,11},{10,... | collective-permute-start | bytes 786440 | tf_op jit(solution)/shard_map/ppermute | solution.py:302
  73.3 9.9 %collective-permute-start.35 = (bf16[2,256,256]{2,1,0:T(8,128)(2,1)S(1)}, bf16[2,256,256]{2,1,0:T(8,128)(2,1)S(1)}, u32[]{:S(2)}, u32[]{:S(2)}) collective-permute-start(bf16[2,256,256]{2,1,0:T(8,128)(2,1)S(1)} %add_convert_fusion), channel_id=1, source_target_pairs={{0,6},{1,7},{2,0},{3,1},{4,2},{5,3},{6,4},{7,5},{8,14},{9,15},{10,... | collective-permute-start | bytes 786440 | tf_op jit(solution)/shard_map/ppermute | solution.py:302
  81.2 21.7 %collective-permute-start.14 = (bf16[4,256,256]{2,1,0:T(8,128)(2,1)}, bf16[4,256,256]{2,1,0:T(8,128)(2,1)S(1)}, u32[]{:S(2)}, u32[]{:S(2)}) collective-permute-start(bf16[4,256,256]{2,1,0:T(8,128)(2,1)} %get-tuple-element.36), channel_id=1, source_target_pairs={{0,2},{1,3},{2,4},{3,5},{4,6},{5,7},{6,0},{7,1},{8,10},{9,11},{10,... | collective-permute-start | bytes 1572872 | tf_op jit(solution)/shard_map/ppermute | solution.py:302
  83.8 20.3 %collective-permute-start.15 = (bf16[4,256,256]{2,1,0:T(8,128)(2,1)}, bf16[4,256,256]{2,1,0:T(8,128)(2,1)S(1)}, u32[]{:S(2)}, u32[]{:S(2)}) collective-permute-start(bf16[4,256,256]{2,1,0:T(8,128)(2,1)} %get-tuple-element.37), channel_id=1, source_target_pairs={{0,6},{1,7},{2,0},{3,1},{4,2},{5,3},{6,4},{7,5},{8,14},{9,15},{10,... | collective-permute-start | bytes 1572872 | tf_op jit(solution)/shard_map/ppermute | solution.py:302
  87.8 8.0 %collective-permute-start.38 = (bf16[256,256]{1,0:T(8,128)(2,1)S(1)}, bf16[256,256]{1,0:T(8,128)(2,1)S(1)}, u32[]{:S(2)}, u32[]{:S(2)}) collective-permute-start(bf16[256,256]{1,0:T(8,128)(2,1)S(1)} %get-tuple-element.52), channel_id=1, source_target_pairs={{0,8},{8,16},{16,24},{24,0},{32,40},{40,48},{48,56},{56,32},{64,72... | collective-permute-start | bytes 393224 | tf_op jit(solution)/shard_map/ppermute | solution.py:294
  99.2 30.2 %all-to-all-start.1 = ((bf16[16,1,128,256]{3,2,1,0:T(8,128)(2,1)}), bf16[16,1,128,256]{3,2,1,0:T(8,128)(2,1)S(1)}, u32[]{:S(2)}, u32[]{:S(2)}) async-start(bf16[16,1,128,256]{3,2,1,0:T(8,128)(2,1)} %pack.3), calls=%async_computation.1 | async-start | bytes 2097152 | tf_op jit(solution)/shard_map/all_to_all | solution.py:328
  104.0 9.8 %collective-permute-start.16 = (bf16[2,256,256]{2,1,0:T(8,128)(2,1)S(1)}, bf16[2,256,256]{2,1,0:T(8,128)(2,1)S(1)}, u32[]{:S(2)}, u32[]{:S(2)}) collective-permute-start(bf16[2,256,256]{2,1,0:T(8,128)(2,1)S(1)} %add_convert_fusion.3), channel_id=1, source_target_pairs={{0,2},{1,3},{2,4},{3,5},{4,6},{5,7},{6,0},{7,1},{8,10},{9,11},{10,... | collective-permute-start | bytes 786440 | tf_op jit(solution)/shard_map/ppermute | solution.py:302
  104.1 9.6 %collective-permute-start.17 = (bf16[2,256,256]{2,1,0:T(8,128)(2,1)S(1)}, bf16[2,256,256]{2,1,0:T(8,128)(2,1)S(1)}, u32[]{:S(2)}, u32[]{:S(2)}) collective-permute-start(bf16[2,256,256]{2,1,0:T(8,128)(2,1)S(1)} %add_convert_fusion.2), channel_id=1, source_target_pairs={{0,6},{1,7},{2,0},{3,1},{4,2},{5,3},{6,4},{7,5},{8,14},{9,15},{10,... | collective-permute-start | bytes 786440 | tf_op jit(solution)/shard_map/ppermute | solution.py:302
  113.9 9.2 %collective-permute-start.18 = (bf16[256,256]{1,0:T(8,128)(2,1)S(1)}, bf16[256,256]{1,0:T(8,128)(2,1)S(1)}, u32[]{:S(2)}, u32[]{:S(2)}) collective-permute-start(bf16[256,256]{1,0:T(8,128)(2,1)S(1)} %get-tuple-element.41), channel_id=1, source_target_pairs={{0,24},{8,0},{16,8},{24,16},{32,56},{40,32},{48,40},{56,48},{64,88... | collective-permute-start | bytes 393224 | tf_op jit(solution)/shard_map/ppermute | solution.py:294
  117.6 8.6 %collective-permute-start.20 = (bf16[256,256]{1,0:T(8,128)(2,1)S(1)}, bf16[256,256]{1,0:T(8,128)(2,1)S(1)}, u32[]{:S(2)}, u32[]{:S(2)}) collective-permute-start(bf16[256,256]{1,0:T(8,128)(2,1)S(1)} %get-tuple-element.43), channel_id=1, source_target_pairs={{0,8},{8,16},{16,24},{24,0},{32,40},{40,48},{48,56},{56,32},{64,72... | collective-permute-start | bytes 393224 | tf_op jit(solution)/shard_map/ppermute | solution.py:294
  129.4 22.4 %all-to-all-start = ((bf16[16,1,128,256]{3,2,1,0:T(8,128)(2,1)}), bf16[16,1,128,256]{3,2,1,0:T(8,128)(2,1)S(1)}, u32[]{:S(2)}, u32[]{:S(2)}) async-start(bf16[16,1,128,256]{3,2,1,0:T(8,128)(2,1)} %pack.2), calls=%async_computation | async-start | bytes 2097152 | tf_op jit(solution)/shard_map/all_to_all | solution.py:328
  (18 other events, 76.6 us)

commit v5 on v4

--- a/solution.py
+++ b/solution.py
@@ -118,9 +118,8 @@
         ).astype(out.dtype)
 
 
-def product_body(*refs, keep):
+def product_body(*refs, first):
     rows, cols = refs[:8], refs[8:16]
-    up, down, next_low, prev_high = refs[16:20]
     rows_ref, cols_ref, row_sems, col_sems = refs[-4:]
     x, _, z, _ = position()
     copies = load(cols, lambda d, across: cols_ref.at[(x + d) % 4, :, across], col_sems)
@@ -129,22 +128,25 @@
         copy.start()
     for copy in copies:
         copy.wait()
+    next_low, prev_high, up, down = refs[16:20]
+    far_up, far_down, at = (refs[20], refs[21], 0) if first else (up, down, 2)
     blocks(rows_ref, cols_ref[(z + 2) % 4], ((up, 0), (up, 1), (down, 0), (down, 1)))
-    blocks(rows_ref, cols_ref[(z + 1) % 4], ((next_low, 0), (next_low, 1), (up, 2), (up, 3)))
-    blocks(rows_ref, cols_ref[(z + 3) % 4], ((down, 2), (down, 3), (prev_high, 0), (prev_high, 1)))
-    if keep:
+    blocks(rows_ref, cols_ref[(z + 1) % 4], ((next_low, 0), (next_low, 1), (far_up, at), (far_up, at + 1)))
+    blocks(rows_ref, cols_ref[(z + 3) % 4], ((far_down, at), (far_down, at + 1), (prev_high, 0), (prev_high, 1)))
+    if not first:
         blocks(rows_ref, cols_ref[z], tuple((refs[20], j) for j in range(4)))
 
 
-def product(rows, cols, keep):
+def product(rows, cols, first):
     four = jax.ShapeDtypeStruct((4, TILE, TILE), jnp.bfloat16)
     two = jax.ShapeDtypeStruct((2, TILE, TILE), jnp.bfloat16)
-    kept = (jax.ShapeDtypeStruct((4, TILE, TILE), jnp.float32),) * keep
-    return pl.pallas_call(
-        lambda *refs: product_body(*refs, keep=keep),
-        out_shape=(four, four, two, two, *kept),
+    kept = jax.ShapeDtypeStruct((4, TILE, TILE), jnp.float32)
+    shapes = (two,) * 6 if first else (two, two, four, four, kept)
+    return pl.pallas_call(
+        lambda *refs: product_body(*refs, first=first),
+        out_shape=shapes,
         in_specs=[pl.BlockSpec(memory_space=pl.ANY)] * 16,
-        out_specs=(pl.BlockSpec(memory_space=pltpu.VMEM),) * (4 + keep),
+        out_specs=(pl.BlockSpec(memory_space=pltpu.VMEM),) * len(shapes),
         scratch_shapes=[
             pltpu.VMEM((4, TILE, 2048), jnp.bfloat16),
             pltpu.VMEM((4, TILE, 2048), jnp.bfloat16),
@@ -192,13 +194,14 @@
     )(*rows, *cols)
 
 
-def finish_body(own, got_up, got_down, sum_up, sum_down, *outs):
+def finish_body(own, far_up, far_down, sum_up, sum_down, *outs):
+    at = far_up.shape[0] - 2
     for j in range(2):
         outs[j][...] = (
-            own[j] + got_down[2 + j].astype(jnp.float32) + sum_up[j].astype(jnp.float32)
+            own[j] + far_down[at + j].astype(jnp.float32) + sum_up[j].astype(jnp.float32)
         ).astype(jnp.bfloat16)
         outs[2 + j][...] = (
-            own[2 + j] + got_up[2 + j].astype(jnp.float32) + sum_down[j].astype(jnp.float32)
+            own[2 + j] + far_up[at + j].astype(jnp.float32) + sum_down[j].astype(jnp.float32)
         ).astype(jnp.bfloat16)
 
 
@@ -311,11 +314,14 @@
 
 
 def reduce_along_z(partials):
-    up, down, next_low, prev_high, own = partials
+    next_low, prev_high, up, down, *far, own = partials
     got_down, got_up = zpass(down, -1), zpass(up, 1)
+    far_down, far_up = got_down, got_up
+    if far:
+        far_down, far_up = zpass(far[1], -1), zpass(far[0], 1)
     sum_down = zpass(add(prev_high, got_down[:2]), -1)
     sum_up = zpass(add(next_low, got_up[:2]), 1)
-    return finish(own, got_up, got_down, sum_up, sum_down)
+    return finish(own, far_up, far_down, sum_up, sum_down)
 
 
 def to_owners(owners, sums):
@@ -341,15 +347,13 @@
     c0, top, low = stage(c0, top, low)
     cols = (c0, c1, cp0, cp1, co0, co1, cm0, cm1)
     halves = []
-    for own, pieces in (
-        (top, (sent_top, top_p, top_o, top_m)), (low, (sent_low, low_p, low_o, low_m))
-    ):
+    for own, pieces in ((top, (sent_top, top_p, top_o, top_m)), (low, (sent_low, low_p, low_o, low_m))):
         others = [swap(value) for value in pieces]
         rows = [piece for pair in zip((own, *pieces[1:]), others) for piece in pair]
         if halves:
-            halves.append(product(rows, cols, 1))
+            halves.append(product(rows, cols, False))
         else:
-            sent = product(rows, cols, 0)
+            sent = product(rows, cols, True)
             halves.append((*sent, kept_product(rows, cols)))
     first = to_owners(owner_rows, reduce_along_z(halves[0]))
     second = to_owners(owner_rows, reduce_along_z(halves[1]))

time: 153 us -> 159 us (1.039)
  starting transfers between devices: 46.4 us -> 51.6 us
    ppermute x8 -> x10, starting transfers between devices: 14.4 us -> 19.6 us  [zpass(): return lax.ppermute(value, 'col', along_z(step))]
    ppermute x6, waiting for transfers between devices: 13.6 us -> 16.9 us  [xpass(): return lax.ppermute(value, 'row', along_x(step))]
    ppermute x12, waiting for transfers between devices: 33.9 us -> 32.1 us  [ypass(): return lax.ppermute(value, 'row', along_y(step))]
    ppermute x8 -> x10, waiting for transfers between devices: 14 us -> 13.2 us  [zpass(): return lax.ppermute(value, 'col', along_z(step))]
  transfers between devices with their start and end apart: 45 -> 47, of which waited for: 18 -> 20; matrix products, arithmetic and copies ran while one was open for 1% -> 1% of each run, Pallas kernels for 11% -> 11%
where the time goes in v5:
time: 159 us
  waiting for transfers between devices  81.7 us (51%)
  starting transfers between devices  51.6 us (32%)
  Pallas kernels  20.9 us (13%)
  local copies, waits for them, and re-layouts  3.13 us (2%)
    ppermute x12, waiting for transfers between devices, ypass(): return lax.ppermute(value, 'row', along_y(step))  32.1 us
    ppermute x10, starting transfers between devices, zpass(): return lax.ppermute(value, 'col', along_z(step))  19.6 us
    all_to_all x2, waiting for transfers between devices, to_owners(): lax.all_to_all(outgoing, 'row', split_axis=0, concat_axis=0, tiled=True)  17.1 us
    ppermute x6, waiting for transfers between devices, xpass(): return lax.ppermute(value, 'row', along_x(step))  16.9 us
    ppermute x12, starting transfers between devices, ypass(): return lax.ppermute(value, 'row', along_y(step))  16.6 us
    ppermute x10, waiting for transfers between devices, zpass(): return lax.ppermute(value, 'col', along_z(step))  13.2 us
    pallas_call x2, Pallas kernels, product(): pl.pallas_call(lambda *refs: product_body(*refs, first=first), out_shape=...  10 us
    all_to_all x2, starting transfers between devices, to_owners(): lax.all_to_all(outgoing, 'row', split_axis=0, concat_axis=0, tiled=True)  8.01 us
  transfers between devices with their start and end apart: 47, of which 20 were waited for; matrix products, arithmetic and copies ran while one was open for 1% of the time, Pallas kernels for 11%

profile of v5, /device:TPU:0, one launch (start us, length us, event | category | flops | bytes accessed | tf_op | source)
XLA Modules:
  0.0 159.0 jit_solution(17760093602389196056)
XLA Ops:
  0.0 2.9 %scale.1 = (bf16[256,1024]{1,0:T(8,128)(2,1)}, bf16[256,1024]{1,0:T(8,128)(2,1)}, bf16[256,1024]{1,0:T(8,128)(2,1)}, bf16[256,1024]{1,0:T(8,128)(2,1)}) custom-call(s32[2,32]{1,0:T(2,128)} %mask_hbm.1, bf16[512,1024]{1,0:T(8,128)(2,1)} %panels_hbm.1, f32[1,1024]{1,0:T(1,128)} %bitcast.1), custom_call_target="tpu_custom_call" | custom-call | tf_op jit(solution)/shard_map/scale/pallas_call | solution.py:69
  2.9 3.2 %collective-permute-start.1 = (bf16[256,1024]{1,0:T(8,128)(2,1)}, bf16[256,1024]{1,0:T(8,128)(2,1)S(1)}, u32[]{:S(2)}, u32[]{:S(2)}) collective-permute-start(bf16[256,1024]{1,0:T(8,128)(2,1)} %get-tuple-element.33.refs_2_), channel_id=1, source_target_pairs={{0,24},{8,0},{16,8},{24,16},{32,56},{40,32},{48,40},{56,48},{64,88... | collective-permute-start | bytes 1572872 | tf_op jit(solution)/shard_map/ppermute | solution.py:297
  6.1 2.8 %collective-permute-start.8 = (bf16[256,1024]{1,0:T(8,128)(2,1)}, bf16[256,1024]{1,0:T(8,128)(2,1)S(1)}, u32[]{:S(2)}, u32[]{:S(2)}) collective-permute-start(bf16[256,1024]{1,0:T(8,128)(2,1)} %get-tuple-element.31.refs_0_), channel_id=1, source_target_pairs={{0,96},{8,104},{16,112},{24,120},{32,0},{40,8},{48,16},{56,24},{64... | collective-permute-start | bytes 1572872 | tf_op jit(solution)/shard_map/ppermute | solution.py:301
  8.8 8.7 %collective-permute-done.1.refs_2_ = bf16[256,1024]{1,0:T(8,128)(2,1)S(1)} collective-permute-done((bf16[256,1024]{1,0:T(8,128)(2,1)}, bf16[256,1024]{1,0:T(8,128)(2,1)S(1)}, u32[]{:S(2)}, u32[]{:S(2)}) %collective-permute-start.1) | collective-permute-done | bytes 524320 | tf_op jit(solution)/shard_map/ppermute | solution.py:297
  17.6 3.6 %collective-permute-start.26 = (bf16[256,1024]{1,0:T(8,128)(2,1)}, bf16[256,1024]{1,0:T(8,128)(2,1)S(1)}, u32[]{:S(2)}, u32[]{:S(2)}) collective-permute-start(bf16[256,1024]{1,0:T(8,128)(2,1)} %get-tuple-element.32.refs_1_), channel_id=1, source_target_pairs={{0,24},{8,0},{16,8},{24,16},{32,56},{40,32},{48,40},{56,48},{64,88... | collective-permute-start | bytes 1572872 | tf_op jit(solution)/shard_map/ppermute | solution.py:297
  21.2 3.4 %collective-permute-start.9 = (bf16[256,1024]{1,0:T(8,128)(2,1)S(1)}, bf16[256,1024]{1,0:T(8,128)(2,1)S(1)}, u32[]{:S(2)}, u32[]{:S(2)}) collective-permute-start(bf16[256,1024]{1,0:T(8,128)(2,1)S(1)} %collective-permute-done.7.refs_9_), channel_id=1, source_target_pairs={{0,96},{8,104},{16,112},{24,120},{32,0},{40,8},{48,16},{56,24},{64... | collective-permute-start | bytes 1572872 | tf_op jit(solution)/shard_map/ppermute | solution.py:301
  24.8 8.5 %collective-permute-done.26.refs_2_ = bf16[256,1024]{1,0:T(8,128)(2,1)S(1)} collective-permute-done((bf16[256,1024]{1,0:T(8,128)(2,1)}, bf16[256,1024]{1,0:T(8,128)(2,1)S(1)}, u32[]{:S(2)}, u32[]{:S(2)}) %collective-permute-start.26) | collective-permute-done | bytes 524320 | tf_op jit(solution)/shard_map/ppermute | solution.py:297
  33.3 2.2 %collective-permute-done.9.refs_11_ = bf16[256,1024]{1,0:T(8,128)(2,1)S(1)} collective-permute-done((bf16[256,1024]{1,0:T(8,128)(2,1)S(1)}, bf16[256,1024]{1,0:T(8,128)(2,1)S(1)}, u32[]{:S(2)}, u32[]{:S(2)}) %collective-permute-start.9) | collective-permute-done | bytes 524320 | tf_op jit(solution)/shard_map/ppermute | solution.py:301
  35.6 5.0 %collective-permute-done.11.refs_12_ = bf16[256,1024]{1,0:T(8,128)(2,1)S(1)} collective-permute-done((bf16[256,1024]{1,0:T(8,128)(2,1)S(1)}, bf16[256,1024]{1,0:T(8,128)(2,1)S(1)}, u32[]{:S(2)}, u32[]{:S(2)}) %collective-permute-start.11) | collective-permute-done | bytes 524320 | tf_op jit(solution)/shard_map/ppermute | solution.py:301
  40.6 9.6 %collective-permute-done.13.refs_15_ = bf16[256,1024]{1,0:T(8,128)(2,1)S(1)} collective-permute-done((bf16[256,1024]{1,0:T(8,128)(2,1)S(1)}, bf16[256,1024]{1,0:T(8,128)(2,1)S(1)}, u32[]{:S(2)}, u32[]{:S(2)}) %collective-permute-start.13) | collective-permute-done | bytes 524320 | tf_op jit(solution)/shard_map/ppermute | solution.py:301
  50.2 3.2 %collective-permute-start.3 = (bf16[256,1024]{1,0:T(8,128)(2,1)S(1)}, bf16[256,1024]{1,0:T(8,128)(2,1)S(1)}, u32[]{:S(2)}, u32[]{:S(2)}) collective-permute-start(bf16[256,1024]{1,0:T(8,128)(2,1)S(1)} %collective-permute-done.1.refs_2_), channel_id=1, source_target_pairs={{0,24},{8,0},{16,8},{24,16},{32,56},{40,32},{48,40},{56,48},{64,88... | collective-permute-start | bytes 1572872 | tf_op jit(solution)/shard_map/ppermute | solution.py:297
  56.8 4.4 %product.3 = (bf16[2,256,256]{2,1,0:T(8,128)(2,1)S(1)}, bf16[2,256,256]{2,1,0:T(8,128)(2,1)S(1)}, bf16[2,256,256]{2,1,0:T(8,128)(2,1)S(1)}, bf16[2,256,256]{2,1,...) custom-call(bf16[256,1024]{1,0:T(8,128)(2,1)S(1)} %get-tuple-element.46.refs_0_, ...), custom_call_target="tpu_custom_call" | custom-call | tf_op jit(solution)/shard_map/product/pallas_call | solution.py:145
  61.1 2.0 %collective-permute-start.34 = (bf16[2,256,256]{2,1,0:T(8,128)(2,1)S(1)}, bf16[2,256,256]{2,1,0:T(8,128)(2,1)S(1)}, u32[]{:S(2)}, u32[]{:S(2)}) collective-permute-start(bf16[2,256,256]{2,1,0:T(8,128)(2,1)S(1)} %get-tuple-element.50), channel_id=1, source_target_pairs={{0,2},{1,3},{2,4},{3,5},{4,6},{5,7},{6,0},{7,1},{8,10},{9,11},{10,... | collective-permute-start | bytes 786440 | tf_op jit(solution)/shard_map/ppermute | solution.py:305
  64.0 4.0 %collective-permute-start.36 = (bf16[2,256,256]{2,1,0:T(8,128)(2,1)S(1)}, bf16[2,256,256]{2,1,0:T(8,128)(2,1)S(1)}, u32[]{:S(2)}, u32[]{:S(2)}) collective-permute-start(bf16[2,256,256]{2,1,0:T(8,128)(2,1)S(1)} %get-tuple-element.52), channel_id=1, source_target_pairs={{0,6},{1,7},{2,0},{3,1},{4,2},{5,3},{6,4},{7,5},{8,14},{9,15},{10,... | collective-permute-start | bytes 786440 | tf_op jit(solution)/shard_map/ppermute | solution.py:305
  68.0 1.6 %collective-permute-done.34 = bf16[2,256,256]{2,1,0:T(8,128)(2,1)S(1)} collective-permute-done((bf16[2,256,256]{2,1,0:T(8,128)(2,1)S(1)}, bf16[2,256,256]{2,1,0:T(8,128)(2,1)S(1)}, u32[]{:S(2)}, u32[]{:S(2)}) %collective-permute-start.34) | collective-permute-done | bytes 262176 | tf_op jit(solution)/shard_map/ppermute | solution.py:305
  69.7 4.5 %collective-permute-done.36 = bf16[2,256,256]{2,1,0:T(8,128)(2,1)S(1)} collective-permute-done((bf16[2,256,256]{2,1,0:T(8,128)(2,1)S(1)}, bf16[2,256,256]{2,1,0:T(8,128)(2,1)S(1)}, u32[]{:S(2)}, u32[]{:S(2)}) %collective-permute-start.36) | collective-permute-done | bytes 262176 | tf_op jit(solution)/shard_map/ppermute | solution.py:305
  74.9 3.2 %collective-permute-start.33 = (bf16[2,256,256]{2,1,0:T(8,128)(2,1)S(1)}, bf16[2,256,256]{2,1,0:T(8,128)(2,1)S(1)}, u32[]{:S(2)}, u32[]{:S(2)}) collective-permute-start(bf16[2,256,256]{2,1,0:T(8,128)(2,1)S(1)} %get-tuple-element.48), channel_id=1, source_target_pairs={{0,6},{1,7},{2,0},{3,1},{4,2},{5,3},{6,4},{7,5},{8,14},{9,15},{10,... | collective-permute-start | bytes 786440 | tf_op jit(solution)/shard_map/ppermute | solution.py:305
  78.1 3.2 %collective-permute-start.37 = (bf16[2,256,256]{2,1,0:T(8,128)(2,1)S(1)}, bf16[2,256,256]{2,1,0:T(8,128)(2,1)S(1)}, u32[]{:S(2)}, u32[]{:S(2)}) collective-permute-start(bf16[2,256,256]{2,1,0:T(8,128)(2,1)S(1)} %add_convert_fusion), channel_id=1, source_target_pairs={{0,6},{1,7},{2,0},{3,1},{4,2},{5,3},{6,4},{7,5},{8,14},{9,15},{10,... | collective-permute-start | bytes 786440 | tf_op jit(solution)/shard_map/ppermute | solution.py:305
  81.4 5.7 %product.2 = (bf16[2,256,256]{2,1,0:T(8,128)(2,1)S(1)}, bf16[2,256,256]{2,1,0:T(8,128)(2,1)S(1)}, bf16[4,256,256]{2,1,0:T(8,128)(2,1)}, bf16[4,256,256]{2,1,0:T(8,128)(2,1)}, f32[4,256,256]{2,1,0:T(8,128)S(1)}) custom-call(bf16[256,1024]{1,0:T(8,128)(2,1)S(1)} %get-tuple-element.34.refs_0_, bf16[256,1024]{1,0:T(8,128)(2,1)S(1)} %collective-permute-done.refs_1_, ...), custom_call_target="tpu_custom_call" | custom-call | tf_op jit(solution)/shard_map/product/pallas_call | solution.py:145
  87.1 1.9 %kept.1.own = f32[4,256,256]{2,1,0:T(8,128)S(1)} custom-call(bf16[256,1024]{1,0:T(8,128)(2,1)S(1)} %get-tuple-element.46.refs_0_, bf16[256,1024]{1,0:T(8,128)(2,1)S(1)} %collective-permute-done.25.refs_1_, bf16[256,1024]{1,0:T(8,128)(2,1)S(1)} %collective-permute-done.26.refs_2_, bf16[256,1024]{1,0:T(8,128)(2,1)S(1)} %collective-permute-done.27.refs_3_, ...), custom_call_target="tpu_custom_call" | custom-call | tf_op jit(solution)/shard_map/kept/pallas_call | solution.py:181
  90.0 3.2 %collective-permute-start.15 = (bf16[4,256,256]{2,1,0:T(8,128)(2,1)}, bf16[4,256,256]{2,1,0:T(8,128)(2,1)S(1)}, u32[]{:S(2)}, u32[]{:S(2)}) collective-permute-start(bf16[4,256,256]{2,1,0:T(8,128)(2,1)} %get-tuple-element.39), channel_id=1, source_target_pairs={{0,6},{1,7},{2,0},{3,1},{4,2},{5,3},{6,4},{7,5},{8,14},{9,15},{10,... | collective-permute-start | bytes 1572872 | tf_op jit(solution)/shard_map/ppermute | solution.py:305
  95.7 4.9 %collective-permute-done.39.refs_2_ = bf16[256,256]{1,0:T(8,128)(2,1)S(1)} collective-permute-done((bf16[256,256]{1,0:T(8,128)(2,1)S(1)}, bf16[256,256]{1,0:T(8,128)(2,1)S(1)}, u32[]{:S(2)}, u32[]{:S(2)}) %collective-permute-start.39) | collective-permute-done | bytes 131104 | tf_op jit(solution)/shard_map/ppermute | solution.py:297
  103.1 1.8 %pack.3 = bf16[16,1,128,256]{3,2,1,0:T(8,128)(2,1)} custom-call(s32[2,4]{1,0:T(2,128)S(1)} %copy-done.4, bf16[256,256]{1,0:T(8,128)(2,1)S(1)} %get-tuple-element.53.refs_0_, bf16[256,256]{1,0:T(8,128)(2,1)S(1)} %collective-permute-done.38.refs_1_, bf16[256,256]{1,0:T(8,128)(2,1)S(1)} %collective-permute-done.39.refs_2_, ...), custom_call_target="tpu_custom_call" | custom-call | tf_op jit(solution)/shard_map/pack/pallas_call | solution.py:263
  104.9 3.7 %all-to-all-start.1 = ((bf16[16,1,128,256]{3,2,1,0:T(8,128)(2,1)}), bf16[16,1,128,256]{3,2,1,0:T(8,128)(2,1)S(1)}, u32[]{:S(2)}, u32[]{:S(2)}) async-start(bf16[16,1,128,256]{3,2,1,0:T(8,128)(2,1)} %pack.3), calls=%async_computation.1 | async-start | bytes 2097152 | tf_op jit(solution)/shard_map/all_to_all | solution.py:334
  109.8 3.3 %collective-permute-start.17 = (bf16[2,256,256]{2,1,0:T(8,128)(2,1)S(1)}, bf16[2,256,256]{2,1,0:T(8,128)(2,1)S(1)}, u32[]{:S(2)}, u32[]{:S(2)}) collective-permute-start(bf16[2,256,256]{2,1,0:T(8,128)(2,1)S(1)} %add_convert_fusion.2), channel_id=1, source_target_pairs={{0,6},{1,7},{2,0},{3,1},{4,2},{5,3},{6,4},{7,5},{8,14},{9,15},{10,... | collective-permute-start | bytes 786440 | tf_op jit(solution)/shard_map/ppermute | solution.py:305
  113.0 6.4 %collective-permute-done.16.sum_up = bf16[2,256,256]{2,1,0:T(8,128)(2,1)S(1)} collective-permute-done((bf16[2,256,256]{2,1,0:T(8,128)(2,1)S(1)}, bf16[2,256,256]{2,1,0:T(8,128)(2,1)S(1)}, u32[]{:S(2)}, u32[]{:S(2)}) %collective-permute-start.16) | collective-permute-done | bytes 262176 | tf_op jit(solution)/shard_map/ppermute | solution.py:305
  119.6 2.8 %collective-permute-start.18 = (bf16[256,256]{1,0:T(8,128)(2,1)S(1)}, bf16[256,256]{1,0:T(8,128)(2,1)S(1)}, u32[]{:S(2)}, u32[]{:S(2)}) collective-permute-start(bf16[256,256]{1,0:T(8,128)(2,1)S(1)} %get-tuple-element.43), channel_id=1, source_target_pairs={{0,24},{8,0},{16,8},{24,16},{32,56},{40,32},{48,40},{56,48},{64,88... | collective-permute-start | bytes 393224 | tf_op jit(solution)/shard_map/ppermute | solution.py:297
  124.1 4.7 %collective-permute-done.18.refs_1_ = bf16[256,256]{1,0:T(8,128)(2,1)S(1)} collective-permute-done((bf16[256,256]{1,0:T(8,128)(2,1)S(1)}, bf16[256,256]{1,0:T(8,128)(2,1)S(1)}, u32[]{:S(2)}, u32[]{:S(2)}) %collective-permute-start.18) | collective-permute-done | bytes 131104 | tf_op jit(solution)/shard_map/ppermute | solution.py:297
  130.3 1.8 %collective-permute-done.20.refs_3_ = bf16[256,256]{1,0:T(8,128)(2,1)S(1)} collective-permute-done((bf16[256,256]{1,0:T(8,128)(2,1)S(1)}, bf16[256,256]{1,0:T(8,128)(2,1)S(1)}, u32[]{:S(2)}, u32[]{:S(2)}) %collective-permute-start.20) | collective-permute-done | bytes 131104 | tf_op jit(solution)/shard_map/ppermute | solution.py:297
  133.5 1.9 %pack.2 = bf16[16,1,128,256]{3,2,1,0:T(8,128)(2,1)} custom-call(s32[2,4]{1,0:T(2,128)S(1)} %copy-done.4, bf16[256,256]{1,0:T(8,128)(2,1)S(1)} %get-tuple-element.42.refs_0_, bf16[256,256]{1,0:T(8,128)(2,1)S(1)} %collective-permute-done.18.refs_1_, bf16[256,256]{1,0:T(8,128)(2,1)S(1)} %collective-permute-done.19.refs_2_, ...), custom_call_target="tpu_custom_call" | custom-call | tf_op jit(solution)/shard_map/pack/pallas_call | solution.py:263
  135.4 4.3 %all-to-all-start = ((bf16[16,1,128,256]{3,2,1,0:T(8,128)(2,1)}), bf16[16,1,128,256]{3,2,1,0:T(8,128)(2,1)S(1)}, u32[]{:S(2)}, u32[]{:S(2)}) async-start(bf16[16,1,128,256]{3,2,1,0:T(8,128)(2,1)} %pack.2), calls=%async_computation | async-start | bytes 2097152 | tf_op jit(solution)/shard_map/all_to_all | solution.py:334
  140.7 17.1 %all-to-all-done.value_ref = bf16[16,1,128,256]{3,2,1,0:T(8,128)(2,1)S(1)} async-done(((bf16[16,1,128,256]{3,2,1,0:T(8,128)(2,1)}), bf16[16,1,128,256]{3,2,1,0:T(8,128)(2,1)S(1)}, u32[]{:S(2)}, u32[]{:S(2)}) %all-to-all-start) | async-done | bytes 1048608 | tf_op jit(solution)/shard_map/all_to_all | solution.py:334
  (87 shorter events, 18.9 us)
Async XLA Ops:
  2.9 14.7 %collective-permute-start.1 = (bf16[256,1024]{1,0:T(8,128)(2,1)}, bf16[256,1024]{1,0:T(8,128)(2,1)S(1)}, u32[]{:S(2)}, u32[]{:S(2)}) collective-permute-start(bf16[256,1024]{1,0:T(8,128)(2,1)} %get-tuple-element.33.refs_2_), channel_id=1, source_target_pairs={{0,24},{8,0},{16,8},{24,16},{32,56},{40,32},{48,40},{56,48},{64,88... | collective-permute-start | bytes 1572872 | tf_op jit(solution)/shard_map/ppermute | solution.py:297
  6.1 11.5 %collective-permute-start.7 = (bf16[256,1024]{1,0:T(8,128)(2,1)}, bf16[256,1024]{1,0:T(8,128)(2,1)S(1)}, u32[]{:S(2)}, u32[]{:S(2)}) collective-permute-start(bf16[256,1024]{1,0:T(8,128)(2,1)} %get-tuple-element.36), channel_id=1, source_target_pairs={{0,1},{1,0},{2,3},{3,2},{4,5},{5,4},{6,7},{7,6},{8,9},{9,8},{10,11... | collective-permute-start | bytes 1572872 | tf_op jit(solution)/shard_map/ppermute | solution.py:309
  6.1 15.1 %collective-permute-start.8 = (bf16[256,1024]{1,0:T(8,128)(2,1)}, bf16[256,1024]{1,0:T(8,128)(2,1)S(1)}, u32[]{:S(2)}, u32[]{:S(2)}) collective-permute-start(bf16[256,1024]{1,0:T(8,128)(2,1)} %get-tuple-element.31.refs_0_), channel_id=1, source_target_pairs={{0,96},{8,104},{16,112},{24,120},{32,0},{40,8},{48,16},{56,24},{64... | collective-permute-start | bytes 1572872 | tf_op jit(solution)/shard_map/ppermute | solution.py:301
  8.8 15.8 %collective-permute-start.10 = (bf16[256,1024]{1,0:T(8,128)(2,1)}, bf16[256,1024]{1,0:T(8,128)(2,1)S(1)}, u32[]{:S(2)}, u32[]{:S(2)}) collective-permute-start(bf16[256,1024]{1,0:T(8,128)(2,1)} %get-tuple-element.31.refs_0_), channel_id=1, source_target_pairs={{0,32},{8,40},{16,48},{24,56},{32,64},{40,72},{48,80},{56,88},{64,... | collective-permute-start | bytes 1572872 | tf_op jit(solution)/shard_map/ppermute | solution.py:301
  8.8 15.8 %collective-permute-start.28 = (bf16[256,1024]{1,0:T(8,128)(2,1)}, bf16[256,1024]{1,0:T(8,128)(2,1)S(1)}, u32[]{:S(2)}, u32[]{:S(2)}) collective-permute-start(bf16[256,1024]{1,0:T(8,128)(2,1)} %get-tuple-element.32.refs_1_), channel_id=1, source_target_pairs={{0,8},{8,16},{16,24},{24,0},{32,40},{40,48},{48,56},{56,32},{64,72... | collective-permute-start | bytes 1572872 | tf_op jit(solution)/shard_map/ppermute | solution.py:297
  17.6 15.8 %collective-permute-start.26 = (bf16[256,1024]{1,0:T(8,128)(2,1)}, bf16[256,1024]{1,0:T(8,128)(2,1)S(1)}, u32[]{:S(2)}, u32[]{:S(2)}) collective-permute-start(bf16[256,1024]{1,0:T(8,128)(2,1)} %get-tuple-element.32.refs_1_), channel_id=1, source_target_pairs={{0,24},{8,0},{16,8},{24,16},{32,56},{40,32},{48,40},{56,48},{64,88... | collective-permute-start | bytes 1572872 | tf_op jit(solution)/shard_map/ppermute | solution.py:297
  21.2 14.4 %collective-permute-start.9 = (bf16[256,1024]{1,0:T(8,128)(2,1)S(1)}, bf16[256,1024]{1,0:T(8,128)(2,1)S(1)}, u32[]{:S(2)}, u32[]{:S(2)}) collective-permute-start(bf16[256,1024]{1,0:T(8,128)(2,1)S(1)} %collective-permute-done.7.refs_9_), channel_id=1, source_target_pairs={{0,96},{8,104},{16,112},{24,120},{32,0},{40,8},{48,16},{56,24},{64... | collective-permute-start | bytes 1572872 | tf_op jit(solution)/shard_map/ppermute | solution.py:301
  24.6 16.0 %collective-permute-start.11 = (bf16[256,1024]{1,0:T(8,128)(2,1)S(1)}, bf16[256,1024]{1,0:T(8,128)(2,1)S(1)}, u32[]{:S(2)}, u32[]{:S(2)}) collective-permute-start(bf16[256,1024]{1,0:T(8,128)(2,1)S(1)} %collective-permute-done.10.refs_14_), channel_id=1, source_target_pairs={{0,32},{8,40},{16,48},{24,56},{32,64},{40,72},{48,80},{56,88},{64,... | collective-permute-start | bytes 1572872 | tf_op jit(solution)/shard_map/ppermute | solution.py:301
  24.6 16.0 %collective-permute-start.29 = (bf16[256,1024]{1,0:T(8,128)(2,1)S(1)}, bf16[256,1024]{1,0:T(8,128)(2,1)S(1)}, u32[]{:S(2)}, u32[]{:S(2)}) collective-permute-start(bf16[256,1024]{1,0:T(8,128)(2,1)S(1)} %collective-permute-done.28.refs_6_), channel_id=1, source_target_pairs={{0,8},{8,16},{16,24},{24,0},{32,40},{40,48},{48,56},{56,32},{64,72... | collective-permute-start | bytes 1572872 | tf_op jit(solution)/shard_map/ppermute | solution.py:297
  24.7 25.5 %collective-permute-start.13 = (bf16[256,1024]{1,0:T(8,128)(2,1)S(1)}, bf16[256,1024]{1,0:T(8,128)(2,1)S(1)}, u32[]{:S(2)}, u32[]{:S(2)}) collective-permute-start(bf16[256,1024]{1,0:T(8,128)(2,1)S(1)} %collective-permute-done.7.refs_9_), channel_id=1, source_target_pairs={{0,32},{8,40},{16,48},{24,56},{32,64},{40,72},{48,80},{56,88},{64,... | collective-permute-start | bytes 1572872 | tf_op jit(solution)/shard_map/ppermute | solution.py:301
  33.3 16.9 %collective-permute-start.27 = (bf16[256,1024]{1,0:T(8,128)(2,1)S(1)}, bf16[256,1024]{1,0:T(8,128)(2,1)S(1)}, u32[]{:S(2)}, u32[]{:S(2)}) collective-permute-start(bf16[256,1024]{1,0:T(8,128)(2,1)S(1)} %collective-permute-done.26.refs_2_), channel_id=1, source_target_pairs={{0,1},{1,0},{2,3},{3,2},{4,5},{5,4},{6,7},{7,6},{8,9},{9,8},{10,11... | collective-permute-start | bytes 1572872 | tf_op jit(solution)/shard_map/ppermute | solution.py:309
  35.6 21.2 %collective-permute-start.31 = (bf16[256,1024]{1,0:T(8,128)(2,1)S(1)}, bf16[256,1024]{1,0:T(8,128)(2,1)S(1)}, u32[]{:S(2)}, u32[]{:S(2)}) collective-permute-start(bf16[256,1024]{1,0:T(8,128)(2,1)S(1)} %collective-permute-done.28.refs_6_), channel_id=1, source_target_pairs={{0,1},{1,0},{2,3},{3,2},{4,5},{5,4},{6,7},{7,6},{8,9},{9,8},{10,11... | collective-permute-start | bytes 1572872 | tf_op jit(solution)/shard_map/ppermute | solution.py:309
  40.6 16.2 %collective-permute-start.12 = (bf16[256,1024]{1,0:T(8,128)(2,1)S(1)}, bf16[256,1024]{1,0:T(8,128)(2,1)S(1)}, u32[]{:S(2)}, u32[]{:S(2)}) collective-permute-start(bf16[256,1024]{1,0:T(8,128)(2,1)S(1)} %collective-permute-done.9.refs_11_), channel_id=1, source_target_pairs={{0,96},{8,104},{16,112},{24,120},{32,0},{40,8},{48,16},{56,24},{64... | collective-permute-start | bytes 1572872 | tf_op jit(solution)/shard_map/ppermute | solution.py:301
  40.6 16.2 %collective-permute-start.30 = (bf16[256,1024]{1,0:T(8,128)(2,1)S(1)}, bf16[256,1024]{1,0:T(8,128)(2,1)S(1)}, u32[]{:S(2)}, u32[]{:S(2)}) collective-permute-start(bf16[256,1024]{1,0:T(8,128)(2,1)S(1)} %collective-permute-done.29.refs_4_), channel_id=1, source_target_pairs={{0,1},{1,0},{2,3},{3,2},{4,5},{5,4},{6,7},{7,6},{8,9},{9,8},{10,11... | collective-permute-start | bytes 1572872 | tf_op jit(solution)/shard_map/ppermute | solution.py:309
  50.2 13.8 %collective-permute-start.5 = (bf16[256,1024]{1,0:T(8,128)(2,1)}, bf16[256,1024]{1,0:T(8,128)(2,1)S(1)}, u32[]{:S(2)}, u32[]{:S(2)}) collective-permute-start(bf16[256,1024]{1,0:T(8,128)(2,1)} %get-tuple-element.33.refs_2_), channel_id=1, source_target_pairs={{0,8},{8,16},{16,24},{24,0},{32,40},{40,48},{48,56},{56,32},{64,72... | collective-permute-start | bytes 1572872 | tf_op jit(solution)/shard_map/ppermute | solution.py:297
  50.2 13.8 %collective-permute-start.3 = (bf16[256,1024]{1,0:T(8,128)(2,1)S(1)}, bf16[256,1024]{1,0:T(8,128)(2,1)S(1)}, u32[]{:S(2)}, u32[]{:S(2)}) collective-permute-start(bf16[256,1024]{1,0:T(8,128)(2,1)S(1)} %collective-permute-done.1.refs_2_), channel_id=1, source_target_pairs={{0,24},{8,0},{16,8},{24,16},{32,56},{40,32},{48,40},{56,48},{64,88... | collective-permute-start | bytes 1572872 | tf_op jit(solution)/shard_map/ppermute | solution.py:297
  63.1 11.8 %collective-permute-start = (bf16[256,1024]{1,0:T(8,128)(2,1)S(1)}, bf16[256,1024]{1,0:T(8,128)(2,1)S(1)}, u32[]{:S(2)}, u32[]{:S(2)}) collective-permute-start(bf16[256,1024]{1,0:T(8,128)(2,1)S(1)} %copy-done), channel_id=1, source_target_pairs={{0,1},{1,0},{2,3},{3,2},{4,5},{5,4},{6,7},{7,6},{8,9},{9,8},{10,11... | collective-permute-start | bytes 1572872 | tf_op jit(solution)/shard_map/ppermute | solution.py:309
  63.1 15.0 %collective-permute-start.2 = (bf16[256,1024]{1,0:T(8,128)(2,1)S(1)}, bf16[256,1024]{1,0:T(8,128)(2,1)S(1)}, u32[]{:S(2)}, u32[]{:S(2)}) collective-permute-start(bf16[256,1024]{1,0:T(8,128)(2,1)S(1)} %collective-permute-done.1.refs_2_), channel_id=1, source_target_pairs={{0,1},{1,0},{2,3},{3,2},{4,5},{5,4},{6,7},{7,6},{8,9},{9,8},{10,11... | collective-permute-start | bytes 1572872 | tf_op jit(solution)/shard_map/ppermute | solution.py:309
  64.0 14.1 %collective-permute-start.6 = (bf16[256,1024]{1,0:T(8,128)(2,1)S(1)}, bf16[256,1024]{1,0:T(8,128)(2,1)S(1)}, u32[]{:S(2)}, u32[]{:S(2)}) collective-permute-start(bf16[256,1024]{1,0:T(8,128)(2,1)S(1)} %collective-permute-done.5.refs_6_), channel_id=1, source_target_pairs={{0,1},{1,0},{2,3},{3,2},{4,5},{5,4},{6,7},{7,6},{8,9},{9,8},{10,11... | collective-permute-start | bytes 1572872 | tf_op jit(solution)/shard_map/ppermute | solution.py:309
  64.0 10.3 %collective-permute-start.36 = (bf16[2,256,256]{2,1,0:T(8,128)(2,1)S(1)}, bf16[2,256,256]{2,1,0:T(8,128)(2,1)S(1)}, u32[]{:S(2)}, u32[]{:S(2)}) collective-permute-start(bf16[2,256,256]{2,1,0:T(8,128)(2,1)S(1)} %get-tuple-element.52), channel_id=1, source_target_pairs={{0,6},{1,7},{2,0},{3,1},{4,2},{5,3},{6,4},{7,5},{8,14},{9,15},{10,... | collective-permute-start | bytes 786440 | tf_op jit(solution)/shard_map/ppermute | solution.py:305
  69.7 11.7 %collective-permute-start.4 = (bf16[256,1024]{1,0:T(8,128)(2,1)S(1)}, bf16[256,1024]{1,0:T(8,128)(2,1)S(1)}, u32[]{:S(2)}, u32[]{:S(2)}) collective-permute-start(bf16[256,1024]{1,0:T(8,128)(2,1)S(1)} %collective-permute-done.3.refs_4_), channel_id=1, source_target_pairs={{0,1},{1,0},{2,3},{3,2},{4,5},{5,4},{6,7},{7,6},{8,9},{9,8},{10,11... | collective-permute-start | bytes 1572872 | tf_op jit(solution)/shard_map/ppermute | solution.py:309
  74.3 14.8 %collective-permute-start.32 = (bf16[2,256,256]{2,1,0:T(8,128)(2,1)S(1)}, bf16[2,256,256]{2,1,0:T(8,128)(2,1)S(1)}, u32[]{:S(2)}, u32[]{:S(2)}) collective-permute-start(bf16[2,256,256]{2,1,0:T(8,128)(2,1)S(1)} %get-tuple-element.47), channel_id=1, source_target_pairs={{0,2},{1,3},{2,4},{3,5},{4,6},{5,7},{6,0},{7,1},{8,10},{9,11},{10,... | collective-permute-start | bytes 786440 | tf_op jit(solution)/shard_map/ppermute | solution.py:305
  74.9 14.2 %collective-permute-start.33 = (bf16[2,256,256]{2,1,0:T(8,128)(2,1)S(1)}, bf16[2,256,256]{2,1,0:T(8,128)(2,1)S(1)}, u32[]{:S(2)}, u32[]{:S(2)}) collective-permute-start(bf16[2,256,256]{2,1,0:T(8,128)(2,1)S(1)} %get-tuple-element.48), channel_id=1, source_target_pairs={{0,6},{1,7},{2,0},{3,1},{4,2},{5,3},{6,4},{7,5},{8,14},{9,15},{10,... | collective-permute-start | bytes 786440 | tf_op jit(solution)/shard_map/ppermute | solution.py:305
  78.1 11.6 %collective-permute-start.35 = (bf16[2,256,256]{2,1,0:T(8,128)(2,1)S(1)}, bf16[2,256,256]{2,1,0:T(8,128)(2,1)S(1)}, u32[]{:S(2)}, u32[]{:S(2)}) collective-permute-start(bf16[2,256,256]{2,1,0:T(8,128)(2,1)S(1)} %add_convert_fusion.1), channel_id=1, source_target_pairs={{0,2},{1,3},{2,4},{3,5},{4,6},{5,7},{6,0},{7,1},{8,10},{9,11},{10,... | collective-permute-start | bytes 786440 | tf_op jit(solution)/shard_map/ppermute | solution.py:305
  78.1 11.6 %collective-permute-start.37 = (bf16[2,256,256]{2,1,0:T(8,128)(2,1)S(1)}, bf16[2,256,256]{2,1,0:T(8,128)(2,1)S(1)}, u32[]{:S(2)}, u32[]{:S(2)}) collective-permute-start(bf16[2,256,256]{2,1,0:T(8,128)(2,1)S(1)} %add_convert_fusion), channel_id=1, source_target_pairs={{0,6},{1,7},{2,0},{3,1},{4,2},{5,3},{6,4},{7,5},{8,14},{9,15},{10,... | collective-permute-start | bytes 786440 | tf_op jit(solution)/shard_map/ppermute | solution.py:305
  87.0 21.5 %collective-permute-start.14 = (bf16[4,256,256]{2,1,0:T(8,128)(2,1)}, bf16[4,256,256]{2,1,0:T(8,128)(2,1)S(1)}, u32[]{:S(2)}, u32[]{:S(2)}) collective-permute-start(bf16[4,256,256]{2,1,0:T(8,128)(2,1)} %get-tuple-element.38), channel_id=1, source_target_pairs={{0,2},{1,3},{2,4},{3,5},{4,6},{5,7},{6,0},{7,1},{8,10},{9,11},{10,... | collective-permute-start | bytes 1572872 | tf_op jit(solution)/shard_map/ppermute | solution.py:305
  90.0 19.7 %collective-permute-start.15 = (bf16[4,256,256]{2,1,0:T(8,128)(2,1)}, bf16[4,256,256]{2,1,0:T(8,128)(2,1)S(1)}, u32[]{:S(2)}, u32[]{:S(2)}) collective-permute-start(bf16[4,256,256]{2,1,0:T(8,128)(2,1)} %get-tuple-element.39), channel_id=1, source_target_pairs={{0,6},{1,7},{2,0},{3,1},{4,2},{5,3},{6,4},{7,5},{8,14},{9,15},{10,... | collective-permute-start | bytes 1572872 | tf_op jit(solution)/shard_map/ppermute | solution.py:305
  104.9 30.5 %all-to-all-start.1 = ((bf16[16,1,128,256]{3,2,1,0:T(8,128)(2,1)}), bf16[16,1,128,256]{3,2,1,0:T(8,128)(2,1)S(1)}, u32[]{:S(2)}, u32[]{:S(2)}) async-start(bf16[16,1,128,256]{3,2,1,0:T(8,128)(2,1)} %pack.3), calls=%async_computation.1 | async-start | bytes 2097152 | tf_op jit(solution)/shard_map/all_to_all | solution.py:334
  109.6 9.8 %collective-permute-start.16 = (bf16[2,256,256]{2,1,0:T(8,128)(2,1)S(1)}, bf16[2,256,256]{2,1,0:T(8,128)(2,1)S(1)}, u32[]{:S(2)}, u32[]{:S(2)}) collective-permute-start(bf16[2,256,256]{2,1,0:T(8,128)(2,1)S(1)} %add_convert_fusion.3), channel_id=1, source_target_pairs={{0,2},{1,3},{2,4},{3,5},{4,6},{5,7},{6,0},{7,1},{8,10},{9,11},{10,... | collective-permute-start | bytes 786440 | tf_op jit(solution)/shard_map/ppermute | solution.py:305
  109.8 9.7 %collective-permute-start.17 = (bf16[2,256,256]{2,1,0:T(8,128)(2,1)S(1)}, bf16[2,256,256]{2,1,0:T(8,128)(2,1)S(1)}, u32[]{:S(2)}, u32[]{:S(2)}) collective-permute-start(bf16[2,256,256]{2,1,0:T(8,128)(2,1)S(1)} %add_convert_fusion.2), channel_id=1, source_target_pairs={{0,6},{1,7},{2,0},{3,1},{4,2},{5,3},{6,4},{7,5},{8,14},{9,15},{10,... | collective-permute-start | bytes 786440 | tf_op jit(solution)/shard_map/ppermute | solution.py:305
  119.6 9.2 %collective-permute-start.18 = (bf16[256,256]{1,0:T(8,128)(2,1)S(1)}, bf16[256,256]{1,0:T(8,128)(2,1)S(1)}, u32[]{:S(2)}, u32[]{:S(2)}) collective-permute-start(bf16[256,256]{1,0:T(8,128)(2,1)S(1)} %get-tuple-element.43), channel_id=1, source_target_pairs={{0,24},{8,0},{16,8},{24,16},{32,56},{40,32},{48,40},{56,48},{64,88... | collective-permute-start | bytes 393224 | tf_op jit(solution)/shard_map/ppermute | solution.py:297
  135.4 22.5 %all-to-all-start = ((bf16[16,1,128,256]{3,2,1,0:T(8,128)(2,1)}), bf16[16,1,128,256]{3,2,1,0:T(8,128)(2,1)S(1)}, u32[]{:S(2)}, u32[]{:S(2)}) async-start(bf16[16,1,128,256]{3,2,1,0:T(8,128)(2,1)} %pack.2), calls=%async_computation | async-start | bytes 2097152 | tf_op jit(solution)/shard_map/all_to_all | solution.py:334
  (20 other events, 97.0 us)

commit v6 on v5

--- a/solution.py
+++ b/solution.py
@@ -31,11 +31,12 @@
 
 
 def scale_body(mask_hbm, panels_hbm, scaling_hbm, mine_ref, swap_ref, top_ref, low_ref, *scratch):
-    mask_ref, panels_ref, scaling_ref, sems = scratch
+    mask_ref, panels_ref, scaling_ref, scaled_ref, sems, out_sems = scratch
     _, _, z, k = position()
     copies = [
-        pltpu.make_async_copy(panels_hbm.at[pl.ds(0, TILE)], panels_ref.at[pl.ds(0, TILE)], sems.at[0]),
-        pltpu.make_async_copy(panels_hbm.at[pl.ds(TILE, TILE)], panels_ref.at[pl.ds(TILE, TILE)], sems.at[1]),
+        pltpu.make_async_copy(panels_hbm.at[pl.ds(i * TILE, TILE)], panels_ref.at[pl.ds(i * TILE, TILE)], sems.at[i])
+        for i in range(2)
+    ] + [
         pltpu.make_async_copy(scaling_hbm, scaling_ref, sems.at[2]),
         pltpu.make_async_copy(mask_hbm, mask_ref, sems.at[3]),
     ]
@@ -44,24 +45,52 @@
     copies[3].wait()
     copies[2].wait()
     root = jnp.sqrt(scaling_ref[...])
+
+    def stores(i):
+        def rows(at, count):
+            return scaled_ref.at[pl.ds(i * TILE + at, count)]
+
+        part = pl.ds(i * HALF, HALF)
+        return (
+            pltpu.make_async_copy(rows(0, TILE), mine_ref, out_sems.at[3 * i]),
+            pltpu.make_async_copy(rows(0, TILE), swap_ref, out_sems.at[3 * i]),
+            pltpu.make_async_copy(rows(0, HALF), top_ref.at[part], out_sems.at[3 * i + 1]),
+            pltpu.make_async_copy(rows(HALF, HALF), low_ref.at[part], out_sems.at[3 * i + 2]),
+        )
+
     for i in range(2):
         copies[i].wait()
         for b in range(4):
             rows, cols = pl.ds(i * TILE, TILE), pl.ds(b * TILE, TILE)
             mask = mask_ref[i, 4 * (2 * z + k) + b].astype(jnp.float32)
-            tile = (
+            scaled_ref[rows, cols] = (
                 panels_ref[rows, cols].astype(jnp.float32) * mask * root[:, b * TILE : (b + 1) * TILE]
             ).astype(jnp.bfloat16)
-            top_ref[pl.ds(i * HALF, HALF), cols] = tile[:HALF]
-            low_ref[pl.ds(i * HALF, HALF), cols] = tile[HALF:]
-
-            @pl.when(k == i)
-            def _():
-                mine_ref[:, cols] = tile
-
-            @pl.when(k != i)
-            def _():
-                swap_ref[:, cols] = tile
+        mine, other, top, low = stores(i)
+
+        @pl.when(k == i)
+        def _():
+            mine.start()
+
+        @pl.when(k != i)
+        def _():
+            other.start()
+
+        top.start()
+        low.start()
+    for i in range(2):
+        mine, other, top, low = stores(i)
+
+        @pl.when(k == i)
+        def _():
+            mine.wait()
+
+        @pl.when(k != i)
+        def _():
+            other.wait()
+
+        top.wait()
+        low.wait()
 
 
 def scale(tile_mask, panels, scaling):
@@ -70,12 +99,14 @@
         scale_body,
         out_shape=(part, part, part, part),
         in_specs=[pl.BlockSpec(memory_space=pltpu.HBM)] * 3,
-        out_specs=tuple(pl.BlockSpec(memory_space=pltpu.VMEM) for _ in range(4)),
+        out_specs=(pl.BlockSpec(memory_space=pl.ANY),) * 4,
         scratch_shapes=[
             pltpu.SMEM(tile_mask.shape, jnp.int32),
             pltpu.VMEM(panels.shape, jnp.bfloat16),
             pltpu.VMEM((1, panels.shape[1]), jnp.float32),
+            pltpu.VMEM(panels.shape, jnp.bfloat16),
             pltpu.SemaphoreType.DMA((4,)),
+            pltpu.SemaphoreType.DMA((6,)),
         ],
         compiler_params=pltpu.CompilerParams(vmem_limit_bytes=58000 * 1024),
         name="scale",
@@ -128,8 +159,8 @@
         copy.start()
     for copy in copies:
         copy.wait()
-    next_low, prev_high, up, down = refs[16:20]
-    far_up, far_down, at = (refs[20], refs[21], 0) if first else (up, down, 2)
+    up, down, next_low, prev_high = refs[16:20]
+    far_up, far_down, at = (refs[20], refs[21], 0) if first else (next_low, prev_high, 2)
     blocks(rows_ref, cols_ref[(z + 2) % 4], ((up, 0), (up, 1), (down, 0), (down, 1)))
     blocks(rows_ref, cols_ref[(z + 1) % 4], ((next_low, 0), (next_low, 1), (far_up, at), (far_up, at + 1)))
     blocks(rows_ref, cols_ref[(z + 3) % 4], ((far_down, at), (far_down, at + 1), (prev_high, 0), (prev_high, 1)))
@@ -215,6 +246,23 @@
         compiler_params=pltpu.CompilerParams(vmem_limit_bytes=8 * 1024 * 1024),
         name="finish",
     )(*parts)
+
+
+def merge_body(share_ref, got_ref, out_ref):
+    for j in range(2):
+        out_ref[j] = (share_ref[j].astype(jnp.float32) + got_ref[j].astype(jnp.float32)).astype(jnp.bfloat16)
+        out_ref[2 + j] = share_ref[2 + j]
+
+
+def merge(share, got):
+    return pl.pallas_call(
+        merge_body,
+        out_shape=jax.ShapeDtypeStruct(share.shape, share.dtype),
+        in_specs=[pl.BlockSpec(memory_space=pltpu.VMEM)] * 2,
+        out_specs=pl.BlockSpec(memory_space=pltpu.VMEM),
+        compiler_params=pltpu.CompilerParams(vmem_limit_bytes=4 * 1024 * 1024),
+        name="merge",
+    )(share, got)
 
 
 def pack_body(owners_ref, *refs):
@@ -314,13 +362,15 @@
 
 
 def reduce_along_z(partials):
-    next_low, prev_high, up, down, *far, own = partials
+    up, down, next_low, prev_high, *far, own = partials
     got_down, got_up = zpass(down, -1), zpass(up, 1)
-    far_down, far_up = got_down, got_up
     if far:
         far_down, far_up = zpass(far[1], -1), zpass(far[0], 1)
-    sum_down = zpass(add(prev_high, got_down[:2]), -1)
-    sum_up = zpass(add(next_low, got_up[:2]), 1)
+        sum_down = zpass(add(prev_high, got_down), -1)
+        sum_up = zpass(add(next_low, got_up), 1)
+    else:
+        far_down = sum_down = zpass(merge(prev_high, got_down), -1)
+        far_up = sum_up = zpass(merge(next_low, got_up), 1)
     return finish(own, far_up, far_down, sum_up, sum_down)
 
 
@@ -347,7 +397,9 @@
     c0, top, low = stage(c0, top, low)
     cols = (c0, c1, cp0, cp1, co0, co1, cm0, cm1)
     halves = []
-    for own, pieces in ((top, (sent_top, top_p, top_o, top_m)), (low, (sent_low, low_p, low_o, low_m))):
+    for own, pieces in (
+        (top, (sent_top, top_p, top_o, top_m)), (low, (sent_low, low_p, low_o, low_m))
+    ):
         others = [swap(value) for value in pieces]
         rows = [piece for pair in zip((own, *pieces[1:]), others) for piece in pair]
         if halves:

time: 159 us -> 168 us (1.057)
  waiting for transfers between devices: 81.7 us -> 96.3 us
  starting transfers between devices: 51.6 us -> 45.8 us
    ppermute x10, waiting for transfers between devices: 13.2 us -> 30.1 us  [zpass(): return lax.ppermute(value, 'col', along_z(step))]
    ppermute x10, starting transfers between devices: 19.6 us -> 15 us  [zpass(): return lax.ppermute(value, 'col', along_z(step))]
  transfers between devices with their start and end apart: 47 -> 47, of which waited for: 20 -> 20; matrix products, arithmetic and copies ran while one was open for 1% -> 0% of each run, Pallas kernels for 11% -> 11%
where the time goes in v6:
time: 168 us; the launch traced here: 167 us
  waiting for transfers between devices  96.3 us (57%)
  starting transfers between devices  45.8 us (27%)
  Pallas kernels  21.5 us (13%)
  local copies, waits for them, and re-layouts  3.13 us (2%)
    ppermute x12, waiting for transfers between devices, ypass(): return lax.ppermute(value, 'row', along_y(step))  30.8 us
    ppermute x10, waiting for transfers between devices, zpass(): return lax.ppermute(value, 'col', along_z(step))  30.1 us
    all_to_all x2, waiting for transfers between devices, to_owners(): lax.all_to_all(outgoing, 'row', split_axis=0, concat_axis=0, tiled=True)  17.1 us
    ppermute x6, waiting for transfers between devices, xpass(): return lax.ppermute(value, 'row', along_x(step))  16.9 us
    ppermute x12, starting transfers between devices, ypass(): return lax.ppermute(value, 'row', along_y(step))  15.5 us
    ppermute x10, starting transfers between devices, zpass(): return lax.ppermute(value, 'col', along_z(step))  15 us
    pallas_call x2, Pallas kernels, product(): pl.pallas_call(lambda *refs: product_body(*refs, first=first), out_shape=...  9.8 us
    all_to_all x2, starting transfers between devices, to_owners(): lax.all_to_all(outgoing, 'row', split_axis=0, concat_axis=0, tiled=True)  8.39 us
  transfers between devices with their start and end apart: 47, of which 20 were waited for; matrix products, arithmetic and copies ran while one was open for 0% of the time, Pallas kernels for 11%

profile of v6, /device:TPU:0, one launch (start us, length us, event | category | flops | bytes accessed | tf_op | source)
XLA Modules:
  0.0 167.3 jit_solution(1677800710614877244)
XLA Ops:
  0.0 2.6 %scale.1 = (bf16[256,1024]{1,0:T(8,128)(2,1)}, bf16[256,1024]{1,0:T(8,128)(2,1)}, bf16[256,1024]{1,0:T(8,128)(2,1)}, bf16[256,1024]{1,0:T(8,128)(2,1)}) custom-call(s32[2,32]{1,0:T(2,128)} %mask_hbm.1, bf16[512,1024]{1,0:T(8,128)(2,1)} %panels_hbm.1, f32[1,1024]{1,0:T(1,128)} %bitcast.1), custom_call_target="tpu_custom_call" | custom-call | tf_op jit(solution)/shard_map/scale/pallas_call | solution.py:98
  2.7 3.2 %collective-permute-start.1 = (bf16[256,1024]{1,0:T(8,128)(2,1)}, bf16[256,1024]{1,0:T(8,128)(2,1)S(1)}, u32[]{:S(2)}, u32[]{:S(2)}) collective-permute-start(bf16[256,1024]{1,0:T(8,128)(2,1)} %get-tuple-element.33.refs_2_), channel_id=1, source_target_pairs={{0,24},{8,0},{16,8},{24,16},{32,56},{40,32},{48,40},{56,48},{64,88... | collective-permute-start | bytes 1572872 | tf_op jit(solution)/shard_map/ppermute | solution.py:345
  5.8 2.8 %collective-permute-start.8 = (bf16[256,1024]{1,0:T(8,128)(2,1)}, bf16[256,1024]{1,0:T(8,128)(2,1)S(1)}, u32[]{:S(2)}, u32[]{:S(2)}) collective-permute-start(bf16[256,1024]{1,0:T(8,128)(2,1)} %get-tuple-element.31.refs_0_), channel_id=1, source_target_pairs={{0,96},{8,104},{16,112},{24,120},{32,0},{40,8},{48,16},{56,24},{64... | collective-permute-start | bytes 1572872 | tf_op jit(solution)/shard_map/ppermute | solution.py:349
  8.6 8.7 %collective-permute-done.1.refs_2_ = bf16[256,1024]{1,0:T(8,128)(2,1)S(1)} collective-permute-done((bf16[256,1024]{1,0:T(8,128)(2,1)}, bf16[256,1024]{1,0:T(8,128)(2,1)S(1)}, u32[]{:S(2)}, u32[]{:S(2)}) %collective-permute-start.1) | collective-permute-done | bytes 524320 | tf_op jit(solution)/shard_map/ppermute | solution.py:345
  17.4 3.6 %collective-permute-start.26 = (bf16[256,1024]{1,0:T(8,128)(2,1)}, bf16[256,1024]{1,0:T(8,128)(2,1)S(1)}, u32[]{:S(2)}, u32[]{:S(2)}) collective-permute-start(bf16[256,1024]{1,0:T(8,128)(2,1)} %get-tuple-element.32.refs_1_), channel_id=1, source_target_pairs={{0,24},{8,0},{16,8},{24,16},{32,56},{40,32},{48,40},{56,48},{64,88... | collective-permute-start | bytes 1572872 | tf_op jit(solution)/shard_map/ppermute | solution.py:345
  20.9 3.4 %collective-permute-start.9 = (bf16[256,1024]{1,0:T(8,128)(2,1)S(1)}, bf16[256,1024]{1,0:T(8,128)(2,1)S(1)}, u32[]{:S(2)}, u32[]{:S(2)}) collective-permute-start(bf16[256,1024]{1,0:T(8,128)(2,1)S(1)} %collective-permute-done.7.refs_9_), channel_id=1, source_target_pairs={{0,96},{8,104},{16,112},{24,120},{32,0},{40,8},{48,16},{56,24},{64... | collective-permute-start | bytes 1572872 | tf_op jit(solution)/shard_map/ppermute | solution.py:349
  24.6 8.5 %collective-permute-done.26.refs_2_ = bf16[256,1024]{1,0:T(8,128)(2,1)S(1)} collective-permute-done((bf16[256,1024]{1,0:T(8,128)(2,1)}, bf16[256,1024]{1,0:T(8,128)(2,1)S(1)}, u32[]{:S(2)}, u32[]{:S(2)}) %collective-permute-start.26) | collective-permute-done | bytes 524320 | tf_op jit(solution)/shard_map/ppermute | solution.py:345
  33.1 2.2 %collective-permute-done.9.refs_11_ = bf16[256,1024]{1,0:T(8,128)(2,1)S(1)} collective-permute-done((bf16[256,1024]{1,0:T(8,128)(2,1)S(1)}, bf16[256,1024]{1,0:T(8,128)(2,1)S(1)}, u32[]{:S(2)}, u32[]{:S(2)}) %collective-permute-start.9) | collective-permute-done | bytes 524320 | tf_op jit(solution)/shard_map/ppermute | solution.py:349
  35.4 5.0 %collective-permute-done.11.refs_12_ = bf16[256,1024]{1,0:T(8,128)(2,1)S(1)} collective-permute-done((bf16[256,1024]{1,0:T(8,128)(2,1)S(1)}, bf16[256,1024]{1,0:T(8,128)(2,1)S(1)}, u32[]{:S(2)}, u32[]{:S(2)}) %collective-permute-start.11) | collective-permute-done | bytes 524320 | tf_op jit(solution)/shard_map/ppermute | solution.py:349
  40.4 9.6 %collective-permute-done.13.refs_15_ = bf16[256,1024]{1,0:T(8,128)(2,1)S(1)} collective-permute-done((bf16[256,1024]{1,0:T(8,128)(2,1)S(1)}, bf16[256,1024]{1,0:T(8,128)(2,1)S(1)}, u32[]{:S(2)}, u32[]{:S(2)}) %collective-permute-start.13) | collective-permute-done | bytes 524320 | tf_op jit(solution)/shard_map/ppermute | solution.py:349
  50.0 3.2 %collective-permute-start.3 = (bf16[256,1024]{1,0:T(8,128)(2,1)S(1)}, bf16[256,1024]{1,0:T(8,128)(2,1)S(1)}, u32[]{:S(2)}, u32[]{:S(2)}) collective-permute-start(bf16[256,1024]{1,0:T(8,128)(2,1)S(1)} %collective-permute-done.1.refs_2_), channel_id=1, source_target_pairs={{0,24},{8,0},{16,8},{24,16},{32,56},{40,32},{48,40},{56,48},{64,88... | collective-permute-start | bytes 1572872 | tf_op jit(solution)/shard_map/ppermute | solution.py:345
  56.6 4.4 %product.3 = (bf16[2,256,256]{2,1,0:T(8,128)(2,1)S(1)}, bf16[2,256,256]{2,1,0:T(8,128)(2,1)S(1)}, bf16[2,256,256]{2,1,0:T(8,128)(2,1)S(1)}, bf16[2,256,256]{2,1,...) custom-call(bf16[256,1024]{1,0:T(8,128)(2,1)S(1)} %get-tuple-element.46.refs_0_, ...), custom_call_target="tpu_custom_call" | custom-call | tf_op jit(solution)/shard_map/product/pallas_call | solution.py:176
  60.9 2.0 %collective-permute-start.34 = (bf16[2,256,256]{2,1,0:T(8,128)(2,1)S(1)}, bf16[2,256,256]{2,1,0:T(8,128)(2,1)S(1)}, u32[]{:S(2)}, u32[]{:S(2)}) collective-permute-start(bf16[2,256,256]{2,1,0:T(8,128)(2,1)S(1)} %get-tuple-element.50), channel_id=1, source_target_pairs={{0,2},{1,3},{2,4},{3,5},{4,6},{5,7},{6,0},{7,1},{8,10},{9,11},{10,... | collective-permute-start | bytes 786440 | tf_op jit(solution)/shard_map/ppermute | solution.py:353
  62.9 1.9 %collective-permute-start.32 = (bf16[2,256,256]{2,1,0:T(8,128)(2,1)S(1)}, bf16[2,256,256]{2,1,0:T(8,128)(2,1)S(1)}, u32[]{:S(2)}, u32[]{:S(2)}) collective-permute-start(bf16[2,256,256]{2,1,0:T(8,128)(2,1)S(1)} %get-tuple-element.47), channel_id=1, source_target_pairs={{0,2},{1,3},{2,4},{3,5},{4,6},{5,7},{6,0},{7,1},{8,10},{9,11},{10,... | collective-permute-start | bytes 786440 | tf_op jit(solution)/shard_map/ppermute | solution.py:353
  66.2 6.0 %collective-permute-done.34 = bf16[2,256,256]{2,1,0:T(8,128)(2,1)S(1)} collective-permute-done((bf16[2,256,256]{2,1,0:T(8,128)(2,1)S(1)}, bf16[2,256,256]{2,1,0:T(8,128)(2,1)S(1)}, u32[]{:S(2)}, u32[]{:S(2)}) %collective-permute-start.34) | collective-permute-done | bytes 262176 | tf_op jit(solution)/shard_map/ppermute | solution.py:353
  72.2 2.0 %collective-permute-start.36 = (bf16[2,256,256]{2,1,0:T(8,128)(2,1)S(1)}, bf16[2,256,256]{2,1,0:T(8,128)(2,1)S(1)}, u32[]{:S(2)}, u32[]{:S(2)}) collective-permute-start(bf16[2,256,256]{2,1,0:T(8,128)(2,1)S(1)} %get-tuple-element.52), channel_id=1, source_target_pairs={{0,6},{1,7},{2,0},{3,1},{4,2},{5,3},{6,4},{7,5},{8,14},{9,15},{10,... | collective-permute-start | bytes 786440 | tf_op jit(solution)/shard_map/ppermute | solution.py:353
  74.5 3.3 %collective-permute-done.32.far_up = bf16[2,256,256]{2,1,0:T(8,128)(2,1)S(1)} collective-permute-done((bf16[2,256,256]{2,1,0:T(8,128)(2,1)S(1)}, bf16[2,256,256]{2,1,0:T(8,128)(2,1)S(1)}, u32[]{:S(2)}, u32[]{:S(2)}) %collective-permute-start.32) | collective-permute-done | bytes 262176 | tf_op jit(solution)/shard_map/ppermute | solution.py:353
  78.7 3.3 %collective-permute-done.35.sum_up = bf16[2,256,256]{2,1,0:T(8,128)(2,1)S(1)} collective-permute-done((bf16[2,256,256]{2,1,0:T(8,128)(2,1)S(1)}, bf16[2,256,256]{2,1,0:T(8,128)(2,1)S(1)}, u32[]{:S(2)}, u32[]{:S(2)}) %collective-permute-start.35) | collective-permute-done | bytes 262176 | tf_op jit(solution)/shard_map/ppermute | solution.py:353
  82.4 1.9 %kept.1.own = f32[4,256,256]{2,1,0:T(8,128)S(1)} custom-call(bf16[256,1024]{1,0:T(8,128)(2,1)S(1)} %get-tuple-element.46.refs_0_, bf16[256,1024]{1,0:T(8,128)(2,1)S(1)} %collective-permute-done.25.refs_1_, bf16[256,1024]{1,0:T(8,128)(2,1)S(1)} %collective-permute-done.26.refs_2_, bf16[256,1024]{1,0:T(8,128)(2,1)S(1)} %collective-permute-done.27.refs_3_, ...), custom_call_target="tpu_custom_call" | custom-call | tf_op jit(solution)/shard_map/kept/pallas_call | solution.py:212
  84.4 4.0 %collective-permute-done.37.sum_down = bf16[2,256,256]{2,1,0:T(8,128)(2,1)S(1)} collective-permute-done((bf16[2,256,256]{2,1,0:T(8,128)(2,1)S(1)}, bf16[2,256,256]{2,1,0:T(8,128)(2,1)S(1)}, u32[]{:S(2)}, u32[]{:S(2)}) %collective-permute-start.37) | collective-permute-done | bytes 262176 | tf_op jit(solution)/shard_map/ppermute | solution.py:353
  90.7 3.7 %collective-permute-done.38.refs_1_ = bf16[256,256]{1,0:T(8,128)(2,1)S(1)} collective-permute-done((bf16[256,256]{1,0:T(8,128)(2,1)S(1)}, bf16[256,256]{1,0:T(8,128)(2,1)S(1)}, u32[]{:S(2)}, u32[]{:S(2)}) %collective-permute-start.38) | collective-permute-done | bytes 131104 | tf_op jit(solution)/shard_map/ppermute | solution.py:345
  94.4 2.1 %collective-permute-done.39.refs_2_ = bf16[256,256]{1,0:T(8,128)(2,1)S(1)} collective-permute-done((bf16[256,256]{1,0:T(8,128)(2,1)S(1)}, bf16[256,256]{1,0:T(8,128)(2,1)S(1)}, u32[]{:S(2)}, u32[]{:S(2)}) %collective-permute-start.39) | collective-permute-done | bytes 131104 | tf_op jit(solution)/shard_map/ppermute | solution.py:345
  97.4 5.4 %product.2 = (bf16[2,256,256]{2,1,0:T(8,128)(2,1)}, bf16[2,256,256]{2,1,0:T(8,128)(2,1)}, bf16[4,256,256]{2,1,0:T(8,128)(2,1)S(1)}, bf16[4,256,256]{2,1,0:T(8,128)(2,1)S(1)}, f32[4,256,256]{2,1,0:T(8,128)S(1)}) custom-call(bf16[256,1024]{1,0:T(8,128)(2,1)S(1)} %get-tuple-element.34.refs_0_, bf16[256,1024]{1,0:T(8,128)(2,1)S(1)} %collective-permute-done.refs_1_, ...), custom_call_target="tpu_custom_call" | custom-call | tf_op jit(solution)/shard_map/product/pallas_call | solution.py:176
  103.0 3.8 %collective-permute-start.16 = (bf16[2,256,256]{2,1,0:T(8,128)(2,1)}, bf16[2,256,256]{2,1,0:T(8,128)(2,1)S(1)}, u32[]{:S(2)}, u32[]{:S(2)}) collective-permute-start(bf16[2,256,256]{2,1,0:T(8,128)(2,1)} %get-tuple-element.41), channel_id=1, source_target_pairs={{0,6},{1,7},{2,0},{3,1},{4,2},{5,3},{6,4},{7,5},{8,14},{9,15},{10,... | collective-permute-start | bytes 786440 | tf_op jit(solution)/shard_map/ppermute | solution.py:353
  108.5 3.7 %all-to-all-start.1 = ((bf16[16,1,128,256]{3,2,1,0:T(8,128)(2,1)}), bf16[16,1,128,256]{3,2,1,0:T(8,128)(2,1)S(1)}, u32[]{:S(2)}, u32[]{:S(2)}) async-start(bf16[16,1,128,256]{3,2,1,0:T(8,128)(2,1)} %pack.3), calls=%async_computation.1 | async-start | bytes 2097152 | tf_op jit(solution)/shard_map/all_to_all | solution.py:384
  115.1 3.3 %collective-permute-start.17 = (bf16[4,256,256]{2,1,0:T(8,128)(2,1)S(1)}, bf16[4,256,256]{2,1,0:T(8,128)(2,1)S(1)}, u32[]{:S(2)}, u32[]{:S(2)}) collective-permute-start(bf16[4,256,256]{2,1,0:T(8,128)(2,1)S(1)} %merge.3), channel_id=1, source_target_pairs={{0,6},{1,7},{2,0},{3,1},{4,2},{5,3},{6,4},{7,5},{8,14},{9,15},{10,... | collective-permute-start | bytes 1572872 | tf_op jit(solution)/shard_map/ppermute | solution.py:353
  118.3 11.6 %collective-permute-done.15.far_up.sum_up = bf16[4,256,256]{2,1,0:T(8,128)(2,1)S(1)} collective-permute-done((bf16[4,256,256]{2,1,0:T(8,128)(2,1)S(1)}, bf16[4,256,256]{2,1,0:T(8,128)(2,1)S(1)}, u32[]{:S(2)}, u32[]{:S(2)}) %collective-permute-start.15) | collective-permute-done | bytes 524320 | tf_op jit(solution)/shard_map/ppermute | solution.py:353
  133.3 2.7 %collective-permute-done.18.refs_1_ = bf16[256,256]{1,0:T(8,128)(2,1)S(1)} collective-permute-done((bf16[256,256]{1,0:T(8,128)(2,1)S(1)}, bf16[256,256]{1,0:T(8,128)(2,1)S(1)}, u32[]{:S(2)}, u32[]{:S(2)}) %collective-permute-start.18) | collective-permute-done | bytes 131104 | tf_op jit(solution)/shard_map/ppermute | solution.py:345
  136.0 2.7 %collective-permute-done.19.refs_2_ = bf16[256,256]{1,0:T(8,128)(2,1)S(1)} collective-permute-done((bf16[256,256]{1,0:T(8,128)(2,1)S(1)}, bf16[256,256]{1,0:T(8,128)(2,1)S(1)}, u32[]{:S(2)}, u32[]{:S(2)}) %collective-permute-start.19) | collective-permute-done | bytes 131104 | tf_op jit(solution)/shard_map/ppermute | solution.py:345
  141.4 1.9 %pack.2 = bf16[16,1,128,256]{3,2,1,0:T(8,128)(2,1)} custom-call(s32[2,4]{1,0:T(2,128)S(1)} %copy-done.3, bf16[256,256]{1,0:T(8,128)(2,1)S(1)} %get-tuple-element.42.refs_0_, bf16[256,256]{1,0:T(8,128)(2,1)S(1)} %collective-permute-done.18.refs_1_, bf16[256,256]{1,0:T(8,128)(2,1)S(1)} %collective-permute-done.19.refs_2_, ...), custom_call_target="tpu_custom_call" | custom-call | tf_op jit(solution)/shard_map/pack/pallas_call | solution.py:311
  143.3 4.7 %all-to-all-start = ((bf16[16,1,128,256]{3,2,1,0:T(8,128)(2,1)}), bf16[16,1,128,256]{3,2,1,0:T(8,128)(2,1)S(1)}, u32[]{:S(2)}, u32[]{:S(2)}) async-start(bf16[16,1,128,256]{3,2,1,0:T(8,128)(2,1)} %pack.2), calls=%async_computation | async-start | bytes 2097152 | tf_op jit(solution)/shard_map/all_to_all | solution.py:384
  149.0 17.1 %all-to-all-done.value_ref = bf16[16,1,128,256]{3,2,1,0:T(8,128)(2,1)S(1)} async-done(((bf16[16,1,128,256]{3,2,1,0:T(8,128)(2,1)}), bf16[16,1,128,256]{3,2,1,0:T(8,128)(2,1)S(1)}, u32[]{:S(2)}, u32[]{:S(2)}) %all-to-all-start) | async-done | bytes 1048608 | tf_op jit(solution)/shard_map/all_to_all | solution.py:384
  (85 shorter events, 22.4 us)
Async XLA Ops:
  2.7 14.7 %collective-permute-start.1 = (bf16[256,1024]{1,0:T(8,128)(2,1)}, bf16[256,1024]{1,0:T(8,128)(2,1)S(1)}, u32[]{:S(2)}, u32[]{:S(2)}) collective-permute-start(bf16[256,1024]{1,0:T(8,128)(2,1)} %get-tuple-element.33.refs_2_), channel_id=1, source_target_pairs={{0,24},{8,0},{16,8},{24,16},{32,56},{40,32},{48,40},{56,48},{64,88... | collective-permute-start | bytes 1572872 | tf_op jit(solution)/shard_map/ppermute | solution.py:345
  5.8 11.5 %collective-permute-start.7 = (bf16[256,1024]{1,0:T(8,128)(2,1)}, bf16[256,1024]{1,0:T(8,128)(2,1)S(1)}, u32[]{:S(2)}, u32[]{:S(2)}) collective-permute-start(bf16[256,1024]{1,0:T(8,128)(2,1)} %get-tuple-element.36), channel_id=1, source_target_pairs={{0,1},{1,0},{2,3},{3,2},{4,5},{5,4},{6,7},{7,6},{8,9},{9,8},{10,11... | collective-permute-start | bytes 1572872 | tf_op jit(solution)/shard_map/ppermute | solution.py:357
  5.8 15.1 %collective-permute-start.8 = (bf16[256,1024]{1,0:T(8,128)(2,1)}, bf16[256,1024]{1,0:T(8,128)(2,1)S(1)}, u32[]{:S(2)}, u32[]{:S(2)}) collective-permute-start(bf16[256,1024]{1,0:T(8,128)(2,1)} %get-tuple-element.31.refs_0_), channel_id=1, source_target_pairs={{0,96},{8,104},{16,112},{24,120},{32,0},{40,8},{48,16},{56,24},{64... | collective-permute-start | bytes 1572872 | tf_op jit(solution)/shard_map/ppermute | solution.py:349
  8.6 15.8 %collective-permute-start.10 = (bf16[256,1024]{1,0:T(8,128)(2,1)}, bf16[256,1024]{1,0:T(8,128)(2,1)S(1)}, u32[]{:S(2)}, u32[]{:S(2)}) collective-permute-start(bf16[256,1024]{1,0:T(8,128)(2,1)} %get-tuple-element.31.refs_0_), channel_id=1, source_target_pairs={{0,32},{8,40},{16,48},{24,56},{32,64},{40,72},{48,80},{56,88},{64,... | collective-permute-start | bytes 1572872 | tf_op jit(solution)/shard_map/ppermute | solution.py:349
  8.6 15.8 %collective-permute-start.28 = (bf16[256,1024]{1,0:T(8,128)(2,1)}, bf16[256,1024]{1,0:T(8,128)(2,1)S(1)}, u32[]{:S(2)}, u32[]{:S(2)}) collective-permute-start(bf16[256,1024]{1,0:T(8,128)(2,1)} %get-tuple-element.32.refs_1_), channel_id=1, source_target_pairs={{0,8},{8,16},{16,24},{24,0},{32,40},{40,48},{48,56},{56,32},{64,72... | collective-permute-start | bytes 1572872 | tf_op jit(solution)/shard_map/ppermute | solution.py:345
  17.4 15.8 %collective-permute-start.26 = (bf16[256,1024]{1,0:T(8,128)(2,1)}, bf16[256,1024]{1,0:T(8,128)(2,1)S(1)}, u32[]{:S(2)}, u32[]{:S(2)}) collective-permute-start(bf16[256,1024]{1,0:T(8,128)(2,1)} %get-tuple-element.32.refs_1_), channel_id=1, source_target_pairs={{0,24},{8,0},{16,8},{24,16},{32,56},{40,32},{48,40},{56,48},{64,88... | collective-permute-start | bytes 1572872 | tf_op jit(solution)/shard_map/ppermute | solution.py:345
  20.9 14.4 %collective-permute-start.9 = (bf16[256,1024]{1,0:T(8,128)(2,1)S(1)}, bf16[256,1024]{1,0:T(8,128)(2,1)S(1)}, u32[]{:S(2)}, u32[]{:S(2)}) collective-permute-start(bf16[256,1024]{1,0:T(8,128)(2,1)S(1)} %collective-permute-done.7.refs_9_), channel_id=1, source_target_pairs={{0,96},{8,104},{16,112},{24,120},{32,0},{40,8},{48,16},{56,24},{64... | collective-permute-start | bytes 1572872 | tf_op jit(solution)/shard_map/ppermute | solution.py:349
  24.4 16.0 %collective-permute-start.11 = (bf16[256,1024]{1,0:T(8,128)(2,1)S(1)}, bf16[256,1024]{1,0:T(8,128)(2,1)S(1)}, u32[]{:S(2)}, u32[]{:S(2)}) collective-permute-start(bf16[256,1024]{1,0:T(8,128)(2,1)S(1)} %collective-permute-done.10.refs_14_), channel_id=1, source_target_pairs={{0,32},{8,40},{16,48},{24,56},{32,64},{40,72},{48,80},{56,88},{64,... | collective-permute-start | bytes 1572872 | tf_op jit(solution)/shard_map/ppermute | solution.py:349
  24.4 16.0 %collective-permute-start.29 = (bf16[256,1024]{1,0:T(8,128)(2,1)S(1)}, bf16[256,1024]{1,0:T(8,128)(2,1)S(1)}, u32[]{:S(2)}, u32[]{:S(2)}) collective-permute-start(bf16[256,1024]{1,0:T(8,128)(2,1)S(1)} %collective-permute-done.28.refs_6_), channel_id=1, source_target_pairs={{0,8},{8,16},{16,24},{24,0},{32,40},{40,48},{48,56},{56,32},{64,72... | collective-permute-start | bytes 1572872 | tf_op jit(solution)/shard_map/ppermute | solution.py:345
  24.5 25.5 %collective-permute-start.13 = (bf16[256,1024]{1,0:T(8,128)(2,1)S(1)}, bf16[256,1024]{1,0:T(8,128)(2,1)S(1)}, u32[]{:S(2)}, u32[]{:S(2)}) collective-permute-start(bf16[256,1024]{1,0:T(8,128)(2,1)S(1)} %collective-permute-done.7.refs_9_), channel_id=1, source_target_pairs={{0,32},{8,40},{16,48},{24,56},{32,64},{40,72},{48,80},{56,88},{64,... | collective-permute-start | bytes 1572872 | tf_op jit(solution)/shard_map/ppermute | solution.py:349
  33.1 16.9 %collective-permute-start.27 = (bf16[256,1024]{1,0:T(8,128)(2,1)S(1)}, bf16[256,1024]{1,0:T(8,128)(2,1)S(1)}, u32[]{:S(2)}, u32[]{:S(2)}) collective-permute-start(bf16[256,1024]{1,0:T(8,128)(2,1)S(1)} %collective-permute-done.26.refs_2_), channel_id=1, source_target_pairs={{0,1},{1,0},{2,3},{3,2},{4,5},{5,4},{6,7},{7,6},{8,9},{9,8},{10,11... | collective-permute-start | bytes 1572872 | tf_op jit(solution)/shard_map/ppermute | solution.py:357
  35.4 21.2 %collective-permute-start.31 = (bf16[256,1024]{1,0:T(8,128)(2,1)S(1)}, bf16[256,1024]{1,0:T(8,128)(2,1)S(1)}, u32[]{:S(2)}, u32[]{:S(2)}) collective-permute-start(bf16[256,1024]{1,0:T(8,128)(2,1)S(1)} %collective-permute-done.28.refs_6_), channel_id=1, source_target_pairs={{0,1},{1,0},{2,3},{3,2},{4,5},{5,4},{6,7},{7,6},{8,9},{9,8},{10,11... | collective-permute-start | bytes 1572872 | tf_op jit(solution)/shard_map/ppermute | solution.py:357
  40.4 16.2 %collective-permute-start.12 = (bf16[256,1024]{1,0:T(8,128)(2,1)S(1)}, bf16[256,1024]{1,0:T(8,128)(2,1)S(1)}, u32[]{:S(2)}, u32[]{:S(2)}) collective-permute-start(bf16[256,1024]{1,0:T(8,128)(2,1)S(1)} %collective-permute-done.9.refs_11_), channel_id=1, source_target_pairs={{0,96},{8,104},{16,112},{24,120},{32,0},{40,8},{48,16},{56,24},{64... | collective-permute-start | bytes 1572872 | tf_op jit(solution)/shard_map/ppermute | solution.py:349
  40.4 16.2 %collective-permute-start.30 = (bf16[256,1024]{1,0:T(8,128)(2,1)S(1)}, bf16[256,1024]{1,0:T(8,128)(2,1)S(1)}, u32[]{:S(2)}, u32[]{:S(2)}) collective-permute-start(bf16[256,1024]{1,0:T(8,128)(2,1)S(1)} %collective-permute-done.29.refs_4_), channel_id=1, source_target_pairs={{0,1},{1,0},{2,3},{3,2},{4,5},{5,4},{6,7},{7,6},{8,9},{9,8},{10,11... | collective-permute-start | bytes 1572872 | tf_op jit(solution)/shard_map/ppermute | solution.py:357
  50.0 24.3 %collective-permute-start.5 = (bf16[256,1024]{1,0:T(8,128)(2,1)}, bf16[256,1024]{1,0:T(8,128)(2,1)S(1)}, u32[]{:S(2)}, u32[]{:S(2)}) collective-permute-start(bf16[256,1024]{1,0:T(8,128)(2,1)} %get-tuple-element.33.refs_2_), channel_id=1, source_target_pairs={{0,8},{8,16},{16,24},{24,0},{32,40},{40,48},{48,56},{56,32},{64,72... | collective-permute-start | bytes 1572872 | tf_op jit(solution)/shard_map/ppermute | solution.py:345
  50.0 24.4 %collective-permute-start.3 = (bf16[256,1024]{1,0:T(8,128)(2,1)S(1)}, bf16[256,1024]{1,0:T(8,128)(2,1)S(1)}, u32[]{:S(2)}, u32[]{:S(2)}) collective-permute-start(bf16[256,1024]{1,0:T(8,128)(2,1)S(1)} %collective-permute-done.1.refs_2_), channel_id=1, source_target_pairs={{0,24},{8,0},{16,8},{24,16},{32,56},{40,32},{48,40},{56,48},{64,88... | collective-permute-start | bytes 1572872 | tf_op jit(solution)/shard_map/ppermute | solution.py:345
  60.9 11.3 %collective-permute-start.34 = (bf16[2,256,256]{2,1,0:T(8,128)(2,1)S(1)}, bf16[2,256,256]{2,1,0:T(8,128)(2,1)S(1)}, u32[]{:S(2)}, u32[]{:S(2)}) collective-permute-start(bf16[2,256,256]{2,1,0:T(8,128)(2,1)S(1)} %get-tuple-element.50), channel_id=1, source_target_pairs={{0,2},{1,3},{2,4},{3,5},{4,6},{5,7},{6,0},{7,1},{8,10},{9,11},{10,... | collective-permute-start | bytes 786440 | tf_op jit(solution)/shard_map/ppermute | solution.py:353
  62.9 14.9 %collective-permute-start.32 = (bf16[2,256,256]{2,1,0:T(8,128)(2,1)S(1)}, bf16[2,256,256]{2,1,0:T(8,128)(2,1)S(1)}, u32[]{:S(2)}, u32[]{:S(2)}) collective-permute-start(bf16[2,256,256]{2,1,0:T(8,128)(2,1)S(1)} %get-tuple-element.47), channel_id=1, source_target_pairs={{0,2},{1,3},{2,4},{3,5},{4,6},{5,7},{6,0},{7,1},{8,10},{9,11},{10,... | collective-permute-start | bytes 786440 | tf_op jit(solution)/shard_map/ppermute | solution.py:353
  64.8 13.0 %collective-permute-start.33 = (bf16[2,256,256]{2,1,0:T(8,128)(2,1)S(1)}, bf16[2,256,256]{2,1,0:T(8,128)(2,1)S(1)}, u32[]{:S(2)}, u32[]{:S(2)}) collective-permute-start(bf16[2,256,256]{2,1,0:T(8,128)(2,1)S(1)} %get-tuple-element.48), channel_id=1, source_target_pairs={{0,6},{1,7},{2,0},{3,1},{4,2},{5,3},{6,4},{7,5},{8,14},{9,15},{10,... | collective-permute-start | bytes 786440 | tf_op jit(solution)/shard_map/ppermute | solution.py:353
  74.4 14.2 %collective-permute-start = (bf16[256,1024]{1,0:T(8,128)(2,1)S(1)}, bf16[256,1024]{1,0:T(8,128)(2,1)S(1)}, u32[]{:S(2)}, u32[]{:S(2)}) collective-permute-start(bf16[256,1024]{1,0:T(8,128)(2,1)S(1)} %copy-done), channel_id=1, source_target_pairs={{0,1},{1,0},{2,3},{3,2},{4,5},{5,4},{6,7},{7,6},{8,9},{9,8},{10,11... | collective-permute-start | bytes 1572872 | tf_op jit(solution)/shard_map/ppermute | solution.py:357
  77.8 11.6 %collective-permute-start.2 = (bf16[256,1024]{1,0:T(8,128)(2,1)S(1)}, bf16[256,1024]{1,0:T(8,128)(2,1)S(1)}, u32[]{:S(2)}, u32[]{:S(2)}) collective-permute-start(bf16[256,1024]{1,0:T(8,128)(2,1)S(1)} %collective-permute-done.1.refs_2_), channel_id=1, source_target_pairs={{0,1},{1,0},{2,3},{3,2},{4,5},{5,4},{6,7},{7,6},{8,9},{9,8},{10,11... | collective-permute-start | bytes 1572872 | tf_op jit(solution)/shard_map/ppermute | solution.py:357
  77.8 12.8 %collective-permute-start.6 = (bf16[256,1024]{1,0:T(8,128)(2,1)S(1)}, bf16[256,1024]{1,0:T(8,128)(2,1)S(1)}, u32[]{:S(2)}, u32[]{:S(2)}) collective-permute-start(bf16[256,1024]{1,0:T(8,128)(2,1)S(1)} %collective-permute-done.5.refs_6_), channel_id=1, source_target_pairs={{0,1},{1,0},{2,3},{3,2},{4,5},{5,4},{6,7},{7,6},{8,9},{9,8},{10,11... | collective-permute-start | bytes 1572872 | tf_op jit(solution)/shard_map/ppermute | solution.py:357
  78.6 18.8 %collective-permute-start.4 = (bf16[256,1024]{1,0:T(8,128)(2,1)S(1)}, bf16[256,1024]{1,0:T(8,128)(2,1)S(1)}, u32[]{:S(2)}, u32[]{:S(2)}) collective-permute-start(bf16[256,1024]{1,0:T(8,128)(2,1)S(1)} %collective-permute-done.3.refs_4_), channel_id=1, source_target_pairs={{0,1},{1,0},{2,3},{3,2},{4,5},{5,4},{6,7},{7,6},{8,9},{9,8},{10,11... | collective-permute-start | bytes 1572872 | tf_op jit(solution)/shard_map/ppermute | solution.py:357
  90.7 12.3 %collective-permute-start.41 = (bf16[256,256]{1,0:T(8,128)(2,1)S(1)}, bf16[256,256]{1,0:T(8,128)(2,1)S(1)}, u32[]{:S(2)}, u32[]{:S(2)}) collective-permute-start(bf16[256,256]{1,0:T(8,128)(2,1)S(1)} %get-tuple-element.53.refs_0_), channel_id=1, source_target_pairs={{0,1},{1,0},{2,3},{3,2},{4,5},{5,4},{6,7},{7,6},{8,9},{9,8},{10,11... | collective-permute-start | bytes 393224 | tf_op jit(solution)/shard_map/ppermute | solution.py:357
  94.4 12.3 %collective-permute-start.42 = (bf16[256,256]{1,0:T(8,128)(2,1)S(1)}, bf16[256,256]{1,0:T(8,128)(2,1)S(1)}, u32[]{:S(2)}, u32[]{:S(2)}) collective-permute-start(bf16[256,256]{1,0:T(8,128)(2,1)S(1)} %collective-permute-done.38.refs_1_), channel_id=1, source_target_pairs={{0,1},{1,0},{2,3},{3,2},{4,5},{5,4},{6,7},{7,6},{8,9},{9,8},{10,11... | collective-permute-start | bytes 393224 | tf_op jit(solution)/shard_map/ppermute | solution.py:357
  96.5 10.2 %collective-permute-start.43 = (bf16[256,256]{1,0:T(8,128)(2,1)S(1)}, bf16[256,256]{1,0:T(8,128)(2,1)S(1)}, u32[]{:S(2)}, u32[]{:S(2)}) collective-permute-start(bf16[256,256]{1,0:T(8,128)(2,1)S(1)} %collective-permute-done.39.refs_2_), channel_id=1, source_target_pairs={{0,1},{1,0},{2,3},{3,2},{4,5},{5,4},{6,7},{7,6},{8,9},{9,8},{10,11... | collective-permute-start | bytes 393224 | tf_op jit(solution)/shard_map/ppermute | solution.py:357
  102.9 11.0 %collective-permute-start.14 = (bf16[2,256,256]{2,1,0:T(8,128)(2,1)}, bf16[2,256,256]{2,1,0:T(8,128)(2,1)}, u32[]{:S(2)}, u32[]{:S(2)}) collective-permute-start(bf16[2,256,256]{2,1,0:T(8,128)(2,1)} %get-tuple-element.39), channel_id=1, source_target_pairs={{0,2},{1,3},{2,4},{3,5},{4,6},{5,7},{6,0},{7,1},{8,10},{9,11},{10,... | collective-permute-start | bytes 786440 | tf_op jit(solution)/shard_map/ppermute | solution.py:353
  103.0 12.0 %collective-permute-start.16 = (bf16[2,256,256]{2,1,0:T(8,128)(2,1)}, bf16[2,256,256]{2,1,0:T(8,128)(2,1)S(1)}, u32[]{:S(2)}, u32[]{:S(2)}) collective-permute-start(bf16[2,256,256]{2,1,0:T(8,128)(2,1)} %get-tuple-element.41), channel_id=1, source_target_pairs={{0,6},{1,7},{2,0},{3,1},{4,2},{5,3},{6,4},{7,5},{8,14},{9,15},{10,... | collective-permute-start | bytes 786440 | tf_op jit(solution)/shard_map/ppermute | solution.py:353
  108.5 34.7 %all-to-all-start.1 = ((bf16[16,1,128,256]{3,2,1,0:T(8,128)(2,1)}), bf16[16,1,128,256]{3,2,1,0:T(8,128)(2,1)S(1)}, u32[]{:S(2)}, u32[]{:S(2)}) async-start(bf16[16,1,128,256]{3,2,1,0:T(8,128)(2,1)} %pack.3), calls=%async_computation.1 | async-start | bytes 2097152 | tf_op jit(solution)/shard_map/all_to_all | solution.py:384
  114.9 15.0 %collective-permute-start.15 = (bf16[4,256,256]{2,1,0:T(8,128)(2,1)S(1)}, bf16[4,256,256]{2,1,0:T(8,128)(2,1)S(1)}, u32[]{:S(2)}, u32[]{:S(2)}) collective-permute-start(bf16[4,256,256]{2,1,0:T(8,128)(2,1)S(1)} %merge.2), channel_id=1, source_target_pairs={{0,2},{1,3},{2,4},{3,5},{4,6},{5,7},{6,0},{7,1},{8,10},{9,11},{10,... | collective-permute-start | bytes 1572872 | tf_op jit(solution)/shard_map/ppermute | solution.py:353
  115.1 14.8 %collective-permute-start.17 = (bf16[4,256,256]{2,1,0:T(8,128)(2,1)S(1)}, bf16[4,256,256]{2,1,0:T(8,128)(2,1)S(1)}, u32[]{:S(2)}, u32[]{:S(2)}) collective-permute-start(bf16[4,256,256]{2,1,0:T(8,128)(2,1)S(1)} %merge.3), channel_id=1, source_target_pairs={{0,6},{1,7},{2,0},{3,1},{4,2},{5,3},{6,4},{7,5},{8,14},{9,15},{10,... | collective-permute-start | bytes 1572872 | tf_op jit(solution)/shard_map/ppermute | solution.py:353
  143.3 22.9 %all-to-all-start = ((bf16[16,1,128,256]{3,2,1,0:T(8,128)(2,1)}), bf16[16,1,128,256]{3,2,1,0:T(8,128)(2,1)S(1)}, u32[]{:S(2)}, u32[]{:S(2)}) async-start(bf16[16,1,128,256]{3,2,1,0:T(8,128)(2,1)} %pack.2), calls=%async_computation | async-start | bytes 2097152 | tf_op jit(solution)/shard_map/all_to_all | solution.py:384
  (19 other events, 105.5 us)

commit v7 on v6

--- a/solution.py
+++ b/solution.py
@@ -8,6 +8,8 @@
 
 TILE = 256
 HALF = 128
+CUT = 192
+PARTS = ((0, CUT), (CUT, TILE - CUT))
 
 
 def along_y(step):
@@ -133,12 +135,28 @@
     )(*values)
 
 
-def load(pieces, place, sems):
+def load_cols(cols, place, sems):
+    return [
+        pltpu.make_async_copy(cols[2 * d + h], place(d, pl.ds(1024 * h, 1024)), sems.at[2 * d + h])
+        for d in range(4)
+        for h in range(2)
+    ]
+
+
+def load_rows(tops, lows, rows_ref, sems, part):
+    first, count = part
     copies = []
-    for d in range(4):
-        for h in range(2):
-            at = 2 * d + h
-            copies.append(pltpu.make_async_copy(pieces[at], place(d, pl.ds(1024 * h, 1024)), sems.at[at]))
+    for i in range(2):
+        for pieces, base in ((tops, 0), (lows, HALF)):
+            low, high = max(first, base), min(first + count, base + HALF)
+            for at in range(8 * (low < high)):
+                copies.append(
+                    pltpu.make_async_copy(
+                        pieces[at].at[pl.ds(i * HALF + low - base, high - low)],
+                        rows_ref.at[at // 2, pl.ds(i * count + low - first, high - low), pl.ds(1024 * (at % 2), 1024)],
+                        sems.at[len(copies)],
+                    )
+                )
     return copies
 
 
@@ -149,52 +167,67 @@
         ).astype(out.dtype)
 
 
-def product_body(*refs, first):
-    rows, cols = refs[:8], refs[8:16]
+def needs(part, tops, lows):
+    first, count = part
+    return (*(tops if first < HALF else ()), *(lows if first + count > HALF else ()))
+
+
+def split_rows(part, refs):
+    first, count = part
+    tops = refs[:8] if first < HALF else ()
+    lows = refs[len(tops) : len(tops) + 8] if first + count > HALF else ()
+    return tops, lows, refs[len(tops) + len(lows) :]
+
+
+def product_body(*refs, part, first):
+    tops, lows, refs = split_rows(part, refs)
+    cols, refs = refs[:8], refs[8:]
     rows_ref, cols_ref, row_sems, col_sems = refs[-4:]
     x, _, z, _ = position()
-    copies = load(cols, lambda d, across: cols_ref.at[(x + d) % 4, :, across], col_sems)
-    copies += load(rows, lambda d, across: rows_ref.at[d, :, across], row_sems)
+    copies = load_cols(cols, lambda d, across: cols_ref.at[(x + d) % 4, :, across], col_sems)
+    copies += load_rows(tops, lows, rows_ref, row_sems, part)
     for copy in copies:
         copy.start()
     for copy in copies:
         copy.wait()
-    up, down, next_low, prev_high = refs[16:20]
-    far_up, far_down, at = (refs[20], refs[21], 0) if first else (next_low, prev_high, 2)
+    up, down, next_low, prev_high = refs[:4]
+    far_up, far_down, at = (refs[4], refs[5], 0) if first else (next_low, prev_high, 2)
     blocks(rows_ref, cols_ref[(z + 2) % 4], ((up, 0), (up, 1), (down, 0), (down, 1)))
     blocks(rows_ref, cols_ref[(z + 1) % 4], ((next_low, 0), (next_low, 1), (far_up, at), (far_up, at + 1)))
     blocks(rows_ref, cols_ref[(z + 3) % 4], ((far_down, at), (far_down, at + 1), (prev_high, 0), (prev_high, 1)))
     if not first:
-        blocks(rows_ref, cols_ref[z], tuple((refs[20], j) for j in range(4)))
-
-
-def product(rows, cols, first):
-    four = jax.ShapeDtypeStruct((4, TILE, TILE), jnp.bfloat16)
-    two = jax.ShapeDtypeStruct((2, TILE, TILE), jnp.bfloat16)
-    kept = jax.ShapeDtypeStruct((4, TILE, TILE), jnp.float32)
+        blocks(rows_ref, cols_ref[z], tuple((refs[4], j) for j in range(4)))
+
+
+def product(part, tops, lows, cols, first):
+    four = jax.ShapeDtypeStruct((4, 2 * part[1], TILE), jnp.bfloat16)
+    two = jax.ShapeDtypeStruct((2, 2 * part[1], TILE), jnp.bfloat16)
+    kept = jax.ShapeDtypeStruct((4, 2 * part[1], TILE), jnp.float32)
     shapes = (two,) * 6 if first else (two, two, four, four, kept)
-    return pl.pallas_call(
-        lambda *refs: product_body(*refs, first=first),
+    operands = (*needs(part, tops, lows), *cols)
+    return pl.pallas_call(
+        lambda *refs: product_body(*refs, part=part, first=first),
         out_shape=shapes,
-        in_specs=[pl.BlockSpec(memory_space=pl.ANY)] * 16,
+        in_specs=[pl.BlockSpec(memory_space=pl.ANY)] * len(operands),
         out_specs=(pl.BlockSpec(memory_space=pltpu.VMEM),) * len(shapes),
         scratch_shapes=[
+            pltpu.VMEM((4, 2 * part[1], 2048), jnp.bfloat16),
             pltpu.VMEM((4, TILE, 2048), jnp.bfloat16),
-            pltpu.VMEM((4, TILE, 2048), jnp.bfloat16),
-            pltpu.SemaphoreType.DMA((8,)),
+            pltpu.SemaphoreType.DMA((32,)),
             pltpu.SemaphoreType.DMA((8,)),
         ],
         compiler_params=pltpu.CompilerParams(vmem_limit_bytes=32 * 1024 * 1024),
         name="product",
-    )(*rows, *cols)
-
-
-def kept_body(*refs):
-    rows, cols, own = refs[:8], refs[8:16], refs[16]
-    rows_ref, right_ref, row_sems, col_sems = refs[17:]
+    )(*operands)
+
+
+def kept_body(*refs, part):
+    tops, lows, refs = split_rows(part, refs)
+    cols, own = refs[:8], refs[8]
+    rows_ref, right_ref, row_sems, col_sems = refs[9:]
     x, _, z, _ = position()
-    right = load(cols, lambda d, across: right_ref.at[:, across], col_sems)
-    copies = load(rows, lambda d, across: rows_ref.at[d, :, across], row_sems)
+    right = load_cols(cols, lambda d, across: right_ref.at[:, across], col_sems)
+    copies = load_rows(tops, lows, rows_ref, row_sems, part)
     for act in (lambda copy: copy.start(), lambda copy: copy.wait()):
         for d in range(4):
 
@@ -208,21 +241,22 @@
     blocks(rows_ref, right_ref[...], tuple((own, j) for j in range(4)))
 
 
-def kept_product(rows, cols):
-    return pl.pallas_call(
-        kept_body,
-        out_shape=jax.ShapeDtypeStruct((4, TILE, TILE), jnp.float32),
-        in_specs=[pl.BlockSpec(memory_space=pl.ANY)] * 16,
+def kept_product(part, tops, lows, cols):
+    operands = (*needs(part, tops, lows), *cols)
+    return pl.pallas_call(
+        lambda *refs: kept_body(*refs, part=part),
+        out_shape=jax.ShapeDtypeStruct((4, 2 * part[1], TILE), jnp.float32),
+        in_specs=[pl.BlockSpec(memory_space=pl.ANY)] * len(operands),
         out_specs=pl.BlockSpec(memory_space=pltpu.VMEM),
         scratch_shapes=[
-            pltpu.VMEM((4, TILE, 2048), jnp.bfloat16),
+            pltpu.VMEM((4, 2 * part[1], 2048), jnp.bfloat16),
             pltpu.VMEM((TILE, 2048), jnp.bfloat16),
-            pltpu.SemaphoreType.DMA((8,)),
+            pltpu.SemaphoreType.DMA((32,)),
             pltpu.SemaphoreType.DMA((8,)),
         ],
         compiler_params=pltpu.CompilerParams(vmem_limit_bytes=32 * 1024 * 1024),
         name="kept",
-    )(*rows, *cols)
+    )(*operands)
 
 
 def finish_body(own, far_up, far_down, sum_up, sum_down, *outs):
@@ -237,7 +271,7 @@
 
 
 def finish(*parts):
-    piece = jax.ShapeDtypeStruct((TILE, TILE), jnp.bfloat16)
+    piece = jax.ShapeDtypeStruct(parts[0].shape[1:], jnp.bfloat16)
     return pl.pallas_call(
         finish_body,
         out_shape=(piece,) * 4,
@@ -265,8 +299,10 @@
     )(share, got)
 
 
-def pack_body(owners_ref, *refs):
-    arrived, out_ref, zero_ref, sems, zero_sems = refs[:8], refs[8], refs[9], refs[10], refs[11]
+def pack_body(owners_ref, *refs, part):
+    arrived = refs[:8]
+    out_ref, zero_ref, sems, zero_sems = refs[-4:]
+    first, count = part
     _, y, _, k = position()
 
     def tiles(e):
@@ -277,8 +313,8 @@
                 owner = owners_ref[i, 2 * (line & 1) + parity]
                 found.append(
                     pltpu.make_async_copy(
-                        source.at[pl.ds(i * HALF, HALF)],
-                        out_ref.at[owner, 0],
+                        source.at[pl.ds(i * count, count)],
+                        out_ref.at[owner, 0, pl.ds(first, count)],
                         sems.at[4 * e + len(found)],
                     )
                 )
@@ -293,8 +329,8 @@
         ]
 
     def each(act):
-        for make, count in ((tiles, 4), (blank, 16)):
-            for at in range(count):
+        for make, many in ((tiles, 4), (blank, 16 * (first == 0))):
+            for at in range(many):
                 wanted, found = make(at)
 
                 @pl.when(wanted)
@@ -302,43 +338,28 @@
                     for copy in found:
                         act(copy)
 
-    zero_ref[...] = jnp.zeros_like(zero_ref)
+    if first == 0:
+        zero_ref[...] = jnp.zeros_like(zero_ref)
     each(lambda copy: copy.start())
     each(lambda copy: copy.wait())
 
 
-def pack(owners, arrived):
-    return pl.pallas_call(
-        pack_body,
-        out_shape=jax.ShapeDtypeStruct((16, 1, HALF, TILE), jnp.bfloat16),
-        in_specs=[pl.BlockSpec(memory_space=pltpu.SMEM)] + [pl.BlockSpec(memory_space=pl.ANY)] * 8,
+def pack(part, owners, arrived, *whole):
+    return pl.pallas_call(
+        lambda *refs: pack_body(*refs, part=part),
+        out_shape=jax.ShapeDtypeStruct((16, 1, TILE, TILE), jnp.bfloat16),
+        in_specs=[pl.BlockSpec(memory_space=pltpu.SMEM)]
+        + [pl.BlockSpec(memory_space=pl.ANY)] * (8 + len(whole)),
         out_specs=pl.BlockSpec(memory_space=pl.ANY),
         scratch_shapes=[
-            pltpu.VMEM((HALF, TILE), jnp.bfloat16),
+            pltpu.VMEM((TILE, TILE), jnp.bfloat16),
             pltpu.SemaphoreType.DMA((16,)),
             pltpu.SemaphoreType.DMA((16,)),
         ],
+        input_output_aliases={9: 0} if whole else {},
         compiler_params=pltpu.CompilerParams(vmem_limit_bytes=2 * 1024 * 1024),
         name="pack",
-    )(owners, *arrived)
-
-
-def place_half(half, value, *whole):
-    def body(value_ref, *refs):
-        out_ref, sem = refs[-2:]
-        copy = pltpu.make_async_copy(value_ref, out_ref.at[:, :, pl.ds(half * HALF, HALF)], sem)
-        copy.start()
-        copy.wait()
-
-    return pl.pallas_call(
-        body,
-        out_shape=jax.ShapeDtypeStruct((16, 1, TILE, TILE), jnp.bfloat16),
-        in_specs=[pl.BlockSpec(memory_space=pl.ANY)] * (1 + len(whole)),
-        out_specs=pl.BlockSpec(memory_space=pl.ANY),
-        scratch_shapes=[pltpu.SemaphoreType.DMA],
-        input_output_aliases={1: 0} if whole else {},
-        compiler_params=pltpu.CompilerParams(vmem_limit_bytes=1024 * 1024),
-    )(value, *whole)
+    )(owners, *arrived, *whole)
 
 
 def ypass(value, step):
@@ -374,14 +395,12 @@
     return finish(own, far_up, far_down, sum_up, sum_down)
 
 
-def to_owners(owners, sums):
+def exchange(sums):
     own, after, opp, before = sums
     from_opp = ypass(opp, 2)
     from_before, from_after = ypass(after, 1), ypass(before, -1)
     mine = (own, from_after, from_opp, from_before)
-    other = [swap(value) for value in mine]
-    outgoing = pack(owners, (*mine, *other))
-    return lax.all_to_all(outgoing, "row", split_axis=0, concat_axis=0, tiled=True)
+    return (*mine, *(swap(value) for value in mine))
 
 
 def shards(panels, scaling, tile_mask, owner_rows):
@@ -396,20 +415,18 @@
     sent_top, sent_low = top, low
     c0, top, low = stage(c0, top, low)
     cols = (c0, c1, cp0, cp1, co0, co1, cm0, cm1)
-    halves = []
+    rows = []
     for own, pieces in (
         (top, (sent_top, top_p, top_o, top_m)), (low, (sent_low, low_p, low_o, low_m))
     ):
         others = [swap(value) for value in pieces]
-        rows = [piece for pair in zip((own, *pieces[1:]), others) for piece in pair]
-        if halves:
-            halves.append(product(rows, cols, False))
-        else:
-            sent = product(rows, cols, True)
-            halves.append((*sent, kept_product(rows, cols)))
-    first = to_owners(owner_rows, reduce_along_z(halves[0]))
-    second = to_owners(owner_rows, reduce_along_z(halves[1]))
-    return place_half(1, second, place_half(0, first))
+        rows.append([piece for pair in zip((own, *pieces[1:]), others) for piece in pair])
+    sent = product(PARTS[0], *rows, cols, True)
+    kept = kept_product(PARTS[0], *rows, cols)
+    later = product(PARTS[1], *rows, cols, False)
+    outgoing = pack(PARTS[0], owner_rows, exchange(reduce_along_z((*sent, kept))))
+    outgoing = pack(PARTS[1], owner_rows, exchange(reduce_along_z(later)), outgoing)
+    return lax.all_to_all(outgoing, "row", split_axis=0, concat_axis=0, tiled=True)
 
 
 def solution(mesh):

time: 168 us -> 189 us (1.12)
  blocking collectives: 0 us -> 33.6 us
  waiting for transfers between devices: 96.3 us -> 82.6 us
  Pallas kernels: 21.5 us -> 24.3 us
  starting transfers between devices: 45.8 us -> 43.8 us
    all_to_all x0 -> x1, blocking collectives: none -> 33.6 us  [shards(): lax.all_to_all(outgoing, 'row', split_axis=0, concat_axis=0, tiled=True)]
    all_to_all x2 -> x0, waiting for transfers between devices: 17.1 us -> none  [to_owners(): lax.all_to_all(outgoing, 'row', split_axis=0, concat_axis=0, tiled=True)]
    ppermute x6, waiting for transfers between devices: 16.9 us -> 31.5 us  [xpass(): return lax.ppermute(value, 'row', along_x(step))]
    ppermute x10, waiting for transfers between devices: 30.1 us -> 17.6 us  [zpass(): return lax.ppermute(value, 'col', along_z(step))]
    all_to_all x2 -> x0, starting transfers between devices: 8.39 us -> none  [to_owners(): lax.all_to_all(outgoing, 'row', split_axis=0, concat_axis=0, tiled=True)]
    pallas_call x7 -> x5, Pallas kernels: 17.3 us -> 21.2 us  [the longest x2 13.3 us: product(): pl.pallas_call(lambda *refs: product_body(*refs, part=part, first=first),...]
    ppermute x10, starting transfers between devices: 15 us -> 18.1 us  [zpass(): return lax.ppermute(value, 'col', along_z(step))]
    ppermute x12, waiting for transfers between devices: 30.8 us -> 33.4 us  [ypass(): return lax.ppermute(value, 'row', along_y(step))]
  transfers between devices with their start and end apart: 47 -> 45, of which waited for: 20 -> 18; matrix products, arithmetic and copies ran while one was open for 0% -> 0% of each run, Pallas kernels for 11% -> 7%
where the time goes in v7:
time: 189 us
  waiting for transfers between devices  82.6 us (44%)
  starting transfers between devices  43.8 us (23%)
  blocking collectives  33.6 us (18%)
  Pallas kernels  24.3 us (13%)
  local copies, waits for them, and re-layouts  4.45 us (2%)
    all_to_all x1, blocking collectives, shards(): lax.all_to_all(outgoing, 'row', split_axis=0, concat_axis=0, tiled=True)  33.6 us
    ppermute x12, waiting for transfers between devices, ypass(): return lax.ppermute(value, 'row', along_y(step))  33.4 us
    ppermute x6, waiting for transfers between devices, xpass(): return lax.ppermute(value, 'row', along_x(step))  31.5 us
    ppermute x10, starting transfers between devices, zpass(): return lax.ppermute(value, 'col', along_z(step))  18.1 us
    ppermute x10, waiting for transfers between devices, zpass(): return lax.ppermute(value, 'col', along_z(step))  17.6 us
    ppermute x12, starting transfers between devices, ypass(): return lax.ppermute(value, 'row', along_y(step))  15.4 us
    pallas_call x2, Pallas kernels, product(): pl.pallas_call(lambda *refs: product_body(*refs, part=part, first=first),...  13.3 us
    ppermute x6, starting transfers between devices, xpass(): return lax.ppermute(value, 'row', along_x(step))  8.71 us
  transfers between devices with their start and end apart: 45, of which 18 were waited for; matrix products, arithmetic and copies ran while one was open for 0% of the time, Pallas kernels for 7%

profile of v7, /device:TPU:0, one launch (start us, length us, event | category | flops | bytes accessed | tf_op | source)
XLA Modules:
  0.0 189.2 jit_solution(7511131607339376819)
XLA Ops:
  0.0 2.6 %scale.1 = (bf16[256,1024]{1,0:T(8,128)(2,1)}, bf16[256,1024]{1,0:T(8,128)(2,1)}, bf16[256,1024]{1,0:T(8,128)(2,1)}, bf16[256,1024]{1,0:T(8,128)(2,1)}) custom-call(s32[2,32]{1,0:T(2,128)} %mask_hbm.1, bf16[512,1024]{1,0:T(8,128)(2,1)} %panels_hbm.1, f32[1,1024]{1,0:T(1,128)} %bitcast.1), custom_call_target="tpu_custom_call" | custom-call | tf_op jit(solution)/shard_map/scale/pallas_call | solution.py:100
  2.7 3.2 %collective-permute-start.1 = (bf16[256,1024]{1,0:T(8,128)(2,1)}, bf16[256,1024]{1,0:T(8,128)(2,1)S(1)}, u32[]{:S(2)}, u32[]{:S(2)}) collective-permute-start(bf16[256,1024]{1,0:T(8,128)(2,1)} %get-tuple-element.33.refs_2_), channel_id=1, source_target_pairs={{0,24},{8,0},{16,8},{24,16},{32,56},{40,32},{48,40},{56,48},{64,88... | collective-permute-start | bytes 1572872 | tf_op jit(solution)/shard_map/ppermute | solution.py:366
  6.4 1.5 collective-permute-start.10
  7.9 9.4 %collective-permute-done.1.refs_2_.refs_10_ = bf16[256,1024]{1,0:T(8,128)(2,1)S(1)} collective-permute-done((bf16[256,1024]{1,0:T(8,128)(2,1)}, bf16[256,1024]{1,0:T(8,128)(2,1)S(1)}, u32[]{:S(2)}, u32[]{:S(2)}) %collective-permute-start.1) | collective-permute-done | bytes 524320 | tf_op jit(solution)/shard_map/ppermute | solution.py:366
  17.3 3.6 %collective-permute-start.26 = (bf16[256,1024]{1,0:T(8,128)(2,1)}, bf16[256,1024]{1,0:T(8,128)(2,1)S(1)}, u32[]{:S(2)}, u32[]{:S(2)}) collective-permute-start(bf16[256,1024]{1,0:T(8,128)(2,1)} %get-tuple-element.32.refs_1_), channel_id=1, source_target_pairs={{0,24},{8,0},{16,8},{24,16},{32,56},{40,32},{48,40},{56,48},{64,88... | collective-permute-start | bytes 1572872 | tf_op jit(solution)/shard_map/ppermute | solution.py:366
  22.1 10.8 %collective-permute-done.5.refs_6_.refs_14_ = bf16[256,1024]{1,0:T(8,128)(2,1)S(1)} collective-permute-done((bf16[256,1024]{1,0:T(8,128)(2,1)}, bf16[256,1024]{1,0:T(8,128)(2,1)S(1)}, u32[]{:S(2)}, u32[]{:S(2)}) %collective-permute-start.5) | collective-permute-done | bytes 524320 | tf_op jit(solution)/shard_map/ppermute | solution.py:366
  32.8 2.8 %collective-permute-start.8 = (bf16[256,1024]{1,0:T(8,128)(2,1)}, bf16[256,1024]{1,0:T(8,128)(2,1)S(1)}, u32[]{:S(2)}, u32[]{:S(2)}) collective-permute-start(bf16[256,1024]{1,0:T(8,128)(2,1)} %get-tuple-element.31.refs_0_), channel_id=1, source_target_pairs={{0,96},{8,104},{16,112},{24,120},{32,0},{40,8},{48,16},{56,24},{64... | collective-permute-start | bytes 1572872 | tf_op jit(solution)/shard_map/ppermute | solution.py:370
  36.5 2.0 %collective-permute-start.29 = (bf16[256,1024]{1,0:T(8,128)(2,1)S(1)}, bf16[256,1024]{1,0:T(8,128)(2,1)S(1)}, u32[]{:S(2)}, u32[]{:S(2)}) collective-permute-start(bf16[256,1024]{1,0:T(8,128)(2,1)S(1)} %collective-permute-done.28.refs_6_), channel_id=1, source_target_pairs={{0,8},{8,16},{16,24},{24,0},{32,40},{40,48},{48,56},{56,32},{64,72... | collective-permute-start | bytes 1572872 | tf_op jit(solution)/shard_map/ppermute | solution.py:366
  38.5 9.8 %collective-permute-done.8.refs_10_.refs_18_ = bf16[256,1024]{1,0:T(8,128)(2,1)S(1)} collective-permute-done((bf16[256,1024]{1,0:T(8,128)(2,1)}, bf16[256,1024]{1,0:T(8,128)(2,1)S(1)}, u32[]{:S(2)}, u32[]{:S(2)}) %collective-permute-start.8) | collective-permute-done | bytes 524320 | tf_op jit(solution)/shard_map/ppermute | solution.py:370
  49.3 8.7 %collective-permute-done.9.refs_11_.refs_19_ = bf16[256,1024]{1,0:T(8,128)(2,1)S(1)} collective-permute-done((bf16[256,1024]{1,0:T(8,128)(2,1)S(1)}, bf16[256,1024]{1,0:T(8,128)(2,1)S(1)}, u32[]{:S(2)}, u32[]{:S(2)}) %collective-permute-start.9) | collective-permute-done | bytes 524320 | tf_op jit(solution)/shard_map/ppermute | solution.py:370
  59.8 5.0 %collective-permute-done.11.refs_12_.refs_20_ = bf16[256,1024]{1,0:T(8,128)(2,1)S(1)} collective-permute-done((bf16[256,1024]{1,0:T(8,128)(2,1)S(1)}, bf16[256,1024]{1,0:T(8,128)(2,1)S(1)}, u32[]{:S(2)}, u32[]{:S(2)}) %collective-permute-start.11) | collective-permute-done | bytes 524320 | tf_op jit(solution)/shard_map/ppermute | solution.py:370
  64.8 1.8 collective-permute-start.12
  69.9 5.8 %collective-permute-done.13.refs_15_.refs_23_ = bf16[256,1024]{1,0:T(8,128)(2,1)S(1)} collective-permute-done((bf16[256,1024]{1,0:T(8,128)(2,1)S(1)}, bf16[256,1024]{1,0:T(8,128)(2,1)S(1)}, u32[]{:S(2)}, u32[]{:S(2)}) %collective-permute-start.13) | collective-permute-done | bytes 524320 | tf_op jit(solution)/shard_map/ppermute | solution.py:370
  75.7 2.3 %collective-permute-done.12.refs_13_.refs_21_ = bf16[256,1024]{1,0:T(8,128)(2,1)S(1)} collective-permute-done((bf16[256,1024]{1,0:T(8,128)(2,1)S(1)}, bf16[256,1024]{1,0:T(8,128)(2,1)S(1)}, u32[]{:S(2)}, u32[]{:S(2)}) %collective-permute-start.12) | collective-permute-done | bytes 524320 | tf_op jit(solution)/shard_map/ppermute | solution.py:370
  78.0 6.6 %product.3 = (bf16[2,384,256]{2,1,0:T(8,128)(2,1)S(1)}, bf16[2,384,256]{2,1,0:T(8,128)(2,1)S(1)}, bf16[2,384,256]{2,1,0:T(8,128)(2,1)S(1)}, bf16[2,384,256]{2,1,...) custom-call(bf16[256,1024]{1,0:T(8,128)(2,1)S(1)} %get-tuple-element.46.refs_0_, ...), custom_call_target="tpu_custom_call" | custom-call | tf_op jit(solution)/shard_map/product/pallas_call | solution.py:208
  84.5 4.3 %collective-permute-start.36 = (bf16[2,384,256]{2,1,0:T(8,128)(2,1)S(1)}, bf16[2,384,256]{2,1,0:T(8,128)(2,1)S(1)}, u32[]{:S(2)}, u32[]{:S(2)}) collective-permute-start(bf16[2,384,256]{2,1,0:T(8,128)(2,1)S(1)} %get-tuple-element.52), channel_id=1, source_target_pairs={{0,6},{1,7},{2,0},{3,1},{4,2},{5,3},{6,4},{7,5},{8,14},{9,15},{10,... | collective-permute-start | bytes 1179656 | tf_op jit(solution)/shard_map/ppermute | solution.py:374
  88.8 3.3 %collective-permute-start.33 = (bf16[2,384,256]{2,1,0:T(8,128)(2,1)S(1)}, bf16[2,384,256]{2,1,0:T(8,128)(2,1)S(1)}, u32[]{:S(2)}, u32[]{:S(2)}) collective-permute-start(bf16[2,384,256]{2,1,0:T(8,128)(2,1)S(1)} %get-tuple-element.48), channel_id=1, source_target_pairs={{0,6},{1,7},{2,0},{3,1},{4,2},{5,3},{6,4},{7,5},{8,14},{9,15},{10,... | collective-permute-start | bytes 1179656 | tf_op jit(solution)/shard_map/ppermute | solution.py:374
  92.1 6.2 %collective-permute-done.36 = bf16[2,384,256]{2,1,0:T(8,128)(2,1)S(1)} collective-permute-done((bf16[2,384,256]{2,1,0:T(8,128)(2,1)S(1)}, bf16[2,384,256]{2,1,0:T(8,128)(2,1)S(1)}, u32[]{:S(2)}, u32[]{:S(2)}) %collective-permute-start.36) | collective-permute-done | bytes 393248 | tf_op jit(solution)/shard_map/ppermute | solution.py:374
  98.4 3.8 %collective-permute-start.37 = (bf16[2,384,256]{2,1,0:T(8,128)(2,1)S(1)}, bf16[2,384,256]{2,1,0:T(8,128)(2,1)S(1)}, u32[]{:S(2)}, u32[]{:S(2)}) collective-permute-start(bf16[2,384,256]{2,1,0:T(8,128)(2,1)S(1)} %add_convert_fusion), channel_id=1, source_target_pairs={{0,6},{1,7},{2,0},{3,1},{4,2},{5,3},{6,4},{7,5},{8,14},{9,15},{10,... | collective-permute-start | bytes 1179656 | tf_op jit(solution)/shard_map/ppermute | solution.py:374
  102.4 6.7 %product.2 = (bf16[2,128,256]{2,1,0:T(8,128)(2,1)S(1)}, bf16[2,128,256]{2,1,0:T(8,128)(2,1)S(1)}, bf16[4,128,256]{2,1,0:T(8,128)(2,1)S(1)}, bf16[4,128,256]{2,1,0:T(8,128)(2,1)S(1)}, f32[4,128,256]{2,1,0:T(8,128)S(1)}) custom-call(bf16[256,1024]{1,0:T(8,128)(2,1)S(1)} %get-tuple-element.34.refs_0_.refs_8_, ...), custom_call_target="tpu_custom_call" | custom-call | tf_op jit(solution)/shard_map/product/pallas_call | solution.py:208
  109.1 3.3 %collective-permute-start.16 = (bf16[2,128,256]{2,1,0:T(8,128)(2,1)S(1)}, bf16[2,128,256]{2,1,0:T(8,128)(2,1)S(1)}, u32[]{:S(2)}, u32[]{:S(2)}) collective-permute-start(bf16[2,128,256]{2,1,0:T(8,128)(2,1)S(1)} %get-tuple-element.41), channel_id=1, source_target_pairs={{0,6},{1,7},{2,0},{3,1},{4,2},{5,3},{6,4},{7,5},{8,14},{9,15},{10,... | collective-permute-start | bytes 393224 | tf_op jit(solution)/shard_map/ppermute | solution.py:374
  112.3 3.2 %collective-permute-done.16.got_ref = bf16[2,128,256]{2,1,0:T(8,128)(2,1)S(1)} collective-permute-done((bf16[2,128,256]{2,1,0:T(8,128)(2,1)S(1)}, bf16[2,128,256]{2,1,0:T(8,128)(2,1)S(1)}, u32[]{:S(2)}, u32[]{:S(2)}) %collective-permute-start.16) | collective-permute-done | bytes 131104 | tf_op jit(solution)/shard_map/ppermute | solution.py:374
  116.1 6.1 %collective-permute-done.14.got_ref = bf16[2,128,256]{2,1,0:T(8,128)(2,1)S(1)} collective-permute-done((bf16[2,128,256]{2,1,0:T(8,128)(2,1)S(1)}, bf16[2,128,256]{2,1,0:T(8,128)(2,1)S(1)}, u32[]{:S(2)}, u32[]{:S(2)}) %collective-permute-start.14) | collective-permute-done | bytes 131104 | tf_op jit(solution)/shard_map/ppermute | solution.py:374
  122.1 2.9 %collective-permute-start.17 = (bf16[4,128,256]{2,1,0:T(8,128)(2,1)S(1)}, bf16[4,128,256]{2,1,0:T(8,128)(2,1)S(1)}, u32[]{:S(2)}, u32[]{:S(2)}) collective-permute-start(bf16[4,128,256]{2,1,0:T(8,128)(2,1)S(1)} %merge.3), channel_id=1, source_target_pairs={{0,6},{1,7},{2,0},{3,1},{4,2},{5,3},{6,4},{7,5},{8,14},{9,15},{10,... | collective-permute-start | bytes 786440 | tf_op jit(solution)/shard_map/ppermute | solution.py:374
  125.1 3.1 %kept.1.own = f32[4,384,256]{2,1,0:T(8,128)S(1)} custom-call(bf16[256,1024]{1,0:T(8,128)(2,1)S(1)} %get-tuple-element.46.refs_0_, bf16[256,1024]{1,0:T(8,128)(2,1)S(1)} %collective-permute-done.25.refs_1_, bf16[256,1024]{1,0:T(8,128)(2,1)S(1)} %collective-permute-done.26.refs_2_, bf16[256,1024]{1,0:T(8,128)(2,1)S(1)} %collective-permute-done.27.refs_3_, ...), custom_call_target="tpu_custom_call" | custom-call | tf_op jit(solution)/shard_map/kept/pallas_call | solution.py:246
  130.6 2.1 %collective-permute-done.15.far_up.sum_up = bf16[4,128,256]{2,1,0:T(8,128)(2,1)S(1)} collective-permute-done((bf16[4,128,256]{2,1,0:T(8,128)(2,1)S(1)}, bf16[4,128,256]{2,1,0:T(8,128)(2,1)S(1)}, u32[]{:S(2)}, u32[]{:S(2)}) %collective-permute-start.15) | collective-permute-done | bytes 262176 | tf_op jit(solution)/shard_map/ppermute | solution.py:374
  134.2 1.7 collective-permute-done.39.refs_3_
  137.1 2.0 %collective-permute-start.19 = (bf16[128,256]{1,0:T(8,128)(2,1)S(1)}, bf16[128,256]{1,0:T(8,128)(2,1)S(1)}, u32[]{:S(2)}, u32[]{:S(2)}) collective-permute-start(bf16[128,256]{1,0:T(8,128)(2,1)S(1)} %get-tuple-element.44), channel_id=1, source_target_pairs={{0,16},{8,24},{16,0},{24,8},{32,48},{40,56},{48,32},{56,40},{64,80... | collective-permute-start | bytes 196616 | tf_op jit(solution)/shard_map/ppermute | solution.py:366
  139.1 3.7 %collective-permute-done.19.refs_3_ = bf16[128,256]{1,0:T(8,128)(2,1)S(1)} collective-permute-done((bf16[128,256]{1,0:T(8,128)(2,1)S(1)}, bf16[128,256]{1,0:T(8,128)(2,1)S(1)}, u32[]{:S(2)}, u32[]{:S(2)}) %collective-permute-start.19) | collective-permute-done | bytes 65568 | tf_op jit(solution)/shard_map/ppermute | solution.py:366
  144.2 4.1 %collective-permute-done.20.refs_4_ = bf16[128,256]{1,0:T(8,128)(2,1)S(1)} collective-permute-done((bf16[128,256]{1,0:T(8,128)(2,1)S(1)}, bf16[128,256]{1,0:T(8,128)(2,1)S(1)}, u32[]{:S(2)}, u32[]{:S(2)}) %collective-permute-start.20) | collective-permute-done | bytes 65568 | tf_op jit(solution)/shard_map/ppermute | solution.py:366
  149.4 3.6 %pack.2.refs_9_ = bf16[16,1,256,256]{3,2,1,0:T(8,128)(2,1)S(1)} custom-call(s32[2,4]{1,0:T(2,128)S(1)} %copy-done.3, bf16[384,256]{1,0:T(8,128)(2,1)S(1)} %get-tuple-element.53.refs_1_, bf16[384,256]{1,0:T(8,128)(2,1)S(1)} %collective-permute-done.38.refs_2_, bf16[384,256]{1,0:T(8,128)(2,1)S(1)} %collective-permute-done.39.refs_3_, ...), custom_call_target="tpu_custom_call" | custom-call | tf_op jit(solution)/shard_map/pack/pallas_call | solution.py:348
  154.3 33.6 %all_to_all.5 = bf16[16,1,256,256]{3,2,1,0:T(8,128)(2,1)S(1)} all-to-all(bf16[16,1,256,256]{3,2,1,0:T(8,128)(2,1)S(1)} %pack.3), channel_id=1, replica_groups=mesh['row'=16,'col'=8] {'row'}, dimensions={0} | all-to-all | bytes 4194304 | tf_op jit(solution)/shard_map/all_to_all | solution.py:429
  (81 shorter events, 19.7 us)
Async XLA Ops:
  2.7 14.7 %collective-permute-start.1 = (bf16[256,1024]{1,0:T(8,128)(2,1)}, bf16[256,1024]{1,0:T(8,128)(2,1)S(1)}, u32[]{:S(2)}, u32[]{:S(2)}) collective-permute-start(bf16[256,1024]{1,0:T(8,128)(2,1)} %get-tuple-element.33.refs_2_), channel_id=1, source_target_pairs={{0,24},{8,0},{16,8},{24,16},{32,56},{40,32},{48,40},{56,48},{64,88... | collective-permute-start | bytes 1572872 | tf_op jit(solution)/shard_map/ppermute | solution.py:366
  5.8 15.1 %collective-permute-start.7 = (bf16[256,1024]{1,0:T(8,128)(2,1)}, bf16[256,1024]{1,0:T(8,128)(2,1)S(1)}, u32[]{:S(2)}, u32[]{:S(2)}) collective-permute-start(bf16[256,1024]{1,0:T(8,128)(2,1)} %get-tuple-element.36), channel_id=1, source_target_pairs={{0,1},{1,0},{2,3},{3,2},{4,5},{5,4},{6,7},{7,6},{8,9},{9,8},{10,11... | collective-permute-start | bytes 1572872 | tf_op jit(solution)/shard_map/ppermute | solution.py:378
  5.8 16.2 %collective-permute-start.28 = (bf16[256,1024]{1,0:T(8,128)(2,1)}, bf16[256,1024]{1,0:T(8,128)(2,1)S(1)}, u32[]{:S(2)}, u32[]{:S(2)}) collective-permute-start(bf16[256,1024]{1,0:T(8,128)(2,1)} %get-tuple-element.32.refs_1_), channel_id=1, source_target_pairs={{0,8},{8,16},{16,24},{24,0},{32,40},{40,48},{48,56},{56,32},{64,72... | collective-permute-start | bytes 1572872 | tf_op jit(solution)/shard_map/ppermute | solution.py:366
  5.9 27.0 %collective-permute-start.5 = (bf16[256,1024]{1,0:T(8,128)(2,1)}, bf16[256,1024]{1,0:T(8,128)(2,1)S(1)}, u32[]{:S(2)}, u32[]{:S(2)}) collective-permute-start(bf16[256,1024]{1,0:T(8,128)(2,1)} %get-tuple-element.33.refs_2_), channel_id=1, source_target_pairs={{0,8},{8,16},{16,24},{24,0},{32,40},{40,48},{48,56},{56,32},{64,72... | collective-permute-start | bytes 1572872 | tf_op jit(solution)/shard_map/ppermute | solution.py:366
  6.4 29.2 %collective-permute-start.10 = (bf16[256,1024]{1,0:T(8,128)(2,1)}, bf16[256,1024]{1,0:T(8,128)(2,1)S(1)}, u32[]{:S(2)}, u32[]{:S(2)}) collective-permute-start(bf16[256,1024]{1,0:T(8,128)(2,1)} %get-tuple-element.31.refs_0_), channel_id=1, source_target_pairs={{0,32},{8,40},{16,48},{24,56},{32,64},{40,72},{48,80},{56,88},{64,... | collective-permute-start | bytes 1572872 | tf_op jit(solution)/shard_map/ppermute | solution.py:370
  17.3 18.3 %collective-permute-start.26 = (bf16[256,1024]{1,0:T(8,128)(2,1)}, bf16[256,1024]{1,0:T(8,128)(2,1)S(1)}, u32[]{:S(2)}, u32[]{:S(2)}) collective-permute-start(bf16[256,1024]{1,0:T(8,128)(2,1)} %get-tuple-element.32.refs_1_), channel_id=1, source_target_pairs={{0,24},{8,0},{16,8},{24,16},{32,56},{40,32},{48,40},{56,48},{64,88... | collective-permute-start | bytes 1572872 | tf_op jit(solution)/shard_map/ppermute | solution.py:366
  20.9 15.6 %collective-permute-start = (bf16[256,1024]{1,0:T(8,128)(2,1)}, bf16[256,1024]{1,0:T(8,128)(2,1)S(1)}, u32[]{:S(2)}, u32[]{:S(2)}) collective-permute-start(bf16[256,1024]{1,0:T(8,128)(2,1)} %get-tuple-element.33.refs_2_), channel_id=1, source_target_pairs={{0,1},{1,0},{2,3},{3,2},{4,5},{5,4},{6,7},{7,6},{8,9},{9,8},{10,11... | collective-permute-start | bytes 1572872 | tf_op jit(solution)/shard_map/ppermute | solution.py:378
  22.1 16.4 %collective-permute-start.25 = (bf16[256,1024]{1,0:T(8,128)(2,1)}, bf16[256,1024]{1,0:T(8,128)(2,1)S(1)}, u32[]{:S(2)}, u32[]{:S(2)}) collective-permute-start(bf16[256,1024]{1,0:T(8,128)(2,1)} %get-tuple-element.32.refs_1_), channel_id=1, source_target_pairs={{0,1},{1,0},{2,3},{3,2},{4,5},{5,4},{6,7},{7,6},{8,9},{9,8},{10,11... | collective-permute-start | bytes 1572872 | tf_op jit(solution)/shard_map/ppermute | solution.py:378
  32.8 15.4 %collective-permute-start.8 = (bf16[256,1024]{1,0:T(8,128)(2,1)}, bf16[256,1024]{1,0:T(8,128)(2,1)S(1)}, u32[]{:S(2)}, u32[]{:S(2)}) collective-permute-start(bf16[256,1024]{1,0:T(8,128)(2,1)} %get-tuple-element.31.refs_0_), channel_id=1, source_target_pairs={{0,96},{8,104},{16,112},{24,120},{32,0},{40,8},{48,16},{56,24},{64... | collective-permute-start | bytes 1572872 | tf_op jit(solution)/shard_map/ppermute | solution.py:370
  35.6 13.2 %collective-permute-start.3 = (bf16[256,1024]{1,0:T(8,128)(2,1)S(1)}, bf16[256,1024]{1,0:T(8,128)(2,1)S(1)}, u32[]{:S(2)}, u32[]{:S(2)}) collective-permute-start(bf16[256,1024]{1,0:T(8,128)(2,1)S(1)} %collective-permute-done.1.refs_2_.refs_10_), channel_id=1, source_target_pairs={{0,24},{8,0},{16,8},{24,16},{32,56},{40,32},{48,40},{56,48},{64,88... | collective-permute-start | bytes 1572872 | tf_op jit(solution)/shard_map/ppermute | solution.py:366
  35.6 22.4 %collective-permute-start.9 = (bf16[256,1024]{1,0:T(8,128)(2,1)S(1)}, bf16[256,1024]{1,0:T(8,128)(2,1)S(1)}, u32[]{:S(2)}, u32[]{:S(2)}) collective-permute-start(bf16[256,1024]{1,0:T(8,128)(2,1)S(1)} %collective-permute-done.7.refs_9_.refs_17_), channel_id=1, source_target_pairs={{0,96},{8,104},{16,112},{24,120},{32,0},{40,8},{48,16},{56,24},{64... | collective-permute-start | bytes 1572872 | tf_op jit(solution)/shard_map/ppermute | solution.py:370
  36.5 21.5 %collective-permute-start.29 = (bf16[256,1024]{1,0:T(8,128)(2,1)S(1)}, bf16[256,1024]{1,0:T(8,128)(2,1)S(1)}, u32[]{:S(2)}, u32[]{:S(2)}) collective-permute-start(bf16[256,1024]{1,0:T(8,128)(2,1)S(1)} %collective-permute-done.28.refs_6_), channel_id=1, source_target_pairs={{0,8},{8,16},{16,24},{24,0},{32,40},{40,48},{48,56},{56,32},{64,72... | collective-permute-start | bytes 1572872 | tf_op jit(solution)/shard_map/ppermute | solution.py:366
  38.5 20.8 %collective-permute-start.2 = (bf16[256,1024]{1,0:T(8,128)(2,1)S(1)}, bf16[256,1024]{1,0:T(8,128)(2,1)S(1)}, u32[]{:S(2)}, u32[]{:S(2)}) collective-permute-start(bf16[256,1024]{1,0:T(8,128)(2,1)S(1)} %collective-permute-done.1.refs_2_.refs_10_), channel_id=1, source_target_pairs={{0,1},{1,0},{2,3},{3,2},{4,5},{5,4},{6,7},{7,6},{8,9},{9,8},{10,11... | collective-permute-start | bytes 1572872 | tf_op jit(solution)/shard_map/ppermute | solution.py:378
  48.2 11.3 %collective-permute-start.6 = (bf16[256,1024]{1,0:T(8,128)(2,1)S(1)}, bf16[256,1024]{1,0:T(8,128)(2,1)S(1)}, u32[]{:S(2)}, u32[]{:S(2)}) collective-permute-start(bf16[256,1024]{1,0:T(8,128)(2,1)S(1)} %collective-permute-done.5.refs_6_.refs_14_), channel_id=1, source_target_pairs={{0,1},{1,0},{2,3},{3,2},{4,5},{5,4},{6,7},{7,6},{8,9},{9,8},{10,11... | collective-permute-start | bytes 1572872 | tf_op jit(solution)/shard_map/ppermute | solution.py:378
  48.8 16.0 %collective-permute-start.11 = (bf16[256,1024]{1,0:T(8,128)(2,1)S(1)}, bf16[256,1024]{1,0:T(8,128)(2,1)S(1)}, u32[]{:S(2)}, u32[]{:S(2)}) collective-permute-start(bf16[256,1024]{1,0:T(8,128)(2,1)S(1)} %collective-permute-done.10.refs_14_.refs_22_), channel_id=1, source_target_pairs={{0,32},{8,40},{16,48},{24,56},{32,64},{40,72},{48,80},{56,88},{64,... | collective-permute-start | bytes 1572872 | tf_op jit(solution)/shard_map/ppermute | solution.py:370
  58.0 8.6 %collective-permute-start.31 = (bf16[256,1024]{1,0:T(8,128)(2,1)S(1)}, bf16[256,1024]{1,0:T(8,128)(2,1)S(1)}, u32[]{:S(2)}, u32[]{:S(2)}) collective-permute-start(bf16[256,1024]{1,0:T(8,128)(2,1)S(1)} %collective-permute-done.28.refs_6_), channel_id=1, source_target_pairs={{0,1},{1,0},{2,3},{3,2},{4,5},{5,4},{6,7},{7,6},{8,9},{9,8},{10,11... | collective-permute-start | bytes 1572872 | tf_op jit(solution)/shard_map/ppermute | solution.py:378
  58.1 17.6 %collective-permute-start.13 = (bf16[256,1024]{1,0:T(8,128)(2,1)S(1)}, bf16[256,1024]{1,0:T(8,128)(2,1)S(1)}, u32[]{:S(2)}, u32[]{:S(2)}) collective-permute-start(bf16[256,1024]{1,0:T(8,128)(2,1)S(1)} %collective-permute-done.7.refs_9_.refs_17_), channel_id=1, source_target_pairs={{0,32},{8,40},{16,48},{24,56},{32,64},{40,72},{48,80},{56,88},{64,... | collective-permute-start | bytes 1572872 | tf_op jit(solution)/shard_map/ppermute | solution.py:370
  59.3 16.4 %collective-permute-start.27 = (bf16[256,1024]{1,0:T(8,128)(2,1)S(1)}, bf16[256,1024]{1,0:T(8,128)(2,1)S(1)}, u32[]{:S(2)}, u32[]{:S(2)}) collective-permute-start(bf16[256,1024]{1,0:T(8,128)(2,1)S(1)} %collective-permute-done.26.refs_2_), channel_id=1, source_target_pairs={{0,1},{1,0},{2,3},{3,2},{4,5},{5,4},{6,7},{7,6},{8,9},{9,8},{10,11... | collective-permute-start | bytes 1572872 | tf_op jit(solution)/shard_map/ppermute | solution.py:378
  59.5 16.2 %collective-permute-start.4 = (bf16[256,1024]{1,0:T(8,128)(2,1)S(1)}, bf16[256,1024]{1,0:T(8,128)(2,1)S(1)}, u32[]{:S(2)}, u32[]{:S(2)}) collective-permute-start(bf16[256,1024]{1,0:T(8,128)(2,1)S(1)} %collective-permute-done.3.refs_4_.refs_12_), channel_id=1, source_target_pairs={{0,1},{1,0},{2,3},{3,2},{4,5},{5,4},{6,7},{7,6},{8,9},{9,8},{10,11... | collective-permute-start | bytes 1572872 | tf_op jit(solution)/shard_map/ppermute | solution.py:378
  64.8 13.1 %collective-permute-start.12 = (bf16[256,1024]{1,0:T(8,128)(2,1)S(1)}, bf16[256,1024]{1,0:T(8,128)(2,1)S(1)}, u32[]{:S(2)}, u32[]{:S(2)}) collective-permute-start(bf16[256,1024]{1,0:T(8,128)(2,1)S(1)} %collective-permute-done.9.refs_11_.refs_19_), channel_id=1, source_target_pairs={{0,96},{8,104},{16,112},{24,120},{32,0},{40,8},{48,16},{56,24},{64... | collective-permute-start | bytes 1572872 | tf_op jit(solution)/shard_map/ppermute | solution.py:370
  66.6 11.3 %collective-permute-start.30 = (bf16[256,1024]{1,0:T(8,128)(2,1)S(1)}, bf16[256,1024]{1,0:T(8,128)(2,1)S(1)}, u32[]{:S(2)}, u32[]{:S(2)}) collective-permute-start(bf16[256,1024]{1,0:T(8,128)(2,1)S(1)} %collective-permute-done.29.refs_4_), channel_id=1, source_target_pairs={{0,1},{1,0},{2,3},{3,2},{4,5},{5,4},{6,7},{7,6},{8,9},{9,8},{10,11... | collective-permute-start | bytes 1572872 | tf_op jit(solution)/shard_map/ppermute | solution.py:378
  84.5 13.8 %collective-permute-start.36 = (bf16[2,384,256]{2,1,0:T(8,128)(2,1)S(1)}, bf16[2,384,256]{2,1,0:T(8,128)(2,1)S(1)}, u32[]{:S(2)}, u32[]{:S(2)}) collective-permute-start(bf16[2,384,256]{2,1,0:T(8,128)(2,1)S(1)} %get-tuple-element.52), channel_id=1, source_target_pairs={{0,6},{1,7},{2,0},{3,1},{4,2},{5,3},{6,4},{7,5},{8,14},{9,15},{10,... | collective-permute-start | bytes 1179656 | tf_op jit(solution)/shard_map/ppermute | solution.py:374
  88.8 13.4 %collective-permute-start.34 = (bf16[2,384,256]{2,1,0:T(8,128)(2,1)S(1)}, bf16[2,384,256]{2,1,0:T(8,128)(2,1)S(1)}, u32[]{:S(2)}, u32[]{:S(2)}) collective-permute-start(bf16[2,384,256]{2,1,0:T(8,128)(2,1)S(1)} %get-tuple-element.50), channel_id=1, source_target_pairs={{0,2},{1,3},{2,4},{3,5},{4,6},{5,7},{6,0},{7,1},{8,10},{9,11},{10,... | collective-permute-start | bytes 1179656 | tf_op jit(solution)/shard_map/ppermute | solution.py:374
  88.8 36.2 %collective-permute-start.32 = (bf16[2,384,256]{2,1,0:T(8,128)(2,1)S(1)}, bf16[2,384,256]{2,1,0:T(8,128)(2,1)S(1)}, u32[]{:S(2)}, u32[]{:S(2)}) collective-permute-start(bf16[2,384,256]{2,1,0:T(8,128)(2,1)S(1)} %get-tuple-element.47), channel_id=1, source_target_pairs={{0,2},{1,3},{2,4},{3,5},{4,6},{5,7},{6,0},{7,1},{8,10},{9,11},{10,... | collective-permute-start | bytes 1179656 | tf_op jit(solution)/shard_map/ppermute | solution.py:374
  88.8 39.4 %collective-permute-start.33 = (bf16[2,384,256]{2,1,0:T(8,128)(2,1)S(1)}, bf16[2,384,256]{2,1,0:T(8,128)(2,1)S(1)}, u32[]{:S(2)}, u32[]{:S(2)}) collective-permute-start(bf16[2,384,256]{2,1,0:T(8,128)(2,1)S(1)} %get-tuple-element.48), channel_id=1, source_target_pairs={{0,6},{1,7},{2,0},{3,1},{4,2},{5,3},{6,4},{7,5},{8,14},{9,15},{10,... | collective-permute-start | bytes 1179656 | tf_op jit(solution)/shard_map/ppermute | solution.py:374
  98.4 29.8 %collective-permute-start.37 = (bf16[2,384,256]{2,1,0:T(8,128)(2,1)S(1)}, bf16[2,384,256]{2,1,0:T(8,128)(2,1)S(1)}, u32[]{:S(2)}, u32[]{:S(2)}) collective-permute-start(bf16[2,384,256]{2,1,0:T(8,128)(2,1)S(1)} %add_convert_fusion), channel_id=1, source_target_pairs={{0,6},{1,7},{2,0},{3,1},{4,2},{5,3},{6,4},{7,5},{8,14},{9,15},{10,... | collective-permute-start | bytes 1179656 | tf_op jit(solution)/shard_map/ppermute | solution.py:374
  102.3 25.9 %collective-permute-start.35 = (bf16[2,384,256]{2,1,0:T(8,128)(2,1)S(1)}, bf16[2,384,256]{2,1,0:T(8,128)(2,1)S(1)}, u32[]{:S(2)}, u32[]{:S(2)}) collective-permute-start(bf16[2,384,256]{2,1,0:T(8,128)(2,1)S(1)} %add_convert_fusion.1), channel_id=1, source_target_pairs={{0,2},{1,3},{2,4},{3,5},{4,6},{5,7},{6,0},{7,1},{8,10},{9,11},{10,... | collective-permute-start | bytes 1179656 | tf_op jit(solution)/shard_map/ppermute | solution.py:374
  129.2 9.9 %collective-permute-start.40 = (bf16[384,256]{1,0:T(8,128)(2,1)S(1)}, bf16[384,256]{1,0:T(8,128)(2,1)S(1)}, u32[]{:S(2)}, u32[]{:S(2)}) collective-permute-start(bf16[384,256]{1,0:T(8,128)(2,1)S(1)} %get-tuple-element.56), channel_id=1, source_target_pairs={{0,8},{8,16},{16,24},{24,0},{32,40},{40,48},{48,56},{56,32},{64,72... | collective-permute-start | bytes 589832 | tf_op jit(solution)/shard_map/ppermute | solution.py:366
  133.4 14.9 %collective-permute-start.41 = (bf16[384,256]{1,0:T(8,128)(2,1)S(1)}, bf16[384,256]{1,0:T(8,128)(2,1)S(1)}, u32[]{:S(2)}, u32[]{:S(2)}) collective-permute-start(bf16[384,256]{1,0:T(8,128)(2,1)S(1)} %get-tuple-element.53.refs_1_), channel_id=1, source_target_pairs={{0,1},{1,0},{2,3},{3,2},{4,5},{5,4},{6,7},{7,6},{8,9},{9,8},{10,11... | collective-permute-start | bytes 589832 | tf_op jit(solution)/shard_map/ppermute | solution.py:378
  134.2 14.7 %collective-permute-start.42 = (bf16[384,256]{1,0:T(8,128)(2,1)S(1)}, bf16[384,256]{1,0:T(8,128)(2,1)S(1)}, u32[]{:S(2)}, u32[]{:S(2)}) collective-permute-start(bf16[384,256]{1,0:T(8,128)(2,1)S(1)} %collective-permute-done.38.refs_2_), channel_id=1, source_target_pairs={{0,1},{1,0},{2,3},{3,2},{4,5},{5,4},{6,7},{7,6},{8,9},{9,8},{10,11... | collective-permute-start | bytes 589832 | tf_op jit(solution)/shard_map/ppermute | solution.py:378
  135.9 13.0 %collective-permute-start.43 = (bf16[384,256]{1,0:T(8,128)(2,1)S(1)}, bf16[384,256]{1,0:T(8,128)(2,1)S(1)}, u32[]{:S(2)}, u32[]{:S(2)}) collective-permute-start(bf16[384,256]{1,0:T(8,128)(2,1)S(1)} %collective-permute-done.39.refs_3_), channel_id=1, source_target_pairs={{0,1},{1,0},{2,3},{3,2},{4,5},{5,4},{6,7},{7,6},{8,9},{9,8},{10,11... | collective-permute-start | bytes 589832 | tf_op jit(solution)/shard_map/ppermute | solution.py:378
  139.1 10.3 %collective-permute-start.44 = (bf16[384,256]{1,0:T(8,128)(2,1)S(1)}, bf16[384,256]{1,0:T(8,128)(2,1)S(1)}, u32[]{:S(2)}, u32[]{:S(2)}) collective-permute-start(bf16[384,256]{1,0:T(8,128)(2,1)S(1)} %collective-permute-done.40.refs_4_), channel_id=1, source_target_pairs={{0,1},{1,0},{2,3},{3,2},{4,5},{5,4},{6,7},{7,6},{8,9},{9,8},{10,11... | collective-permute-start | bytes 589832 | tf_op jit(solution)/shard_map/ppermute | solution.py:378
  (17 other events, 99.7 us)

commit v8 on v7

--- a/solution.py
+++ b/solution.py
@@ -8,7 +8,7 @@
 
 TILE = 256
 HALF = 128
-CUT = 192
+CUT = 128
 PARTS = ((0, CUT), (CUT, TILE - CUT))
 
 
@@ -390,8 +390,9 @@
         sum_down = zpass(add(prev_high, got_down), -1)
         sum_up = zpass(add(next_low, got_up), 1)
     else:
-        far_down = sum_down = zpass(merge(prev_high, got_down), -1)
-        far_up = sum_up = zpass(merge(next_low, got_up), 1)
+        merged_down, merged_up = merge(prev_high, got_down), merge(next_low, got_up)
+        far_down = sum_down = zpass(merged_down, -1)
+        far_up = sum_up = zpass(merged_up, 1)
     return finish(own, far_up, far_down, sum_up, sum_down)
 
 
@@ -424,7 +425,8 @@
     sent = product(PARTS[0], *rows, cols, True)
     kept = kept_product(PARTS[0], *rows, cols)
     later = product(PARTS[1], *rows, cols, False)
-    outgoing = pack(PARTS[0], owner_rows, exchange(reduce_along_z((*sent, kept))))
+    arrived = exchange(reduce_along_z((*sent, kept)))
+    outgoing = pack(PARTS[0], owner_rows, arrived)
     outgoing = pack(PARTS[1], owner_rows, exchange(reduce_along_z(later)), outgoing)
     return lax.all_to_all(outgoing, "row", split_axis=0, concat_axis=0, tiled=True)
 

time: 189 us -> 172 us (0.910)
  waiting for transfers between devices: 82.6 us -> 71.4 us
  Pallas kernels: 24.3 us -> 20.3 us
    ppermute x6, waiting for transfers between devices: 31.5 us -> 13.2 us  [xpass(): return lax.ppermute(value, 'row', along_x(step))]
    ppermute x10, starting transfers between devices: 18.1 us -> 13.6 us  [zpass(): return lax.ppermute(value, 'col', along_z(step))]
    ppermute x12, waiting for transfers between devices: 33.4 us -> 37.7 us  [ypass(): return lax.ppermute(value, 'row', along_y(step))]
    pallas_call x2, Pallas kernels: 13.3 us -> 10.1 us  [product(): pl.pallas_call(lambda *refs: product_body(*refs, part=part, first=first),...]
    ppermute x10, waiting for transfers between devices: 17.6 us -> 20.5 us  [zpass(): return lax.ppermute(value, 'col', along_z(step))]
    ppermute x6, starting transfers between devices: 8.71 us -> 11.3 us  [xpass(): return lax.ppermute(value, 'row', along_x(step))]
  transfers between devices with their start and end apart: 45 -> 45, of which waited for: 18 -> 14; matrix products, arithmetic and copies ran while one was open for 0% -> 0% of each run, Pallas kernels for 7% -> 9%
where the time goes in v8:
time: 172 us
  waiting for transfers between devices  71.4 us (42%)
  starting transfers between devices  43.6 us (25%)
  blocking collectives  32 us (19%)
  Pallas kernels  20.3 us (12%)
  local copies, waits for them, and re-layouts  4.45 us (3%)
    ppermute x12, waiting for transfers between devices, ypass(): return lax.ppermute(value, 'row', along_y(step))  37.7 us
    all_to_all x1, blocking collectives, shards(): lax.all_to_all(outgoing, 'row', split_axis=0, concat_axis=0, tiled=True)  32 us
    ppermute x10, waiting for transfers between devices, zpass(): return lax.ppermute(value, 'col', along_z(step))  20.5 us
    ppermute x12, starting transfers between devices, ypass(): return lax.ppermute(value, 'row', along_y(step))  16.5 us
    ppermute x10, starting transfers between devices, zpass(): return lax.ppermute(value, 'col', along_z(step))  13.6 us
    ppermute x6, waiting for transfers between devices, xpass(): return lax.ppermute(value, 'row', along_x(step))  13.2 us
    ppermute x6, starting transfers between devices, xpass(): return lax.ppermute(value, 'row', along_x(step))  11.3 us
    pallas_call x2, Pallas kernels, product(): pl.pallas_call(lambda *refs: product_body(*refs, part=part, first=first),...  10.1 us
  transfers between devices with their start and end apart: 45, of which 14 were waited for; matrix products, arithmetic and copies ran while one was open for 0% of the time, Pallas kernels for 9%

profile of v8, /device:TPU:0, one launch (start us, length us, event | category | flops | bytes accessed | tf_op | source)
XLA Modules:
  0.0 172.2 jit_solution(4958791667129980435)
XLA Ops:
  0.0 2.6 %scale.1 = (bf16[256,1024]{1,0:T(8,128)(2,1)}, bf16[256,1024]{1,0:T(8,128)(2,1)}, bf16[256,1024]{1,0:T(8,128)(2,1)}, bf16[256,1024]{1,0:T(8,128)(2,1)}) custom-call(s32[2,32]{1,0:T(2,128)} %mask_hbm.1, bf16[512,1024]{1,0:T(8,128)(2,1)} %panels_hbm.1, f32[1,1024]{1,0:T(1,128)} %bitcast.1), custom_call_target="tpu_custom_call" | custom-call | tf_op jit(solution)/shard_map/scale/pallas_call | solution.py:100
  2.7 3.2 %collective-permute-start.1 = (bf16[256,1024]{1,0:T(8,128)(2,1)}, bf16[256,1024]{1,0:T(8,128)(2,1)S(1)}, u32[]{:S(2)}, u32[]{:S(2)}) collective-permute-start(bf16[256,1024]{1,0:T(8,128)(2,1)} %get-tuple-element.33.refs_2_), channel_id=1, source_target_pairs={{0,24},{8,0},{16,8},{24,16},{32,56},{40,32},{48,40},{56,48},{64,88... | collective-permute-start | bytes 1572872 | tf_op jit(solution)/shard_map/ppermute | solution.py:366
  6.1 2.8 %collective-permute-start.8 = (bf16[256,1024]{1,0:T(8,128)(2,1)}, bf16[256,1024]{1,0:T(8,128)(2,1)S(1)}, u32[]{:S(2)}, u32[]{:S(2)}) collective-permute-start(bf16[256,1024]{1,0:T(8,128)(2,1)} %get-tuple-element.31.refs_0_), channel_id=1, source_target_pairs={{0,96},{8,104},{16,112},{24,120},{32,0},{40,8},{48,16},{56,24},{64... | collective-permute-start | bytes 1572872 | tf_op jit(solution)/shard_map/ppermute | solution.py:370
  8.9 9.2 %collective-permute-done.1.refs_2_ = bf16[256,1024]{1,0:T(8,128)(2,1)S(1)} collective-permute-done((bf16[256,1024]{1,0:T(8,128)(2,1)}, bf16[256,1024]{1,0:T(8,128)(2,1)S(1)}, u32[]{:S(2)}, u32[]{:S(2)}) %collective-permute-start.1) | collective-permute-done | bytes 524320 | tf_op jit(solution)/shard_map/ppermute | solution.py:366
  18.0 3.6 %collective-permute-start.26 = (bf16[256,1024]{1,0:T(8,128)(2,1)}, bf16[256,1024]{1,0:T(8,128)(2,1)S(1)}, u32[]{:S(2)}, u32[]{:S(2)}) collective-permute-start(bf16[256,1024]{1,0:T(8,128)(2,1)} %get-tuple-element.32.refs_1_), channel_id=1, source_target_pairs={{0,24},{8,0},{16,8},{24,16},{32,56},{40,32},{48,40},{56,48},{64,88... | collective-permute-start | bytes 1572872 | tf_op jit(solution)/shard_map/ppermute | solution.py:366
  21.7 3.2 %collective-permute-start.3 = (bf16[256,1024]{1,0:T(8,128)(2,1)S(1)}, bf16[256,1024]{1,0:T(8,128)(2,1)S(1)}, u32[]{:S(2)}, u32[]{:S(2)}) collective-permute-start(bf16[256,1024]{1,0:T(8,128)(2,1)S(1)} %collective-permute-done.1.refs_2_), channel_id=1, source_target_pairs={{0,24},{8,0},{16,8},{24,16},{32,56},{40,32},{48,40},{56,48},{64,88... | collective-permute-start | bytes 1572872 | tf_op jit(solution)/shard_map/ppermute | solution.py:366
  25.1 9.1 %collective-permute-done.26.refs_2_ = bf16[256,1024]{1,0:T(8,128)(2,1)S(1)} collective-permute-done((bf16[256,1024]{1,0:T(8,128)(2,1)}, bf16[256,1024]{1,0:T(8,128)(2,1)S(1)}, u32[]{:S(2)}, u32[]{:S(2)}) %collective-permute-start.26) | collective-permute-done | bytes 524320 | tf_op jit(solution)/shard_map/ppermute | solution.py:366
  34.2 2.8 %collective-permute-start.9 = (bf16[256,1024]{1,0:T(8,128)(2,1)S(1)}, bf16[256,1024]{1,0:T(8,128)(2,1)S(1)}, u32[]{:S(2)}, u32[]{:S(2)}) collective-permute-start(bf16[256,1024]{1,0:T(8,128)(2,1)S(1)} %collective-permute-done.7.refs_9_), channel_id=1, source_target_pairs={{0,96},{8,104},{16,112},{24,120},{32,0},{40,8},{48,16},{56,24},{64... | collective-permute-start | bytes 1572872 | tf_op jit(solution)/shard_map/ppermute | solution.py:370
  39.2 4.8 %collective-permute-done.3.refs_4_ = bf16[256,1024]{1,0:T(8,128)(2,1)S(1)} collective-permute-done((bf16[256,1024]{1,0:T(8,128)(2,1)S(1)}, bf16[256,1024]{1,0:T(8,128)(2,1)S(1)}, u32[]{:S(2)}, u32[]{:S(2)}) %collective-permute-start.3) | collective-permute-done | bytes 524320 | tf_op jit(solution)/shard_map/ppermute | solution.py:366
  44.0 1.7 collective-permute-done.9.refs_11_
  45.7 3.7 %collective-permute-start.12 = (bf16[256,1024]{1,0:T(8,128)(2,1)S(1)}, bf16[256,1024]{1,0:T(8,128)(2,1)S(1)}, u32[]{:S(2)}, u32[]{:S(2)}) collective-permute-start(bf16[256,1024]{1,0:T(8,128)(2,1)S(1)} %collective-permute-done.9.refs_11_), channel_id=1, source_target_pairs={{0,96},{8,104},{16,112},{24,120},{32,0},{40,8},{48,16},{56,24},{64... | collective-permute-start | bytes 1572872 | tf_op jit(solution)/shard_map/ppermute | solution.py:370
  49.4 3.6 %collective-permute-done.11.refs_12_ = bf16[256,1024]{1,0:T(8,128)(2,1)S(1)} collective-permute-done((bf16[256,1024]{1,0:T(8,128)(2,1)S(1)}, bf16[256,1024]{1,0:T(8,128)(2,1)S(1)}, u32[]{:S(2)}, u32[]{:S(2)}) %collective-permute-start.11) | collective-permute-done | bytes 524320 | tf_op jit(solution)/shard_map/ppermute | solution.py:370
  53.0 7.9 %collective-permute-done.13.refs_15_ = bf16[256,1024]{1,0:T(8,128)(2,1)S(1)} collective-permute-done((bf16[256,1024]{1,0:T(8,128)(2,1)S(1)}, bf16[256,1024]{1,0:T(8,128)(2,1)S(1)}, u32[]{:S(2)}, u32[]{:S(2)}) %collective-permute-start.13) | collective-permute-done | bytes 524320 | tf_op jit(solution)/shard_map/ppermute | solution.py:370
  64.8 5.6 %product.2 = (bf16[2,256,256]{2,1,0:T(8,128)(2,1)S(1)}, bf16[2,256,256]{2,1,0:T(8,128)(2,1)S(1)}, bf16[4,256,256]{2,1,0:T(8,128)(2,1)S(1)}, bf16[4,256,256]{2,1,0:T(8,128)(2,1)S(1)}, f32[4,256,256]{2,1,0:T(8,128)S(1)}) custom-call(bf16[256,1024]{1,0:T(8,128)(2,1)S(1)} %get-tuple-element.34.refs_0_, bf16[256,1024]{1,0:T(8,128)(2,1)S(1)} %collective-permute-done.refs_1_, ...), custom_call_target="tpu_custom_call" | custom-call | tf_op jit(solution)/shard_map/product/pallas_call | solution.py:208
  70.4 2.0 %collective-permute-start.14 = (bf16[2,256,256]{2,1,0:T(8,128)(2,1)S(1)}, bf16[2,256,256]{2,1,0:T(8,128)(2,1)S(1)}, u32[]{:S(2)}, u32[]{:S(2)}) collective-permute-start(bf16[2,256,256]{2,1,0:T(8,128)(2,1)S(1)} %get-tuple-element.39), channel_id=1, source_target_pairs={{0,2},{1,3},{2,4},{3,5},{4,6},{5,7},{6,0},{7,1},{8,10},{9,11},{10,... | collective-permute-start | bytes 786440 | tf_op jit(solution)/shard_map/ppermute | solution.py:374
  72.4 2.4 %collective-permute-start.16 = (bf16[2,256,256]{2,1,0:T(8,128)(2,1)S(1)}, bf16[2,256,256]{2,1,0:T(8,128)(2,1)S(1)}, u32[]{:S(2)}, u32[]{:S(2)}) collective-permute-start(bf16[2,256,256]{2,1,0:T(8,128)(2,1)S(1)} %get-tuple-element.41), channel_id=1, source_target_pairs={{0,6},{1,7},{2,0},{3,1},{4,2},{5,3},{6,4},{7,5},{8,14},{9,15},{10,... | collective-permute-start | bytes 786440 | tf_op jit(solution)/shard_map/ppermute | solution.py:374
  74.8 4.5 %product.3 = (bf16[2,256,256]{2,1,0:T(8,128)(2,1)S(1)}, bf16[2,256,256]{2,1,0:T(8,128)(2,1)S(1)}, bf16[2,256,256]{2,1,0:T(8,128)(2,1)S(1)}, bf16[2,256,256]{2,1,...) custom-call(bf16[256,1024]{1,0:T(8,128)(2,1)S(1)} %get-tuple-element.46.refs_0_, ...), custom_call_target="tpu_custom_call" | custom-call | tf_op jit(solution)/shard_map/product/pallas_call | solution.py:208
  79.4 3.2 %collective-permute-start.36 = (bf16[2,256,256]{2,1,0:T(8,128)(2,1)S(1)}, bf16[2,256,256]{2,1,0:T(8,128)(2,1)S(1)}, u32[]{:S(2)}, u32[]{:S(2)}) collective-permute-start(bf16[2,256,256]{2,1,0:T(8,128)(2,1)S(1)} %get-tuple-element.52), channel_id=1, source_target_pairs={{0,6},{1,7},{2,0},{3,1},{4,2},{5,3},{6,4},{7,5},{8,14},{9,15},{10,... | collective-permute-start | bytes 786440 | tf_op jit(solution)/shard_map/ppermute | solution.py:374
  82.6 3.2 %collective-permute-start.33 = (bf16[2,256,256]{2,1,0:T(8,128)(2,1)S(1)}, bf16[2,256,256]{2,1,0:T(8,128)(2,1)S(1)}, u32[]{:S(2)}, u32[]{:S(2)}) collective-permute-start(bf16[2,256,256]{2,1,0:T(8,128)(2,1)S(1)} %get-tuple-element.48), channel_id=1, source_target_pairs={{0,6},{1,7},{2,0},{3,1},{4,2},{5,3},{6,4},{7,5},{8,14},{9,15},{10,... | collective-permute-start | bytes 786440 | tf_op jit(solution)/shard_map/ppermute | solution.py:374
  86.1 3.7 %collective-permute-done.34 = bf16[2,256,256]{2,1,0:T(8,128)(2,1)S(1)} collective-permute-done((bf16[2,256,256]{2,1,0:T(8,128)(2,1)S(1)}, bf16[2,256,256]{2,1,0:T(8,128)(2,1)S(1)}, u32[]{:S(2)}, u32[]{:S(2)}) %collective-permute-start.34) | collective-permute-done | bytes 262176 | tf_op jit(solution)/shard_map/ppermute | solution.py:374
  92.0 3.4 %collective-permute-done.32.far_up = bf16[2,256,256]{2,1,0:T(8,128)(2,1)S(1)} collective-permute-done((bf16[2,256,256]{2,1,0:T(8,128)(2,1)S(1)}, bf16[2,256,256]{2,1,0:T(8,128)(2,1)S(1)}, u32[]{:S(2)}, u32[]{:S(2)}) %collective-permute-start.32) | collective-permute-done | bytes 262176 | tf_op jit(solution)/shard_map/ppermute | solution.py:374
  95.9 2.1 %kept.1.own = f32[4,256,256]{2,1,0:T(8,128)S(1)} custom-call(bf16[256,1024]{1,0:T(8,128)(2,1)S(1)} %get-tuple-element.46.refs_0_, bf16[256,1024]{1,0:T(8,128)(2,1)S(1)} %collective-permute-done.25.refs_1_, bf16[256,1024]{1,0:T(8,128)(2,1)S(1)} %collective-permute-done.26.refs_2_, bf16[256,1024]{1,0:T(8,128)(2,1)S(1)} %collective-permute-done.27.refs_3_, ...), custom_call_target="tpu_custom_call" | custom-call | tf_op jit(solution)/shard_map/kept/pallas_call | solution.py:246
  98.1 13.4 %collective-permute-done.35.sum_up = bf16[2,256,256]{2,1,0:T(8,128)(2,1)S(1)} collective-permute-done((bf16[2,256,256]{2,1,0:T(8,128)(2,1)S(1)}, bf16[2,256,256]{2,1,0:T(8,128)(2,1)S(1)}, u32[]{:S(2)}, u32[]{:S(2)}) %collective-permute-start.35) | collective-permute-done | bytes 262176 | tf_op jit(solution)/shard_map/ppermute | solution.py:374
  111.6 3.1 %collective-permute-start.38 = (bf16[256,256]{1,0:T(8,128)(2,1)S(1)}, bf16[256,256]{1,0:T(8,128)(2,1)S(1)}, u32[]{:S(2)}, u32[]{:S(2)}) collective-permute-start(bf16[256,256]{1,0:T(8,128)(2,1)S(1)} %get-tuple-element.54), channel_id=1, source_target_pairs={{0,24},{8,0},{16,8},{24,16},{32,56},{40,32},{48,40},{56,48},{64,88... | collective-permute-start | bytes 393224 | tf_op jit(solution)/shard_map/ppermute | solution.py:366
  115.7 4.1 %collective-permute-done.38.refs_2_ = bf16[256,256]{1,0:T(8,128)(2,1)S(1)} collective-permute-done((bf16[256,256]{1,0:T(8,128)(2,1)S(1)}, bf16[256,256]{1,0:T(8,128)(2,1)S(1)}, u32[]{:S(2)}, u32[]{:S(2)}) %collective-permute-start.38) | collective-permute-done | bytes 131104 | tf_op jit(solution)/shard_map/ppermute | solution.py:366
  119.8 2.3 %collective-permute-done.39.refs_3_ = bf16[256,256]{1,0:T(8,128)(2,1)S(1)} collective-permute-done((bf16[256,256]{1,0:T(8,128)(2,1)S(1)}, bf16[256,256]{1,0:T(8,128)(2,1)S(1)}, u32[]{:S(2)}, u32[]{:S(2)}) %collective-permute-start.39) | collective-permute-done | bytes 131104 | tf_op jit(solution)/shard_map/ppermute | solution.py:366
  125.7 4.7 %collective-permute-done.18.refs_2_ = bf16[256,256]{1,0:T(8,128)(2,1)S(1)} collective-permute-done((bf16[256,256]{1,0:T(8,128)(2,1)S(1)}, bf16[256,256]{1,0:T(8,128)(2,1)S(1)}, u32[]{:S(2)}, u32[]{:S(2)}) %collective-permute-start.18) | collective-permute-done | bytes 131104 | tf_op jit(solution)/shard_map/ppermute | solution.py:366
  130.5 1.7 %collective-permute-done.19.refs_3_ = bf16[256,256]{1,0:T(8,128)(2,1)S(1)} collective-permute-done((bf16[256,256]{1,0:T(8,128)(2,1)S(1)}, bf16[256,256]{1,0:T(8,128)(2,1)S(1)}, u32[]{:S(2)}, u32[]{:S(2)}) %collective-permute-start.19) | collective-permute-done | bytes 131104 | tf_op jit(solution)/shard_map/ppermute | solution.py:366
  132.2 1.7 collective-permute-done.20.refs_4_
  133.9 3.3 %pack.2.refs_9_ = bf16[16,1,256,256]{3,2,1,0:T(8,128)(2,1)S(1)} custom-call(s32[2,4]{1,0:T(2,128)S(1)} %copy-done.3, bf16[256,256]{1,0:T(8,128)(2,1)S(1)} %get-tuple-element.53.refs_1_, bf16[256,256]{1,0:T(8,128)(2,1)S(1)} %collective-permute-done.38.refs_2_, bf16[256,256]{1,0:T(8,128)(2,1)S(1)} %collective-permute-done.39.refs_3_, ...), custom_call_target="tpu_custom_call" | custom-call | tf_op jit(solution)/shard_map/pack/pallas_call | solution.py:348
  137.2 1.6 pack.3
  138.8 32.0 %all_to_all.5 = bf16[16,1,256,256]{3,2,1,0:T(8,128)(2,1)S(1)} all-to-all(bf16[16,1,256,256]{3,2,1,0:T(8,128)(2,1)S(1)} %pack.3), channel_id=1, replica_groups=mesh['row'=16,'col'=8] {'row'}, dimensions={0} | all-to-all | bytes 4194304 | tf_op jit(solution)/shard_map/all_to_all | solution.py:431
  (81 shorter events, 15.7 us)
Async XLA Ops:
  2.7 15.3 %collective-permute-start.1 = (bf16[256,1024]{1,0:T(8,128)(2,1)}, bf16[256,1024]{1,0:T(8,128)(2,1)S(1)}, u32[]{:S(2)}, u32[]{:S(2)}) collective-permute-start(bf16[256,1024]{1,0:T(8,128)(2,1)} %get-tuple-element.33.refs_2_), channel_id=1, source_target_pairs={{0,24},{8,0},{16,8},{24,16},{32,56},{40,32},{48,40},{56,48},{64,88... | collective-permute-start | bytes 1572872 | tf_op jit(solution)/shard_map/ppermute | solution.py:366
  5.9 15.7 %collective-permute-start.5 = (bf16[256,1024]{1,0:T(8,128)(2,1)}, bf16[256,1024]{1,0:T(8,128)(2,1)S(1)}, u32[]{:S(2)}, u32[]{:S(2)}) collective-permute-start(bf16[256,1024]{1,0:T(8,128)(2,1)} %get-tuple-element.33.refs_2_), channel_id=1, source_target_pairs={{0,8},{8,16},{16,24},{24,0},{32,40},{40,48},{48,56},{56,32},{64,72... | collective-permute-start | bytes 1572872 | tf_op jit(solution)/shard_map/ppermute | solution.py:366
  5.9 15.7 %collective-permute-start.7 = (bf16[256,1024]{1,0:T(8,128)(2,1)}, bf16[256,1024]{1,0:T(8,128)(2,1)S(1)}, u32[]{:S(2)}, u32[]{:S(2)}) collective-permute-start(bf16[256,1024]{1,0:T(8,128)(2,1)} %get-tuple-element.36), channel_id=1, source_target_pairs={{0,1},{1,0},{2,3},{3,2},{4,5},{5,4},{6,7},{7,6},{8,9},{9,8},{10,11... | collective-permute-start | bytes 1572872 | tf_op jit(solution)/shard_map/ppermute | solution.py:378
  6.1 15.6 %collective-permute-start.8 = (bf16[256,1024]{1,0:T(8,128)(2,1)}, bf16[256,1024]{1,0:T(8,128)(2,1)S(1)}, u32[]{:S(2)}, u32[]{:S(2)}) collective-permute-start(bf16[256,1024]{1,0:T(8,128)(2,1)} %get-tuple-element.31.refs_0_), channel_id=1, source_target_pairs={{0,96},{8,104},{16,112},{24,120},{32,0},{40,8},{48,16},{56,24},{64... | collective-permute-start | bytes 1572872 | tf_op jit(solution)/shard_map/ppermute | solution.py:370
  8.9 16.1 %collective-permute-start.10 = (bf16[256,1024]{1,0:T(8,128)(2,1)}, bf16[256,1024]{1,0:T(8,128)(2,1)S(1)}, u32[]{:S(2)}, u32[]{:S(2)}) collective-permute-start(bf16[256,1024]{1,0:T(8,128)(2,1)} %get-tuple-element.31.refs_0_), channel_id=1, source_target_pairs={{0,32},{8,40},{16,48},{24,56},{32,64},{40,72},{48,80},{56,88},{64,... | collective-permute-start | bytes 1572872 | tf_op jit(solution)/shard_map/ppermute | solution.py:370
  18.0 16.2 %collective-permute-start.26 = (bf16[256,1024]{1,0:T(8,128)(2,1)}, bf16[256,1024]{1,0:T(8,128)(2,1)S(1)}, u32[]{:S(2)}, u32[]{:S(2)}) collective-permute-start(bf16[256,1024]{1,0:T(8,128)(2,1)} %get-tuple-element.32.refs_1_), channel_id=1, source_target_pairs={{0,24},{8,0},{16,8},{24,16},{32,56},{40,32},{48,40},{56,48},{64,88... | collective-permute-start | bytes 1572872 | tf_op jit(solution)/shard_map/ppermute | solution.py:366
  21.6 15.4 %collective-permute-start.28 = (bf16[256,1024]{1,0:T(8,128)(2,1)}, bf16[256,1024]{1,0:T(8,128)(2,1)S(1)}, u32[]{:S(2)}, u32[]{:S(2)}) collective-permute-start(bf16[256,1024]{1,0:T(8,128)(2,1)} %get-tuple-element.32.refs_1_), channel_id=1, source_target_pairs={{0,8},{8,16},{16,24},{24,0},{32,40},{40,48},{48,56},{56,32},{64,72... | collective-permute-start | bytes 1572872 | tf_op jit(solution)/shard_map/ppermute | solution.py:366
  21.6 16.0 %collective-permute-start.2 = (bf16[256,1024]{1,0:T(8,128)(2,1)S(1)}, bf16[256,1024]{1,0:T(8,128)(2,1)S(1)}, u32[]{:S(2)}, u32[]{:S(2)}) collective-permute-start(bf16[256,1024]{1,0:T(8,128)(2,1)S(1)} %collective-permute-done.1.refs_2_), channel_id=1, source_target_pairs={{0,1},{1,0},{2,3},{3,2},{4,5},{5,4},{6,7},{7,6},{8,9},{9,8},{10,11... | collective-permute-start | bytes 1572872 | tf_op jit(solution)/shard_map/ppermute | solution.py:378
  21.7 22.2 %collective-permute-start.3 = (bf16[256,1024]{1,0:T(8,128)(2,1)S(1)}, bf16[256,1024]{1,0:T(8,128)(2,1)S(1)}, u32[]{:S(2)}, u32[]{:S(2)}) collective-permute-start(bf16[256,1024]{1,0:T(8,128)(2,1)S(1)} %collective-permute-done.1.refs_2_), channel_id=1, source_target_pairs={{0,24},{8,0},{16,8},{24,16},{32,56},{40,32},{48,40},{56,48},{64,88... | collective-permute-start | bytes 1572872 | tf_op jit(solution)/shard_map/ppermute | solution.py:366
  24.9 19.0 %collective-permute-start.6 = (bf16[256,1024]{1,0:T(8,128)(2,1)S(1)}, bf16[256,1024]{1,0:T(8,128)(2,1)S(1)}, u32[]{:S(2)}, u32[]{:S(2)}) collective-permute-start(bf16[256,1024]{1,0:T(8,128)(2,1)S(1)} %collective-permute-done.5.refs_6_), channel_id=1, source_target_pairs={{0,1},{1,0},{2,3},{3,2},{4,5},{5,4},{6,7},{7,6},{8,9},{9,8},{10,11... | collective-permute-start | bytes 1572872 | tf_op jit(solution)/shard_map/ppermute | solution.py:378
  34.2 11.4 %collective-permute-start.9 = (bf16[256,1024]{1,0:T(8,128)(2,1)S(1)}, bf16[256,1024]{1,0:T(8,128)(2,1)S(1)}, u32[]{:S(2)}, u32[]{:S(2)}) collective-permute-start(bf16[256,1024]{1,0:T(8,128)(2,1)S(1)} %collective-permute-done.7.refs_9_), channel_id=1, source_target_pairs={{0,96},{8,104},{16,112},{24,120},{32,0},{40,8},{48,16},{56,24},{64... | collective-permute-start | bytes 1572872 | tf_op jit(solution)/shard_map/ppermute | solution.py:370
  37.0 16.0 %collective-permute-start.11 = (bf16[256,1024]{1,0:T(8,128)(2,1)S(1)}, bf16[256,1024]{1,0:T(8,128)(2,1)S(1)}, u32[]{:S(2)}, u32[]{:S(2)}) collective-permute-start(bf16[256,1024]{1,0:T(8,128)(2,1)S(1)} %collective-permute-done.10.refs_14_), channel_id=1, source_target_pairs={{0,32},{8,40},{16,48},{24,56},{32,64},{40,72},{48,80},{56,88},{64,... | collective-permute-start | bytes 1572872 | tf_op jit(solution)/shard_map/ppermute | solution.py:370
  37.7 23.2 %collective-permute-start.13 = (bf16[256,1024]{1,0:T(8,128)(2,1)S(1)}, bf16[256,1024]{1,0:T(8,128)(2,1)S(1)}, u32[]{:S(2)}, u32[]{:S(2)}) collective-permute-start(bf16[256,1024]{1,0:T(8,128)(2,1)S(1)} %collective-permute-done.7.refs_9_), channel_id=1, source_target_pairs={{0,32},{8,40},{16,48},{24,56},{32,64},{40,72},{48,80},{56,88},{64,... | collective-permute-start | bytes 1572872 | tf_op jit(solution)/shard_map/ppermute | solution.py:370
  44.0 16.9 %collective-permute-start.29 = (bf16[256,1024]{1,0:T(8,128)(2,1)S(1)}, bf16[256,1024]{1,0:T(8,128)(2,1)S(1)}, u32[]{:S(2)}, u32[]{:S(2)}) collective-permute-start(bf16[256,1024]{1,0:T(8,128)(2,1)S(1)} %collective-permute-done.28.refs_6_), channel_id=1, source_target_pairs={{0,8},{8,16},{16,24},{24,0},{32,40},{40,48},{48,56},{56,32},{64,72... | collective-permute-start | bytes 1572872 | tf_op jit(solution)/shard_map/ppermute | solution.py:366
  44.0 17.4 %collective-permute-start.4 = (bf16[256,1024]{1,0:T(8,128)(2,1)S(1)}, bf16[256,1024]{1,0:T(8,128)(2,1)S(1)}, u32[]{:S(2)}, u32[]{:S(2)}) collective-permute-start(bf16[256,1024]{1,0:T(8,128)(2,1)S(1)} %collective-permute-done.3.refs_4_), channel_id=1, source_target_pairs={{0,1},{1,0},{2,3},{3,2},{4,5},{5,4},{6,7},{7,6},{8,9},{9,8},{10,11... | collective-permute-start | bytes 1572872 | tf_op jit(solution)/shard_map/ppermute | solution.py:378
  45.7 19.1 %collective-permute-start.12 = (bf16[256,1024]{1,0:T(8,128)(2,1)S(1)}, bf16[256,1024]{1,0:T(8,128)(2,1)S(1)}, u32[]{:S(2)}, u32[]{:S(2)}) collective-permute-start(bf16[256,1024]{1,0:T(8,128)(2,1)S(1)} %collective-permute-done.9.refs_11_), channel_id=1, source_target_pairs={{0,96},{8,104},{16,112},{24,120},{32,0},{40,8},{48,16},{56,24},{64... | collective-permute-start | bytes 1572872 | tf_op jit(solution)/shard_map/ppermute | solution.py:370
  53.0 19.4 %collective-permute-start.25 = (bf16[256,1024]{1,0:T(8,128)(2,1)}, bf16[256,1024]{1,0:T(8,128)(2,1)S(1)}, u32[]{:S(2)}, u32[]{:S(2)}) collective-permute-start(bf16[256,1024]{1,0:T(8,128)(2,1)} %get-tuple-element.32.refs_1_), channel_id=1, source_target_pairs={{0,1},{1,0},{2,3},{3,2},{4,5},{5,4},{6,7},{7,6},{8,9},{9,8},{10,11... | collective-permute-start | bytes 1572872 | tf_op jit(solution)/shard_map/ppermute | solution.py:378
  60.9 13.9 %collective-permute-start.31 = (bf16[256,1024]{1,0:T(8,128)(2,1)S(1)}, bf16[256,1024]{1,0:T(8,128)(2,1)S(1)}, u32[]{:S(2)}, u32[]{:S(2)}) collective-permute-start(bf16[256,1024]{1,0:T(8,128)(2,1)S(1)} %collective-permute-done.28.refs_6_), channel_id=1, source_target_pairs={{0,1},{1,0},{2,3},{3,2},{4,5},{5,4},{6,7},{7,6},{8,9},{9,8},{10,11... | collective-permute-start | bytes 1572872 | tf_op jit(solution)/shard_map/ppermute | solution.py:378
  60.9 13.9 %collective-permute-start.27 = (bf16[256,1024]{1,0:T(8,128)(2,1)S(1)}, bf16[256,1024]{1,0:T(8,128)(2,1)S(1)}, u32[]{:S(2)}, u32[]{:S(2)}) collective-permute-start(bf16[256,1024]{1,0:T(8,128)(2,1)S(1)} %collective-permute-done.26.refs_2_), channel_id=1, source_target_pairs={{0,1},{1,0},{2,3},{3,2},{4,5},{5,4},{6,7},{7,6},{8,9},{9,8},{10,11... | collective-permute-start | bytes 1572872 | tf_op jit(solution)/shard_map/ppermute | solution.py:378
  61.4 13.4 %collective-permute-start.30 = (bf16[256,1024]{1,0:T(8,128)(2,1)S(1)}, bf16[256,1024]{1,0:T(8,128)(2,1)S(1)}, u32[]{:S(2)}, u32[]{:S(2)}) collective-permute-start(bf16[256,1024]{1,0:T(8,128)(2,1)S(1)} %collective-permute-done.29.refs_4_), channel_id=1, source_target_pairs={{0,1},{1,0},{2,3},{3,2},{4,5},{5,4},{6,7},{7,6},{8,9},{9,8},{10,11... | collective-permute-start | bytes 1572872 | tf_op jit(solution)/shard_map/ppermute | solution.py:378
  70.4 12.2 %collective-permute-start.14 = (bf16[2,256,256]{2,1,0:T(8,128)(2,1)S(1)}, bf16[2,256,256]{2,1,0:T(8,128)(2,1)S(1)}, u32[]{:S(2)}, u32[]{:S(2)}) collective-permute-start(bf16[2,256,256]{2,1,0:T(8,128)(2,1)S(1)} %get-tuple-element.39), channel_id=1, source_target_pairs={{0,2},{1,3},{2,4},{3,5},{4,6},{5,7},{6,0},{7,1},{8,10},{9,11},{10,... | collective-permute-start | bytes 786440 | tf_op jit(solution)/shard_map/ppermute | solution.py:374
  72.4 13.6 %collective-permute-start.16 = (bf16[2,256,256]{2,1,0:T(8,128)(2,1)S(1)}, bf16[2,256,256]{2,1,0:T(8,128)(2,1)S(1)}, u32[]{:S(2)}, u32[]{:S(2)}) collective-permute-start(bf16[2,256,256]{2,1,0:T(8,128)(2,1)S(1)} %get-tuple-element.41), channel_id=1, source_target_pairs={{0,6},{1,7},{2,0},{3,1},{4,2},{5,3},{6,4},{7,5},{8,14},{9,15},{10,... | collective-permute-start | bytes 786440 | tf_op jit(solution)/shard_map/ppermute | solution.py:374
  79.3 10.5 %collective-permute-start.34 = (bf16[2,256,256]{2,1,0:T(8,128)(2,1)S(1)}, bf16[2,256,256]{2,1,0:T(8,128)(2,1)S(1)}, u32[]{:S(2)}, u32[]{:S(2)}) collective-permute-start(bf16[2,256,256]{2,1,0:T(8,128)(2,1)S(1)} %get-tuple-element.50), channel_id=1, source_target_pairs={{0,2},{1,3},{2,4},{3,5},{4,6},{5,7},{6,0},{7,1},{8,10},{9,11},{10,... | collective-permute-start | bytes 786440 | tf_op jit(solution)/shard_map/ppermute | solution.py:374
  79.4 11.0 %collective-permute-start.36 = (bf16[2,256,256]{2,1,0:T(8,128)(2,1)S(1)}, bf16[2,256,256]{2,1,0:T(8,128)(2,1)S(1)}, u32[]{:S(2)}, u32[]{:S(2)}) collective-permute-start(bf16[2,256,256]{2,1,0:T(8,128)(2,1)S(1)} %get-tuple-element.52), channel_id=1, source_target_pairs={{0,6},{1,7},{2,0},{3,1},{4,2},{5,3},{6,4},{7,5},{8,14},{9,15},{10,... | collective-permute-start | bytes 786440 | tf_op jit(solution)/shard_map/ppermute | solution.py:374
  82.6 12.8 %collective-permute-start.32 = (bf16[2,256,256]{2,1,0:T(8,128)(2,1)S(1)}, bf16[2,256,256]{2,1,0:T(8,128)(2,1)S(1)}, u32[]{:S(2)}, u32[]{:S(2)}) collective-permute-start(bf16[2,256,256]{2,1,0:T(8,128)(2,1)S(1)} %get-tuple-element.47), channel_id=1, source_target_pairs={{0,2},{1,3},{2,4},{3,5},{4,6},{5,7},{6,0},{7,1},{8,10},{9,11},{10,... | collective-permute-start | bytes 786440 | tf_op jit(solution)/shard_map/ppermute | solution.py:374
  82.6 15.4 %collective-permute-start.33 = (bf16[2,256,256]{2,1,0:T(8,128)(2,1)S(1)}, bf16[2,256,256]{2,1,0:T(8,128)(2,1)S(1)}, u32[]{:S(2)}, u32[]{:S(2)}) collective-permute-start(bf16[2,256,256]{2,1,0:T(8,128)(2,1)S(1)} %get-tuple-element.48), channel_id=1, source_target_pairs={{0,6},{1,7},{2,0},{3,1},{4,2},{5,3},{6,4},{7,5},{8,14},{9,15},{10,... | collective-permute-start | bytes 786440 | tf_op jit(solution)/shard_map/ppermute | solution.py:374
  85.9 36.1 %collective-permute-start.15 = (bf16[4,256,256]{2,1,0:T(8,128)(2,1)S(1)}, bf16[4,256,256]{2,1,0:T(8,128)(2,1)S(1)}, u32[]{:S(2)}, u32[]{:S(2)}) collective-permute-start(bf16[4,256,256]{2,1,0:T(8,128)(2,1)S(1)} %merge.2), channel_id=1, source_target_pairs={{0,2},{1,3},{2,4},{3,5},{4,6},{5,7},{6,0},{7,1},{8,10},{9,11},{10,... | collective-permute-start | bytes 1572872 | tf_op jit(solution)/shard_map/ppermute | solution.py:374
  89.8 32.8 %collective-permute-start.17 = (bf16[4,256,256]{2,1,0:T(8,128)(2,1)S(1)}, bf16[4,256,256]{2,1,0:T(8,128)(2,1)S(1)}, u32[]{:S(2)}, u32[]{:S(2)}) collective-permute-start(bf16[4,256,256]{2,1,0:T(8,128)(2,1)S(1)} %merge.3), channel_id=1, source_target_pairs={{0,6},{1,7},{2,0},{3,1},{4,2},{5,3},{6,4},{7,5},{8,14},{9,15},{10,... | collective-permute-start | bytes 1572872 | tf_op jit(solution)/shard_map/ppermute | solution.py:374
  90.4 21.0 %collective-permute-start.35 = (bf16[2,256,256]{2,1,0:T(8,128)(2,1)S(1)}, bf16[2,256,256]{2,1,0:T(8,128)(2,1)S(1)}, u32[]{:S(2)}, u32[]{:S(2)}) collective-permute-start(bf16[2,256,256]{2,1,0:T(8,128)(2,1)S(1)} %add_convert_fusion.1), channel_id=1, source_target_pairs={{0,2},{1,3},{2,4},{3,5},{4,6},{5,7},{6,0},{7,1},{8,10},{9,11},{10,... | collective-permute-start | bytes 786440 | tf_op jit(solution)/shard_map/ppermute | solution.py:374
  95.4 16.0 %collective-permute-start.37 = (bf16[2,256,256]{2,1,0:T(8,128)(2,1)S(1)}, bf16[2,256,256]{2,1,0:T(8,128)(2,1)S(1)}, u32[]{:S(2)}, u32[]{:S(2)}) collective-permute-start(bf16[2,256,256]{2,1,0:T(8,128)(2,1)S(1)} %add_convert_fusion), channel_id=1, source_target_pairs={{0,6},{1,7},{2,0},{3,1},{4,2},{5,3},{6,4},{7,5},{8,14},{9,15},{10,... | collective-permute-start | bytes 786440 | tf_op jit(solution)/shard_map/ppermute | solution.py:374
  124.3 9.6 %collective-permute-start.20 = (bf16[256,256]{1,0:T(8,128)(2,1)S(1)}, bf16[256,256]{1,0:T(8,128)(2,1)S(1)}, u32[]{:S(2)}, u32[]{:S(2)}) collective-permute-start(bf16[256,256]{1,0:T(8,128)(2,1)S(1)} %get-tuple-element.45), channel_id=1, source_target_pairs={{0,8},{8,16},{16,24},{24,0},{32,40},{40,48},{48,56},{56,32},{64,72... | collective-permute-start | bytes 393224 | tf_op jit(solution)/shard_map/ppermute | solution.py:366
  125.2 12.0 %collective-permute-start.21 = (bf16[256,256]{1,0:T(8,128)(2,1)S(1)}, bf16[256,256]{1,0:T(8,128)(2,1)S(1)}, u32[]{:S(2)}, u32[]{:S(2)}) collective-permute-start(bf16[256,256]{1,0:T(8,128)(2,1)S(1)} %get-tuple-element.42.refs_1_), channel_id=1, source_target_pairs={{0,1},{1,0},{2,3},{3,2},{4,5},{5,4},{6,7},{7,6},{8,9},{9,8},{10,11... | collective-permute-start | bytes 393224 | tf_op jit(solution)/shard_map/ppermute | solution.py:378
  (17 other events, 106.9 us)

commit v9 on v7

--- a/solution.py
+++ b/solution.py
@@ -190,20 +190,20 @@
         copy.start()
     for copy in copies:
         copy.wait()
-    up, down, next_low, prev_high = refs[:4]
-    far_up, far_down, at = (refs[4], refs[5], 0) if first else (next_low, prev_high, 2)
-    blocks(rows_ref, cols_ref[(z + 2) % 4], ((up, 0), (up, 1), (down, 0), (down, 1)))
-    blocks(rows_ref, cols_ref[(z + 1) % 4], ((next_low, 0), (next_low, 1), (far_up, at), (far_up, at + 1)))
-    blocks(rows_ref, cols_ref[(z + 3) % 4], ((far_down, at), (far_down, at + 1), (prev_high, 0), (prev_high, 1)))
+    next_low, prev_high, far_up, far_down = refs[:4]
     if not first:
-        blocks(rows_ref, cols_ref[z], tuple((refs[4], j) for j in range(4)))
+        up, down, own = refs[4:7]
+        blocks(rows_ref, cols_ref[(z + 2) % 4], ((up, 0), (up, 1), (down, 0), (down, 1)))
+    blocks(rows_ref, cols_ref[(z + 1) % 4], ((next_low, 0), (next_low, 1), (far_up, 0), (far_up, 1)))
+    blocks(rows_ref, cols_ref[(z + 3) % 4], ((far_down, 0), (far_down, 1), (prev_high, 0), (prev_high, 1)))
+    if not first:
+        blocks(rows_ref, cols_ref[z], tuple((own, j) for j in range(4)))
 
 
 def product(part, tops, lows, cols, first):
-    four = jax.ShapeDtypeStruct((4, 2 * part[1], TILE), jnp.bfloat16)
     two = jax.ShapeDtypeStruct((2, 2 * part[1], TILE), jnp.bfloat16)
     kept = jax.ShapeDtypeStruct((4, 2 * part[1], TILE), jnp.float32)
-    shapes = (two,) * 6 if first else (two, two, four, four, kept)
+    shapes = (two,) * 4 if first else (*(two,) * 6, kept)
     operands = (*needs(part, tops, lows), *cols)
     return pl.pallas_call(
         lambda *refs: product_body(*refs, part=part, first=first),
@@ -221,33 +221,34 @@
     )(*operands)
 
 
-def kept_body(*refs, part):
+def chunk_body(*refs, part, step):
     tops, lows, refs = split_rows(part, refs)
-    cols, own = refs[:8], refs[8]
-    rows_ref, right_ref, row_sems, col_sems = refs[9:]
+    cols, outs = refs[:8], refs[8:-4]
+    rows_ref, right_ref, row_sems, col_sems = refs[-4:]
     x, _, z, _ = position()
     right = load_cols(cols, lambda d, across: right_ref.at[:, across], col_sems)
     copies = load_rows(tops, lows, rows_ref, row_sems, part)
     for act in (lambda copy: copy.start(), lambda copy: copy.wait()):
         for d in range(4):
 
-            @pl.when((x + d) % 4 == z)
+            @pl.when((x + d) % 4 == (z + step) % 4)
             def _():
                 for copy in right[2 * d : 2 * d + 2]:
                     act(copy)
 
         for copy in copies:
             act(copy)
-    blocks(rows_ref, right_ref[...], tuple((own, j) for j in range(4)))
-
-
-def kept_product(part, tops, lows, cols):
+    each = 4 // len(outs)
+    blocks(rows_ref, right_ref[...], tuple((outs[j // each], j % each) for j in range(4)))
+
+
+def chunk_product(part, tops, lows, cols, step, shapes):
     operands = (*needs(part, tops, lows), *cols)
     return pl.pallas_call(
-        lambda *refs: kept_body(*refs, part=part),
-        out_shape=jax.ShapeDtypeStruct((4, 2 * part[1], TILE), jnp.float32),
+        lambda *refs: chunk_body(*refs, part=part, step=step),
+        out_shape=tuple(jax.ShapeDtypeStruct((n, 2 * part[1], TILE), dtype) for n, dtype in shapes),
         in_specs=[pl.BlockSpec(memory_space=pl.ANY)] * len(operands),
-        out_specs=pl.BlockSpec(memory_space=pltpu.VMEM),
+        out_specs=(pl.BlockSpec(memory_space=pltpu.VMEM),) * len(shapes),
         scratch_shapes=[
             pltpu.VMEM((4, 2 * part[1], 2048), jnp.bfloat16),
             pltpu.VMEM((TILE, 2048), jnp.bfloat16),
@@ -255,18 +256,16 @@
             pltpu.SemaphoreType.DMA((8,)),
         ],
         compiler_params=pltpu.CompilerParams(vmem_limit_bytes=32 * 1024 * 1024),
-        name="kept",
     )(*operands)
 
 
 def finish_body(own, far_up, far_down, sum_up, sum_down, *outs):
-    at = far_up.shape[0] - 2
     for j in range(2):
         outs[j][...] = (
-            own[j] + far_down[at + j].astype(jnp.float32) + sum_up[j].astype(jnp.float32)
+            own[j] + far_down[j].astype(jnp.float32) + sum_up[j].astype(jnp.float32)
         ).astype(jnp.bfloat16)
         outs[2 + j][...] = (
-            own[2 + j] + far_up[at + j].astype(jnp.float32) + sum_down[j].astype(jnp.float32)
+            own[2 + j] + far_up[j].astype(jnp.float32) + sum_down[j].astype(jnp.float32)
         ).astype(jnp.bfloat16)
 
 
@@ -280,23 +279,6 @@
         compiler_params=pltpu.CompilerParams(vmem_limit_bytes=8 * 1024 * 1024),
         name="finish",
     )(*parts)
-
-
-def merge_body(share_ref, got_ref, out_ref):
-    for j in range(2):
-        out_ref[j] = (share_ref[j].astype(jnp.float32) + got_ref[j].astype(jnp.float32)).astype(jnp.bfloat16)
-        out_ref[2 + j] = share_ref[2 + j]
-
-
-def merge(share, got):
-    return pl.pallas_call(
-        merge_body,
-        out_shape=jax.ShapeDtypeStruct(share.shape, share.dtype),
-        in_specs=[pl.BlockSpec(memory_space=pltpu.VMEM)] * 2,
-        out_specs=pl.BlockSpec(memory_space=pltpu.VMEM),
-        compiler_params=pltpu.CompilerParams(vmem_limit_bytes=4 * 1024 * 1024),
-        name="merge",
-    )(share, got)
 
 
 def pack_body(owners_ref, *refs, part):
@@ -382,16 +364,13 @@
     return sum(part.astype(jnp.float32) for part in parts).astype(jnp.bfloat16)
 
 
-def reduce_along_z(partials):
-    up, down, next_low, prev_high, *far, own = partials
+def reduce_along_z(shares, sides, own):
+    up, down = shares
+    next_low, prev_high, far_up, far_down = sides
     got_down, got_up = zpass(down, -1), zpass(up, 1)
-    if far:
-        far_down, far_up = zpass(far[1], -1), zpass(far[0], 1)
-        sum_down = zpass(add(prev_high, got_down), -1)
-        sum_up = zpass(add(next_low, got_up), 1)
-    else:
-        far_down = sum_down = zpass(merge(prev_high, got_down), -1)
-        far_up = sum_up = zpass(merge(next_low, got_up), 1)
+    far_down, far_up = zpass(far_down, -1), zpass(far_up, 1)
+    sum_down = zpass(add(prev_high, got_down), -1)
+    sum_up = zpass(add(next_low, got_up), 1)
     return finish(own, far_up, far_down, sum_up, sum_down)
 
 
@@ -416,16 +395,17 @@
     c0, top, low = stage(c0, top, low)
     cols = (c0, c1, cp0, cp1, co0, co1, cm0, cm1)
     rows = []
-    for own, pieces in (
-        (top, (sent_top, top_p, top_o, top_m)), (low, (sent_low, low_p, low_o, low_m))
-    ):
+    for own, pieces in ((top, (sent_top, top_p, top_o, top_m)), (low, (sent_low, low_p, low_o, low_m))):
         others = [swap(value) for value in pieces]
         rows.append([piece for pair in zip((own, *pieces[1:]), others) for piece in pair])
-    sent = product(PARTS[0], *rows, cols, True)
-    kept = kept_product(PARTS[0], *rows, cols)
-    later = product(PARTS[1], *rows, cols, False)
-    outgoing = pack(PARTS[0], owner_rows, exchange(reduce_along_z((*sent, kept))))
-    outgoing = pack(PARTS[1], owner_rows, exchange(reduce_along_z(later)), outgoing)
+    shares = chunk_product(PARTS[0], *rows, cols, 2, ((2, jnp.bfloat16),) * 2)
+    sides = product(PARTS[0], *rows, cols, True)
+    kept = chunk_product(PARTS[0], *rows, cols, 0, ((4, jnp.float32),))
+    *later_sides, later_up, later_down, later_kept = product(PARTS[1], *rows, cols, False)
+    arrived = exchange(reduce_along_z(shares, sides, *kept))
+    outgoing = pack(PARTS[0], owner_rows, arrived)
+    arrived = exchange(reduce_along_z((later_up, later_down), later_sides, later_kept))
+    outgoing = pack(PARTS[1], owner_rows, arrived, outgoing)
     return lax.all_to_all(outgoing, "row", split_axis=0, concat_axis=0, tiled=True)
 
 

time: 189 us -> 185 us (0.979)
  waiting for transfers between devices: 82.6 us -> 72.1 us
  starting transfers between devices: 43.8 us -> 48.2 us
    ppermute x10 -> x12, waiting for transfers between devices: 17.6 us -> 8.44 us  [zpass(): return lax.ppermute(value, 'col', along_z(step))]
    pallas_call x3 -> x2, Pallas kernels: 3.13 us -> 6.08 us  [chunk_product(): pl.pallas_call(lambda *refs: chunk_body(*refs, part=part, step=step), out...]
    ppermute x10 -> x12, starting transfers between devices: 18.1 us -> 20.1 us  [zpass(): return lax.ppermute(value, 'col', along_z(step))]
  transfers between devices with their start and end apart: 45 -> 47, of which waited for: 18 -> 18; matrix products, arithmetic and copies ran while one was open for 0% -> 0% of each run, Pallas kernels for 7% -> 10%
where the time goes in v9:
time: 185 us
  waiting for transfers between devices  72.1 us (39%)
  starting transfers between devices  48.2 us (26%)
  blocking collectives  34 us (18%)
  Pallas kernels  25.7 us (14%)
  local copies, waits for them, and re-layouts  4.44 us (2%)
    all_to_all x1, blocking collectives, shards(): lax.all_to_all(outgoing, 'row', split_axis=0, concat_axis=0, tiled=True)  34 us
    ppermute x12, waiting for transfers between devices, ypass(): return lax.ppermute(value, 'row', along_y(step))  32.1 us
    ppermute x6, waiting for transfers between devices, xpass(): return lax.ppermute(value, 'row', along_x(step))  31.5 us
    ppermute x12, starting transfers between devices, zpass(): return lax.ppermute(value, 'col', along_z(step))  20.1 us
    ppermute x12, starting transfers between devices, ypass(): return lax.ppermute(value, 'row', along_y(step))  17.2 us
    pallas_call x2, Pallas kernels, product(): pl.pallas_call(lambda *refs: product_body(*refs, part=part, first=first),...  11.7 us
    ppermute x6, starting transfers between devices, xpass(): return lax.ppermute(value, 'row', along_x(step))  8.71 us
    ppermute x12, waiting for transfers between devices, zpass(): return lax.ppermute(value, 'col', along_z(step))  8.44 us
  transfers between devices with their start and end apart: 47, of which 18 were waited for; matrix products, arithmetic and copies ran while one was open for 0% of the time, Pallas kernels for 10%

profile of v9, /device:TPU:0, one launch (start us, length us, event | category | flops | bytes accessed | tf_op | source)
XLA Modules:
  0.0 184.9 jit_solution(16509317762425304599)
XLA Ops:
  0.0 2.6 %scale.1 = (bf16[256,1024]{1,0:T(8,128)(2,1)}, bf16[256,1024]{1,0:T(8,128)(2,1)}, bf16[256,1024]{1,0:T(8,128)(2,1)}, bf16[256,1024]{1,0:T(8,128)(2,1)}) custom-call(s32[2,32]{1,0:T(2,128)} %mask_hbm.1, bf16[512,1024]{1,0:T(8,128)(2,1)} %panels_hbm.1, f32[1,1024]{1,0:T(1,128)} %bitcast.1), custom_call_target="tpu_custom_call" | custom-call | tf_op jit(solution)/shard_map/scale/pallas_call | solution.py:100
  2.7 3.2 %collective-permute-start.1 = (bf16[256,1024]{1,0:T(8,128)(2,1)}, bf16[256,1024]{1,0:T(8,128)(2,1)S(1)}, u32[]{:S(2)}, u32[]{:S(2)}) collective-permute-start(bf16[256,1024]{1,0:T(8,128)(2,1)} %get-tuple-element.35.refs_2_), channel_id=1, source_target_pairs={{0,24},{8,0},{16,8},{24,16},{32,56},{40,32},{48,40},{56,48},{64,88... | collective-permute-start | bytes 1572872 | tf_op jit(solution)/shard_map/ppermute | solution.py:348
  7.9 9.4 %collective-permute-done.1.refs_2_.refs_10_ = bf16[256,1024]{1,0:T(8,128)(2,1)S(1)} collective-permute-done((bf16[256,1024]{1,0:T(8,128)(2,1)}, bf16[256,1024]{1,0:T(8,128)(2,1)S(1)}, u32[]{:S(2)}, u32[]{:S(2)}) %collective-permute-start.1) | collective-permute-done | bytes 524320 | tf_op jit(solution)/shard_map/ppermute | solution.py:348
  17.3 3.6 %collective-permute-start.28 = (bf16[256,1024]{1,0:T(8,128)(2,1)}, bf16[256,1024]{1,0:T(8,128)(2,1)S(1)}, u32[]{:S(2)}, u32[]{:S(2)}) collective-permute-start(bf16[256,1024]{1,0:T(8,128)(2,1)} %get-tuple-element.34.refs_1_), channel_id=1, source_target_pairs={{0,24},{8,0},{16,8},{24,16},{32,56},{40,32},{48,40},{56,48},{64,88... | collective-permute-start | bytes 1572872 | tf_op jit(solution)/shard_map/ppermute | solution.py:348
  22.1 10.8 %collective-permute-done.5.refs_6_.refs_14_ = bf16[256,1024]{1,0:T(8,128)(2,1)S(1)} collective-permute-done((bf16[256,1024]{1,0:T(8,128)(2,1)}, bf16[256,1024]{1,0:T(8,128)(2,1)S(1)}, u32[]{:S(2)}, u32[]{:S(2)}) %collective-permute-start.5) | collective-permute-done | bytes 524320 | tf_op jit(solution)/shard_map/ppermute | solution.py:348
  32.8 2.8 %collective-permute-start.8 = (bf16[256,1024]{1,0:T(8,128)(2,1)}, bf16[256,1024]{1,0:T(8,128)(2,1)S(1)}, u32[]{:S(2)}, u32[]{:S(2)}) collective-permute-start(bf16[256,1024]{1,0:T(8,128)(2,1)} %get-tuple-element.33.refs_0_), channel_id=1, source_target_pairs={{0,96},{8,104},{16,112},{24,120},{32,0},{40,8},{48,16},{56,24},{64... | collective-permute-start | bytes 1572872 | tf_op jit(solution)/shard_map/ppermute | solution.py:352
  36.5 2.0 %collective-permute-start.31 = (bf16[256,1024]{1,0:T(8,128)(2,1)S(1)}, bf16[256,1024]{1,0:T(8,128)(2,1)S(1)}, u32[]{:S(2)}, u32[]{:S(2)}) collective-permute-start(bf16[256,1024]{1,0:T(8,128)(2,1)S(1)} %collective-permute-done.30.refs_6_), channel_id=1, source_target_pairs={{0,8},{8,16},{16,24},{24,0},{32,40},{40,48},{48,56},{56,32},{64,72... | collective-permute-start | bytes 1572872 | tf_op jit(solution)/shard_map/ppermute | solution.py:348
  38.5 9.8 %collective-permute-done.8.refs_10_.refs_18_ = bf16[256,1024]{1,0:T(8,128)(2,1)S(1)} collective-permute-done((bf16[256,1024]{1,0:T(8,128)(2,1)}, bf16[256,1024]{1,0:T(8,128)(2,1)S(1)}, u32[]{:S(2)}, u32[]{:S(2)}) %collective-permute-start.8) | collective-permute-done | bytes 524320 | tf_op jit(solution)/shard_map/ppermute | solution.py:352
  49.3 8.7 %collective-permute-done.9.refs_11_.refs_19_ = bf16[256,1024]{1,0:T(8,128)(2,1)S(1)} collective-permute-done((bf16[256,1024]{1,0:T(8,128)(2,1)S(1)}, bf16[256,1024]{1,0:T(8,128)(2,1)S(1)}, u32[]{:S(2)}, u32[]{:S(2)}) %collective-permute-start.9) | collective-permute-done | bytes 524320 | tf_op jit(solution)/shard_map/ppermute | solution.py:352
  59.8 5.0 %collective-permute-done.11.refs_12_.refs_20_ = bf16[256,1024]{1,0:T(8,128)(2,1)S(1)} collective-permute-done((bf16[256,1024]{1,0:T(8,128)(2,1)S(1)}, bf16[256,1024]{1,0:T(8,128)(2,1)S(1)}, u32[]{:S(2)}, u32[]{:S(2)}) %collective-permute-start.11) | collective-permute-done | bytes 524320 | tf_op jit(solution)/shard_map/ppermute | solution.py:352
  64.8 1.8 collective-permute-start.12
  69.9 5.8 %collective-permute-done.13.refs_15_.refs_23_ = bf16[256,1024]{1,0:T(8,128)(2,1)S(1)} collective-permute-done((bf16[256,1024]{1,0:T(8,128)(2,1)S(1)}, bf16[256,1024]{1,0:T(8,128)(2,1)S(1)}, u32[]{:S(2)}, u32[]{:S(2)}) %collective-permute-start.13) | collective-permute-done | bytes 524320 | tf_op jit(solution)/shard_map/ppermute | solution.py:352
  75.7 2.3 %collective-permute-done.12.refs_13_.refs_21_ = bf16[256,1024]{1,0:T(8,128)(2,1)S(1)} collective-permute-done((bf16[256,1024]{1,0:T(8,128)(2,1)S(1)}, bf16[256,1024]{1,0:T(8,128)(2,1)S(1)}, u32[]{:S(2)}, u32[]{:S(2)}) %collective-permute-start.12) | collective-permute-done | bytes 524320 | tf_op jit(solution)/shard_map/ppermute | solution.py:352
  78.0 3.0 %shard_map.47 = (bf16[2,384,256]{2,1,0:T(8,128)(2,1)S(1)}, bf16[2,384,256]{2,1,0:T(8,128)(2,1)S(1)}) custom-call(bf16[256,1024]{1,0:T(8,128)(2,1)S(1)} %get-tuple-element.50.refs_0_, bf16[256,1024]{1,0:T(8,128)(2,1)S(1)} %collective-permute-done.27.refs_1_, bf16[256,1024]{1,0:T(8,128)(2,1)S(1)} %collective-permute-done.28.refs_2_, ...), custom_call_target="tpu_custom_call" | custom-call | tf_op jit(solution)/shard_map/pallas_call | solution.py:247
  81.0 4.1 %collective-permute-start.38 = (bf16[2,384,256]{2,1,0:T(8,128)(2,1)S(1)}, bf16[2,384,256]{2,1,0:T(8,128)(2,1)S(1)}, u32[]{:S(2)}, u32[]{:S(2)}) collective-permute-start(bf16[2,384,256]{2,1,0:T(8,128)(2,1)S(1)} %get-tuple-element.56), channel_id=1, source_target_pairs={{0,6},{1,7},{2,0},{3,1},{4,2},{5,3},{6,4},{7,5},{8,14},{9,15},{10,... | collective-permute-start | bytes 1179656 | tf_op jit(solution)/shard_map/ppermute | solution.py:356
  85.1 4.9 %product.3 = (bf16[2,384,256]{2,1,0:T(8,128)(2,1)S(1)}, bf16[2,384,256]{2,1,0:T(8,128)(2,1)S(1)}, bf16[2,384,256]{2,1,0:T(8,128)(2,1)S(1)}, bf16[2,384,256]{2,1,0:T(8,128)(2,1)S(1)}) custom-call(bf16[256,1024]{1,0:T(8,128)(2,1)S(1)} %get-tuple-element.50.refs_0_, bf16[256,1024]{1,0:T(8,128)(2,1)S(1)} %collective-permute-done.27.refs_1_, ...), custom_call_target="tpu_custom_call" | custom-call | tf_op jit(solution)/shard_map/product/pallas_call | solution.py:208
  90.2 3.3 %collective-permute-start.35 = (bf16[2,384,256]{2,1,0:T(8,128)(2,1)S(1)}, bf16[2,384,256]{2,1,0:T(8,128)(2,1)S(1)}, u32[]{:S(2)}, u32[]{:S(2)}) collective-permute-start(bf16[2,384,256]{2,1,0:T(8,128)(2,1)S(1)} %get-tuple-element.52), channel_id=1, source_target_pairs={{0,6},{1,7},{2,0},{3,1},{4,2},{5,3},{6,4},{7,5},{8,14},{9,15},{10,... | collective-permute-start | bytes 1179656 | tf_op jit(solution)/shard_map/ppermute | solution.py:356
  93.6 3.1 %collective-permute-start.39 = (bf16[2,384,256]{2,1,0:T(8,128)(2,1)S(1)}, bf16[2,384,256]{2,1,0:T(8,128)(2,1)S(1)}, u32[]{:S(2)}, u32[]{:S(2)}) collective-permute-start(bf16[2,384,256]{2,1,0:T(8,128)(2,1)S(1)} %add_convert_fusion), channel_id=1, source_target_pairs={{0,6},{1,7},{2,0},{3,1},{4,2},{5,3},{6,4},{7,5},{8,14},{9,15},{10,... | collective-permute-start | bytes 1179656 | tf_op jit(solution)/shard_map/ppermute | solution.py:356
  96.6 1.7 collective-permute-done.36
  98.5 6.7 %product.2 = (bf16[2,128,256]{2,1,0:T(8,128)(2,1)S(1)}, bf16[2,128,256]{2,1,0:T(8,128)(2,1)S(1)}, bf16[2,128,256]{2,1,0:T(8,128)(2,1)S(1)}, bf16[2,128,256]{2,1,...) custom-call(bf16[256,1024]{1,0:T(8,128)(2,1)S(1)} %get-tuple-element, ...), custom_call_target="tpu_custom_call" | custom-call | tf_op jit(solution)/shard_map/product/pallas_call | solution.py:208
  105.2 3.3 %collective-permute-start.18 = (bf16[2,128,256]{2,1,0:T(8,128)(2,1)S(1)}, bf16[2,128,256]{2,1,0:T(8,128)(2,1)S(1)}, u32[]{:S(2)}, u32[]{:S(2)}) collective-permute-start(bf16[2,128,256]{2,1,0:T(8,128)(2,1)S(1)} %get-tuple-element.45), channel_id=1, source_target_pairs={{0,6},{1,7},{2,0},{3,1},{4,2},{5,3},{6,4},{7,5},{8,14},{9,15},{10,... | collective-permute-start | bytes 393224 | tf_op jit(solution)/shard_map/ppermute | solution.py:356
  108.5 3.0 %shard_map.46.own = f32[4,384,256]{2,1,0:T(8,128)S(1)} custom-call(bf16[256,1024]{1,0:T(8,128)(2,1)S(1)} %get-tuple-element.50.refs_0_, bf16[256,1024]{1,0:T(8,128)(2,1)S(1)} %collective-permute-done.27.refs_1_, bf16[256,1024]{1,0:T(8,128)(2,1)S(1)} %collective-permute-done.28.refs_2_, bf16[256,1024]{1,0:T(8,128)(2,1)S(1)} %collective-permute-done.29.refs_3_, ...), custom_call_target="tpu_custom_call" | custom-call | tf_op jit(solution)/shard_map/pallas_call | solution.py:247
  113.0 1.8 collective-permute-start.14
  114.8 1.5 collective-permute-start.15
  121.4 4.6 %collective-permute-done.17.sum_up = bf16[2,128,256]{2,1,0:T(8,128)(2,1)S(1)} collective-permute-done((bf16[2,128,256]{2,1,0:T(8,128)(2,1)S(1)}, bf16[2,128,256]{2,1,0:T(8,128)(2,1)S(1)}, u32[]{:S(2)}, u32[]{:S(2)}) %collective-permute-start.17) | collective-permute-done | bytes 131104 | tf_op jit(solution)/shard_map/ppermute | solution.py:356
  126.1 3.3 %collective-permute-start.20 = (bf16[128,256]{1,0:T(8,128)(2,1)S(1)}, bf16[128,256]{1,0:T(8,128)(2,1)S(1)}, u32[]{:S(2)}, u32[]{:S(2)}) collective-permute-start(bf16[128,256]{1,0:T(8,128)(2,1)S(1)} %get-tuple-element.47), channel_id=1, source_target_pairs={{0,24},{8,0},{16,8},{24,16},{32,56},{40,32},{48,40},{56,48},{64,88... | collective-permute-start | bytes 196616 | tf_op jit(solution)/shard_map/ppermute | solution.py:348
  131.3 1.8 collective-permute-start.21
  133.1 4.0 %collective-permute-done.21.refs_3_ = bf16[128,256]{1,0:T(8,128)(2,1)S(1)} collective-permute-done((bf16[128,256]{1,0:T(8,128)(2,1)S(1)}, bf16[128,256]{1,0:T(8,128)(2,1)S(1)}, u32[]{:S(2)}, u32[]{:S(2)}) %collective-permute-start.21) | collective-permute-done | bytes 65568 | tf_op jit(solution)/shard_map/ppermute | solution.py:348
  137.1 1.6 collective-permute-start.22
  138.7 4.9 %collective-permute-done.22.refs_4_ = bf16[128,256]{1,0:T(8,128)(2,1)S(1)} collective-permute-done((bf16[128,256]{1,0:T(8,128)(2,1)S(1)}, bf16[128,256]{1,0:T(8,128)(2,1)S(1)}, u32[]{:S(2)}, u32[]{:S(2)}) %collective-permute-start.22) | collective-permute-done | bytes 65568 | tf_op jit(solution)/shard_map/ppermute | solution.py:348
  144.6 3.6 %pack.2.refs_9_ = bf16[16,1,256,256]{3,2,1,0:T(8,128)(2,1)S(1)} custom-call(s32[2,4]{1,0:T(2,128)S(1)} %copy-done.3, bf16[384,256]{1,0:T(8,128)(2,1)S(1)} %get-tuple-element.57.refs_1_, bf16[384,256]{1,0:T(8,128)(2,1)S(1)} %collective-permute-done.40.refs_2_, bf16[384,256]{1,0:T(8,128)(2,1)S(1)} %collective-permute-done.41.refs_3_, ...), custom_call_target="tpu_custom_call" | custom-call | tf_op jit(solution)/shard_map/pack/pallas_call | solution.py:330
  149.6 34.0 %all_to_all.5 = bf16[16,1,256,256]{3,2,1,0:T(8,128)(2,1)S(1)} all-to-all(bf16[16,1,256,256]{3,2,1,0:T(8,128)(2,1)S(1)} %pack.3), channel_id=1, replica_groups=mesh['row'=16,'col'=8] {'row'}, dimensions={0} | all-to-all | bytes 4194304 | tf_op jit(solution)/shard_map/all_to_all | solution.py:409
  (86 shorter events, 22.8 us)
Async XLA Ops:
  2.7 14.7 %collective-permute-start.1 = (bf16[256,1024]{1,0:T(8,128)(2,1)}, bf16[256,1024]{1,0:T(8,128)(2,1)S(1)}, u32[]{:S(2)}, u32[]{:S(2)}) collective-permute-start(bf16[256,1024]{1,0:T(8,128)(2,1)} %get-tuple-element.35.refs_2_), channel_id=1, source_target_pairs={{0,24},{8,0},{16,8},{24,16},{32,56},{40,32},{48,40},{56,48},{64,88... | collective-permute-start | bytes 1572872 | tf_op jit(solution)/shard_map/ppermute | solution.py:348
  5.8 15.1 %collective-permute-start.7 = (bf16[256,1024]{1,0:T(8,128)(2,1)}, bf16[256,1024]{1,0:T(8,128)(2,1)S(1)}, u32[]{:S(2)}, u32[]{:S(2)}) collective-permute-start(bf16[256,1024]{1,0:T(8,128)(2,1)} %get-tuple-element.38), channel_id=1, source_target_pairs={{0,1},{1,0},{2,3},{3,2},{4,5},{5,4},{6,7},{7,6},{8,9},{9,8},{10,11... | collective-permute-start | bytes 1572872 | tf_op jit(solution)/shard_map/ppermute | solution.py:360
  5.8 16.2 %collective-permute-start.30 = (bf16[256,1024]{1,0:T(8,128)(2,1)}, bf16[256,1024]{1,0:T(8,128)(2,1)S(1)}, u32[]{:S(2)}, u32[]{:S(2)}) collective-permute-start(bf16[256,1024]{1,0:T(8,128)(2,1)} %get-tuple-element.34.refs_1_), channel_id=1, source_target_pairs={{0,8},{8,16},{16,24},{24,0},{32,40},{40,48},{48,56},{56,32},{64,72... | collective-permute-start | bytes 1572872 | tf_op jit(solution)/shard_map/ppermute | solution.py:348
  5.9 27.0 %collective-permute-start.5 = (bf16[256,1024]{1,0:T(8,128)(2,1)}, bf16[256,1024]{1,0:T(8,128)(2,1)S(1)}, u32[]{:S(2)}, u32[]{:S(2)}) collective-permute-start(bf16[256,1024]{1,0:T(8,128)(2,1)} %get-tuple-element.35.refs_2_), channel_id=1, source_target_pairs={{0,8},{8,16},{16,24},{24,0},{32,40},{40,48},{48,56},{56,32},{64,72... | collective-permute-start | bytes 1572872 | tf_op jit(solution)/shard_map/ppermute | solution.py:348
  6.4 29.2 %collective-permute-start.10 = (bf16[256,1024]{1,0:T(8,128)(2,1)}, bf16[256,1024]{1,0:T(8,128)(2,1)S(1)}, u32[]{:S(2)}, u32[]{:S(2)}) collective-permute-start(bf16[256,1024]{1,0:T(8,128)(2,1)} %get-tuple-element.33.refs_0_), channel_id=1, source_target_pairs={{0,32},{8,40},{16,48},{24,56},{32,64},{40,72},{48,80},{56,88},{64,... | collective-permute-start | bytes 1572872 | tf_op jit(solution)/shard_map/ppermute | solution.py:352
  17.3 18.3 %collective-permute-start.28 = (bf16[256,1024]{1,0:T(8,128)(2,1)}, bf16[256,1024]{1,0:T(8,128)(2,1)S(1)}, u32[]{:S(2)}, u32[]{:S(2)}) collective-permute-start(bf16[256,1024]{1,0:T(8,128)(2,1)} %get-tuple-element.34.refs_1_), channel_id=1, source_target_pairs={{0,24},{8,0},{16,8},{24,16},{32,56},{40,32},{48,40},{56,48},{64,88... | collective-permute-start | bytes 1572872 | tf_op jit(solution)/shard_map/ppermute | solution.py:348
  20.9 15.6 %collective-permute-start = (bf16[256,1024]{1,0:T(8,128)(2,1)}, bf16[256,1024]{1,0:T(8,128)(2,1)S(1)}, u32[]{:S(2)}, u32[]{:S(2)}) collective-permute-start(bf16[256,1024]{1,0:T(8,128)(2,1)} %get-tuple-element.35.refs_2_), channel_id=1, source_target_pairs={{0,1},{1,0},{2,3},{3,2},{4,5},{5,4},{6,7},{7,6},{8,9},{9,8},{10,11... | collective-permute-start | bytes 1572872 | tf_op jit(solution)/shard_map/ppermute | solution.py:360
  22.1 16.4 %collective-permute-start.27 = (bf16[256,1024]{1,0:T(8,128)(2,1)}, bf16[256,1024]{1,0:T(8,128)(2,1)S(1)}, u32[]{:S(2)}, u32[]{:S(2)}) collective-permute-start(bf16[256,1024]{1,0:T(8,128)(2,1)} %get-tuple-element.34.refs_1_), channel_id=1, source_target_pairs={{0,1},{1,0},{2,3},{3,2},{4,5},{5,4},{6,7},{7,6},{8,9},{9,8},{10,11... | collective-permute-start | bytes 1572872 | tf_op jit(solution)/shard_map/ppermute | solution.py:360
  32.8 15.4 %collective-permute-start.8 = (bf16[256,1024]{1,0:T(8,128)(2,1)}, bf16[256,1024]{1,0:T(8,128)(2,1)S(1)}, u32[]{:S(2)}, u32[]{:S(2)}) collective-permute-start(bf16[256,1024]{1,0:T(8,128)(2,1)} %get-tuple-element.33.refs_0_), channel_id=1, source_target_pairs={{0,96},{8,104},{16,112},{24,120},{32,0},{40,8},{48,16},{56,24},{64... | collective-permute-start | bytes 1572872 | tf_op jit(solution)/shard_map/ppermute | solution.py:352
  35.6 13.2 %collective-permute-start.3 = (bf16[256,1024]{1,0:T(8,128)(2,1)S(1)}, bf16[256,1024]{1,0:T(8,128)(2,1)S(1)}, u32[]{:S(2)}, u32[]{:S(2)}) collective-permute-start(bf16[256,1024]{1,0:T(8,128)(2,1)S(1)} %collective-permute-done.1.refs_2_.refs_10_), channel_id=1, source_target_pairs={{0,24},{8,0},{16,8},{24,16},{32,56},{40,32},{48,40},{56,48},{64,88... | collective-permute-start | bytes 1572872 | tf_op jit(solution)/shard_map/ppermute | solution.py:348
  35.6 22.4 %collective-permute-start.9 = (bf16[256,1024]{1,0:T(8,128)(2,1)S(1)}, bf16[256,1024]{1,0:T(8,128)(2,1)S(1)}, u32[]{:S(2)}, u32[]{:S(2)}) collective-permute-start(bf16[256,1024]{1,0:T(8,128)(2,1)S(1)} %collective-permute-done.7.refs_9_.refs_17_), channel_id=1, source_target_pairs={{0,96},{8,104},{16,112},{24,120},{32,0},{40,8},{48,16},{56,24},{64... | collective-permute-start | bytes 1572872 | tf_op jit(solution)/shard_map/ppermute | solution.py:352
  36.5 21.5 %collective-permute-start.31 = (bf16[256,1024]{1,0:T(8,128)(2,1)S(1)}, bf16[256,1024]{1,0:T(8,128)(2,1)S(1)}, u32[]{:S(2)}, u32[]{:S(2)}) collective-permute-start(bf16[256,1024]{1,0:T(8,128)(2,1)S(1)} %collective-permute-done.30.refs_6_), channel_id=1, source_target_pairs={{0,8},{8,16},{16,24},{24,0},{32,40},{40,48},{48,56},{56,32},{64,72... | collective-permute-start | bytes 1572872 | tf_op jit(solution)/shard_map/ppermute | solution.py:348
  38.5 20.8 %collective-permute-start.2 = (bf16[256,1024]{1,0:T(8,128)(2,1)S(1)}, bf16[256,1024]{1,0:T(8,128)(2,1)S(1)}, u32[]{:S(2)}, u32[]{:S(2)}) collective-permute-start(bf16[256,1024]{1,0:T(8,128)(2,1)S(1)} %collective-permute-done.1.refs_2_.refs_10_), channel_id=1, source_target_pairs={{0,1},{1,0},{2,3},{3,2},{4,5},{5,4},{6,7},{7,6},{8,9},{9,8},{10,11... | collective-permute-start | bytes 1572872 | tf_op jit(solution)/shard_map/ppermute | solution.py:360
  48.8 16.0 %collective-permute-start.11 = (bf16[256,1024]{1,0:T(8,128)(2,1)S(1)}, bf16[256,1024]{1,0:T(8,128)(2,1)S(1)}, u32[]{:S(2)}, u32[]{:S(2)}) collective-permute-start(bf16[256,1024]{1,0:T(8,128)(2,1)S(1)} %collective-permute-done.10.refs_14_.refs_22_), channel_id=1, source_target_pairs={{0,32},{8,40},{16,48},{24,56},{32,64},{40,72},{48,80},{56,88},{64,... | collective-permute-start | bytes 1572872 | tf_op jit(solution)/shard_map/ppermute | solution.py:352
  58.1 17.6 %collective-permute-start.13 = (bf16[256,1024]{1,0:T(8,128)(2,1)S(1)}, bf16[256,1024]{1,0:T(8,128)(2,1)S(1)}, u32[]{:S(2)}, u32[]{:S(2)}) collective-permute-start(bf16[256,1024]{1,0:T(8,128)(2,1)S(1)} %collective-permute-done.7.refs_9_.refs_17_), channel_id=1, source_target_pairs={{0,32},{8,40},{16,48},{24,56},{32,64},{40,72},{48,80},{56,88},{64,... | collective-permute-start | bytes 1572872 | tf_op jit(solution)/shard_map/ppermute | solution.py:352
  59.3 16.4 %collective-permute-start.29 = (bf16[256,1024]{1,0:T(8,128)(2,1)S(1)}, bf16[256,1024]{1,0:T(8,128)(2,1)S(1)}, u32[]{:S(2)}, u32[]{:S(2)}) collective-permute-start(bf16[256,1024]{1,0:T(8,128)(2,1)S(1)} %collective-permute-done.28.refs_2_), channel_id=1, source_target_pairs={{0,1},{1,0},{2,3},{3,2},{4,5},{5,4},{6,7},{7,6},{8,9},{9,8},{10,11... | collective-permute-start | bytes 1572872 | tf_op jit(solution)/shard_map/ppermute | solution.py:360
  59.5 16.2 %collective-permute-start.4 = (bf16[256,1024]{1,0:T(8,128)(2,1)S(1)}, bf16[256,1024]{1,0:T(8,128)(2,1)S(1)}, u32[]{:S(2)}, u32[]{:S(2)}) collective-permute-start(bf16[256,1024]{1,0:T(8,128)(2,1)S(1)} %collective-permute-done.3.refs_4_.refs_12_), channel_id=1, source_target_pairs={{0,1},{1,0},{2,3},{3,2},{4,5},{5,4},{6,7},{7,6},{8,9},{9,8},{10,11... | collective-permute-start | bytes 1572872 | tf_op jit(solution)/shard_map/ppermute | solution.py:360
  64.8 13.1 %collective-permute-start.12 = (bf16[256,1024]{1,0:T(8,128)(2,1)S(1)}, bf16[256,1024]{1,0:T(8,128)(2,1)S(1)}, u32[]{:S(2)}, u32[]{:S(2)}) collective-permute-start(bf16[256,1024]{1,0:T(8,128)(2,1)S(1)} %collective-permute-done.9.refs_11_.refs_19_), channel_id=1, source_target_pairs={{0,96},{8,104},{16,112},{24,120},{32,0},{40,8},{48,16},{56,24},{64... | collective-permute-start | bytes 1572872 | tf_op jit(solution)/shard_map/ppermute | solution.py:352
  66.6 11.3 %collective-permute-start.32 = (bf16[256,1024]{1,0:T(8,128)(2,1)S(1)}, bf16[256,1024]{1,0:T(8,128)(2,1)S(1)}, u32[]{:S(2)}, u32[]{:S(2)}) collective-permute-start(bf16[256,1024]{1,0:T(8,128)(2,1)S(1)} %collective-permute-done.31.refs_4_), channel_id=1, source_target_pairs={{0,1},{1,0},{2,3},{3,2},{4,5},{5,4},{6,7},{7,6},{8,9},{9,8},{10,11... | collective-permute-start | bytes 1572872 | tf_op jit(solution)/shard_map/ppermute | solution.py:360
  81.0 12.5 %collective-permute-start.38 = (bf16[2,384,256]{2,1,0:T(8,128)(2,1)S(1)}, bf16[2,384,256]{2,1,0:T(8,128)(2,1)S(1)}, u32[]{:S(2)}, u32[]{:S(2)}) collective-permute-start(bf16[2,384,256]{2,1,0:T(8,128)(2,1)S(1)} %get-tuple-element.56), channel_id=1, source_target_pairs={{0,6},{1,7},{2,0},{3,1},{4,2},{5,3},{6,4},{7,5},{8,14},{9,15},{10,... | collective-permute-start | bytes 1179656 | tf_op jit(solution)/shard_map/ppermute | solution.py:356
  85.1 13.2 %collective-permute-start.36 = (bf16[2,384,256]{2,1,0:T(8,128)(2,1)S(1)}, bf16[2,384,256]{2,1,0:T(8,128)(2,1)S(1)}, u32[]{:S(2)}, u32[]{:S(2)}) collective-permute-start(bf16[2,384,256]{2,1,0:T(8,128)(2,1)S(1)} %get-tuple-element.54), channel_id=1, source_target_pairs={{0,2},{1,3},{2,4},{3,5},{4,6},{5,7},{6,0},{7,1},{8,10},{9,11},{10,... | collective-permute-start | bytes 1179656 | tf_op jit(solution)/shard_map/ppermute | solution.py:356
  90.1 22.9 %collective-permute-start.34 = (bf16[2,384,256]{2,1,0:T(8,128)(2,1)S(1)}, bf16[2,384,256]{2,1,0:T(8,128)(2,1)S(1)}, u32[]{:S(2)}, u32[]{:S(2)}) collective-permute-start(bf16[2,384,256]{2,1,0:T(8,128)(2,1)S(1)} %get-tuple-element.51), channel_id=1, source_target_pairs={{0,2},{1,3},{2,4},{3,5},{4,6},{5,7},{6,0},{7,1},{8,10},{9,11},{10,... | collective-permute-start | bytes 1179656 | tf_op jit(solution)/shard_map/ppermute | solution.py:356
  90.2 24.6 %collective-permute-start.35 = (bf16[2,384,256]{2,1,0:T(8,128)(2,1)S(1)}, bf16[2,384,256]{2,1,0:T(8,128)(2,1)S(1)}, u32[]{:S(2)}, u32[]{:S(2)}) collective-permute-start(bf16[2,384,256]{2,1,0:T(8,128)(2,1)S(1)} %get-tuple-element.52), channel_id=1, source_target_pairs={{0,6},{1,7},{2,0},{3,1},{4,2},{5,3},{6,4},{7,5},{8,14},{9,15},{10,... | collective-permute-start | bytes 1179656 | tf_op jit(solution)/shard_map/ppermute | solution.py:356
  93.6 22.7 %collective-permute-start.39 = (bf16[2,384,256]{2,1,0:T(8,128)(2,1)S(1)}, bf16[2,384,256]{2,1,0:T(8,128)(2,1)S(1)}, u32[]{:S(2)}, u32[]{:S(2)}) collective-permute-start(bf16[2,384,256]{2,1,0:T(8,128)(2,1)S(1)} %add_convert_fusion), channel_id=1, source_target_pairs={{0,6},{1,7},{2,0},{3,1},{4,2},{5,3},{6,4},{7,5},{8,14},{9,15},{10,... | collective-permute-start | bytes 1179656 | tf_op jit(solution)/shard_map/ppermute | solution.py:356
  98.4 19.3 %collective-permute-start.37 = (bf16[2,384,256]{2,1,0:T(8,128)(2,1)S(1)}, bf16[2,384,256]{2,1,0:T(8,128)(2,1)S(1)}, u32[]{:S(2)}, u32[]{:S(2)}) collective-permute-start(bf16[2,384,256]{2,1,0:T(8,128)(2,1)S(1)} %add_convert_fusion.1), channel_id=1, source_target_pairs={{0,2},{1,3},{2,4},{3,5},{4,6},{5,7},{6,0},{7,1},{8,10},{9,11},{10,... | collective-permute-start | bytes 1179656 | tf_op jit(solution)/shard_map/ppermute | solution.py:356
  118.0 11.4 %collective-permute-start.40 = (bf16[384,256]{1,0:T(8,128)(2,1)S(1)}, bf16[384,256]{1,0:T(8,128)(2,1)S(1)}, u32[]{:S(2)}, u32[]{:S(2)}) collective-permute-start(bf16[384,256]{1,0:T(8,128)(2,1)S(1)} %get-tuple-element.58), channel_id=1, source_target_pairs={{0,24},{8,0},{16,8},{24,16},{32,56},{40,32},{48,40},{56,48},{64,88... | collective-permute-start | bytes 589832 | tf_op jit(solution)/shard_map/ppermute | solution.py:348
  118.4 11.5 %collective-permute-start.41 = (bf16[384,256]{1,0:T(8,128)(2,1)S(1)}, bf16[384,256]{1,0:T(8,128)(2,1)S(1)}, u32[]{:S(2)}, u32[]{:S(2)}) collective-permute-start(bf16[384,256]{1,0:T(8,128)(2,1)S(1)} %get-tuple-element.59), channel_id=1, source_target_pairs={{0,16},{8,24},{16,0},{24,8},{32,48},{40,56},{48,32},{56,40},{64,80... | collective-permute-start | bytes 589832 | tf_op jit(solution)/shard_map/ppermute | solution.py:348
  120.2 12.9 %collective-permute-start.42 = (bf16[384,256]{1,0:T(8,128)(2,1)S(1)}, bf16[384,256]{1,0:T(8,128)(2,1)S(1)}, u32[]{:S(2)}, u32[]{:S(2)}) collective-permute-start(bf16[384,256]{1,0:T(8,128)(2,1)S(1)} %get-tuple-element.60), channel_id=1, source_target_pairs={{0,8},{8,16},{16,24},{24,0},{32,40},{40,48},{48,56},{56,32},{64,72... | collective-permute-start | bytes 589832 | tf_op jit(solution)/shard_map/ppermute | solution.py:348
  129.4 14.2 %collective-permute-start.43 = (bf16[384,256]{1,0:T(8,128)(2,1)S(1)}, bf16[384,256]{1,0:T(8,128)(2,1)S(1)}, u32[]{:S(2)}, u32[]{:S(2)}) collective-permute-start(bf16[384,256]{1,0:T(8,128)(2,1)S(1)} %get-tuple-element.57.refs_1_), channel_id=1, source_target_pairs={{0,1},{1,0},{2,3},{3,2},{4,5},{5,4},{6,7},{7,6},{8,9},{9,8},{10,11... | collective-permute-start | bytes 589832 | tf_op jit(solution)/shard_map/ppermute | solution.py:360
  129.4 14.7 %collective-permute-start.44 = (bf16[384,256]{1,0:T(8,128)(2,1)S(1)}, bf16[384,256]{1,0:T(8,128)(2,1)S(1)}, u32[]{:S(2)}, u32[]{:S(2)}) collective-permute-start(bf16[384,256]{1,0:T(8,128)(2,1)S(1)} %collective-permute-done.40.refs_2_), channel_id=1, source_target_pairs={{0,1},{1,0},{2,3},{3,2},{4,5},{5,4},{6,7},{7,6},{8,9},{9,8},{10,11... | collective-permute-start | bytes 589832 | tf_op jit(solution)/shard_map/ppermute | solution.py:360
  129.9 14.3 %collective-permute-start.45 = (bf16[384,256]{1,0:T(8,128)(2,1)S(1)}, bf16[384,256]{1,0:T(8,128)(2,1)S(1)}, u32[]{:S(2)}, u32[]{:S(2)}) collective-permute-start(bf16[384,256]{1,0:T(8,128)(2,1)S(1)} %collective-permute-done.41.refs_3_), channel_id=1, source_target_pairs={{0,1},{1,0},{2,3},{3,2},{4,5},{5,4},{6,7},{7,6},{8,9},{9,8},{10,11... | collective-permute-start | bytes 589832 | tf_op jit(solution)/shard_map/ppermute | solution.py:360
  133.1 11.5 %collective-permute-start.46 = (bf16[384,256]{1,0:T(8,128)(2,1)S(1)}, bf16[384,256]{1,0:T(8,128)(2,1)S(1)}, u32[]{:S(2)}, u32[]{:S(2)}) collective-permute-start(bf16[384,256]{1,0:T(8,128)(2,1)S(1)} %collective-permute-done.42.refs_4_), channel_id=1, source_target_pairs={{0,1},{1,0},{2,3},{3,2},{4,5},{5,4},{6,7},{7,6},{8,9},{9,8},{10,11... | collective-permute-start | bytes 589832 | tf_op jit(solution)/shard_map/ppermute | solution.py:360
  (19 other events, 124.5 us)

commit v10 on v8

--- a/solution.py
+++ b/solution.py
@@ -8,7 +8,7 @@
 
 TILE = 256
 HALF = 128
-CUT = 128
+CUT = 160
 PARTS = ((0, CUT), (CUT, TILE - CUT))
 
 
@@ -190,20 +190,24 @@
         copy.start()
     for copy in copies:
         copy.wait()
-    up, down, next_low, prev_high = refs[:4]
-    far_up, far_down, at = (refs[4], refs[5], 0) if first else (next_low, prev_high, 2)
-    blocks(rows_ref, cols_ref[(z + 2) % 4], ((up, 0), (up, 1), (down, 0), (down, 1)))
+    if first:
+        next_low, prev_high, far_up, far_down = refs[:4]
+        at = 0
+    else:
+        up, down, next_low, prev_high, own = refs[:5]
+        far_up, far_down, at = next_low, prev_high, 2
+        blocks(rows_ref, cols_ref[(z + 2) % 4], ((up, 0), (up, 1), (down, 0), (down, 1)))
     blocks(rows_ref, cols_ref[(z + 1) % 4], ((next_low, 0), (next_low, 1), (far_up, at), (far_up, at + 1)))
     blocks(rows_ref, cols_ref[(z + 3) % 4], ((far_down, at), (far_down, at + 1), (prev_high, 0), (prev_high, 1)))
     if not first:
-        blocks(rows_ref, cols_ref[z], tuple((refs[4], j) for j in range(4)))
+        blocks(rows_ref, cols_ref[z], tuple((own, j) for j in range(4)))
 
 
 def product(part, tops, lows, cols, first):
     four = jax.ShapeDtypeStruct((4, 2 * part[1], TILE), jnp.bfloat16)
     two = jax.ShapeDtypeStruct((2, 2 * part[1], TILE), jnp.bfloat16)
     kept = jax.ShapeDtypeStruct((4, 2 * part[1], TILE), jnp.float32)
-    shapes = (two,) * 6 if first else (two, two, four, four, kept)
+    shapes = (two,) * 4 if first else (two, two, four, four, kept)
     operands = (*needs(part, tops, lows), *cols)
     return pl.pallas_call(
         lambda *refs: product_body(*refs, part=part, first=first),
@@ -221,33 +225,34 @@
     )(*operands)
 
 
-def kept_body(*refs, part):
+def chunk_body(*refs, part, step):
     tops, lows, refs = split_rows(part, refs)
-    cols, own = refs[:8], refs[8]
-    rows_ref, right_ref, row_sems, col_sems = refs[9:]
+    cols, outs = refs[:8], refs[8:-4]
+    rows_ref, right_ref, row_sems, col_sems = refs[-4:]
     x, _, z, _ = position()
     right = load_cols(cols, lambda d, across: right_ref.at[:, across], col_sems)
     copies = load_rows(tops, lows, rows_ref, row_sems, part)
     for act in (lambda copy: copy.start(), lambda copy: copy.wait()):
         for d in range(4):
 
-            @pl.when((x + d) % 4 == z)
+            @pl.when((x + d) % 4 == (z + step) % 4)
             def _():
                 for copy in right[2 * d : 2 * d + 2]:
                     act(copy)
 
         for copy in copies:
             act(copy)
-    blocks(rows_ref, right_ref[...], tuple((own, j) for j in range(4)))
-
-
-def kept_product(part, tops, lows, cols):
+    each = 4 // len(outs)
+    blocks(rows_ref, right_ref[...], tuple((outs[j // each], j % each) for j in range(4)))
+
+
+def chunk_product(part, tops, lows, cols, step, shapes):
     operands = (*needs(part, tops, lows), *cols)
     return pl.pallas_call(
-        lambda *refs: kept_body(*refs, part=part),
-        out_shape=jax.ShapeDtypeStruct((4, 2 * part[1], TILE), jnp.float32),
+        lambda *refs: chunk_body(*refs, part=part, step=step),
+        out_shape=tuple(jax.ShapeDtypeStruct((n, 2 * part[1], TILE), dtype) for n, dtype in shapes),
         in_specs=[pl.BlockSpec(memory_space=pl.ANY)] * len(operands),
-        out_specs=pl.BlockSpec(memory_space=pltpu.VMEM),
+        out_specs=(pl.BlockSpec(memory_space=pltpu.VMEM),) * len(shapes),
         scratch_shapes=[
             pltpu.VMEM((4, 2 * part[1], 2048), jnp.bfloat16),
             pltpu.VMEM((TILE, 2048), jnp.bfloat16),
@@ -255,7 +260,6 @@
             pltpu.SemaphoreType.DMA((8,)),
         ],
         compiler_params=pltpu.CompilerParams(vmem_limit_bytes=32 * 1024 * 1024),
-        name="kept",
     )(*operands)
 
 
@@ -417,15 +421,14 @@
     c0, top, low = stage(c0, top, low)
     cols = (c0, c1, cp0, cp1, co0, co1, cm0, cm1)
     rows = []
-    for own, pieces in (
-        (top, (sent_top, top_p, top_o, top_m)), (low, (sent_low, low_p, low_o, low_m))
-    ):
+    for own, pieces in ((top, (sent_top, top_p, top_o, top_m)), (low, (sent_low, low_p, low_o, low_m))):
         others = [swap(value) for value in pieces]
         rows.append([piece for pair in zip((own, *pieces[1:]), others) for piece in pair])
-    sent = product(PARTS[0], *rows, cols, True)
-    kept = kept_product(PARTS[0], *rows, cols)
+    shares = chunk_product(PARTS[0], *rows, cols, 2, ((2, jnp.bfloat16),) * 2)
+    sides = product(PARTS[0], *rows, cols, True)
+    kept = chunk_product(PARTS[0], *rows, cols, 0, ((4, jnp.float32),))
     later = product(PARTS[1], *rows, cols, False)
-    arrived = exchange(reduce_along_z((*sent, kept)))
+    arrived = exchange(reduce_along_z((*shares, *sides, *kept)))
     outgoing = pack(PARTS[0], owner_rows, arrived)
     outgoing = pack(PARTS[1], owner_rows, exchange(reduce_along_z(later)), outgoing)
     return lax.all_to_all(outgoing, "row", split_axis=0, concat_axis=0, tiled=True)

time: 172 us -> 187 us (1.087)
  waiting for transfers between devices: 71.4 us -> 83 us
  Pallas kernels: 20.3 us -> 24.7 us
  starting transfers between devices: 43.6 us -> 39.9 us
  blocking collectives: 32 us -> 33.9 us
    ppermute x6, waiting for transfers between devices: 13.2 us -> 31.5 us  [xpass(): return lax.ppermute(value, 'row', along_x(step))]
    ppermute x12, waiting for transfers between devices: 37.7 us -> 31 us  [ypass(): return lax.ppermute(value, 'row', along_y(step))]
    pallas_call x1 -> x2, Pallas kernels: 2.09 us -> 5.53 us  [chunk_product(): pl.pallas_call(lambda *refs: chunk_body(*refs, part=part, step=step), out...]
    ppermute x6, starting transfers between devices: 11.3 us -> 8.71 us  [xpass(): return lax.ppermute(value, 'row', along_x(step))]
    all_to_all x1, blocking collectives: 32 us -> 33.9 us  [shards(): lax.all_to_all(outgoing, 'row', split_axis=0, concat_axis=0, tiled=True)]
  transfers between devices with their start and end apart: 45 -> 45, of which waited for: 14 -> 17; matrix products, arithmetic and copies ran while one was open for 0% -> 0% of each run, Pallas kernels for 9% -> 10%
where the time goes in v10:
time: 187 us; the launch traced here: 186 us
  waiting for transfers between devices  83 us (44%)
  starting transfers between devices  39.9 us (21%)
  blocking collectives  33.9 us (18%)
  Pallas kernels  24.7 us (13%)
  local copies, waits for them, and re-layouts  4.45 us (2%)
    all_to_all x1, blocking collectives, shards(): lax.all_to_all(outgoing, 'row', split_axis=0, concat_axis=0, tiled=True)  33.9 us
    ppermute x6, waiting for transfers between devices, xpass(): return lax.ppermute(value, 'row', along_x(step))  31.5 us
    ppermute x12, waiting for transfers between devices, ypass(): return lax.ppermute(value, 'row', along_y(step))  31 us
    ppermute x10, waiting for transfers between devices, zpass(): return lax.ppermute(value, 'col', along_z(step))  20.4 us
    ppermute x12, starting transfers between devices, ypass(): return lax.ppermute(value, 'row', along_y(step))  16.7 us
    ppermute x10, starting transfers between devices, zpass(): return lax.ppermute(value, 'col', along_z(step))  12.3 us
    pallas_call x2, Pallas kernels, product(): pl.pallas_call(lambda *refs: product_body(*refs, part=part, first=first),...  11.2 us
    ppermute x6, starting transfers between devices, xpass(): return lax.ppermute(value, 'row', along_x(step))  8.71 us
  transfers between devices with their start and end apart: 45, of which 17 were waited for; matrix products, arithmetic and copies ran while one was open for 0% of the time, Pallas kernels for 10%

profile of v10, /device:TPU:0, one launch (start us, length us, event | category | flops | bytes accessed | tf_op | source)
XLA Modules:
  0.0 186.4 jit_solution(1384480762708635764)
XLA Ops:
  0.0 2.6 %scale.1 = (bf16[256,1024]{1,0:T(8,128)(2,1)}, bf16[256,1024]{1,0:T(8,128)(2,1)}, bf16[256,1024]{1,0:T(8,128)(2,1)}, bf16[256,1024]{1,0:T(8,128)(2,1)}) custom-call(s32[2,32]{1,0:T(2,128)} %mask_hbm.1, bf16[512,1024]{1,0:T(8,128)(2,1)} %panels_hbm.1, f32[1,1024]{1,0:T(1,128)} %bitcast.1), custom_call_target="tpu_custom_call" | custom-call | tf_op jit(solution)/shard_map/scale/pallas_call | solution.py:100
  2.6 3.2 %collective-permute-start.1 = (bf16[256,1024]{1,0:T(8,128)(2,1)}, bf16[256,1024]{1,0:T(8,128)(2,1)S(1)}, u32[]{:S(2)}, u32[]{:S(2)}) collective-permute-start(bf16[256,1024]{1,0:T(8,128)(2,1)} %get-tuple-element.33.refs_2_), channel_id=1, source_target_pairs={{0,24},{8,0},{16,8},{24,16},{32,56},{40,32},{48,40},{56,48},{64,88... | collective-permute-start | bytes 1572872 | tf_op jit(solution)/shard_map/ppermute | solution.py:370
  6.4 1.5 collective-permute-start.10
  7.9 9.4 %collective-permute-done.1.refs_2_.refs_10_ = bf16[256,1024]{1,0:T(8,128)(2,1)S(1)} collective-permute-done((bf16[256,1024]{1,0:T(8,128)(2,1)}, bf16[256,1024]{1,0:T(8,128)(2,1)S(1)}, u32[]{:S(2)}, u32[]{:S(2)}) %collective-permute-start.1) | collective-permute-done | bytes 524320 | tf_op jit(solution)/shard_map/ppermute | solution.py:370
  17.3 3.6 %collective-permute-start.26 = (bf16[256,1024]{1,0:T(8,128)(2,1)}, bf16[256,1024]{1,0:T(8,128)(2,1)S(1)}, u32[]{:S(2)}, u32[]{:S(2)}) collective-permute-start(bf16[256,1024]{1,0:T(8,128)(2,1)} %get-tuple-element.32.refs_1_), channel_id=1, source_target_pairs={{0,24},{8,0},{16,8},{24,16},{32,56},{40,32},{48,40},{56,48},{64,88... | collective-permute-start | bytes 1572872 | tf_op jit(solution)/shard_map/ppermute | solution.py:370
  22.1 10.8 %collective-permute-done.5.refs_6_.refs_14_ = bf16[256,1024]{1,0:T(8,128)(2,1)S(1)} collective-permute-done((bf16[256,1024]{1,0:T(8,128)(2,1)}, bf16[256,1024]{1,0:T(8,128)(2,1)S(1)}, u32[]{:S(2)}, u32[]{:S(2)}) %collective-permute-start.5) | collective-permute-done | bytes 524320 | tf_op jit(solution)/shard_map/ppermute | solution.py:370
  32.8 2.8 %collective-permute-start.8 = (bf16[256,1024]{1,0:T(8,128)(2,1)}, bf16[256,1024]{1,0:T(8,128)(2,1)S(1)}, u32[]{:S(2)}, u32[]{:S(2)}) collective-permute-start(bf16[256,1024]{1,0:T(8,128)(2,1)} %get-tuple-element.31.refs_0_), channel_id=1, source_target_pairs={{0,96},{8,104},{16,112},{24,120},{32,0},{40,8},{48,16},{56,24},{64... | collective-permute-start | bytes 1572872 | tf_op jit(solution)/shard_map/ppermute | solution.py:374
  36.5 2.0 %collective-permute-start.29 = (bf16[256,1024]{1,0:T(8,128)(2,1)S(1)}, bf16[256,1024]{1,0:T(8,128)(2,1)S(1)}, u32[]{:S(2)}, u32[]{:S(2)}) collective-permute-start(bf16[256,1024]{1,0:T(8,128)(2,1)S(1)} %collective-permute-done.28.refs_6_), channel_id=1, source_target_pairs={{0,8},{8,16},{16,24},{24,0},{32,40},{40,48},{48,56},{56,32},{64,72... | collective-permute-start | bytes 1572872 | tf_op jit(solution)/shard_map/ppermute | solution.py:370
  38.5 9.8 %collective-permute-done.8.refs_10_.refs_18_ = bf16[256,1024]{1,0:T(8,128)(2,1)S(1)} collective-permute-done((bf16[256,1024]{1,0:T(8,128)(2,1)}, bf16[256,1024]{1,0:T(8,128)(2,1)S(1)}, u32[]{:S(2)}, u32[]{:S(2)}) %collective-permute-start.8) | collective-permute-done | bytes 524320 | tf_op jit(solution)/shard_map/ppermute | solution.py:374
  49.3 8.7 %collective-permute-done.9.refs_11_.refs_19_ = bf16[256,1024]{1,0:T(8,128)(2,1)S(1)} collective-permute-done((bf16[256,1024]{1,0:T(8,128)(2,1)S(1)}, bf16[256,1024]{1,0:T(8,128)(2,1)S(1)}, u32[]{:S(2)}, u32[]{:S(2)}) %collective-permute-start.9) | collective-permute-done | bytes 524320 | tf_op jit(solution)/shard_map/ppermute | solution.py:374
  59.8 5.0 %collective-permute-done.11.refs_12_.refs_20_ = bf16[256,1024]{1,0:T(8,128)(2,1)S(1)} collective-permute-done((bf16[256,1024]{1,0:T(8,128)(2,1)S(1)}, bf16[256,1024]{1,0:T(8,128)(2,1)S(1)}, u32[]{:S(2)}, u32[]{:S(2)}) %collective-permute-start.11) | collective-permute-done | bytes 524320 | tf_op jit(solution)/shard_map/ppermute | solution.py:374
  64.8 1.8 collective-permute-start.12
  69.9 5.8 %collective-permute-done.13.refs_15_.refs_23_ = bf16[256,1024]{1,0:T(8,128)(2,1)S(1)} collective-permute-done((bf16[256,1024]{1,0:T(8,128)(2,1)S(1)}, bf16[256,1024]{1,0:T(8,128)(2,1)S(1)}, u32[]{:S(2)}, u32[]{:S(2)}) %collective-permute-start.13) | collective-permute-done | bytes 524320 | tf_op jit(solution)/shard_map/ppermute | solution.py:374
  75.7 2.3 %collective-permute-done.12.refs_13_.refs_21_ = bf16[256,1024]{1,0:T(8,128)(2,1)S(1)} collective-permute-done((bf16[256,1024]{1,0:T(8,128)(2,1)S(1)}, bf16[256,1024]{1,0:T(8,128)(2,1)S(1)}, u32[]{:S(2)}, u32[]{:S(2)}) %collective-permute-start.12) | collective-permute-done | bytes 524320 | tf_op jit(solution)/shard_map/ppermute | solution.py:374
  78.0 2.8 %shard_map.47 = (bf16[2,320,256]{2,1,0:T(8,128)(2,1)S(1)}, bf16[2,320,256]{2,1,0:T(8,128)(2,1)S(1)}) custom-call(bf16[256,1024]{1,0:T(8,128)(2,1)S(1)} %get-tuple-element.46.refs_0_, bf16[256,1024]{1,0:T(8,128)(2,1)S(1)} %collective-permute-done.25.refs_1_, bf16[256,1024]{1,0:T(8,128)(2,1)S(1)} %collective-permute-done.26.refs_2_, ...), custom_call_target="tpu_custom_call" | custom-call | tf_op jit(solution)/shard_map/pallas_call | solution.py:251
  80.7 4.3 %collective-permute-start.36 = (bf16[2,320,256]{2,1,0:T(8,128)(2,1)S(1)}, bf16[2,320,256]{2,1,0:T(8,128)(2,1)S(1)}, u32[]{:S(2)}, u32[]{:S(2)}) collective-permute-start(bf16[2,320,256]{2,1,0:T(8,128)(2,1)S(1)} %get-tuple-element.52), channel_id=1, source_target_pairs={{0,6},{1,7},{2,0},{3,1},{4,2},{5,3},{6,4},{7,5},{8,14},{9,15},{10,... | collective-permute-start | bytes 983048 | tf_op jit(solution)/shard_map/ppermute | solution.py:378
  85.0 6.8 %product.2 = (bf16[2,192,256]{2,1,0:T(8,128)(2,1)S(1)}, bf16[2,192,256]{2,1,0:T(8,128)(2,1)S(1)}, bf16[4,192,256]{2,1,0:T(8,128)(2,1)S(1)}, bf16[4,192,256]{2,1,0:T(8,128)(2,1)S(1)}, f32[4,192,256]{2,1,0:T(8,128)S(1)}) custom-call(bf16[256,1024]{1,0:T(8,128)(2,1)S(1)} %get-tuple-element.34.refs_0_.refs_8_, ...), custom_call_target="tpu_custom_call" | custom-call | tf_op jit(solution)/shard_map/product/pallas_call | solution.py:212
  92.3 1.6 collective-permute-start.14
  93.9 4.4 %product.3 = (bf16[2,320,256]{2,1,0:T(8,128)(2,1)S(1)}, bf16[2,320,256]{2,1,0:T(8,128)(2,1)S(1)}, bf16[2,320,256]{2,1,0:T(8,128)(2,1)S(1)}, bf16[2,320,256]{2,1,0:T(8,128)(2,1)S(1)}) custom-call(bf16[256,1024]{1,0:T(8,128)(2,1)S(1)} %get-tuple-element.46.refs_0_, bf16[256,1024]{1,0:T(8,128)(2,1)S(1)} %collective-permute-done.25.refs_1_, ...), custom_call_target="tpu_custom_call" | custom-call | tf_op jit(solution)/shard_map/product/pallas_call | solution.py:212
  98.4 3.3 %collective-permute-start.33 = (bf16[2,320,256]{2,1,0:T(8,128)(2,1)S(1)}, bf16[2,320,256]{2,1,0:T(8,128)(2,1)S(1)}, u32[]{:S(2)}, u32[]{:S(2)}) collective-permute-start(bf16[2,320,256]{2,1,0:T(8,128)(2,1)S(1)} %get-tuple-element.48), channel_id=1, source_target_pairs={{0,6},{1,7},{2,0},{3,1},{4,2},{5,3},{6,4},{7,5},{8,14},{9,15},{10,... | collective-permute-start | bytes 983048 | tf_op jit(solution)/shard_map/ppermute | solution.py:378
  101.8 2.0 %collective-permute-start.17 = (bf16[4,192,256]{2,1,0:T(8,128)(2,1)S(1)}, bf16[4,192,256]{2,1,0:T(8,128)(2,1)S(1)}, u32[]{:S(2)}, u32[]{:S(2)}) collective-permute-start(bf16[4,192,256]{2,1,0:T(8,128)(2,1)S(1)} %merge.3), channel_id=1, source_target_pairs={{0,6},{1,7},{2,0},{3,1},{4,2},{5,3},{6,4},{7,5},{8,14},{9,15},{10,... | collective-permute-start | bytes 1179656 | tf_op jit(solution)/shard_map/ppermute | solution.py:378
  104.1 4.2 %collective-permute-done.34 = bf16[2,320,256]{2,1,0:T(8,128)(2,1)S(1)} collective-permute-done((bf16[2,320,256]{2,1,0:T(8,128)(2,1)S(1)}, bf16[2,320,256]{2,1,0:T(8,128)(2,1)S(1)}, u32[]{:S(2)}, u32[]{:S(2)}) %collective-permute-start.34) | collective-permute-done | bytes 327712 | tf_op jit(solution)/shard_map/ppermute | solution.py:378
  108.4 6.9 %collective-permute-done.32.far_up = bf16[2,320,256]{2,1,0:T(8,128)(2,1)S(1)} collective-permute-done((bf16[2,320,256]{2,1,0:T(8,128)(2,1)S(1)}, bf16[2,320,256]{2,1,0:T(8,128)(2,1)S(1)}, u32[]{:S(2)}, u32[]{:S(2)}) %collective-permute-start.32) | collective-permute-done | bytes 327712 | tf_op jit(solution)/shard_map/ppermute | solution.py:378
  115.7 2.8 %shard_map.46.own = f32[4,320,256]{2,1,0:T(8,128)S(1)} custom-call(bf16[256,1024]{1,0:T(8,128)(2,1)S(1)} %get-tuple-element.46.refs_0_, bf16[256,1024]{1,0:T(8,128)(2,1)S(1)} %collective-permute-done.25.refs_1_, bf16[256,1024]{1,0:T(8,128)(2,1)S(1)} %collective-permute-done.26.refs_2_, bf16[256,1024]{1,0:T(8,128)(2,1)S(1)} %collective-permute-done.27.refs_3_, ...), custom_call_target="tpu_custom_call" | custom-call | tf_op jit(solution)/shard_map/pallas_call | solution.py:251
  118.5 3.3 %collective-permute-done.37.sum_down = bf16[2,320,256]{2,1,0:T(8,128)(2,1)S(1)} collective-permute-done((bf16[2,320,256]{2,1,0:T(8,128)(2,1)S(1)}, bf16[2,320,256]{2,1,0:T(8,128)(2,1)S(1)}, u32[]{:S(2)}, u32[]{:S(2)}) %collective-permute-start.37) | collective-permute-done | bytes 327712 | tf_op jit(solution)/shard_map/ppermute | solution.py:378
  121.8 5.9 %collective-permute-done.35.sum_up = bf16[2,320,256]{2,1,0:T(8,128)(2,1)S(1)} collective-permute-done((bf16[2,320,256]{2,1,0:T(8,128)(2,1)S(1)}, bf16[2,320,256]{2,1,0:T(8,128)(2,1)S(1)}, u32[]{:S(2)}, u32[]{:S(2)}) %collective-permute-start.35) | collective-permute-done | bytes 327712 | tf_op jit(solution)/shard_map/ppermute | solution.py:378
  128.5 4.6 %collective-permute-start.18 = (bf16[192,256]{1,0:T(8,128)(2,1)S(1)}, bf16[192,256]{1,0:T(8,128)(2,1)S(1)}, u32[]{:S(2)}, u32[]{:S(2)}) collective-permute-start(bf16[192,256]{1,0:T(8,128)(2,1)S(1)} %get-tuple-element.43), channel_id=1, source_target_pairs={{0,24},{8,0},{16,8},{24,16},{32,56},{40,32},{48,40},{56,48},{64,88... | collective-permute-start | bytes 294920 | tf_op jit(solution)/shard_map/ppermute | solution.py:370
  133.1 1.5 collective-permute-start.19
  134.6 3.4 %collective-permute-done.18.refs_2_ = bf16[192,256]{1,0:T(8,128)(2,1)S(1)} collective-permute-done((bf16[192,256]{1,0:T(8,128)(2,1)S(1)}, bf16[192,256]{1,0:T(8,128)(2,1)S(1)}, u32[]{:S(2)}, u32[]{:S(2)}) %collective-permute-start.18) | collective-permute-done | bytes 98336 | tf_op jit(solution)/shard_map/ppermute | solution.py:370
  140.7 4.5 %collective-permute-done.20.refs_4_ = bf16[192,256]{1,0:T(8,128)(2,1)S(1)} collective-permute-done((bf16[192,256]{1,0:T(8,128)(2,1)S(1)}, bf16[192,256]{1,0:T(8,128)(2,1)S(1)}, u32[]{:S(2)}, u32[]{:S(2)}) %collective-permute-start.20) | collective-permute-done | bytes 98336 | tf_op jit(solution)/shard_map/ppermute | solution.py:370
  146.2 3.4 %pack.2.refs_9_ = bf16[16,1,256,256]{3,2,1,0:T(8,128)(2,1)S(1)} custom-call(s32[2,4]{1,0:T(2,128)S(1)} %copy-done.3, bf16[320,256]{1,0:T(8,128)(2,1)S(1)} %get-tuple-element.53.refs_1_, bf16[320,256]{1,0:T(8,128)(2,1)S(1)} %collective-permute-done.38.refs_2_, bf16[320,256]{1,0:T(8,128)(2,1)S(1)} %collective-permute-done.39.refs_3_, ...), custom_call_target="tpu_custom_call" | custom-call | tf_op jit(solution)/shard_map/pack/pallas_call | solution.py:352
  151.1 33.9 %all_to_all.5 = bf16[16,1,256,256]{3,2,1,0:T(8,128)(2,1)S(1)} all-to-all(bf16[16,1,256,256]{3,2,1,0:T(8,128)(2,1)S(1)} %pack.3), channel_id=1, replica_groups=mesh['row'=16,'col'=8] {'row'}, dimensions={0} | all-to-all | bytes 4194304 | tf_op jit(solution)/shard_map/all_to_all | solution.py:434
  (82 shorter events, 17.4 us)
Async XLA Ops:
  2.6 14.7 %collective-permute-start.1 = (bf16[256,1024]{1,0:T(8,128)(2,1)}, bf16[256,1024]{1,0:T(8,128)(2,1)S(1)}, u32[]{:S(2)}, u32[]{:S(2)}) collective-permute-start(bf16[256,1024]{1,0:T(8,128)(2,1)} %get-tuple-element.33.refs_2_), channel_id=1, source_target_pairs={{0,24},{8,0},{16,8},{24,16},{32,56},{40,32},{48,40},{56,48},{64,88... | collective-permute-start | bytes 1572872 | tf_op jit(solution)/shard_map/ppermute | solution.py:370
  5.8 15.1 %collective-permute-start.7 = (bf16[256,1024]{1,0:T(8,128)(2,1)}, bf16[256,1024]{1,0:T(8,128)(2,1)S(1)}, u32[]{:S(2)}, u32[]{:S(2)}) collective-permute-start(bf16[256,1024]{1,0:T(8,128)(2,1)} %get-tuple-element.36), channel_id=1, source_target_pairs={{0,1},{1,0},{2,3},{3,2},{4,5},{5,4},{6,7},{7,6},{8,9},{9,8},{10,11... | collective-permute-start | bytes 1572872 | tf_op jit(solution)/shard_map/ppermute | solution.py:382
  5.8 16.2 %collective-permute-start.28 = (bf16[256,1024]{1,0:T(8,128)(2,1)}, bf16[256,1024]{1,0:T(8,128)(2,1)S(1)}, u32[]{:S(2)}, u32[]{:S(2)}) collective-permute-start(bf16[256,1024]{1,0:T(8,128)(2,1)} %get-tuple-element.32.refs_1_), channel_id=1, source_target_pairs={{0,8},{8,16},{16,24},{24,0},{32,40},{40,48},{48,56},{56,32},{64,72... | collective-permute-start | bytes 1572872 | tf_op jit(solution)/shard_map/ppermute | solution.py:370
  5.8 27.0 %collective-permute-start.5 = (bf16[256,1024]{1,0:T(8,128)(2,1)}, bf16[256,1024]{1,0:T(8,128)(2,1)S(1)}, u32[]{:S(2)}, u32[]{:S(2)}) collective-permute-start(bf16[256,1024]{1,0:T(8,128)(2,1)} %get-tuple-element.33.refs_2_), channel_id=1, source_target_pairs={{0,8},{8,16},{16,24},{24,0},{32,40},{40,48},{48,56},{56,32},{64,72... | collective-permute-start | bytes 1572872 | tf_op jit(solution)/shard_map/ppermute | solution.py:370
  6.4 29.2 %collective-permute-start.10 = (bf16[256,1024]{1,0:T(8,128)(2,1)}, bf16[256,1024]{1,0:T(8,128)(2,1)S(1)}, u32[]{:S(2)}, u32[]{:S(2)}) collective-permute-start(bf16[256,1024]{1,0:T(8,128)(2,1)} %get-tuple-element.31.refs_0_), channel_id=1, source_target_pairs={{0,32},{8,40},{16,48},{24,56},{32,64},{40,72},{48,80},{56,88},{64,... | collective-permute-start | bytes 1572872 | tf_op jit(solution)/shard_map/ppermute | solution.py:374
  17.3 18.3 %collective-permute-start.26 = (bf16[256,1024]{1,0:T(8,128)(2,1)}, bf16[256,1024]{1,0:T(8,128)(2,1)S(1)}, u32[]{:S(2)}, u32[]{:S(2)}) collective-permute-start(bf16[256,1024]{1,0:T(8,128)(2,1)} %get-tuple-element.32.refs_1_), channel_id=1, source_target_pairs={{0,24},{8,0},{16,8},{24,16},{32,56},{40,32},{48,40},{56,48},{64,88... | collective-permute-start | bytes 1572872 | tf_op jit(solution)/shard_map/ppermute | solution.py:370
  20.9 15.6 %collective-permute-start = (bf16[256,1024]{1,0:T(8,128)(2,1)}, bf16[256,1024]{1,0:T(8,128)(2,1)S(1)}, u32[]{:S(2)}, u32[]{:S(2)}) collective-permute-start(bf16[256,1024]{1,0:T(8,128)(2,1)} %get-tuple-element.33.refs_2_), channel_id=1, source_target_pairs={{0,1},{1,0},{2,3},{3,2},{4,5},{5,4},{6,7},{7,6},{8,9},{9,8},{10,11... | collective-permute-start | bytes 1572872 | tf_op jit(solution)/shard_map/ppermute | solution.py:382
  22.1 16.4 %collective-permute-start.25 = (bf16[256,1024]{1,0:T(8,128)(2,1)}, bf16[256,1024]{1,0:T(8,128)(2,1)S(1)}, u32[]{:S(2)}, u32[]{:S(2)}) collective-permute-start(bf16[256,1024]{1,0:T(8,128)(2,1)} %get-tuple-element.32.refs_1_), channel_id=1, source_target_pairs={{0,1},{1,0},{2,3},{3,2},{4,5},{5,4},{6,7},{7,6},{8,9},{9,8},{10,11... | collective-permute-start | bytes 1572872 | tf_op jit(solution)/shard_map/ppermute | solution.py:382
  32.8 15.4 %collective-permute-start.8 = (bf16[256,1024]{1,0:T(8,128)(2,1)}, bf16[256,1024]{1,0:T(8,128)(2,1)S(1)}, u32[]{:S(2)}, u32[]{:S(2)}) collective-permute-start(bf16[256,1024]{1,0:T(8,128)(2,1)} %get-tuple-element.31.refs_0_), channel_id=1, source_target_pairs={{0,96},{8,104},{16,112},{24,120},{32,0},{40,8},{48,16},{56,24},{64... | collective-permute-start | bytes 1572872 | tf_op jit(solution)/shard_map/ppermute | solution.py:374
  35.6 13.2 %collective-permute-start.3 = (bf16[256,1024]{1,0:T(8,128)(2,1)S(1)}, bf16[256,1024]{1,0:T(8,128)(2,1)S(1)}, u32[]{:S(2)}, u32[]{:S(2)}) collective-permute-start(bf16[256,1024]{1,0:T(8,128)(2,1)S(1)} %collective-permute-done.1.refs_2_.refs_10_), channel_id=1, source_target_pairs={{0,24},{8,0},{16,8},{24,16},{32,56},{40,32},{48,40},{56,48},{64,88... | collective-permute-start | bytes 1572872 | tf_op jit(solution)/shard_map/ppermute | solution.py:370
  35.6 22.4 %collective-permute-start.9 = (bf16[256,1024]{1,0:T(8,128)(2,1)S(1)}, bf16[256,1024]{1,0:T(8,128)(2,1)S(1)}, u32[]{:S(2)}, u32[]{:S(2)}) collective-permute-start(bf16[256,1024]{1,0:T(8,128)(2,1)S(1)} %collective-permute-done.7.refs_9_.refs_17_), channel_id=1, source_target_pairs={{0,96},{8,104},{16,112},{24,120},{32,0},{40,8},{48,16},{56,24},{64... | collective-permute-start | bytes 1572872 | tf_op jit(solution)/shard_map/ppermute | solution.py:374
  36.5 21.5 %collective-permute-start.29 = (bf16[256,1024]{1,0:T(8,128)(2,1)S(1)}, bf16[256,1024]{1,0:T(8,128)(2,1)S(1)}, u32[]{:S(2)}, u32[]{:S(2)}) collective-permute-start(bf16[256,1024]{1,0:T(8,128)(2,1)S(1)} %collective-permute-done.28.refs_6_), channel_id=1, source_target_pairs={{0,8},{8,16},{16,24},{24,0},{32,40},{40,48},{48,56},{56,32},{64,72... | collective-permute-start | bytes 1572872 | tf_op jit(solution)/shard_map/ppermute | solution.py:370
  38.5 20.8 %collective-permute-start.2 = (bf16[256,1024]{1,0:T(8,128)(2,1)S(1)}, bf16[256,1024]{1,0:T(8,128)(2,1)S(1)}, u32[]{:S(2)}, u32[]{:S(2)}) collective-permute-start(bf16[256,1024]{1,0:T(8,128)(2,1)S(1)} %collective-permute-done.1.refs_2_.refs_10_), channel_id=1, source_target_pairs={{0,1},{1,0},{2,3},{3,2},{4,5},{5,4},{6,7},{7,6},{8,9},{9,8},{10,11... | collective-permute-start | bytes 1572872 | tf_op jit(solution)/shard_map/ppermute | solution.py:382
  48.2 11.3 %collective-permute-start.6 = (bf16[256,1024]{1,0:T(8,128)(2,1)S(1)}, bf16[256,1024]{1,0:T(8,128)(2,1)S(1)}, u32[]{:S(2)}, u32[]{:S(2)}) collective-permute-start(bf16[256,1024]{1,0:T(8,128)(2,1)S(1)} %collective-permute-done.5.refs_6_.refs_14_), channel_id=1, source_target_pairs={{0,1},{1,0},{2,3},{3,2},{4,5},{5,4},{6,7},{7,6},{8,9},{9,8},{10,11... | collective-permute-start | bytes 1572872 | tf_op jit(solution)/shard_map/ppermute | solution.py:382
  48.8 16.0 %collective-permute-start.11 = (bf16[256,1024]{1,0:T(8,128)(2,1)S(1)}, bf16[256,1024]{1,0:T(8,128)(2,1)S(1)}, u32[]{:S(2)}, u32[]{:S(2)}) collective-permute-start(bf16[256,1024]{1,0:T(8,128)(2,1)S(1)} %collective-permute-done.10.refs_14_.refs_22_), channel_id=1, source_target_pairs={{0,32},{8,40},{16,48},{24,56},{32,64},{40,72},{48,80},{56,88},{64,... | collective-permute-start | bytes 1572872 | tf_op jit(solution)/shard_map/ppermute | solution.py:374
  58.0 17.6 %collective-permute-start.13 = (bf16[256,1024]{1,0:T(8,128)(2,1)S(1)}, bf16[256,1024]{1,0:T(8,128)(2,1)S(1)}, u32[]{:S(2)}, u32[]{:S(2)}) collective-permute-start(bf16[256,1024]{1,0:T(8,128)(2,1)S(1)} %collective-permute-done.7.refs_9_.refs_17_), channel_id=1, source_target_pairs={{0,32},{8,40},{16,48},{24,56},{32,64},{40,72},{48,80},{56,88},{64,... | collective-permute-start | bytes 1572872 | tf_op jit(solution)/shard_map/ppermute | solution.py:374
  59.3 16.4 %collective-permute-start.27 = (bf16[256,1024]{1,0:T(8,128)(2,1)S(1)}, bf16[256,1024]{1,0:T(8,128)(2,1)S(1)}, u32[]{:S(2)}, u32[]{:S(2)}) collective-permute-start(bf16[256,1024]{1,0:T(8,128)(2,1)S(1)} %collective-permute-done.26.refs_2_), channel_id=1, source_target_pairs={{0,1},{1,0},{2,3},{3,2},{4,5},{5,4},{6,7},{7,6},{8,9},{9,8},{10,11... | collective-permute-start | bytes 1572872 | tf_op jit(solution)/shard_map/ppermute | solution.py:382
  59.5 16.2 %collective-permute-start.4 = (bf16[256,1024]{1,0:T(8,128)(2,1)S(1)}, bf16[256,1024]{1,0:T(8,128)(2,1)S(1)}, u32[]{:S(2)}, u32[]{:S(2)}) collective-permute-start(bf16[256,1024]{1,0:T(8,128)(2,1)S(1)} %collective-permute-done.3.refs_4_.refs_12_), channel_id=1, source_target_pairs={{0,1},{1,0},{2,3},{3,2},{4,5},{5,4},{6,7},{7,6},{8,9},{9,8},{10,11... | collective-permute-start | bytes 1572872 | tf_op jit(solution)/shard_map/ppermute | solution.py:382
  64.8 13.1 %collective-permute-start.12 = (bf16[256,1024]{1,0:T(8,128)(2,1)S(1)}, bf16[256,1024]{1,0:T(8,128)(2,1)S(1)}, u32[]{:S(2)}, u32[]{:S(2)}) collective-permute-start(bf16[256,1024]{1,0:T(8,128)(2,1)S(1)} %collective-permute-done.9.refs_11_.refs_19_), channel_id=1, source_target_pairs={{0,96},{8,104},{16,112},{24,120},{32,0},{40,8},{48,16},{56,24},{64... | collective-permute-start | bytes 1572872 | tf_op jit(solution)/shard_map/ppermute | solution.py:374
  66.6 11.3 %collective-permute-start.30 = (bf16[256,1024]{1,0:T(8,128)(2,1)S(1)}, bf16[256,1024]{1,0:T(8,128)(2,1)S(1)}, u32[]{:S(2)}, u32[]{:S(2)}) collective-permute-start(bf16[256,1024]{1,0:T(8,128)(2,1)S(1)} %collective-permute-done.29.refs_4_), channel_id=1, source_target_pairs={{0,1},{1,0},{2,3},{3,2},{4,5},{5,4},{6,7},{7,6},{8,9},{9,8},{10,11... | collective-permute-start | bytes 1572872 | tf_op jit(solution)/shard_map/ppermute | solution.py:382
  80.7 23.1 %collective-permute-start.36 = (bf16[2,320,256]{2,1,0:T(8,128)(2,1)S(1)}, bf16[2,320,256]{2,1,0:T(8,128)(2,1)S(1)}, u32[]{:S(2)}, u32[]{:S(2)}) collective-permute-start(bf16[2,320,256]{2,1,0:T(8,128)(2,1)S(1)} %get-tuple-element.52), channel_id=1, source_target_pairs={{0,6},{1,7},{2,0},{3,1},{4,2},{5,3},{6,4},{7,5},{8,14},{9,15},{10,... | collective-permute-start | bytes 983048 | tf_op jit(solution)/shard_map/ppermute | solution.py:378
  92.3 9.5 %collective-permute-start.14 = (bf16[2,192,256]{2,1,0:T(8,128)(2,1)S(1)}, bf16[2,192,256]{2,1,0:T(8,128)(2,1)S(1)}, u32[]{:S(2)}, u32[]{:S(2)}) collective-permute-start(bf16[2,192,256]{2,1,0:T(8,128)(2,1)S(1)} %get-tuple-element.39), channel_id=1, source_target_pairs={{0,2},{1,3},{2,4},{3,5},{4,6},{5,7},{6,0},{7,1},{8,10},{9,11},{10,... | collective-permute-start | bytes 589832 | tf_op jit(solution)/shard_map/ppermute | solution.py:378
  93.9 14.4 %collective-permute-start.34 = (bf16[2,320,256]{2,1,0:T(8,128)(2,1)S(1)}, bf16[2,320,256]{2,1,0:T(8,128)(2,1)S(1)}, u32[]{:S(2)}, u32[]{:S(2)}) collective-permute-start(bf16[2,320,256]{2,1,0:T(8,128)(2,1)S(1)} %get-tuple-element.50), channel_id=1, source_target_pairs={{0,2},{1,3},{2,4},{3,5},{4,6},{5,7},{6,0},{7,1},{8,10},{9,11},{10,... | collective-permute-start | bytes 983048 | tf_op jit(solution)/shard_map/ppermute | solution.py:378
  98.3 17.0 %collective-permute-start.32 = (bf16[2,320,256]{2,1,0:T(8,128)(2,1)S(1)}, bf16[2,320,256]{2,1,0:T(8,128)(2,1)S(1)}, u32[]{:S(2)}, u32[]{:S(2)}) collective-permute-start(bf16[2,320,256]{2,1,0:T(8,128)(2,1)S(1)} %get-tuple-element.47), channel_id=1, source_target_pairs={{0,2},{1,3},{2,4},{3,5},{4,6},{5,7},{6,0},{7,1},{8,10},{9,11},{10,... | collective-permute-start | bytes 983048 | tf_op jit(solution)/shard_map/ppermute | solution.py:378
  98.4 20.1 %collective-permute-start.33 = (bf16[2,320,256]{2,1,0:T(8,128)(2,1)S(1)}, bf16[2,320,256]{2,1,0:T(8,128)(2,1)S(1)}, u32[]{:S(2)}, u32[]{:S(2)}) collective-permute-start(bf16[2,320,256]{2,1,0:T(8,128)(2,1)S(1)} %get-tuple-element.48), channel_id=1, source_target_pairs={{0,6},{1,7},{2,0},{3,1},{4,2},{5,3},{6,4},{7,5},{8,14},{9,15},{10,... | collective-permute-start | bytes 983048 | tf_op jit(solution)/shard_map/ppermute | solution.py:378
  101.8 26.6 %collective-permute-start.17 = (bf16[4,192,256]{2,1,0:T(8,128)(2,1)S(1)}, bf16[4,192,256]{2,1,0:T(8,128)(2,1)S(1)}, u32[]{:S(2)}, u32[]{:S(2)}) collective-permute-start(bf16[4,192,256]{2,1,0:T(8,128)(2,1)S(1)} %merge.3), channel_id=1, source_target_pairs={{0,6},{1,7},{2,0},{3,1},{4,2},{5,3},{6,4},{7,5},{8,14},{9,15},{10,... | collective-permute-start | bytes 1179656 | tf_op jit(solution)/shard_map/ppermute | solution.py:378
  103.8 24.6 %collective-permute-start.15 = (bf16[4,192,256]{2,1,0:T(8,128)(2,1)S(1)}, bf16[4,192,256]{2,1,0:T(8,128)(2,1)S(1)}, u32[]{:S(2)}, u32[]{:S(2)}) collective-permute-start(bf16[4,192,256]{2,1,0:T(8,128)(2,1)S(1)} %merge.2), channel_id=1, source_target_pairs={{0,2},{1,3},{2,4},{3,5},{4,6},{5,7},{6,0},{7,1},{8,10},{9,11},{10,... | collective-permute-start | bytes 1179656 | tf_op jit(solution)/shard_map/ppermute | solution.py:378
  108.3 13.5 %collective-permute-start.37 = (bf16[2,320,256]{2,1,0:T(8,128)(2,1)S(1)}, bf16[2,320,256]{2,1,0:T(8,128)(2,1)S(1)}, u32[]{:S(2)}, u32[]{:S(2)}) collective-permute-start(bf16[2,320,256]{2,1,0:T(8,128)(2,1)S(1)} %add_convert_fusion), channel_id=1, source_target_pairs={{0,6},{1,7},{2,0},{3,1},{4,2},{5,3},{6,4},{7,5},{8,14},{9,15},{10,... | collective-permute-start | bytes 983048 | tf_op jit(solution)/shard_map/ppermute | solution.py:378
  115.3 12.4 %collective-permute-start.35 = (bf16[2,320,256]{2,1,0:T(8,128)(2,1)S(1)}, bf16[2,320,256]{2,1,0:T(8,128)(2,1)S(1)}, u32[]{:S(2)}, u32[]{:S(2)}) collective-permute-start(bf16[2,320,256]{2,1,0:T(8,128)(2,1)S(1)} %add_convert_fusion.1), channel_id=1, source_target_pairs={{0,2},{1,3},{2,4},{3,5},{4,6},{5,7},{6,0},{7,1},{8,10},{9,11},{10,... | collective-permute-start | bytes 983048 | tf_op jit(solution)/shard_map/ppermute | solution.py:378
  127.9 10.2 %collective-permute-start.38 = (bf16[320,256]{1,0:T(8,128)(2,1)S(1)}, bf16[320,256]{1,0:T(8,128)(2,1)S(1)}, u32[]{:S(2)}, u32[]{:S(2)}) collective-permute-start(bf16[320,256]{1,0:T(8,128)(2,1)S(1)} %get-tuple-element.54), channel_id=1, source_target_pairs={{0,24},{8,0},{16,8},{24,16},{32,56},{40,32},{48,40},{56,48},{64,88... | collective-permute-start | bytes 491528 | tf_op jit(solution)/shard_map/ppermute | solution.py:370
  128.2 10.4 %collective-permute-start.39 = (bf16[320,256]{1,0:T(8,128)(2,1)S(1)}, bf16[320,256]{1,0:T(8,128)(2,1)S(1)}, u32[]{:S(2)}, u32[]{:S(2)}) collective-permute-start(bf16[320,256]{1,0:T(8,128)(2,1)S(1)} %get-tuple-element.55), channel_id=1, source_target_pairs={{0,16},{8,24},{16,0},{24,8},{32,48},{40,56},{48,32},{56,40},{64,80... | collective-permute-start | bytes 491528 | tf_op jit(solution)/shard_map/ppermute | solution.py:370
  128.5 9.5 %collective-permute-start.18 = (bf16[192,256]{1,0:T(8,128)(2,1)S(1)}, bf16[192,256]{1,0:T(8,128)(2,1)S(1)}, u32[]{:S(2)}, u32[]{:S(2)}) collective-permute-start(bf16[192,256]{1,0:T(8,128)(2,1)S(1)} %get-tuple-element.43), channel_id=1, source_target_pairs={{0,24},{8,0},{16,8},{24,16},{32,56},{40,32},{48,40},{56,48},{64,88... | collective-permute-start | bytes 294920 | tf_op jit(solution)/shard_map/ppermute | solution.py:370
  (17 other events, 109.9 us)
